TPU v7x, 128 devices: a whole 4x4x4 slice. The times are simulated.
128 devices in a mesh: lat: 4 (over z_hi, core), lon: 32 (over y, z_lo, x).
Axes of the slice: x: 4, y: 4, z: 4 (z_hi: 2, z_lo: 2; z = z_hi * 2 + z_lo), core: 2. Of those that a mesh axis runs over, the one named last changes fastest.
Arguments:
- features: bfloat16 [8, 128, 1024, 256], P(None, 'lat', 'lon'), may hold values from -16 to 16
- band_points: int32 [128], replicated, may hold values from 256 to 1024, as said below
- survival_flags: int32 [8, 2], replicated, may hold values 0 or 1
- first_kernel_weight: bfloat16 [3, 3, 256, 256], replicated, may hold values from -0.125 to 0.125
- second_kernel_weight: bfloat16 [3, 3, 256, 256], replicated, may hold values from -0.125 to 0.125
Outputs:
- section_result: bfloat16 [8, 128, 1024, 256], P(None, 'lat', 'lon')
Inputs may be any that keep to these rules, and one draw needn't show every extreme that they name: `band_points`: the live points of a row are its first ones.
All inputs are finite; a program needn't handle non-finite values.
Results may differ from a plain program's by a relative error of at most 0.0006.
The roundings to bfloat16 on the way count: a program that leaves them out, or rounds other values in their place, can miss the bound.
Values may be sent and summed in bfloat16 or wider, within the bound.
No kernel may reach another device: no remote copies, remote signals or barrier semaphores. Data moves between devices by JAX's collectives and lax.ppermute only.
A program may use at most 320 MiB of HBM per device.

v0:
```python
import jax
import jax.numpy as jnp
from jax import lax
from jax.sharding import PartitionSpec as P

GROUPS = 32
FIRST_DILATION = 2
SECOND_DILATION = 4


EPS = 1e-05
KEEP_RATE = 0.8


def extended(array, sides, width, wrap):
    for axis, dim in sides:
        peers, length = (lax.axis_size(axis), array.shape[dim])
        up = [(i, (i + 1) % peers) for i in range(peers if wrap else peers - 1)]
        down = [(j, i) for i, j in up]
        last = lax.slice_in_dim(array, length - width, length, axis=dim)
        leading = lax.slice_in_dim(array, 0, width, axis=dim)
        before = lax.ppermute(last, axis, up)
        after = lax.ppermute(leading, axis, down)
        array = jnp.concatenate([before, array, after], axis=dim)
    return array


def widen_border(field_in, reach_cells):
    lat_padded = extended(field_in, (("lat", 1),), reach_cells, False)
    return extended(lat_padded, (("lon", 2),), reach_cells, True)


def live_cells(band_points, tile_rows, tile_cols, margin):
    lat_total = band_points.shape[0]
    lon_total = tile_cols * lax.axis_size("lon")
    row_index = (
        lax.axis_index("lat") * tile_rows
        - margin
        + jnp.arange(tile_rows + 2 * margin, dtype=jnp.int32)
    )
    col_index = (
        lax.axis_index("lon") * tile_cols
        - margin
        + jnp.arange(tile_cols + 2 * margin, dtype=jnp.int32)
    )
    col_index = jnp.mod(col_index, lon_total)
    matches = row_index[:, None] == jnp.arange(lat_total, dtype=jnp.int32)[None, :]
    row_points = jnp.sum(jnp.where(matches, band_points[None, :], 0), axis=1)
    return (col_index[None, :] < row_points[:, None]).astype(jnp.float32)


def statistics(values_in, live_mask, live_count, group_size):
    samples = values_in.shape[0]
    masked = values_in * live_mask[None, :, :, None]

    def group_total(chan_sums):
        return chan_sums.reshape(samples, GROUPS, group_size).sum(axis=2)

    group_means = lax.psum(group_total(jnp.sum(masked, axis=(1, 2))), ("lat", "lon")) / live_count
    shifted = values_in - jnp.repeat(group_means, group_size, axis=1)[:, None, None, :]
    squares = shifted * shifted * live_mask[None, :, :, None]
    group_vars = lax.psum(group_total(jnp.sum(squares, axis=(1, 2))), ("lat", "lon")) / live_count
    return (group_means, group_vars)


def activate(values_in, group_means, group_vars, live_mask, group_size):
    centre = jnp.repeat(group_means, group_size, axis=1)[:, None, None, :]
    inv_std = jnp.repeat(lax.rsqrt(group_vars + EPS), group_size, axis=1)[:, None, None, :]
    return (jax.nn.silu((values_in - centre) * inv_std) * live_mask[None, :, :, None]).astype(
        jnp.bfloat16
    )


def apply_kernel(padded, weight, dilation):
    out_rows = padded.shape[1] - 2 * dilation
    out_cols = padded.shape[2] - 2 * dilation
    summed = None
    for row_tap in range(3):
        for col_tap in range(3):
            shifted = padded[
                :,
                row_tap * dilation : row_tap * dilation + out_rows,
                col_tap * dilation : col_tap * dilation + out_cols,
                :,
            ]
            tap_term = jnp.einsum(
                "bijc,cd->bijd",
                shifted,
                weight[row_tap, col_tap],
                preferred_element_type=jnp.float32,
            )
            summed = tap_term if summed is None else summed + tap_term
    return summed


def residual_branch(padded, weight, dilation, kept):
    result = apply_kernel(padded, weight, dilation)
    return result * (kept.astype(jnp.float32) / KEEP_RATE)[:, None, None, None]


def per_device(features, band_points, survival_flags, first_kernel_weight, second_kernel_weight):
    tile_rows = features.shape[1]
    tile_cols = features.shape[2]
    group_size = features.shape[3] // GROUPS
    live_count = jnp.sum(band_points).astype(jnp.float32) * group_size
    live_inner = live_cells(band_points, tile_rows, tile_cols, 0)
    initial_feature_map = features.astype(jnp.float32)
    first_means, first_vars = statistics(initial_feature_map, live_inner, live_count, group_size)
    first_hidden = activate(initial_feature_map, first_means, first_vars, live_inner, group_size)
    first_result = (
        initial_feature_map
        + residual_branch(
            widen_border(first_hidden, FIRST_DILATION),
            first_kernel_weight,
            FIRST_DILATION,
            survival_flags[:, 0],
        )
    ).astype(jnp.bfloat16)
    first_result = lax.optimization_barrier(first_result)
    first_feature_map = first_result.astype(jnp.float32)
    second_means, second_vars = statistics(first_feature_map, live_inner, live_count, group_size)
    second_hidden = activate(first_feature_map, second_means, second_vars, live_inner, group_size)
    section_result = first_feature_map + residual_branch(
        widen_border(second_hidden, SECOND_DILATION),
        second_kernel_weight,
        SECOND_DILATION,
        survival_flags[:, 1],
    )
    return section_result.astype(jnp.bfloat16)


def solution(mesh):
    in_specs = (P(None, "lat", "lon", None), P(), P(), P(), P())
    out_specs = P(None, "lat", "lon", None)
    return jax.shard_map(
        per_device, mesh=mesh, in_specs=in_specs, out_specs=out_specs, check_vma=False
    )
```

profile of v0, /device:TPU:1, one launch (start us, length us, event | category | flops | bytes accessed | tf_op | source)
XLA Modules:
  0.0 468.8 jit_solution(17577725118338050617)
XLA Ops:
  0.0 0.8 select_reduce_fusion
  0.8 0.1 compare_convert_fusion
  0.9 3.1 fusion.22
  4.0 0.1 reshape.85
  4.1 0.1 reduce_sum.92
  4.2 68.7 %psum.28 = f32[8,32]{1,0:T(8,128)S(1)} all-reduce(f32[8,32]{1,0:T(8,128)S(1)} %reduce_sum.92), channel_id=1, replica_groups=mesh['lat'=4,'lon'=32] {'lat','lon'}, use_global_device_ids=true, to_apply=%region_3.4 | all-reduce | flops 256 | bytes 2048 | tf_op jit(solution)/shard_map/psum | solution.py:59
  72.9 1.3 reduce_sum.93
  74.9 0.1 broadcast_in_dim.22
  75.0 0.1 sub.12
  75.1 0.0 copy-start.2
  75.1 3.7 fusion.21
  78.8 0.1 reshape.86
  78.9 0.1 reduce_sum.95
  79.0 62.6 %psum.29 = f32[8,32]{1,0:T(8,128)S(1)} all-reduce(f32[8,32]{1,0:T(8,128)S(1)} %reduce_sum.95), channel_id=1, replica_groups=mesh['lat'=4,'lon'=32] {'lat','lon'}, use_global_device_ids=true, to_apply=%region_7.8 | all-reduce | flops 256 | bytes 2048 | tf_op jit(solution)/shard_map/psum | solution.py:62
  141.6 0.1 broadcast_in_dim.23
  141.7 0.1 mul.103
  141.9 4.3 fusion.12
  146.2 3.8 collective-permute-start
  150.1 0.0 copy-start.4
  150.1 1.9 collective-permute-start.1
  152.0 4.5 fusion.84
  156.5 2.8 collective-permute-done.1
  159.3 0.5 pad_maximum_fusion.5
  159.7 1.0 collective-permute-start.2
  160.8 5.2 %collective-permute-start.3 = (bf16[8,36,2,256]{3,2,1,0:T(2,128)(2,1)S(1)}, bf16[8,36,2,256]{3,2,1,0:T(2,128)(2,1)S(1)}, u32[]{:S(2)}, u32[]{:S(2)}) collective-permute-start(bf16[8,36,2,256]{3,2,1,0:T(2,128)(2,1)S(1)} %get-tuple-element.11), channel_id=1, source_target_pairs={{1,0},{2,1},{3,2},{4,3},{5,4},{6,5},{7,6},{8,7},{9,8},{10,9},{11,1... | collective-permute-start | bytes 884744 | tf_op jit(solution)/shard_map/ppermute | solution.py:23
  165.9 4.5 fusion.34
  170.4 4.5 fusion.38
  174.9 7.4 %pad_maximum_fusion.1 = (bf16[8,36,34,256]{3,2,1,0:T(8,128)(2,1)S(1)}, bf16[8,36,34,256]{3,2,1,0:T(8,128)(2,1)S(1)}) fusion(bf16[8,36,2,256]{3,2,1,0:T(2,128)(2,1)S(1)} %collective-permute-done.3, bf16[8,2,32,256]{3,2,1,0:T(8,128)(2,1)S(1)} %collective-permute-done.1, bf16[8,32,32,256]{3,2,1,0:T(8,128)(2,1)S(1)} %fusion.12, ...), kind=kLoop, calls=%fused_computation.35 | loop fusion | flops 40108032 | bytes 15335424 | tf_op jit(solution)/shard_map/concatenate | solution.py:24
  182.3 4.9 %fusion.56 = f32[8,32,32,256]{3,2,1,0:T(8,128)} fusion(bf16[8,36,34,256]{3,2,1,0:T(8,128)(2,1)S(1)} %get-tuple-element.10, bf16[3,3,256,256]{3,2,1,0:T(8,128)(2,1)S(1)} %copy-done.2), kind=kOutput, calls=%fused_computation.66 | convolution fusion | flops 1073741824 | bytes 12713984 | tf_op jit(solution)/shard_map/bijc,cd->bijd/dot_general | solution.py:86
  187.2 4.4 fusion.60
  191.6 4.5 fusion.58
  196.1 4.5 fusion.62
  200.6 4.5 fusion.64
  205.1 26.7 %fusion.23 = bf16[8,32,32,256]{3,2,1,0:T(8,128)(2,1)} fusion(bf16[8,32,32,256]{3,2,1,0:T(8,128)(2,1)} %param.5, f32[8,32,32,256]{3,2,1,0:T(8,128)} %fusion.38, f32[8,32,32,256]{3,2,1,0:T(8,128)} %fusion.56, f32[8,32,32,256]{3,2,1,0:T(8,128)} %fusion.58, f32[8,32,32,256]{3,2,1,0:T(8,128)} %fusion.84, f32[8,32,32,256]{3,2,1,0:T(8,128)} %fusion.60, ...), kind=kOutput, calls=%fused_computation.29 | convolution fusion | flops 1098907648 | bytes 79823360 | tf_op jit(solution)/shard_map/bijc,cd->bijd/dot_general | solution.py:86
  231.8 3.1 fusion.24
  234.9 0.1 reshape.87
  235.0 0.1 reduce_sum.97
  235.1 62.3 %psum.30 = f32[8,32]{1,0:T(8,128)S(1)} all-reduce(f32[8,32]{1,0:T(8,128)S(1)} %reduce_sum.97), channel_id=1, replica_groups=mesh['lat'=4,'lon'=32] {'lat','lon'}, use_global_device_ids=true, to_apply=%region_10.11 | all-reduce | flops 256 | bytes 2048 | tf_op jit(solution)/shard_map/psum | solution.py:59
  297.4 0.1 broadcast_in_dim.24
  297.5 0.1 sub.15
  297.7 3.6 fusion.19
  301.2 0.1 reshape.88
  301.4 0.1 reduce_sum.99
  301.5 62.9 %psum.31 = f32[8,32]{1,0:T(8,128)S(1)} all-reduce(f32[8,32]{1,0:T(8,128)S(1)} %reduce_sum.99), channel_id=1, replica_groups=mesh['lat'=4,'lon'=32] {'lat','lon'}, use_global_device_ids=true, to_apply=%region_13.14 | all-reduce | flops 256 | bytes 2048 | tf_op jit(solution)/shard_map/psum | solution.py:62
  364.3 0.1 broadcast_in_dim.25
  364.4 0.1 mul.113
  364.6 4.3 fusion.17
  368.9 0.1 fusion.113
  369.0 4.1 collective-permute-start.4
  373.1 1.9 collective-permute-start.5
  375.0 4.5 fusion.74
  379.5 19.6 %collective-permute-done.5 = bf16[8,4,32,256]{3,2,1,0:T(8,128)(2,1)S(1)} collective-permute-done((bf16[8,4,32,256]{3,2,1,0:T(8,128)(2,1)S(1)}, bf16[8,4,32,256]{3,2,1,0:T(8,128)(2,1)S(1)}, u32[]{:S(2)}, u32[]{:S(2)}) %collective-permute-start.5) | collective-permute-done | bytes 524320 | tf_op jit(solution)/shard_map/ppermute | solution.py:23
  399.1 0.6 pad_maximum_fusion.2
  399.7 0.1 collective-permute-start.6
  399.8 5.9 %collective-permute-start.7 = (bf16[8,40,4,256]{3,2,1,0:T(4,128)(2,1)S(1)}, bf16[8,40,4,256]{3,2,1,0:T(4,128)(2,1)S(1)}, u32[]{:S(2)}, u32[]{:S(2)}) collective-permute-start(bf16[8,40,4,256]{3,2,1,0:T(4,128)(2,1)S(1)} %get-tuple-element.7), channel_id=1, source_target_pairs={{1,0},{2,1},{3,2},{4,3},{5,4},{6,5},{7,6},{8,7},{9,8},{10,9},{11,1... | collective-permute-start | bytes 1966088 | tf_op jit(solution)/shard_map/ppermute | solution.py:23
  405.7 4.4 fusion.26
  410.1 4.5 fusion.30
  414.6 4.5 pad_maximum_fusion
  419.1 4.9 %fusion.44 = f32[8,32,32,256]{3,2,1,0:T(8,128)} fusion(bf16[8,40,36,256]{3,2,1,0:T(8,128)(2,1)S(1)} %get-tuple-element.6, bf16[3,3,256,256]{3,2,1,0:T(8,128)(2,1)S(1)} %copy-done.3), kind=kOutput, calls=%fused_computation.54 | convolution fusion | flops 1073741824 | bytes 12713984 | tf_op jit(solution)/shard_map/bijc,cd->bijd/dot_general | solution.py:86
  424.0 4.5 fusion.48
  428.4 4.5 fusion.46
  432.9 4.5 fusion.50
  437.4 4.5 fusion.52
  441.9 26.7 %fusion.25 = bf16[8,32,32,256]{3,2,1,0:T(8,128)(2,1)} fusion(bf16[8,32,32,256]{3,2,1,0:T(8,128)(2,1)} %fusion.23, f32[8,32,32,256]{3,2,1,0:T(8,128)} %fusion.30, f32[8,32,32,256]{3,2,1,0:T(8,128)} %fusion.44, f32[8,32,32,256]{3,2,1,0:T(8,128)} %fusion.46, f32[8,32,32,256]{3,2,1,0:T(8,128)} %fusion.74, f32[8,32,32,256]{3,2,1,0:T(8,128)} %fusion.48, ...), kind=kOutput, calls=%fused_computation.31 | convolution fusion | flops 1098907648 | bytes 79823360 | tf_op jit(solution)/shard_map/bijc,cd->bijd/dot_general | solution.py:86
  (22 shorter events, 0.1 us)
Async XLA Ops:
  75.1 76.9 %copy-start.2 = (bf16[3,3,256,256]{3,2,1,0:T(8,128)(2,1)S(1)}, bf16[3,3,256,256]{3,2,1,0:T(8,128)(2,1)}, u32[]{:S(2)}) copy-start(bf16[3,3,256,256]{3,2,1,0:T(8,128)(2,1)} %param.8) | copy-start | bytes 3538948
  146.2 10.3 %collective-permute-start = (bf16[8,2,32,256]{3,2,1,0:T(8,128)(2,1)S(1)}, bf16[8,2,32,256]{3,2,1,0:T(8,128)(2,1)S(1)}, u32[]{:S(2)}, u32[]{:S(2)}) collective-permute-start(bf16[8,2,32,256]{3,2,1,0:T(8,128)(2,1)S(1)} %get-tuple-element.15), channel_id=1, source_target_pairs={{0,32},{32,64},{64,96},{1,33},{33,65},{65,97},{2,34},{34,66},{66,9... | collective-permute-start | bytes 786440 | tf_op jit(solution)/shard_map/ppermute | solution.py:22
  150.1 6.4 %copy-start.4 = (s32[8,2]{0,1:T(2,128)S(1)}, s32[8,2]{0,1:T(2,128)}, u32[]{:S(2)}) copy-start(s32[8,2]{0,1:T(2,128)} %param.7) | copy-start | bytes 196
  150.1 9.2 %collective-permute-start.1 = (bf16[8,2,32,256]{3,2,1,0:T(8,128)(2,1)S(1)}, bf16[8,2,32,256]{3,2,1,0:T(8,128)(2,1)S(1)}, u32[]{:S(2)}, u32[]{:S(2)}) collective-permute-start(bf16[8,2,32,256]{3,2,1,0:T(8,128)(2,1)S(1)} %get-tuple-element.16), channel_id=1, source_target_pairs={{32,0},{64,32},{96,64},{33,1},{65,33},{97,65},{34,2},{66,34},{98,6... | collective-permute-start | bytes 786440 | tf_op jit(solution)/shard_map/ppermute | solution.py:23
  159.7 15.1 %collective-permute-start.2 = (bf16[8,36,2,256]{3,2,1,0:T(2,128)(2,1)S(1)}, bf16[8,36,2,256]{3,2,1,0:T(2,128)(2,1)S(1)}, u32[]{:S(2)}, u32[]{:S(2)}) collective-permute-start(bf16[8,36,2,256]{3,2,1,0:T(2,128)(2,1)S(1)} %get-tuple-element.12), channel_id=1, source_target_pairs={{0,1},{1,2},{2,3},{3,4},{4,5},{5,6},{6,7},{7,8},{8,9},{9,10},{10,1... | collective-permute-start | bytes 884744 | tf_op jit(solution)/shard_map/ppermute | solution.py:22
  160.8 14.1 %collective-permute-start.3 = (bf16[8,36,2,256]{3,2,1,0:T(2,128)(2,1)S(1)}, bf16[8,36,2,256]{3,2,1,0:T(2,128)(2,1)S(1)}, u32[]{:S(2)}, u32[]{:S(2)}) collective-permute-start(bf16[8,36,2,256]{3,2,1,0:T(2,128)(2,1)S(1)} %get-tuple-element.11), channel_id=1, source_target_pairs={{1,0},{2,1},{3,2},{4,3},{5,4},{6,5},{7,6},{8,7},{9,8},{10,9},{11,1... | collective-permute-start | bytes 884744 | tf_op jit(solution)/shard_map/ppermute | solution.py:23
  182.3 13.8 %copy-start = (bf16[8,36,34,256]{3,2,1,0:T(8,128)(2,1)}, bf16[8,36,34,256]{3,2,1,0:T(8,128)(2,1)S(1)}, u32[]{:S(2)}) copy-start(bf16[8,36,34,256]{3,2,1,0:T(8,128)(2,1)S(1)} %get-tuple-element.9) | copy-start | bytes 15040516
  301.2 73.8 %copy-start.3 = (bf16[3,3,256,256]{3,2,1,0:T(8,128)(2,1)S(1)}, bf16[3,3,256,256]{3,2,1,0:T(8,128)(2,1)}, u32[]{:S(2)}) copy-start(bf16[3,3,256,256]{3,2,1,0:T(8,128)(2,1)} %param.9) | copy-start | bytes 3538948
  369.0 10.5 %collective-permute-start.4 = (bf16[8,4,32,256]{3,2,1,0:T(8,128)(2,1)S(1)}, bf16[8,4,32,256]{3,2,1,0:T(8,128)(2,1)S(1)}, u32[]{:S(2)}, u32[]{:S(2)}) collective-permute-start(bf16[8,4,32,256]{3,2,1,0:T(8,128)(2,1)S(1)} %get-tuple-element.13), channel_id=1, source_target_pairs={{0,32},{32,64},{64,96},{1,33},{33,65},{65,97},{2,34},{34,66},{66,9... | collective-permute-start | bytes 1572872 | tf_op jit(solution)/shard_map/ppermute | solution.py:22
  373.1 26.0 %collective-permute-start.5 = (bf16[8,4,32,256]{3,2,1,0:T(8,128)(2,1)S(1)}, bf16[8,4,32,256]{3,2,1,0:T(8,128)(2,1)S(1)}, u32[]{:S(2)}, u32[]{:S(2)}) collective-permute-start(bf16[8,4,32,256]{3,2,1,0:T(8,128)(2,1)S(1)} %get-tuple-element.14), channel_id=1, source_target_pairs={{32,0},{64,32},{96,64},{33,1},{65,33},{97,65},{34,2},{66,34},{98,6... | collective-permute-start | bytes 1572872 | tf_op jit(solution)/shard_map/ppermute | solution.py:23
  399.7 14.9 %collective-permute-start.6 = (bf16[8,40,4,256]{3,2,1,0:T(4,128)(2,1)S(1)}, bf16[8,40,4,256]{3,2,1,0:T(4,128)(2,1)S(1)}, u32[]{:S(2)}, u32[]{:S(2)}) collective-permute-start(bf16[8,40,4,256]{3,2,1,0:T(4,128)(2,1)S(1)} %get-tuple-element.8), channel_id=1, source_target_pairs={{0,1},{1,2},{2,3},{3,4},{4,5},{5,6},{6,7},{7,8},{8,9},{9,10},{10,1... | collective-permute-start | bytes 1966088 | tf_op jit(solution)/shard_map/ppermute | solution.py:22
  399.8 14.8 %collective-permute-start.7 = (bf16[8,40,4,256]{3,2,1,0:T(4,128)(2,1)S(1)}, bf16[8,40,4,256]{3,2,1,0:T(4,128)(2,1)S(1)}, u32[]{:S(2)}, u32[]{:S(2)}) collective-permute-start(bf16[8,40,4,256]{3,2,1,0:T(4,128)(2,1)S(1)} %get-tuple-element.7), channel_id=1, source_target_pairs={{1,0},{2,1},{3,2},{4,3},{5,4},{6,5},{7,6},{8,7},{9,8},{10,9},{11,1... | collective-permute-start | bytes 1966088 | tf_op jit(solution)/shard_map/ppermute | solution.py:23
  419.1 13.8 %copy-start.1 = (bf16[8,40,36,256]{3,2,1,0:T(8,128)(2,1)}, bf16[8,40,36,256]{3,2,1,0:T(8,128)(2,1)S(1)}, u32[]{:S(2)}) copy-start(bf16[8,40,36,256]{3,2,1,0:T(8,128)(2,1)S(1)} %get-tuple-element.5) | copy-start | bytes 17694724
where the time goes:
time: 476 us; the launch traced here: 469 us
  blocking collectives  257 us (54%)
  matrix products  126 us (26%)
  other arithmetic  37.6 us (8%)
  starting transfers between devices  23.9 us (5%)
  waiting for transfers between devices  22.4 us (5%)
    psum x2, blocking collectives, statistics(): lax.psum(group_total(jnp.sum(masked, axis=(1, 2))), ('lat', 'lon'))  131 us
    dot_general x18, matrix products, apply_kernel(): jnp.einsum('bijc,cd->bijd', shifted, weight[row_tap, col_tap], preferred_...  126 us
    psum x2, blocking collectives, statistics(): lax.psum(group_total(jnp.sum(squares, axis=(1, 2))), ('lat', 'lon'))  125 us
    ppermute x4, waiting for transfers between devices, extended(): after = lax.ppermute(leading, axis, down)  22.4 us
    ppermute x4, starting transfers between devices, extended(): after = lax.ppermute(leading, axis, down)  14.9 us
    concatenate x4, other arithmetic, extended(): array = jnp.concatenate([before, array, after], axis=dim)  13 us
  transfers between devices with their start and end apart: 8, of which 2 were waited for; matrix products, arithmetic and copies ran while one was open for 6% of the time, Pallas kernels for 0%

commit v1 on v0

v1 whole, which is shorter than its diff:
```python
import functools

import jax
import jax.numpy as jnp
from jax import lax
from jax.experimental import pallas as pl
from jax.experimental.pallas import tpu as pltpu
from jax.sharding import Mesh, PartitionSpec as P

GROUPS = 32
FIRST_DILATION = 2
SECOND_DILATION = 4
EPS = 1e-05
KEEP_RATE = 0.8

LAT = ("zh", "core")
LON = ("y", "zl", "x")
CHIPS = ("zh", "y", "zl", "x")
LANES = 128
VMEM_LIMIT = 56 * 1024 * 1024
HIGHEST = lax.Precision.HIGHEST


def exact_dot(a, b):
    return jnp.dot(a, b, precision=HIGHEST, preferred_element_type=jnp.float32)


def fold_matrix(channels, slot):
    size = channels // GROUPS
    row = lax.broadcasted_iota(jnp.int32, (channels, LANES), 0)
    col = lax.broadcasted_iota(jnp.int32, (channels, LANES), 1)
    low = row - (col - slot * GROUPS) * size
    inside = (col >= slot * GROUPS) & (col < (slot + 1) * GROUPS)
    return jnp.where(inside & (low >= 0) & (low < size), 1.0, 0.0).astype(jnp.float32)


def spread_matrix(channels, slot):
    size = channels // GROUPS
    row = lax.broadcasted_iota(jnp.int32, (LANES, channels), 0)
    col = lax.broadcasted_iota(jnp.int32, (LANES, channels), 1)
    low = col - (row - slot * GROUPS) * size
    inside = (row >= slot * GROUPS) & (row < (slot + 1) * GROUPS)
    return jnp.where(inside & (low >= 0) & (low < size), 1.0, 0.0).astype(jnp.float32)


def store_group_stats(sums_ref, squares_ref, count, out_ref):
    samples, channels = sums_ref.shape
    slots = LANES // GROUPS
    per_channel = jnp.maximum(count, 1.0)
    total = jnp.zeros((samples // slots, LANES), jnp.float32)
    spread = jnp.zeros((samples // slots, LANES), jnp.float32)
    size = channels // GROUPS
    for slot in range(slots):
        pick = [slot + k * slots for k in range(samples // slots)]
        sums = jnp.concatenate([sums_ref[b : b + 1] for b in pick], axis=0)
        squares = jnp.concatenate([squares_ref[b : b + 1] for b in pick], axis=0)
        fold = fold_matrix(channels, slot)
        group_sum = exact_dot(sums, fold)
        centre = exact_dot(group_sum, spread_matrix(channels, slot)) / (per_channel * size)
        offset = sums / per_channel - centre
        total = total + group_sum
        spread = spread + exact_dot(squares + count * offset * offset, fold)
    out_ref[0] = total
    out_ref[1] = spread


def row_statistics(rows, limits, count, sums_ref, squares_ref, b):
    cols, channels = rows(0).shape
    lane = lax.broadcasted_iota(jnp.int32, (cols, channels), 0)
    acc = jnp.zeros((8, channels), jnp.float32)
    for h in range(len(limits)):
        value = jnp.where(lane < limits[h], rows(h), 0.0)
        acc = acc + value.reshape(cols // 8, 8, channels).sum(axis=0)
    sums = acc.sum(axis=0, keepdims=True)
    centre = sums / jnp.maximum(count, 1.0)
    acc = jnp.zeros((8, channels), jnp.float32)
    for h in range(len(limits)):
        value = jnp.where(lane < limits[h], rows(h) - centre, 0.0)
        acc = acc + (value * value).reshape(cols // 8, 8, channels).sum(axis=0)
    sums_ref[pl.ds(b, 1)] = sums
    squares_ref[pl.ds(b, 1)] = acc.sum(axis=0, keepdims=True)


def live_in_tile(points_ref, origin, rows, cols, margin):
    return [jnp.clip(points_ref[margin + h] - origin, 0, cols) for h in range(rows)]


def stats_kernel(points_ref, cols_ref, x_ref, out_ref, sums_ref, squares_ref):
    b = pl.program_id(0)
    _, rows, cols, _ = x_ref.shape
    limits = live_in_tile(points_ref, cols_ref[1], rows, cols, FIRST_DILATION)
    count = functools.reduce(lambda a, c: a + c, limits).astype(jnp.float32)
    row_statistics(
        lambda h: x_ref[0, h].astype(jnp.float32), limits, count, sums_ref, squares_ref, b
    )

    @pl.when(b == pl.num_programs(0) - 1)
    def _():
        store_group_stats(sums_ref, squares_ref, count, out_ref)


def local_statistics(x, points, cols):
    samples, rows, width, channels = x.shape
    return pl.pallas_call(
        stats_kernel,
        out_shape=jax.ShapeDtypeStruct((2, samples * GROUPS // LANES, LANES), jnp.float32),
        grid_spec=pltpu.PrefetchScalarGridSpec(
            num_scalar_prefetch=2,
            grid=(samples,),
            in_specs=[pl.BlockSpec((1, rows, width, channels), lambda b, *_: (b, 0, 0, 0))],
            out_specs=pl.BlockSpec(
                (2, samples * GROUPS // LANES, LANES), lambda b, *_: (0, 0, 0)
            ),
            scratch_shapes=[
                pltpu.VMEM((samples, channels), jnp.float32),
                pltpu.VMEM((samples, channels), jnp.float32),
            ],
        ),
        compiler_params=pltpu.CompilerParams(
            dimension_semantics=("arbitrary",), vmem_limit_bytes=VMEM_LIMIT
        ),
        cost_estimate=pl.CostEstimate(
            flops=8 * x.size, bytes_accessed=2 * x.size, transcendentals=0
        ),
        name="stats",
    )(points, cols, x)


def combine_statistics(parts_ref, counts_ref, norm_ref, samples, channels):
    slots = LANES // GROUPS
    counts = counts_ref[...][:, None, :]
    sums = parts_ref[:, 0]
    squares = parts_ref[:, 1]
    count = counts.sum(axis=0)
    mean = sums.sum(axis=0) / count
    offset = sums / jnp.maximum(counts, 1.0) - mean[None]
    var = (squares + counts * offset * offset).sum(axis=0) / count
    half = 0.5 * lax.rsqrt(var + EPS)
    for slot in range(slots):
        spread = spread_matrix(channels, slot)
        means = exact_dot(mean, spread)
        halves = exact_dot(half, spread)
        for k in range(samples // slots):
            norm_ref[slot + k * slots, 0:1] = means[k : k + 1]
            norm_ref[slot + k * slots, 1:2] = halves[k : k + 1]


def conv_kernel(
    dilation, chunk, with_stats, points_ref, cols_ref, scale_ref, parts_ref, counts_ref, x_ref, top_ref, bottom_ref,
    left_ref, right_ref, w_ref, out_ref, *rest
):
    if with_stats:
        stats_ref, norm_ref, act_ref, sums_ref, squares_ref = rest
    else:
        norm_ref, act_ref = rest
    b = pl.program_id(0)
    d = dilation
    _, rows, cols, channels = x_ref.shape

    @pl.when(b == 0)
    def _():
        combine_statistics(parts_ref, counts_ref, norm_ref, pl.num_programs(0), channels)

    mean = norm_ref[b, 0:1]
    half = norm_ref[b, 1:2]

    def activated(value):
        t = (value.astype(jnp.float32) - mean) * half
        return t + t * jnp.tanh(t)

    column = lax.broadcasted_iota(jnp.int32, (cols, channels), 0)
    edge = lax.broadcasted_iota(jnp.int32, (d, channels), 0)
    left = activated(left_ref[0])
    right = activated(right_ref[0])
    for e in range(rows + 2 * d):
        if e < d:
            source = top_ref[0, e]
        elif e < rows + d:
            source = x_ref[0, e - d]
        else:
            source = bottom_ref[0, e - rows - d]
        points = points_ref[e]
        mid = jnp.where(column < points - cols_ref[1], activated(source), 0.0)
        lhs = jnp.where(edge < points - cols_ref[0], left[e * d : (e + 1) * d], 0.0)
        rhs = jnp.where(edge < points - cols_ref[2], right[e * d : (e + 1) * d], 0.0)
        before = jnp.concatenate([lhs, mid[: cols - d]], axis=0)
        after = jnp.concatenate([mid[d:], rhs], axis=0)
        act_ref[e, :, 0:channels] = before.astype(jnp.bfloat16)
        act_ref[e, :, channels : 2 * channels] = mid.astype(jnp.bfloat16)
        act_ref[e, :, 2 * channels :] = after.astype(jnp.bfloat16)

    scale = scale_ref[b]
    for start in range(0, rows, chunk):
        acc = None
        for tap in range(3):
            lo = start + tap * d
            taken = act_ref[lo : lo + chunk].reshape(chunk * cols, 3 * channels)
            term = jnp.dot(taken, w_ref[tap], preferred_element_type=jnp.float32)
            acc = term if acc is None else acc + term
        base = x_ref[0, start : start + chunk].astype(jnp.float32)
        result = base + scale * acc.reshape(chunk, cols, channels)
        out_ref[0, start : start + chunk] = result.astype(jnp.bfloat16)

    if with_stats:
        limits = live_in_tile(points_ref, cols_ref[1], rows, cols, d)
        count = functools.reduce(lambda a, c: a + c, limits).astype(jnp.float32)
        row_statistics(
            lambda h: out_ref[0, h].astype(jnp.float32), limits, count, sums_ref, squares_ref, b
        )

        @pl.when(b == pl.num_programs(0) - 1)
        def _():
            store_group_stats(sums_ref, squares_ref, count, stats_ref)


def convolve(x, halos, weight, parts, counts, points, cols, scale, dilation, with_stats):
    samples, rows, width, channels = x.shape
    d = dilation
    top, bottom, left, right = halos
    out_shape = [jax.ShapeDtypeStruct(x.shape, jnp.bfloat16)]
    out_specs = [pl.BlockSpec((1, rows, width, channels), lambda b, *_: (b, 0, 0, 0))]
    scratch = [
        pltpu.VMEM((samples, 2, channels), jnp.float32),
        pltpu.VMEM((rows + 2 * d, width, 3 * channels), jnp.bfloat16),
    ]
    if with_stats:
        shape = (2, samples * GROUPS // LANES, LANES)
        out_shape.append(jax.ShapeDtypeStruct(shape, jnp.float32))
        out_specs.append(pl.BlockSpec(shape, lambda b, *_: (0, 0, 0)))
        scratch += [pltpu.VMEM((samples, channels), jnp.float32)] * 2
    edge = (rows + 2 * d) * d
    return pl.pallas_call(
        functools.partial(conv_kernel, d, 8, with_stats),
        out_shape=out_shape,
        grid_spec=pltpu.PrefetchScalarGridSpec(
            num_scalar_prefetch=3,
            grid=(samples,),
            in_specs=[
                pl.BlockSpec(parts.shape, lambda b, *_: (0, 0, 0, 0)),
                pl.BlockSpec(counts.shape, lambda b, *_: (0, 0)),
                pl.BlockSpec((1, rows, width, channels), lambda b, *_: (b, 0, 0, 0)),
                pl.BlockSpec((1, d, width, channels), lambda b, *_: (b, 0, 0, 0)),
                pl.BlockSpec((1, d, width, channels), lambda b, *_: (b, 0, 0, 0)),
                pl.BlockSpec((1, edge, channels), lambda b, *_: (b, 0, 0)),
                pl.BlockSpec((1, edge, channels), lambda b, *_: (b, 0, 0)),
                pl.BlockSpec(weight.shape, lambda b, *_: (0, 0, 0)),
            ],
            out_specs=out_specs,
            scratch_shapes=scratch,
        ),
        compiler_params=pltpu.CompilerParams(
            dimension_semantics=("arbitrary",), vmem_limit_bytes=VMEM_LIMIT
        ),
        cost_estimate=pl.CostEstimate(
            flops=2 * x.size * 9 * channels, bytes_accessed=5 * x.size, transcendentals=2 * x.size
        ),
        name="conv%d" % d,
    )(points, cols, scale, parts, counts, x, top, bottom, left, right, weight)


def exchange(x, d):
    samples, rows, width, channels = x.shape
    lat, lon = lax.axis_size(LAT), lax.axis_size(LON)
    up = [(i, i + 1) for i in range(lat - 1)]
    down = [(i + 1, i) for i in range(lat - 1)]
    top = lax.ppermute(x[:, rows - d :], LAT, up)
    bottom = lax.ppermute(x[:, :d], LAT, down)
    east = [(i, (i + 1) % lon) for i in range(lon)]
    west = [((i + 1) % lon, i) for i in range(lon)]

    def packed(lo, hi):
        strip = jnp.concatenate([top[:, :, lo:hi], x[:, :, lo:hi], bottom[:, :, lo:hi]], axis=1)
        return strip.reshape(samples, (rows + 2 * d) * d, channels)

    left = lax.ppermute(packed(width - d, width), LON, east)
    right = lax.ppermute(packed(0, d), LON, west)
    return top, bottom, left, right


def share_statistics(local, own_count, other_count, core_axis="core"):
    other = lax.ppermute(local, core_axis, [(0, 1), (1, 0)])
    both = own_count + other_count
    gap = local[0] / jnp.maximum(own_count, 1.0) - other[0] / jnp.maximum(other_count, 1.0)
    squares = local[1] + other[1] + gap * gap * (own_count * other_count / jnp.maximum(both, 1.0))
    merged = jnp.stack([local[0] + other[0], squares])
    chips = lax.axis_size(CHIPS)
    return lax.all_to_all(jnp.broadcast_to(merged[None], (chips, *merged.shape)), CHIPS, 0, 0)


def per_device(features, band_points, survival_flags, first_kernel_weight, second_kernel_weight):
    _, rows, width, channels = features.shape
    lat_total = band_points.shape[0]
    lat, lon = lax.axis_size(LAT), lax.axis_size(LON)
    i, j = lax.axis_index(LAT), lax.axis_index(LON)
    lon_total = lon * width
    origin = j * width

    def placed(d):
        padded = jnp.pad(band_points, (d, d))
        points = lax.dynamic_slice(padded, (i * rows,), (rows + 2 * d,))
        cols = jnp.stack([(origin - d) % lon_total, origin, (origin + width) % lon_total])
        return points, cols.astype(jnp.int32)

    group_size = channels // GROUPS
    starts = jnp.arange(lon, dtype=jnp.int32) * width
    inside = jnp.clip(band_points[:, None] - starts[None, :], 0, width)
    tile_counts = inside.reshape(lat, rows, lon).sum(axis=1) * group_size
    tile_counts = tile_counts.astype(jnp.float32)
    core_counts = tile_counts.reshape(lax.axis_size("zh"), lax.axis_size("core"), lon)
    chip_counts = core_counts.sum(axis=1).reshape(-1, 1)
    counts = jnp.broadcast_to(chip_counts, (chip_counts.shape[0], LANES))
    own_count = tile_counts[i, j]
    both_count = core_counts.sum(axis=1)[lax.axis_index("zh"), j]
    other_count = both_count - own_count
    scales = survival_flags.astype(jnp.float32) / KEEP_RATE

    points, cols = placed(FIRST_DILATION)
    local = local_statistics(features, points, cols)
    halos = exchange(features, FIRST_DILATION)
    parts = share_statistics(local, own_count, other_count)
    weight = first_kernel_weight.reshape(3, 3 * channels, channels)
    first, local = convolve(
        features, halos, weight, parts, counts, points, cols, scales[:, 0], FIRST_DILATION, True
    )

    points, cols = placed(SECOND_DILATION)
    halos = exchange(first, SECOND_DILATION)
    parts = share_statistics(local, own_count, other_count)
    weight = second_kernel_weight.reshape(3, 3 * channels, channels)
    (section,) = convolve(
        first, halos, weight, parts, counts, points, cols, scales[:, 1], SECOND_DILATION, False
    )
    return section


def solution(mesh):
    grid = Mesh(mesh.devices.reshape(2, 2, 4, 2, 4), (LAT + LON))
    spec = P(None, LAT, LON, None)
    return jax.shard_map(
        per_device, mesh=grid, in_specs=(spec, P(), P(), P(), P()), out_specs=spec, check_vma=False
    )
```

time: 476 us -> 144 us (0.30); the launches traced: 469 us -> 143 us
  blocking collectives: 257 us -> 0 us
  matrix products: 126 us -> 0 us
  Pallas kernels: 0 us -> 46.9 us
  other arithmetic: 37.6 us -> 3.15 us
  starting transfers between devices: 23.9 us -> 39.2 us
  local copies, waits for them, and re-layouts: 1.39 us -> 14.5 us
  waiting for transfers between devices: 22.4 us -> 35 us
    psum x4 -> x0, blocking collectives: 257 us -> none  [the longest x2 131 us: statistics(): lax.psum(group_total(jnp.sum(masked, axis=(1, 2))), ('lat', 'lon'))]
    dot_general x18 -> x0, matrix products: 126 us -> none  [apply_kernel(): jnp.einsum('bijc,cd->bijd', shifted, weight[row_tap, col_tap], preferred_...]
    pallas_call x0 -> x3, Pallas kernels: none -> 46.9 us  [the longest x2 37.9 us: convolve(): pl.pallas_call(functools.partial(conv_kernel, d, 8, with_stats), out_shap...]
    all_to_all x0 -> x2, waiting for transfers between devices: none -> 15.9 us  [share_statistics(): lax.all_to_all(jnp.broadcast_to(merged[None], (chips, *merged.shape)), CH...]
    reduce_sum x10 -> x2, other arithmetic: 15.9 us -> 0.12 us  [the longest x1 0.1 us: per_device(): tile_counts = inside.reshape(lat, rows, lon).sum(axis=1) * group_size]
    concatenate x4, other arithmetic: 13 us -> 1.01 us  [packed(): jnp.concatenate([top[:, :, lo:hi], x[:, :, lo:hi], bottom[:, :, lo:hi]],...]
    all_to_all x0 -> x2, starting transfers between devices: none -> 11.4 us  [share_statistics(): lax.all_to_all(jnp.broadcast_to(merged[None], (chips, *merged.shape)), CH...]
    convert_element_type x3 -> x1, other arithmetic: 8.66 us -> 0.01 us  [per_device(): tile_counts = tile_counts.astype(jnp.float32)]
  transfers between devices with their start and end apart: 8 -> 12, of which waited for: 2 -> 5; matrix products, arithmetic and copies ran while one was open for 6% -> 8% of each run, Pallas kernels for 0% -> 0%
where the time goes in v1:
time: 144 us; the launch traced here: 143 us
  Pallas kernels  46.9 us (33%)
  starting transfers between devices  39.2 us (27%)
  waiting for transfers between devices  35 us (24%)
  local copies, waits for them, and re-layouts  14.5 us (10%)
  between operations  3.72 us (3%)
  other arithmetic  3.15 us (2%)
    pallas_call x2, Pallas kernels, convolve(): pl.pallas_call(functools.partial(conv_kernel, d, 8, with_stats), out_shap...  37.9 us
    all_to_all x2, waiting for transfers between devices, share_statistics(): lax.all_to_all(jnp.broadcast_to(merged[None], (chips, *merged.shape)), CH...  15.9 us
    ppermute x2, waiting for transfers between devices, exchange(): top = lax.ppermute(x[:, rows - d:], LAT, up)  15.2 us
    all_to_all x2, starting transfers between devices, share_statistics(): lax.all_to_all(jnp.broadcast_to(merged[None], (chips, *merged.shape)), CH...  11.4 us
    ppermute x2, starting transfers between devices, exchange(): right = lax.ppermute(packed(0, d), LON, west)  10.6 us
    ppermute x2, starting transfers between devices, exchange(): top = lax.ppermute(x[:, rows - d:], LAT, up)  9.35 us
    pallas_call x1, Pallas kernels, local_statistics(): pl.pallas_call(stats_kernel, out_shape=jax.ShapeDtypeStruct((2, samples *...  9.05 us
    ppermute x2, starting transfers between devices, exchange(): bottom = lax.ppermute(x[:, :d], LAT, down)  5.11 us
  transfers between devices with their start and end apart: 12, of which 5 were waited for; matrix products, arithmetic and copies ran while one was open for 8% of the time, Pallas kernels for 0%

profile of v1, /device:TPU:1, one launch (start us, length us, event | category | flops | bytes accessed | tf_op | source)
XLA Modules:
  0.0 142.5 jit_solution(2140358225660997370)
XLA Ops:
  0.0 1.4 pad_dynamic-slice_fusion.points_ref
  1.4 0.7 add_add_fusion.1.cols_ref
  2.1 9.1 %stats.1 = f32[2,2,128]{2,1,0:T(2,128)} custom-call(s32[36]{0:T(128)} %pad_dynamic-slice_fusion.points_ref, s32[3]{0:T(128)} %add_add_fusion.1.cols_ref, bf16[8,32,32,256]{3,2,1,0:T(8,128)(2,1)} %x_ref.3), custom_call_target="tpu_custom_call" | custom-call | flops 16777216 | bytes 4194304 | tf_op jit(solution)/shard_map/stats/pallas_call | solution.py:104
  11.1 1.4 collective-permute-start
  12.5 1.1 fusion.7
  13.6 1.9 %collective-permute-start.2 = (bf16[8,2,32,256]{3,2,1,0:T(8,128)(2,1)S(1)}, bf16[8,2,32,256]{3,2,1,0:T(8,128)(2,1)S(1)}, u32[]{:S(2)}, u32[]{:S(2)}) collective-permute-start(bf16[8,2,32,256]{3,2,1,0:T(8,128)(2,1)S(1)} %get-tuple-element.15), channel_id=1, source_target_pairs={{32,0},{64,32},{96,64},{33,1},{65,33},{97,65},{34,2},{66,34},{98,6... | collective-permute-start | bytes 786440 | tf_op jit(solution)/shard_map/ppermute | solution.py:267
  15.5 5.5 %collective-permute-start.1 = (bf16[8,2,32,256]{3,2,1,0:T(8,128)(2,1)S(1)}, bf16[8,2,32,256]{3,2,1,0:T(8,128)(2,1)S(1)}, u32[]{:S(2)}, u32[]{:S(2)}) collective-permute-start(bf16[8,2,32,256]{3,2,1,0:T(8,128)(2,1)S(1)} %get-tuple-element.16), channel_id=1, source_target_pairs={{0,32},{32,64},{64,96},{1,33},{33,65},{65,97},{2,34},{34,66},{66,9... | collective-permute-start | bytes 786440 | tf_op jit(solution)/shard_map/ppermute | solution.py:266
  21.0 0.0 copy-done.8
  21.0 0.1 sub.35
  21.1 2.1 %fusion.6 = (bf16[8,32,2,256]{3,2,1,0:T(2,128)(2,1)S(1)}, bf16[8,32,2,256]{3,2,1,0:T(2,128)(2,1)S(1)}) fusion(bf16[8,32,32,256]{3,2,1,0:T(8,128)(2,1)} %x_ref.3), kind=kLoop, calls=%fused_computation.28 | loop fusion | bytes 1048576 | tf_op jit(solution)/shard_map/slice | solution.py:272
  23.2 0.1 clamp_reduce_fusion
  23.3 0.0 copy-done.7
  23.3 0.7 dynamic_slice.14
  24.0 0.6 dynamic_slice.15
  27.9 0.1 broadcast_in_dim.9
  28.0 0.2 copy.23
  28.2 0.2 copy.22
  28.5 0.0 collective-permute-done
  28.5 0.7 slice_add_fusion.3
  29.2 0.0 collective-permute-done.2.bottom_ref
  29.3 0.0 collective-permute-done.1.top_ref
  29.3 0.0 copy-start.5
  29.4 0.1 copy.21
  29.6 0.1 copy.17
  29.6 1.3 collective-permute-start.3
  30.9 4.9 %collective-permute-start.4 = (bf16[8,72,256]{2,1,0:T(8,128)(2,1)S(1)}, bf16[8,72,256]{2,1,0:T(8,128)(2,1)S(1)}, u32[]{:S(2)}, u32[]{:S(2)}) collective-permute-start(bf16[8,72,256]{2,1,0:T(8,128)(2,1)S(1)} %copy.21), channel_id=1, source_target_pairs={{1,0},{2,1},{3,2},{4,3},{5,4},{6,5},{7,6},{8,7},{9,8},{10,9},{11,1... | collective-permute-start | bytes 884744 | tf_op jit(solution)/shard_map/ppermute | solution.py:276
  35.8 0.7 broadcast_in_dim.8
  36.5 4.6 %all-to-all-start = ((f32[64,2,2,128]{3,2,1,0:T(2,128)}), f32[64,2,2,128]{3,2,1,0:T(2,128)S(1)}, u32[]{:S(2)}, u32[]{:S(2)}) async-start(f32[64,2,2,128]{3,2,1,0:T(2,128)} %broadcast_in_dim.8), calls=%async_computation | async-start | bytes 262144 | tf_op jit(solution)/shard_map/all_to_all | solution.py:287
  41.1 0.6 slice_bitcast_fusion
  41.7 8.3 %all-to-all-done.parts_ref = f32[64,2,2,128]{3,2,1,0:T(2,128)S(1)} async-done(((f32[64,2,2,128]{3,2,1,0:T(2,128)}), f32[64,2,2,128]{3,2,1,0:T(2,128)S(1)}, u32[]{:S(2)}, u32[]{:S(2)}) %all-to-all-start) | async-done | bytes 131104 | tf_op jit(solution)/shard_map/all_to_all | solution.py:287
  50.0 0.0 collective-permute-done.3.left_ref
  50.0 0.0 collective-permute-done.4.right_ref
  50.1 0.0 copy-start.10
  50.1 0.8 broadcast_in_dim.10.counts_ref
  50.9 0.0 copy-done.4
  50.9 0.0 copy-done.5
  50.9 21.0 %conv2.1 = (bf16[8,32,32,256]{3,2,1,0:T(8,128)(2,1)}, f32[2,2,128]{2,1,0:T(2,128)}) custom-call(s32[36]{0:T(128)} %pad_dynamic-slice_fusion.points_ref, s32[3]{0:T(128)} %add_add_fusion.1.cols_ref, f32[8]{0:T(128)} %get-tuple-element.29.scale_ref, f32[64,2,2,128]{3,2,1,0:T(2,128)} %copy-done.1, f32[64,128]{1,0:T(8,128)} %broadcast_in_dim.10.counts_ref, ...), custom_call_target="tpu_custom_call" | custom-call | flops 9663676416 | bytes 10485760 | tf_op jit(solution)/shard_map/conv2/pallas_call | solution.py:232
  71.9 1.3 fusion.5
  73.2 3.2 %collective-permute-start.7 = (bf16[8,4,32,256]{3,2,1,0:T(8,128)(2,1)S(1)}, bf16[8,4,32,256]{3,2,1,0:T(8,128)(2,1)S(1)}, u32[]{:S(2)}, u32[]{:S(2)}) collective-permute-start(bf16[8,4,32,256]{3,2,1,0:T(8,128)(2,1)S(1)} %get-tuple-element.11), channel_id=1, source_target_pairs={{32,0},{64,32},{96,64},{33,1},{65,33},{97,65},{34,2},{66,34},{98,6... | collective-permute-start | bytes 1572872 | tf_op jit(solution)/shard_map/ppermute | solution.py:267
  76.4 3.9 %collective-permute-start.6 = (bf16[8,4,32,256]{3,2,1,0:T(8,128)(2,1)S(1)}, bf16[8,4,32,256]{3,2,1,0:T(8,128)(2,1)S(1)}, u32[]{:S(2)}, u32[]{:S(2)}) collective-permute-start(bf16[8,4,32,256]{3,2,1,0:T(8,128)(2,1)S(1)} %get-tuple-element.12), channel_id=1, source_target_pairs={{0,32},{32,64},{64,96},{1,33},{33,65},{65,97},{2,34},{34,66},{66,9... | collective-permute-start | bytes 1572872 | tf_op jit(solution)/shard_map/ppermute | solution.py:266
  80.3 2.1 %fusion.4 = (bf16[8,32,4,256]{3,2,1,0:T(4,128)(2,1)S(1)}, bf16[8,32,4,256]{3,2,1,0:T(4,128)(2,1)S(1)}) fusion(bf16[8,32,32,256]{3,2,1,0:T(8,128)(2,1)} %get-tuple-element.8.x_ref), kind=kLoop, calls=%fused_computation.26 | loop fusion | bytes 2097152 | tf_op jit(solution)/shard_map/slice | solution.py:272
  82.4 2.8 %collective-permute-done.7.bottom_ref = bf16[8,4,32,256]{3,2,1,0:T(8,128)(2,1)S(1)} collective-permute-done((bf16[8,4,32,256]{3,2,1,0:T(8,128)(2,1)S(1)}, bf16[8,4,32,256]{3,2,1,0:T(8,128)(2,1)S(1)}, u32[]{:S(2)}, u32[]{:S(2)}) %collective-permute-start.7) | collective-permute-done | bytes 524320 | tf_op jit(solution)/shard_map/ppermute | solution.py:267
  85.2 0.1 fusion.9
  85.3 15.2 %collective-permute-done.6.top_ref = bf16[8,4,32,256]{3,2,1,0:T(8,128)(2,1)S(1)} collective-permute-done((bf16[8,4,32,256]{3,2,1,0:T(8,128)(2,1)S(1)}, bf16[8,4,32,256]{3,2,1,0:T(8,128)(2,1)S(1)}, u32[]{:S(2)}, u32[]{:S(2)}) %collective-permute-start.6) | collective-permute-done | bytes 524320 | tf_op jit(solution)/shard_map/ppermute | solution.py:266
  100.4 0.1 fusion.8
  100.5 0.5 pad_maximum_fusion.1
  101.0 0.2 reshape.47
  101.1 0.5 pad_maximum_fusion
  101.6 0.2 reshape.46
  101.8 0.1 collective-permute-start.8
  101.9 5.7 %collective-permute-start.9 = (bf16[8,160,256]{2,1,0:T(8,128)(2,1)S(1)}, bf16[8,160,256]{2,1,0:T(8,128)(2,1)}, u32[]{:S(2)}, u32[]{:S(2)}) collective-permute-start(bf16[8,160,256]{2,1,0:T(8,128)(2,1)S(1)} %reshape.47), channel_id=1, source_target_pairs={{1,0},{2,1},{3,2},{4,3},{5,4},{6,5},{7,6},{8,7},{9,8},{10,9},{11,1... | collective-permute-start | bytes 1966088 | tf_op jit(solution)/shard_map/ppermute | solution.py:276
  107.5 0.0 collective-permute-start.5
  107.5 1.2 collective-permute-done.5
  108.7 0.7 broadcast_in_dim.11
  109.4 6.8 %all-to-all-start.1 = ((f32[64,2,2,128]{3,2,1,0:T(2,128)}), f32[64,2,2,128]{3,2,1,0:T(2,128)S(1)}, u32[]{:S(2)}, u32[]{:S(2)}) async-start(f32[64,2,2,128]{3,2,1,0:T(2,128)} %broadcast_in_dim.11), calls=%async_computation.1 | async-start | bytes 262144 | tf_op jit(solution)/shard_map/all_to_all | solution.py:287
  116.2 0.6 add_add_fusion.cols_ref
  116.8 0.6 pad_dynamic-slice_fusion.1.points_ref
  117.4 7.5 %all-to-all-done.1.parts_ref = f32[64,2,2,128]{3,2,1,0:T(2,128)S(1)} async-done(((f32[64,2,2,128]{3,2,1,0:T(2,128)}), f32[64,2,2,128]{3,2,1,0:T(2,128)S(1)}, u32[]{:S(2)}, u32[]{:S(2)}) %all-to-all-start.1) | async-done | bytes 131104 | tf_op jit(solution)/shard_map/all_to_all | solution.py:287
  125.0 0.0 collective-permute-done.8.left_ref
  125.0 0.0 collective-permute-done.9.right_ref
  125.0 0.0 copy-done.2
  125.0 0.0 copy-done.3
  125.0 0.6 copy-done
  125.6 16.9 %conv4.1 = bf16[8,32,32,256]{3,2,1,0:T(8,128)(2,1)} custom-call(s32[40]{0:T(128)} %pad_dynamic-slice_fusion.1.points_ref, s32[3]{0:T(128)} %add_add_fusion.cols_ref, f32[8]{0:T(128)} %get-tuple-element.30.scale_ref, f32[64,2,2,128]{3,2,1,0:T(2,128)} %copy-done, f32[64,128]{1,0:T(8,128)} %broadcast_in_dim.10.counts_ref, ...), custom_call_target="tpu_custom_call" | custom-call | flops 9663676416 | bytes 10485760 | tf_op jit(solution)/shard_map/conv4/pallas_call | solution.py:232
  (28 shorter events, 0.2 us)
Async XLA Ops:
  0.0 21.0 %copy-start.8 = (s32[128]{0:T(128)S(1)}, s32[128]{0:T(128)}, u32[]{:S(2)}) copy-start(s32[128]{0:T(128)} %param.6) | copy-start | bytes 1540
  0.0 23.3 %copy-start.7 = (s32[8,2]{0,1:T(2,128)S(1)}, s32[8,2]{0,1:T(2,128)}, u32[]{:S(2)}) copy-start(s32[8,2]{0,1:T(2,128)} %param.7) | copy-start | bytes 196
  11.1 17.4 %collective-permute-start = (f32[2,2,128]{2,1,0:T(2,128)}, f32[2,2,128]{2,1,0:T(2,128)S(1)}, u32[]{:S(2)}, u32[]{:S(2)}) collective-permute-start(f32[2,2,128]{2,1,0:T(2,128)} %stats.1), channel_id=1, source_target_pairs={{0,32},{32,0},{1,33},{33,1},{2,34},{34,2},{3,35},{35,3},{4,36},{36... | collective-permute-start | bytes 6152 | tf_op jit(solution)/shard_map/ppermute | solution.py:281
  13.6 15.6 %collective-permute-start.2 = (bf16[8,2,32,256]{3,2,1,0:T(8,128)(2,1)S(1)}, bf16[8,2,32,256]{3,2,1,0:T(8,128)(2,1)S(1)}, u32[]{:S(2)}, u32[]{:S(2)}) collective-permute-start(bf16[8,2,32,256]{3,2,1,0:T(8,128)(2,1)S(1)} %get-tuple-element.15), channel_id=1, source_target_pairs={{32,0},{64,32},{96,64},{33,1},{65,33},{97,65},{34,2},{66,34},{98,6... | collective-permute-start | bytes 786440 | tf_op jit(solution)/shard_map/ppermute | solution.py:267
  15.5 13.8 %collective-permute-start.1 = (bf16[8,2,32,256]{3,2,1,0:T(8,128)(2,1)S(1)}, bf16[8,2,32,256]{3,2,1,0:T(8,128)(2,1)S(1)}, u32[]{:S(2)}, u32[]{:S(2)}) collective-permute-start(bf16[8,2,32,256]{3,2,1,0:T(8,128)(2,1)S(1)} %get-tuple-element.16), channel_id=1, source_target_pairs={{0,32},{32,64},{64,96},{1,33},{33,65},{65,97},{2,34},{34,66},{66,9... | collective-permute-start | bytes 786440 | tf_op jit(solution)/shard_map/ppermute | solution.py:266
  29.2 21.7 %copy-start.4 = (bf16[8,2,32,256]{3,2,1,0:T(8,128)(2,1)}, bf16[8,2,32,256]{3,2,1,0:T(8,128)(2,1)S(1)}, u32[]{:S(2)}) copy-start(bf16[8,2,32,256]{3,2,1,0:T(8,128)(2,1)S(1)} %collective-permute-done.2.bottom_ref) | copy-start | bytes 786436
  29.3 21.6 %copy-start.5 = (bf16[8,2,32,256]{3,2,1,0:T(8,128)(2,1)}, bf16[8,2,32,256]{3,2,1,0:T(8,128)(2,1)S(1)}, u32[]{:S(2)}) copy-start(bf16[8,2,32,256]{3,2,1,0:T(8,128)(2,1)S(1)} %collective-permute-done.1.top_ref) | copy-start | bytes 786436
  29.6 20.4 %collective-permute-start.3 = (bf16[8,72,256]{2,1,0:T(8,128)(2,1)S(1)}, bf16[8,72,256]{2,1,0:T(8,128)(2,1)S(1)}, u32[]{:S(2)}, u32[]{:S(2)}) collective-permute-start(bf16[8,72,256]{2,1,0:T(8,128)(2,1)S(1)} %copy.17), channel_id=1, source_target_pairs={{0,1},{1,2},{2,3},{3,4},{4,5},{5,6},{6,7},{7,8},{8,9},{9,10},{10,1... | collective-permute-start | bytes 884744 | tf_op jit(solution)/shard_map/ppermute | solution.py:275
  30.9 19.1 %collective-permute-start.4 = (bf16[8,72,256]{2,1,0:T(8,128)(2,1)S(1)}, bf16[8,72,256]{2,1,0:T(8,128)(2,1)S(1)}, u32[]{:S(2)}, u32[]{:S(2)}) collective-permute-start(bf16[8,72,256]{2,1,0:T(8,128)(2,1)S(1)} %copy.21), channel_id=1, source_target_pairs={{1,0},{2,1},{3,2},{4,3},{5,4},{6,5},{7,6},{8,7},{9,8},{10,9},{11,1... | collective-permute-start | bytes 884744 | tf_op jit(solution)/shard_map/ppermute | solution.py:276
  36.5 13.5 %all-to-all-start = ((f32[64,2,2,128]{3,2,1,0:T(2,128)}), f32[64,2,2,128]{3,2,1,0:T(2,128)S(1)}, u32[]{:S(2)}, u32[]{:S(2)}) async-start(f32[64,2,2,128]{3,2,1,0:T(2,128)} %broadcast_in_dim.8), calls=%async_computation | async-start | bytes 262144 | tf_op jit(solution)/shard_map/all_to_all | solution.py:287
  50.0 0.9 copy-start.1
  50.0 0.9 copy-start.9
  50.1 0.9 copy-start.10
  73.2 34.3 %copy-start.6 = (f32[2,2,128]{2,1,0:T(2,128)S(1)}, f32[2,2,128]{2,1,0:T(2,128)}, u32[]{:S(2)}) copy-start(f32[2,2,128]{2,1,0:T(2,128)} %get-tuple-element.7) | copy-start | bytes 6148
  73.2 12.0 %collective-permute-start.7 = (bf16[8,4,32,256]{3,2,1,0:T(8,128)(2,1)S(1)}, bf16[8,4,32,256]{3,2,1,0:T(8,128)(2,1)S(1)}, u32[]{:S(2)}, u32[]{:S(2)}) collective-permute-start(bf16[8,4,32,256]{3,2,1,0:T(8,128)(2,1)S(1)} %get-tuple-element.11), channel_id=1, source_target_pairs={{32,0},{64,32},{96,64},{33,1},{65,33},{97,65},{34,2},{66,34},{98,6... | collective-permute-start | bytes 1572872 | tf_op jit(solution)/shard_map/ppermute | solution.py:267
  76.4 24.0 %collective-permute-start.6 = (bf16[8,4,32,256]{3,2,1,0:T(8,128)(2,1)S(1)}, bf16[8,4,32,256]{3,2,1,0:T(8,128)(2,1)S(1)}, u32[]{:S(2)}, u32[]{:S(2)}) collective-permute-start(bf16[8,4,32,256]{3,2,1,0:T(8,128)(2,1)S(1)} %get-tuple-element.12), channel_id=1, source_target_pairs={{0,32},{32,64},{64,96},{1,33},{33,65},{65,97},{2,34},{34,66},{66,9... | collective-permute-start | bytes 1572872 | tf_op jit(solution)/shard_map/ppermute | solution.py:266
  85.2 39.8 %copy-start.2 = (bf16[8,4,32,256]{3,2,1,0:T(8,128)(2,1)}, bf16[8,4,32,256]{3,2,1,0:T(8,128)(2,1)S(1)}, u32[]{:S(2)}) copy-start(bf16[8,4,32,256]{3,2,1,0:T(8,128)(2,1)S(1)} %collective-permute-done.7.bottom_ref) | copy-start | bytes 1572868
  100.4 24.6 %copy-start.3 = (bf16[8,4,32,256]{3,2,1,0:T(8,128)(2,1)}, bf16[8,4,32,256]{3,2,1,0:T(8,128)(2,1)S(1)}, u32[]{:S(2)}) copy-start(bf16[8,4,32,256]{3,2,1,0:T(8,128)(2,1)S(1)} %collective-permute-done.6.top_ref) | copy-start | bytes 1572868
  101.8 23.2 %collective-permute-start.8 = (bf16[8,160,256]{2,1,0:T(8,128)(2,1)S(1)}, bf16[8,160,256]{2,1,0:T(8,128)(2,1)}, u32[]{:S(2)}, u32[]{:S(2)}) collective-permute-start(bf16[8,160,256]{2,1,0:T(8,128)(2,1)S(1)} %reshape.46), channel_id=1, source_target_pairs={{0,1},{1,2},{2,3},{3,4},{4,5},{5,6},{6,7},{7,8},{8,9},{9,10},{10,1... | collective-permute-start | bytes 1966088 | tf_op jit(solution)/shard_map/ppermute | solution.py:275
  101.9 23.1 %collective-permute-start.9 = (bf16[8,160,256]{2,1,0:T(8,128)(2,1)S(1)}, bf16[8,160,256]{2,1,0:T(8,128)(2,1)}, u32[]{:S(2)}, u32[]{:S(2)}) collective-permute-start(bf16[8,160,256]{2,1,0:T(8,128)(2,1)S(1)} %reshape.47), channel_id=1, source_target_pairs={{1,0},{2,1},{3,2},{4,3},{5,4},{6,5},{7,6},{8,7},{9,8},{10,9},{11,1... | collective-permute-start | bytes 1966088 | tf_op jit(solution)/shard_map/ppermute | solution.py:276
  107.5 1.2 collective-permute-start.5
  109.4 15.6 %all-to-all-start.1 = ((f32[64,2,2,128]{3,2,1,0:T(2,128)}), f32[64,2,2,128]{3,2,1,0:T(2,128)S(1)}, u32[]{:S(2)}, u32[]{:S(2)}) async-start(f32[64,2,2,128]{3,2,1,0:T(2,128)} %broadcast_in_dim.11), calls=%async_computation.1 | async-start | bytes 262144 | tf_op jit(solution)/shard_map/all_to_all | solution.py:287
  125.0 0.6 copy-start

commit v2 on v1

v2 whole, which is shorter than its diff:
```python
import functools

import jax
import jax.numpy as jnp
from jax import lax
from jax.experimental import pallas as pl
from jax.experimental.pallas import tpu as pltpu
from jax.sharding import Mesh, PartitionSpec as P

GROUPS = 32
FIRST_DILATION = 2
SECOND_DILATION = 4
EPS = 1e-05
KEEP_RATE = 0.8

LAT = ("zh", "core")
LON = ("y", "zl", "x")
CHIPS = ("zh", "y", "zl", "x")
LANES = 128
VMEM_LIMIT = 59_300_000
CHUNK = 8


def exact_dot(a, selection):
    high = a.astype(jnp.bfloat16)
    rest = a - high.astype(jnp.float32)
    middle = rest.astype(jnp.bfloat16)
    low = (rest - middle.astype(jnp.float32)).astype(jnp.bfloat16)
    m = a.shape[0]
    parts = jnp.concatenate([high.astype(jnp.float32), middle.astype(jnp.float32), low.astype(jnp.float32)], axis=0)
    terms = jnp.dot(parts.astype(jnp.bfloat16), selection, preferred_element_type=jnp.float32)
    return terms[:m] + terms[m : 2 * m] + terms[2 * m :]


def selection_matrix(shape, channel_dim, channels):
    size = channels // GROUPS
    channel = lax.broadcasted_iota(jnp.int32, shape, channel_dim)
    lane = lax.broadcasted_iota(jnp.int32, shape, 1 - channel_dim)
    return jnp.where(channel // size == lane % GROUPS, 1.0, 0.0).astype(jnp.bfloat16)


def slot_lanes(samples):
    row = lax.broadcasted_iota(jnp.int32, (samples, LANES), 0)
    lane = lax.broadcasted_iota(jnp.int32, (samples, LANES), 1)
    return lane // GROUPS == row % (LANES // GROUPS)


def store_group_stats(sums_ref, squares_ref, count, out_ref):
    samples, channels = sums_ref.shape
    slots = LANES // GROUPS
    size = channels // GROUPS
    own = slot_lanes(samples)
    fold = selection_matrix((channels, LANES), 0, channels)
    spread = selection_matrix((LANES, channels), 1, channels)
    per_channel = jnp.maximum(count, 1.0)
    sums = sums_ref[...]

    def packed(value):
        return jnp.where(own, value, 0.0).reshape(samples // slots, slots, LANES).sum(axis=1)

    group_sum = exact_dot(sums, fold)
    centre = exact_dot(jnp.where(own, group_sum, 0.0), spread) / (per_channel * size)
    offset = sums / per_channel - centre
    group_squares = exact_dot(squares_ref[...] + count * offset * offset, fold)
    out_ref[0] = packed(group_sum)
    out_ref[1] = packed(group_squares)


def row_statistics(rows, limits, count, sums_ref, squares_ref, b):
    some = 16
    cols, channels = rows(0, None).shape
    column = lax.broadcasted_iota(jnp.int32, (cols, channels), 0)
    few = sum(jnp.minimum(limit, some) for limit in limits).astype(jnp.float32)
    total = jnp.zeros((some, channels), jnp.float32)
    for h in range(len(limits)):
        total = total + jnp.where(column[:some] < limits[h], rows(h, some), 0.0)
    pivot = total.sum(axis=0, keepdims=True) / jnp.maximum(few, 1.0)
    first = jnp.zeros((cols, channels), jnp.float32)
    second = jnp.zeros((cols, channels), jnp.float32)
    for h in range(len(limits)):
        value = jnp.where(column < limits[h], rows(h, None) - pivot, 0.0)
        first = first + value
        second = second + value * value
    moved = first.sum(axis=0, keepdims=True)
    squares = second.sum(axis=0, keepdims=True) - moved * moved / jnp.maximum(count, 1.0)
    sums_ref[pl.ds(b, 1)] = moved + count * pivot
    squares_ref[pl.ds(b, 1)] = jnp.maximum(squares, 0.0)


def tile_position():
    lat = lax.axis_index("zh") * lax.axis_size("core") + lax.axis_index("core")
    lon = (lax.axis_index("y") * lax.axis_size("zl") + lax.axis_index("zl")) * lax.axis_size("x")
    return lat, lon + lax.axis_index("x")


def row_points(points_ref, lat, rows, e):
    row = lat * rows + e
    if 0 <= e < rows:
        return points_ref[row]
    total = points_ref.shape[0]
    inside = (row >= 0) & (row < total)
    return jnp.where(inside, points_ref[jnp.clip(row, 0, total - 1)], 0)


def live_limits(points_ref, rows, cols):
    lat, lon = tile_position()
    return [jnp.clip(points_ref[lat * rows + h] - lon * cols, 0, cols) for h in range(rows)]


def live_count(limits):
    return functools.reduce(lambda a, c: a + c, limits).astype(jnp.float32)


def in_vmem():
    return pl.BlockSpec(memory_space=pltpu.VMEM)


def fetch(x_hbm_ref, x_ref, sems, b):
    return pltpu.make_async_copy(x_hbm_ref.at[b], x_ref.at[b], sems.at[b])


def stats_kernel(points_ref, x_hbm_ref, out_ref, x_ref, sems, sums_ref, squares_ref):
    g = pl.program_id(0)

    @pl.when(g == 0)
    def _():
        for b in range(x_ref.shape[0]):
            fetch(x_hbm_ref, x_ref, sems, b).start()

    fetch(x_hbm_ref, x_ref, sems, g).wait()
    _, rows, cols, _ = x_ref.shape
    limits = live_limits(points_ref, rows, cols)
    count = live_count(limits)
    row_statistics(
        lambda h, n: x_ref[g, h, :n].astype(jnp.float32), limits, count, sums_ref, squares_ref, g
    )

    @pl.when(g == pl.num_programs(0) - 1)
    def _():
        store_group_stats(sums_ref, squares_ref, count, out_ref)


def local_statistics(x, points):
    samples, rows, width, channels = x.shape
    shape = (2, samples * GROUPS // LANES, LANES)
    return pl.pallas_call(
        stats_kernel,
        out_shape=jax.ShapeDtypeStruct(shape, jnp.float32),
        grid_spec=pltpu.PrefetchScalarGridSpec(
            num_scalar_prefetch=1,
            grid=(samples,),
            in_specs=[pl.BlockSpec(memory_space=pltpu.HBM)],
            out_specs=pl.BlockSpec(shape, lambda g, *_: (0, 0, 0)),
            scratch_shapes=[
                pltpu.VMEM(x.shape, x.dtype),
                pltpu.SemaphoreType.DMA((samples,)),
                pltpu.VMEM((samples, channels), jnp.float32),
                pltpu.VMEM((samples, channels), jnp.float32),
            ],
        ),
        compiler_params=pltpu.CompilerParams(
            dimension_semantics=("arbitrary",), vmem_limit_bytes=VMEM_LIMIT
        ),
        cost_estimate=pl.CostEstimate(
            flops=8 * x.size, bytes_accessed=2 * x.size, transcendentals=0
        ),
        name="stats",
    )(points, x)


def chip_counts(points, chips, rows, cols, size):
    total = points.shape[1]
    lons = chips // lax.axis_size("zh")
    chip = lax.broadcasted_iota(jnp.int32, (chips, total), 0)
    row = lax.broadcasted_iota(jnp.int32, (chips, total), 1)
    live = jnp.clip(points - (chip % lons) * cols, 0, cols)
    mine = row // (rows * lax.axis_size("core")) == chip // lons
    return jnp.where(mine, live, 0).astype(jnp.float32).sum(axis=1, keepdims=True) * size


def combine_statistics(parts_ref, points_ref, norm_ref, rows, cols):
    _, samples, channels = norm_ref.shape
    slots = LANES // GROUPS
    chips = parts_ref.shape[0]
    counts = chip_counts(points_ref[...], chips, rows, cols, channels // GROUPS)[:, None, :]
    sums = parts_ref[:, 0]
    squares = parts_ref[:, 1]
    count = counts.sum(axis=0)
    mean = sums.sum(axis=0) / count
    offset = sums / jnp.maximum(counts, 1.0) - mean[None]
    var = (squares + counts * offset * offset).sum(axis=0) / count
    half = 0.5 * lax.rsqrt(var + EPS)
    own = slot_lanes(samples)
    spread = selection_matrix((LANES, channels), 1, channels)

    def unpacked(value):
        rows = jnp.broadcast_to(value[:, None], (samples // slots, slots, LANES)).reshape(samples, LANES)
        return jnp.where(own, rows, 0.0)

    both = exact_dot(jnp.concatenate([unpacked(mean), unpacked(half)], axis=0), spread)
    norm_ref[0] = both[:samples]
    norm_ref[1] = both[samples:]


def conv_kernel(dilation, chunk, which, with_stats, points_ref, flags_ref, parts_ref, points_row_ref, *refs):
    d = dilation
    x_hbm_ref, top_ref, bottom_ref, left_ref, right_ref, left_end_ref, right_end_ref, w_ref, out_hbm_ref, *rest = refs
    if with_stats:
        stats_ref, x_ref, sems, out_ref, out_sems, norm_ref, even_ref, odd_ref, sums_ref, squares_ref, kept_ref = rest
    else:
        x_ref, sems, out_ref, out_sems, norm_ref, even_ref, odd_ref = rest
    g = pl.program_id(0)
    samples = norm_ref.shape[1]
    _, rows, cols, channels = x_ref.shape
    lat, lon = tile_position()
    lon_total = lax.axis_size(LON) * cols
    origin = lon * cols
    column = lax.broadcasted_iota(jnp.int32, (cols, channels), 0)
    edge = lax.broadcasted_iota(jnp.int32, (d, channels), 0)
    points = [row_points(points_ref, lat, rows, e - d) for e in range(rows + 2 * d)]
    limits = [jnp.clip(points[d + h] - origin, 0, cols) for h in range(rows)]
    before_origin = (origin + lon_total - d) % lon_total
    after_origin = (origin + cols) % lon_total

    def activate_rows(b, act_ref, lo, hi):
        mean = norm_ref[0, pl.ds(b, 1)]
        half = norm_ref[1, pl.ds(b, 1)]

        def activated(value):
            t = (value.astype(jnp.float32) - mean) * half
            return t + t * jnp.tanh(t)

        for e in range(lo, hi):
            if e < d:
                row, side = top_ref[b, e], (left_end_ref, right_end_ref, e)
            elif e < rows + d:
                row, side = x_ref[b, e - d], (left_ref, right_ref, e - d)
            else:
                row, side = bottom_ref[b, e - rows - d], (left_end_ref, right_end_ref, e - rows)
            at = slice(side[2] * d, (side[2] + 1) * d)
            left = activated(side[0][b, at])
            right = activated(side[1][b, at])
            mid = jnp.where(column < points[e] - origin, activated(row), 0.0)
            lhs = jnp.where(edge < points[e] - before_origin, left, 0.0)
            rhs = jnp.where(edge < points[e] - after_origin, right, 0.0)
            before = jnp.concatenate([lhs, mid[: cols - d]], axis=0)
            after = jnp.concatenate([mid[d:], rhs], axis=0)
            act_ref[e, :, 0:channels] = before.astype(jnp.bfloat16)
            act_ref[e, :, channels : 2 * channels] = mid.astype(jnp.bfloat16)
            act_ref[e, :, 2 * channels :] = after.astype(jnp.bfloat16)

    def convolve_rows(k, scale, act_ref, start):
        acc = None
        for tap in range(3):
            lo = start + tap * d
            taken = act_ref[lo : lo + chunk].reshape(chunk * cols, 3 * channels)
            term = jnp.dot(taken, w_ref[tap], preferred_element_type=jnp.float32)
            acc = term if acc is None else acc + term
        base = x_ref[2 * g + k, start : start + chunk].astype(jnp.float32)
        result = (base + scale * acc.reshape(chunk, cols, channels)).astype(jnp.bfloat16)
        out_ref[2 * g + k, start : start + chunk] = result
        if with_stats and k == 1:
            kept_ref[start : start + chunk] = result

    def phase(k, act_ref, follow, next_ref):
        scale = flags_ref[2 * g + k, which].astype(jnp.float32) * (1.0 / KEEP_RATE)
        steps = rows // chunk
        each = (rows + 2 * d) // steps
        for step in range(steps):
            last = rows + 2 * d if step == steps - 1 else (step + 1) * each
            activate_rows(follow, next_ref, step * each, last)
            convolve_rows(k, scale, act_ref, step * chunk)
        store(2 * g + k).start()

    def store(b):
        return pltpu.make_async_copy(out_ref.at[b], out_hbm_ref.at[b], out_sems.at[b])

    @pl.when(g == 0)
    def _():
        for b in range(samples):
            fetch(x_hbm_ref, x_ref, sems, b).start()
        combine_statistics(parts_ref, points_row_ref, norm_ref, rows, cols)
        fetch(x_hbm_ref, x_ref, sems, 0).wait()
        activate_rows(0, even_ref, 0, rows + 2 * d)
        if with_stats:
            kept_ref[...] = jnp.zeros_like(kept_ref)

    @pl.when(g < samples // 2 - 1)
    def _():
        fetch(x_hbm_ref, x_ref, sems, 2 * g + 2).wait()

    fetch(x_hbm_ref, x_ref, sems, 2 * g + 1).wait()
    count = live_count(limits)
    phase(0, even_ref, 2 * g + 1, odd_ref)
    if with_stats:
        row_statistics(
            lambda h, n: kept_ref[h, :n].astype(jnp.float32), limits, count, sums_ref, squares_ref, jnp.maximum(2 * g - 1, 0)
        )
    phase(1, odd_ref, jnp.minimum(2 * g + 2, samples - 1), even_ref)
    if with_stats:
        row_statistics(
            lambda h, n: out_ref[2 * g, h, :n].astype(jnp.float32), limits, count, sums_ref, squares_ref, 2 * g
        )

        @pl.when(g == pl.num_programs(0) - 1)
        def _():
            row_statistics(
                lambda h, n: out_ref[2 * g + 1, h, :n].astype(jnp.float32), limits, count, sums_ref, squares_ref, samples - 1
            )
            store_group_stats(sums_ref, squares_ref, count, stats_ref)

    @pl.when(g == pl.num_programs(0) - 1)
    def _():
        for b in range(samples):
            store(b).wait()


def convolve(x, halos, weight, parts, points, flags, dilation, which, with_stats):
    samples, rows, width, channels = x.shape
    d = dilation
    def whole(shape):
        return pl.BlockSpec(shape, lambda g, *_: (0,) * len(shape))

    out_shape = [jax.ShapeDtypeStruct(x.shape, jnp.bfloat16)]
    out_specs = [pl.BlockSpec(memory_space=pltpu.HBM)]
    act = pltpu.VMEM((rows + 2 * d, width, 3 * channels), jnp.bfloat16)
    scratch = [pltpu.VMEM(x.shape, x.dtype), pltpu.SemaphoreType.DMA((samples,))] * 2
    scratch += [pltpu.VMEM((2, samples, channels), jnp.float32), act, act]
    if with_stats:
        shape = (2, samples * GROUPS // LANES, LANES)
        out_shape.append(jax.ShapeDtypeStruct(shape, jnp.float32))
        out_specs.append(whole(shape))
        scratch += [pltpu.VMEM((samples, channels), jnp.float32)] * 2
        scratch += [pltpu.VMEM((rows, width, channels), jnp.bfloat16)]
    return pl.pallas_call(
        functools.partial(conv_kernel, d, CHUNK, which, with_stats),
        out_shape=out_shape,
        grid_spec=pltpu.PrefetchScalarGridSpec(
            num_scalar_prefetch=2,
            grid=(samples // 2,),
            in_specs=[
                in_vmem(),
                in_vmem(),
                pl.BlockSpec(memory_space=pltpu.HBM),
                *[in_vmem()] * len(halos),
                in_vmem(),
            ],
            out_specs=out_specs,
            scratch_shapes=scratch,
        ),
        compiler_params=pltpu.CompilerParams(
            dimension_semantics=("arbitrary",), vmem_limit_bytes=VMEM_LIMIT
        ),
        cost_estimate=pl.CostEstimate(
            flops=2 * x.size * 9 * channels, bytes_accessed=5 * x.size, transcendentals=2 * x.size
        ),
        name="conv%d" % d,
    )(points, flags, parts, points[None], x, *halos, weight)


def exchange_sides(x, d):
    samples, rows, width, channels = x.shape
    lat, lon = lax.axis_size(LAT), lax.axis_size(LON)
    up = [(i, i + 1) for i in range(lat - 1)]
    down = [(i + 1, i) for i in range(lat - 1)]
    top = lax.ppermute(x[:, rows - d :], LAT, up)
    bottom = lax.ppermute(x[:, :d], LAT, down)
    east = [(i, (i + 1) % lon) for i in range(lon)]
    west = [((i + 1) % lon, i) for i in range(lon)]
    left = lax.ppermute(x[:, :, width - d :].reshape(samples, rows * d, channels), LON, east)
    right = lax.ppermute(x[:, :, :d].reshape(samples, rows * d, channels), LON, west)
    return top, bottom, left, right


def exchange_corners(top, bottom):
    samples, d, width, channels = top.shape
    lon = lax.axis_size(LON)
    east = [(i, (i + 1) % lon) for i in range(lon)]
    west = [((i + 1) % lon, i) for i in range(lon)]

    def packed(lo, hi):
        ends = jnp.concatenate([top[:, :, lo:hi], bottom[:, :, lo:hi]], axis=1)
        return ends.reshape(samples, 2 * d * d, channels)

    left = lax.ppermute(packed(width - d, width), LON, east)
    right = lax.ppermute(packed(0, d), LON, west)
    return left, right


def share_statistics(local, own_count, other_count, core_axis="core"):
    other = lax.ppermute(local, core_axis, [(0, 1), (1, 0)])
    both = own_count + other_count
    gap = local[0] / jnp.maximum(own_count, 1.0) - other[0] / jnp.maximum(other_count, 1.0)
    squares = local[1] + other[1] + gap * gap * (own_count * other_count / jnp.maximum(both, 1.0))
    merged = jnp.stack([local[0] + other[0], squares])
    chips = lax.axis_size(CHIPS)
    return lax.all_to_all(jnp.broadcast_to(merged[None], (chips, *merged.shape)), CHIPS, 0, 0)


def tile_count(band_points, rows, width, size, core):
    _, lon = tile_position()
    lat = lax.axis_index("zh") * lax.axis_size("core") + core
    row = jnp.arange(band_points.shape[0], dtype=jnp.int32)
    live = jnp.clip(band_points - lon * width, 0, width)
    return jnp.where(row // rows == lat, live, 0).sum().astype(jnp.float32) * size


def per_device(features, band_points, survival_flags, first_kernel_weight, second_kernel_weight):
    _, rows, width, channels = features.shape
    core = lax.axis_index("core")
    size = channels // GROUPS
    own_count = tile_count(band_points, rows, width, size, core)
    other_count = tile_count(band_points, rows, width, size, 1 - core)
    first_weight = first_kernel_weight.reshape(3, 3 * channels, channels)
    second_weight = second_kernel_weight.reshape(3, 3 * channels, channels)

    top, bottom, left, right = exchange_sides(features, FIRST_DILATION)
    local = local_statistics(features, band_points)
    local, top, bottom = lax.optimization_barrier((local, top, bottom))
    ends = exchange_corners(top, bottom)
    parts = share_statistics(local, own_count, other_count)
    halos = (top, bottom, left, right, *ends)
    first, local = convolve(
        features, halos, first_weight, parts, band_points, survival_flags, FIRST_DILATION, 0, True
    )
    top, bottom, left, right = exchange_sides(first, SECOND_DILATION)
    parts = share_statistics(local, own_count, other_count)
    ends = exchange_corners(top, bottom)
    halos = (top, bottom, left, right, *ends)
    (section,) = convolve(
        first, halos, second_weight, parts, band_points, survival_flags, SECOND_DILATION, 1, False
    )
    return section


def solution(mesh):
    grid = Mesh(mesh.devices.reshape(2, 2, 4, 2, 4), (LAT + LON))
    spec = P(None, LAT, LON, None)
    return jax.shard_map(
        per_device, mesh=grid, in_specs=(spec, P(), P(), P(), P()), out_specs=spec, check_vma=False
    )
```

time: 144 us -> 135 us (0.938)
  the two profiles are of different devices: /device:TPU:1 before, /device:TPU:0 now
where the time goes in v2:
time: 135 us
  Pallas kernels  44.4 us (33%)
  starting transfers between devices  43 us (32%)
  blocking collectives  28.5 us (21%)
  local copies, waits for them, and re-layouts  11.4 us (8%)
  waiting for transfers between devices  4.1 us (3%)
  between operations  1.82 us (1%)
  other arithmetic  1.64 us (1%)
    pallas_call x2, Pallas kernels, convolve(): pl.pallas_call(functools.partial(conv_kernel, d, CHUNK, which, with_stats...  38.3 us
    all_to_all x1, blocking collectives, share_statistics(): lax.all_to_all(jnp.broadcast_to(merged[None], (chips, *merged.shape)), CH...  28.5 us
    ppermute x2, starting transfers between devices, exchange_sides(): lax.ppermute(x[:, :, :d].reshape(samples, rows * d, channels), LON, west)  11.2 us
    ppermute x2, starting transfers between devices, exchange_corners(): right = lax.ppermute(packed(0, d), LON, west)  10.9 us
    pallas_call x1, Pallas kernels, local_statistics(): pl.pallas_call(stats_kernel, out_shape=jax.ShapeDtypeStruct(shape, jnp.fl...  6.08 us
    ppermute x2, starting transfers between devices, exchange_sides(): top = lax.ppermute(x[:, rows - d:], LAT, up)  5.79 us
    all_to_all x1, starting transfers between devices, share_statistics(): lax.all_to_all(jnp.broadcast_to(merged[None], (chips, *merged.shape)), CH...  5 us
    slice x2, local copies, waits for them, and re-layouts, exchange_sides(): x[:, :, :d].reshape(samples, rows * d, channels)  4.14 us
  transfers between devices with their start and end apart: 15, of which 3 were waited for; matrix products, arithmetic and copies ran while one was open for 7% of the time, Pallas kernels for 5%

profile of v2, /device:TPU:0, one launch (start us, length us, event | category | flops | bytes accessed | tf_op | source)
XLA Modules:
  0.0 134.8 jit_solution(4022478764180249326)
XLA Ops:
  0.0 1.1 fusion.9
  1.1 0.0 copy-start.6
  1.1 1.3 collective-permute-start.1
  2.4 3.0 %collective-permute-start = (bf16[8,2,32,256]{3,2,1,0:T(8,128)(2,1)S(1)}, bf16[8,2,32,256]{3,2,1,0:T(8,128)(2,1)S(1)}, u32[]{:S(2)}, u32[]{:S(2)}) collective-permute-start(bf16[8,2,32,256]{3,2,1,0:T(8,128)(2,1)S(1)} %get-tuple-element.24), channel_id=1, source_target_pairs={{0,32},{32,64},{64,96},{1,33},{33,65},{65,97},{2,34},{34,66},{66,9... | collective-permute-start | bytes 786440 | tf_op jit(solution)/shard_map/ppermute | solution.py:366
  5.5 2.1 %fusion.8 = (bf16[8,32,2,256]{3,2,1,0:T(2,128)(2,1)S(1)}, bf16[8,32,2,256]{3,2,1,0:T(2,128)(2,1)S(1)}) fusion(bf16[8,32,32,256]{3,2,1,0:T(8,128)(2,1)} %refs_0_.1), kind=kLoop, calls=%fused_computation.27 | loop fusion | bytes 1048576 | tf_op jit(solution)/shard_map/slice | solution.py:371
  7.5 0.2 copy.14
  7.8 1.6 %collective-permute-start.3 = (bf16[8,64,256]{2,1,0:T(8,128)(2,1)S(1)}, bf16[8,64,256]{2,1,0:T(8,128)(2,1)S(1)}, u32[]{:S(2)}, u32[]{:S(2)}) collective-permute-start(bf16[8,64,256]{2,1,0:T(8,128)(2,1)S(1)} %copy.9), channel_id=1, source_target_pairs={{0,1},{1,2},{2,3},{3,4},{4,5},{5,6},{6,7},{7,8},{8,9},{9,10},{10,1... | collective-permute-start | bytes 786440 | tf_op jit(solution)/shard_map/ppermute | solution.py:370
  9.5 0.2 copy.15
  9.7 5.2 %collective-permute-start.4 = (bf16[8,64,256]{2,1,0:T(8,128)(2,1)S(1)}, bf16[8,64,256]{2,1,0:T(8,128)(2,1)S(1)}, u32[]{:S(2)}, u32[]{:S(2)}) collective-permute-start(bf16[8,64,256]{2,1,0:T(8,128)(2,1)S(1)} %copy.11), channel_id=1, source_target_pairs={{1,0},{2,1},{3,2},{4,3},{5,4},{6,5},{7,6},{8,7},{9,8},{10,9},{11,1... | collective-permute-start | bytes 786440 | tf_op jit(solution)/shard_map/ppermute | solution.py:371
  14.9 0.0 copy-done.4
  14.9 0.7 fusion.5
  16.9 6.1 %stats.1 = f32[2,2,128]{2,1,0:T(2,128)} custom-call(s32[128]{0:T(128)} %points_ref.5, bf16[8,32,32,256]{3,2,1,0:T(8,128)(2,1)} %refs_0_.1), custom_call_target="tpu_custom_call" | custom-call | flops 16777216 | bytes 4194304 | tf_op jit(solution)/shard_map/stats/pallas_call | solution.py:146
  23.0 0.0 collective-permute-done.1.refs_2_
  23.0 0.0 copy-start.2
  23.0 0.0 collective-permute-done.refs_1_
  23.0 0.0 copy-start.3
  23.0 2.7 %collective-permute-start.2 = (f32[2,2,128]{2,1,0:T(2,128)}, f32[2,2,128]{2,1,0:T(2,128)S(1)}, u32[]{:S(2)}, u32[]{:S(2)}) collective-permute-start(f32[2,2,128]{2,1,0:T(2,128)} %stats.1), channel_id=1, source_target_pairs={{0,32},{32,0},{1,33},{33,1},{2,34},{34,2},{3,35},{35,3},{4,36},{36... | collective-permute-start | bytes 6152 | tf_op jit(solution)/shard_map/ppermute | solution.py:391
  25.7 0.1 fusion.12
  25.8 0.9 collective-permute-done.2
  26.7 0.7 slice_add_fusion.3
  27.4 0.7 broadcast_in_dim.9
  28.1 5.0 %all-to-all-start = ((f32[64,2,2,128]{3,2,1,0:T(2,128)}), f32[64,2,2,128]{3,2,1,0:T(2,128)S(1)}, u32[]{:S(2)}, u32[]{:S(2)}) async-start(f32[64,2,2,128]{3,2,1,0:T(2,128)} %broadcast_in_dim.9), calls=%async_computation | async-start | bytes 262144 | tf_op jit(solution)/shard_map/all_to_all | solution.py:397
  33.2 1.6 %collective-permute-start.5 = (bf16[8,8,256]{2,1,0:T(8,128)(2,1)S(1)}, bf16[8,8,256]{2,1,0:T(8,128)(2,1)S(1)}, u32[]{:S(2)}, u32[]{:S(2)}) collective-permute-start(bf16[8,8,256]{2,1,0:T(8,128)(2,1)S(1)} %reshape.34), channel_id=1, source_target_pairs={{0,1},{1,2},{2,3},{3,4},{4,5},{5,6},{6,7},{7,8},{8,9},{9,10},{10,1... | collective-permute-start | bytes 98312 | tf_op jit(solution)/shard_map/ppermute | solution.py:385
  34.8 4.7 %collective-permute-start.6 = (bf16[8,8,256]{2,1,0:T(8,128)(2,1)S(1)}, bf16[8,8,256]{2,1,0:T(8,128)(2,1)S(1)}, u32[]{:S(2)}, u32[]{:S(2)}) collective-permute-start(bf16[8,8,256]{2,1,0:T(8,128)(2,1)S(1)} %reshape.35), channel_id=1, source_target_pairs={{1,0},{2,1},{3,2},{4,3},{5,4},{6,5},{7,6},{8,7},{9,8},{10,9},{11,1... | collective-permute-start | bytes 98312 | tf_op jit(solution)/shard_map/ppermute | solution.py:386
  39.5 0.0 copy-done.6
  39.5 0.7 copy.13.flags_ref
  40.2 0.0 collective-permute-done.3.refs_3_
  40.2 0.0 collective-permute-done.4.refs_4_
  40.2 1.3 collective-permute-done.5.refs_5_
  41.5 0.0 collective-permute-done.6.refs_6_
  41.5 1.9 %all-to-all-done.parts_ref = f32[64,2,2,128]{3,2,1,0:T(2,128)S(1)} async-done(((f32[64,2,2,128]{3,2,1,0:T(2,128)}), f32[64,2,2,128]{3,2,1,0:T(2,128)S(1)}, u32[]{:S(2)}, u32[]{:S(2)}) %all-to-all-start) | async-done | bytes 131104 | tf_op jit(solution)/shard_map/all_to_all | solution.py:397
  43.4 0.0 copy-done.3
  43.4 0.0 copy-done.8
  43.4 0.0 copy-done.11
  43.4 0.0 copy-done.12
  43.4 0.6 copy-done
  44.0 20.1 %conv2.1 = (bf16[8,32,32,256]{3,2,1,0:T(8,128)(2,1)}, f32[2,2,128]{2,1,0:T(2,128)}) custom-call(s32[128]{0:T(128)} %points_ref.5, s32[8,2]{1,0:T(8,128)} %copy.13.flags_ref, f32[64,2,2,128]{3,2,1,0:T(2,128)} %copy-done, s32[1,128]{1,0:T(1,128)} %bitcast.7, bf16[8,32,32,256]{3,2,1,0:T(8,128)(2,1)} %refs_0_.1, bf16[8,2,32,256]{3,2,1,0:T(8,128)(2,1)} %copy-done.3, ...), custom_call_target="tpu_custom_call" | custom-call | flops 9663676416 | bytes 10485760 | tf_op jit(solution)/shard_map/conv2/pallas_call | solution.py:335
  64.1 0.0 copy-start.5
  64.2 1.3 fusion.7
  65.5 1.3 collective-permute-start.9
  66.8 1.2 collective-permute-start.7
  68.0 2.7 %collective-permute-start.8 = (bf16[8,4,32,256]{3,2,1,0:T(8,128)(2,1)S(1)}, bf16[8,4,32,256]{3,2,1,0:T(8,128)(2,1)}, u32[]{:S(2)}, u32[]{:S(2)}) collective-permute-start(bf16[8,4,32,256]{3,2,1,0:T(8,128)(2,1)S(1)} %get-tuple-element.20), channel_id=1, source_target_pairs={{0,32},{32,64},{64,96},{1,33},{33,65},{65,97},{2,34},{34,66},{66,9... | collective-permute-start | bytes 1572872 | tf_op jit(solution)/shard_map/ppermute | solution.py:366
  70.7 2.1 %fusion.6 = (bf16[8,32,4,256]{3,2,1,0:T(4,128)(2,1)S(1)}, bf16[8,32,4,256]{3,2,1,0:T(4,128)(2,1)S(1)}) fusion(bf16[8,32,32,256]{3,2,1,0:T(8,128)(2,1)} %get-tuple-element.14.refs_0_), kind=kLoop, calls=%fused_computation.25 | loop fusion | bytes 2097152 | tf_op jit(solution)/shard_map/slice | solution.py:371
  72.8 0.1 reshape.38
  72.9 0.1 reshape.37
  73.0 0.3 collective-permute-start.10
  73.3 6.0 %collective-permute-start.11 = (bf16[8,128,256]{2,1,0:T(8,128)(2,1)S(1)}, bf16[8,128,256]{2,1,0:T(8,128)(2,1)}, u32[]{:S(2)}, u32[]{:S(2)}) collective-permute-start(bf16[8,128,256]{2,1,0:T(8,128)(2,1)S(1)} %reshape.38), channel_id=1, source_target_pairs={{1,0},{2,1},{3,2},{4,3},{5,4},{6,5},{7,6},{8,7},{9,8},{10,9},{11,1... | collective-permute-start | bytes 1572872 | tf_op jit(solution)/shard_map/ppermute | solution.py:371
  79.4 0.0 collective-permute-done.7
  79.4 0.0 collective-permute-done.9.refs_2_
  79.4 0.1 fusion.11
  79.5 0.0 collective-permute-done.8.refs_1_
  79.5 1.1 fusion.10
  80.6 0.1 pad_maximum_fusion.1
  80.8 0.1 pad_maximum_fusion
  80.9 0.1 collective-permute-start.12
  81.0 6.2 %collective-permute-start.13 = (bf16[8,32,256]{2,1,0:T(8,128)(2,1)S(1)}, bf16[8,32,256]{2,1,0:T(8,128)(2,1)S(1)}, u32[]{:S(2)}, u32[]{:S(2)}) collective-permute-start(bf16[8,32,256]{2,1,0:T(8,128)(2,1)S(1)} %reshape.40), channel_id=1, source_target_pairs={{1,0},{2,1},{3,2},{4,3},{5,4},{6,5},{7,6},{8,7},{9,8},{10,9},{11,1... | collective-permute-start | bytes 393224 | tf_op jit(solution)/shard_map/ppermute | solution.py:386
  87.3 28.5 %all_to_all.10.parts_ref = f32[64,2,2,128]{3,2,1,0:T(2,128)} all-to-all(f32[64,2,2,128]{3,2,1,0:T(2,128)S(1)} %broadcast_in_dim.11), channel_id=1, replica_groups=mesh['zh'=2,'core'=2,'y'=4,'zl'=2,'x'=4] {'zh','y','zl','x'}, dimensions={0} | all-to-all | bytes 262144 | tf_op jit(solution)/shard_map/all_to_all | solution.py:397
  115.7 0.0 collective-permute-done.10.refs_3_
  115.7 0.0 collective-permute-done.11.refs_4_
  115.7 0.0 collective-permute-done.12.refs_5_
  115.7 0.0 collective-permute-done.13.refs_6_
  115.8 0.6 copy-done.9
  116.4 0.1 copy-done.10
  116.4 18.2 %conv4.1 = bf16[8,32,32,256]{3,2,1,0:T(8,128)(2,1)} custom-call(s32[128]{0:T(128)} %points_ref.5, s32[8,2]{1,0:T(8,128)} %copy.13.flags_ref, f32[64,2,2,128]{3,2,1,0:T(2,128)} %all_to_all.10.parts_ref, s32[1,128]{1,0:T(1,128)} %bitcast.8, bf16[8,32,32,256]{3,2,1,0:T(8,128)(2,1)} %get-tuple-element.14.refs_0_, ...), custom_call_target="tpu_custom_call" | custom-call | flops 9663676416 | bytes 10485760 | tf_op jit(solution)/shard_map/conv4/pallas_call | solution.py:335
  (25 shorter events, 0.4 us)
Async XLA Ops:
  0.0 14.9 %copy-start.4 = (s32[128]{0:T(128)S(1)}, s32[128]{0:T(128)}, u32[]{:S(2)}) copy-start(s32[128]{0:T(128)} %points_ref.5) | copy-start | bytes 1540
  1.1 38.4 %copy-start.6 = (s32[8,2]{0,1:T(2,128)S(1)}, s32[8,2]{0,1:T(2,128)}, u32[]{:S(2)}) copy-start(s32[8,2]{0,1:T(2,128)} %param.7) | copy-start | bytes 196
  1.1 21.9 %collective-permute-start.1 = (bf16[8,2,32,256]{3,2,1,0:T(8,128)(2,1)S(1)}, bf16[8,2,32,256]{3,2,1,0:T(8,128)(2,1)S(1)}, u32[]{:S(2)}, u32[]{:S(2)}) collective-permute-start(bf16[8,2,32,256]{3,2,1,0:T(8,128)(2,1)S(1)} %get-tuple-element.23), channel_id=1, source_target_pairs={{32,0},{64,32},{96,64},{33,1},{65,33},{97,65},{34,2},{66,34},{98,6... | collective-permute-start | bytes 786440 | tf_op jit(solution)/shard_map/ppermute | solution.py:367
  2.4 20.6 %collective-permute-start = (bf16[8,2,32,256]{3,2,1,0:T(8,128)(2,1)S(1)}, bf16[8,2,32,256]{3,2,1,0:T(8,128)(2,1)S(1)}, u32[]{:S(2)}, u32[]{:S(2)}) collective-permute-start(bf16[8,2,32,256]{3,2,1,0:T(8,128)(2,1)S(1)} %get-tuple-element.24), channel_id=1, source_target_pairs={{0,32},{32,64},{64,96},{1,33},{33,65},{65,97},{2,34},{34,66},{66,9... | collective-permute-start | bytes 786440 | tf_op jit(solution)/shard_map/ppermute | solution.py:366
  7.8 32.3 %collective-permute-start.3 = (bf16[8,64,256]{2,1,0:T(8,128)(2,1)S(1)}, bf16[8,64,256]{2,1,0:T(8,128)(2,1)S(1)}, u32[]{:S(2)}, u32[]{:S(2)}) collective-permute-start(bf16[8,64,256]{2,1,0:T(8,128)(2,1)S(1)} %copy.9), channel_id=1, source_target_pairs={{0,1},{1,2},{2,3},{3,4},{4,5},{5,6},{6,7},{7,8},{8,9},{9,10},{10,1... | collective-permute-start | bytes 786440 | tf_op jit(solution)/shard_map/ppermute | solution.py:370
  9.7 30.4 %collective-permute-start.4 = (bf16[8,64,256]{2,1,0:T(8,128)(2,1)S(1)}, bf16[8,64,256]{2,1,0:T(8,128)(2,1)S(1)}, u32[]{:S(2)}, u32[]{:S(2)}) collective-permute-start(bf16[8,64,256]{2,1,0:T(8,128)(2,1)S(1)} %copy.11), channel_id=1, source_target_pairs={{1,0},{2,1},{3,2},{4,3},{5,4},{6,5},{7,6},{8,7},{9,8},{10,9},{11,1... | collective-permute-start | bytes 786440 | tf_op jit(solution)/shard_map/ppermute | solution.py:371
  23.0 20.4 %copy-start.2 = (bf16[8,2,32,256]{3,2,1,0:T(8,128)(2,1)}, bf16[8,2,32,256]{3,2,1,0:T(8,128)(2,1)S(1)}, u32[]{:S(2)}) copy-start(bf16[8,2,32,256]{3,2,1,0:T(8,128)(2,1)S(1)} %collective-permute-done.1.refs_2_) | copy-start | bytes 786436
  23.0 20.4 %copy-start.3 = (bf16[8,2,32,256]{3,2,1,0:T(8,128)(2,1)}, bf16[8,2,32,256]{3,2,1,0:T(8,128)(2,1)S(1)}, u32[]{:S(2)}) copy-start(bf16[8,2,32,256]{3,2,1,0:T(8,128)(2,1)S(1)} %collective-permute-done.refs_1_) | copy-start | bytes 786436
  23.0 3.7 %collective-permute-start.2 = (f32[2,2,128]{2,1,0:T(2,128)}, f32[2,2,128]{2,1,0:T(2,128)S(1)}, u32[]{:S(2)}, u32[]{:S(2)}) collective-permute-start(f32[2,2,128]{2,1,0:T(2,128)} %stats.1), channel_id=1, source_target_pairs={{0,32},{32,0},{1,33},{33,1},{2,34},{34,2},{3,35},{35,3},{4,36},{36... | collective-permute-start | bytes 6152 | tf_op jit(solution)/shard_map/ppermute | solution.py:391
  28.1 15.3 %all-to-all-start = ((f32[64,2,2,128]{3,2,1,0:T(2,128)}), f32[64,2,2,128]{3,2,1,0:T(2,128)S(1)}, u32[]{:S(2)}, u32[]{:S(2)}) async-start(f32[64,2,2,128]{3,2,1,0:T(2,128)} %broadcast_in_dim.9), calls=%async_computation | async-start | bytes 262144 | tf_op jit(solution)/shard_map/all_to_all | solution.py:397
  33.2 8.3 %collective-permute-start.5 = (bf16[8,8,256]{2,1,0:T(8,128)(2,1)S(1)}, bf16[8,8,256]{2,1,0:T(8,128)(2,1)S(1)}, u32[]{:S(2)}, u32[]{:S(2)}) collective-permute-start(bf16[8,8,256]{2,1,0:T(8,128)(2,1)S(1)} %reshape.34), channel_id=1, source_target_pairs={{0,1},{1,2},{2,3},{3,4},{4,5},{5,6},{6,7},{7,8},{8,9},{9,10},{10,1... | collective-permute-start | bytes 98312 | tf_op jit(solution)/shard_map/ppermute | solution.py:385
  34.8 6.7 %collective-permute-start.6 = (bf16[8,8,256]{2,1,0:T(8,128)(2,1)S(1)}, bf16[8,8,256]{2,1,0:T(8,128)(2,1)S(1)}, u32[]{:S(2)}, u32[]{:S(2)}) collective-permute-start(bf16[8,8,256]{2,1,0:T(8,128)(2,1)S(1)} %reshape.35), channel_id=1, source_target_pairs={{1,0},{2,1},{3,2},{4,3},{5,4},{6,5},{7,6},{8,7},{9,8},{10,9},{11,1... | collective-permute-start | bytes 98312 | tf_op jit(solution)/shard_map/ppermute | solution.py:386
  40.2 3.2 %copy-start.7 = (bf16[8,64,256]{2,1,0:T(8,128)(2,1)}, bf16[8,64,256]{2,1,0:T(8,128)(2,1)S(1)}, u32[]{:S(2)}) copy-start(bf16[8,64,256]{2,1,0:T(8,128)(2,1)S(1)} %collective-permute-done.3.refs_3_) | copy-start | bytes 786436
  40.2 3.2 %copy-start.8 = (bf16[8,64,256]{2,1,0:T(8,128)(2,1)}, bf16[8,64,256]{2,1,0:T(8,128)(2,1)S(1)}, u32[]{:S(2)}) copy-start(bf16[8,64,256]{2,1,0:T(8,128)(2,1)S(1)} %collective-permute-done.4.refs_4_) | copy-start | bytes 786436
  41.5 1.9 %copy-start.11 = (bf16[8,8,256]{2,1,0:T(8,128)(2,1)}, bf16[8,8,256]{2,1,0:T(8,128)(2,1)S(1)}, u32[]{:S(2)}) copy-start(bf16[8,8,256]{2,1,0:T(8,128)(2,1)S(1)} %collective-permute-done.5.refs_5_) | copy-start | bytes 98308
  41.5 1.9 %copy-start.12 = (bf16[8,8,256]{2,1,0:T(8,128)(2,1)}, bf16[8,8,256]{2,1,0:T(8,128)(2,1)S(1)}, u32[]{:S(2)}) copy-start(bf16[8,8,256]{2,1,0:T(8,128)(2,1)S(1)} %collective-permute-done.6.refs_6_) | copy-start | bytes 98308
  43.4 0.7 copy-start
  64.1 15.2 %copy-start.5 = (f32[2,2,128]{2,1,0:T(2,128)S(1)}, f32[2,2,128]{2,1,0:T(2,128)}, u32[]{:S(2)}) copy-start(f32[2,2,128]{2,1,0:T(2,128)} %get-tuple-element.13) | copy-start | bytes 6148
  65.5 13.9 %collective-permute-start.9 = (bf16[8,4,32,256]{3,2,1,0:T(8,128)(2,1)S(1)}, bf16[8,4,32,256]{3,2,1,0:T(8,128)(2,1)S(1)}, u32[]{:S(2)}, u32[]{:S(2)}) collective-permute-start(bf16[8,4,32,256]{3,2,1,0:T(8,128)(2,1)S(1)} %get-tuple-element.19), channel_id=1, source_target_pairs={{32,0},{64,32},{96,64},{33,1},{65,33},{97,65},{34,2},{66,34},{98,6... | collective-permute-start | bytes 1572872 | tf_op jit(solution)/shard_map/ppermute | solution.py:367
  66.8 12.6 %collective-permute-start.7 = (f32[2,2,128]{2,1,0:T(2,128)}, f32[2,2,128]{2,1,0:T(2,128)S(1)}, u32[]{:S(2)}, u32[]{:S(2)}) collective-permute-start(f32[2,2,128]{2,1,0:T(2,128)} %get-tuple-element.13), channel_id=1, source_target_pairs={{0,32},{32,0},{1,33},{33,1},{2,34},{34,2},{3,35},{35,3},{4,36},{36... | collective-permute-start | bytes 6152 | tf_op jit(solution)/shard_map/ppermute | solution.py:391
  68.0 11.5 %collective-permute-start.8 = (bf16[8,4,32,256]{3,2,1,0:T(8,128)(2,1)S(1)}, bf16[8,4,32,256]{3,2,1,0:T(8,128)(2,1)}, u32[]{:S(2)}, u32[]{:S(2)}) collective-permute-start(bf16[8,4,32,256]{3,2,1,0:T(8,128)(2,1)S(1)} %get-tuple-element.20), channel_id=1, source_target_pairs={{0,32},{32,64},{64,96},{1,33},{33,65},{65,97},{2,34},{34,66},{66,9... | collective-permute-start | bytes 1572872 | tf_op jit(solution)/shard_map/ppermute | solution.py:366
  73.0 42.7 %collective-permute-start.10 = (bf16[8,128,256]{2,1,0:T(8,128)(2,1)S(1)}, bf16[8,128,256]{2,1,0:T(8,128)(2,1)}, u32[]{:S(2)}, u32[]{:S(2)}) collective-permute-start(bf16[8,128,256]{2,1,0:T(8,128)(2,1)S(1)} %reshape.37), channel_id=1, source_target_pairs={{0,1},{1,2},{2,3},{3,4},{4,5},{5,6},{6,7},{7,8},{8,9},{9,10},{10,1... | collective-permute-start | bytes 1572872 | tf_op jit(solution)/shard_map/ppermute | solution.py:370
  73.3 42.4 %collective-permute-start.11 = (bf16[8,128,256]{2,1,0:T(8,128)(2,1)S(1)}, bf16[8,128,256]{2,1,0:T(8,128)(2,1)}, u32[]{:S(2)}, u32[]{:S(2)}) collective-permute-start(bf16[8,128,256]{2,1,0:T(8,128)(2,1)S(1)} %reshape.38), channel_id=1, source_target_pairs={{1,0},{2,1},{3,2},{4,3},{5,4},{6,5},{7,6},{8,7},{9,8},{10,9},{11,1... | collective-permute-start | bytes 1572872 | tf_op jit(solution)/shard_map/ppermute | solution.py:371
  79.4 36.4 %copy-start.1 = (bf16[8,4,32,256]{3,2,1,0:T(8,128)(2,1)}, bf16[8,4,32,256]{3,2,1,0:T(8,128)(2,1)S(1)}, u32[]{:S(2)}) copy-start(bf16[8,4,32,256]{3,2,1,0:T(8,128)(2,1)S(1)} %collective-permute-done.9.refs_2_) | copy-start | bytes 1572868
  80.9 34.8 %collective-permute-start.12 = (bf16[8,32,256]{2,1,0:T(8,128)(2,1)S(1)}, bf16[8,32,256]{2,1,0:T(8,128)(2,1)S(1)}, u32[]{:S(2)}, u32[]{:S(2)}) collective-permute-start(bf16[8,32,256]{2,1,0:T(8,128)(2,1)S(1)} %reshape.39), channel_id=1, source_target_pairs={{0,1},{1,2},{2,3},{3,4},{4,5},{5,6},{6,7},{7,8},{8,9},{9,10},{10,1... | collective-permute-start | bytes 393224 | tf_op jit(solution)/shard_map/ppermute | solution.py:385
  81.0 34.8 %collective-permute-start.13 = (bf16[8,32,256]{2,1,0:T(8,128)(2,1)S(1)}, bf16[8,32,256]{2,1,0:T(8,128)(2,1)S(1)}, u32[]{:S(2)}, u32[]{:S(2)}) collective-permute-start(bf16[8,32,256]{2,1,0:T(8,128)(2,1)S(1)} %reshape.40), channel_id=1, source_target_pairs={{1,0},{2,1},{3,2},{4,3},{5,4},{6,5},{7,6},{8,7},{9,8},{10,9},{11,1... | collective-permute-start | bytes 393224 | tf_op jit(solution)/shard_map/ppermute | solution.py:386
  115.7 0.6 copy-start.9
  115.7 0.7 copy-start.10

commit v3 on v2

--- a/solution.py
+++ b/solution.py
@@ -64,6 +64,7 @@
     group_squares = exact_dot(squares_ref[...] + count * offset * offset, fold)
     out_ref[0] = packed(group_sum)
     out_ref[1] = packed(group_squares)
+    out_ref[2] = jnp.full(out_ref.shape[1:], count * size, jnp.float32)
 
 
 def row_statistics(rows, limits, count, sums_ref, squares_ref, b):
@@ -115,11 +116,35 @@
     return pl.BlockSpec(memory_space=pltpu.VMEM)
 
 
-def fetch(x_hbm_ref, x_ref, sems, b):
-    return pltpu.make_async_copy(x_hbm_ref.at[b], x_ref.at[b], sems.at[b])
-
-
-def stats_kernel(points_ref, x_hbm_ref, out_ref, x_ref, sems, sums_ref, squares_ref):
+def fetch(x_hbm_ref, x_ref, sems, b, base=0):
+    return pltpu.make_async_copy(x_hbm_ref.at[base + b], x_ref.at[b], sems.at[b])
+
+
+def pack_edges(x_ref, b, d, edges, k):
+    _, rows, cols, _ = x_ref.shape
+    first_row_ref, last_row_ref, first_col_ref, last_col_ref = edges
+    first_row_ref[k] = x_ref[b, :d]
+    last_row_ref[k] = x_ref[b, rows - d :]
+    for h in range(rows):
+        first_col_ref[k, h * d : (h + 1) * d] = x_ref[b, h, :d]
+        last_col_ref[k, h * d : (h + 1) * d] = x_ref[b, h, cols - d :]
+
+
+def edge_shapes(x, d):
+    samples, rows, width, channels = x.shape
+    shapes = [(samples, d, width, channels)] * 2 + [(samples, rows * d, channels)] * 2
+    return [jax.ShapeDtypeStruct(shape, x.dtype) for shape in shapes]
+
+
+def edge_specs(x, d, block):
+    return [
+        pl.BlockSpec((block, *e.shape[1:]), lambda g, *_, n=len(e.shape): (g,) + (0,) * (n - 1))
+        for e in edge_shapes(x, d)
+    ]
+
+
+def stats_kernel(points_ref, x_hbm_ref, out_ref, *refs):
+    *edges, x_ref, sems, sums_ref, squares_ref = refs
     g = pl.program_id(0)
 
     @pl.when(g == 0)
@@ -134,6 +159,7 @@
     row_statistics(
         lambda h, n: x_ref[g, h, :n].astype(jnp.float32), limits, count, sums_ref, squares_ref, g
     )
+    pack_edges(x_ref, g, FIRST_DILATION, edges, 0)
 
     @pl.when(g == pl.num_programs(0) - 1)
     def _():
@@ -142,15 +168,18 @@
 
 def local_statistics(x, points):
     samples, rows, width, channels = x.shape
-    shape = (2, samples * GROUPS // LANES, LANES)
+    shape = (3, samples * GROUPS // LANES, LANES)
     return pl.pallas_call(
         stats_kernel,
-        out_shape=jax.ShapeDtypeStruct(shape, jnp.float32),
+        out_shape=[jax.ShapeDtypeStruct(shape, jnp.float32), *edge_shapes(x, FIRST_DILATION)],
         grid_spec=pltpu.PrefetchScalarGridSpec(
             num_scalar_prefetch=1,
             grid=(samples,),
             in_specs=[pl.BlockSpec(memory_space=pltpu.HBM)],
-            out_specs=pl.BlockSpec(shape, lambda g, *_: (0, 0, 0)),
+            out_specs=[
+                pl.BlockSpec(shape, lambda g, *_: (0, 0, 0)),
+                *edge_specs(x, FIRST_DILATION, 1),
+            ],
             scratch_shapes=[
                 pltpu.VMEM(x.shape, x.dtype),
                 pltpu.SemaphoreType.DMA((samples,)),
@@ -202,15 +231,19 @@
     norm_ref[1] = both[samples:]
 
 
-def conv_kernel(dilation, chunk, which, with_stats, points_ref, flags_ref, parts_ref, points_row_ref, *refs):
+def conv_kernel(dilation, chunk, which, with_stats, first, base, halo, points_ref, flags_ref, parts_ref, *refs):
     d = dilation
-    x_hbm_ref, top_ref, bottom_ref, left_ref, right_ref, left_end_ref, right_end_ref, w_ref, out_hbm_ref, *rest = refs
+    points_row_ref, x_hbm_ref, top_ref, bottom_ref, left_ref, right_ref, w_ref, *refs = refs
+    if first:
+        given_ref, *refs = refs
+    out_hbm_ref, *rest = refs
     if with_stats:
-        stats_ref, x_ref, sems, out_ref, out_sems, norm_ref, even_ref, odd_ref, sums_ref, squares_ref, kept_ref = rest
+        stats_ref, *edges = rest[:5]
+        x_ref, sems, out_ref, out_sems, norm_ref, even_ref, odd_ref, sums_ref, squares_ref, kept_ref = rest[5:]
     else:
         x_ref, sems, out_ref, out_sems, norm_ref, even_ref, odd_ref = rest
     g = pl.program_id(0)
-    samples = norm_ref.shape[1]
+    samples = x_ref.shape[0]
     _, rows, cols, channels = x_ref.shape
     lat, lon = tile_position()
     lon_total = lax.axis_size(LON) * cols
@@ -223,8 +256,8 @@
     after_origin = (origin + cols) % lon_total
 
     def activate_rows(b, act_ref, lo, hi):
-        mean = norm_ref[0, pl.ds(b, 1)]
-        half = norm_ref[1, pl.ds(b, 1)]
+        mean = norm_ref[0, pl.ds(first + b, 1)]
+        half = norm_ref[1, pl.ds(first + b, 1)]
 
         def activated(value):
             t = (value.astype(jnp.float32) - mean) * half
@@ -232,14 +265,14 @@
 
         for e in range(lo, hi):
             if e < d:
-                row, side = top_ref[b, e], (left_end_ref, right_end_ref, e)
+                row = top_ref[halo + b, e]
             elif e < rows + d:
-                row, side = x_ref[b, e - d], (left_ref, right_ref, e - d)
+                row = x_ref[b, e - d]
             else:
-                row, side = bottom_ref[b, e - rows - d], (left_end_ref, right_end_ref, e - rows)
-            at = slice(side[2] * d, (side[2] + 1) * d)
-            left = activated(side[0][b, at])
-            right = activated(side[1][b, at])
+                row = bottom_ref[halo + b, e - rows - d]
+            at = slice(e * d, (e + 1) * d)
+            left = activated(left_ref[halo + b, at])
+            right = activated(right_ref[halo + b, at])
             mid = jnp.where(column < points[e] - origin, activated(row), 0.0)
             lhs = jnp.where(edge < points[e] - before_origin, left, 0.0)
             rhs = jnp.where(edge < points[e] - after_origin, right, 0.0)
@@ -263,7 +296,7 @@
             kept_ref[start : start + chunk] = result
 
     def phase(k, act_ref, follow, next_ref):
-        scale = flags_ref[2 * g + k, which].astype(jnp.float32) * (1.0 / KEEP_RATE)
+        scale = flags_ref[first + 2 * g + k, which].astype(jnp.float32) * (1.0 / KEEP_RATE)
         steps = rows // chunk
         each = (rows + 2 * d) // steps
         for step in range(steps):
@@ -271,25 +304,28 @@
             activate_rows(follow, next_ref, step * each, last)
             convolve_rows(k, scale, act_ref, step * chunk)
         store(2 * g + k).start()
+        if with_stats:
+            pack_edges(out_ref, 2 * g + k, SECOND_DILATION, edges, k)
 
     def store(b):
-        return pltpu.make_async_copy(out_ref.at[b], out_hbm_ref.at[b], out_sems.at[b])
+        place = b if with_stats else first + b
+        return pltpu.make_async_copy(out_ref.at[b], out_hbm_ref.at[place], out_sems.at[b])
 
     @pl.when(g == 0)
     def _():
         for b in range(samples):
-            fetch(x_hbm_ref, x_ref, sems, b).start()
+            fetch(x_hbm_ref, x_ref, sems, b, base).start()
         combine_statistics(parts_ref, points_row_ref, norm_ref, rows, cols)
-        fetch(x_hbm_ref, x_ref, sems, 0).wait()
+        fetch(x_hbm_ref, x_ref, sems, 0, base).wait()
         activate_rows(0, even_ref, 0, rows + 2 * d)
         if with_stats:
             kept_ref[...] = jnp.zeros_like(kept_ref)
 
     @pl.when(g < samples // 2 - 1)
     def _():
-        fetch(x_hbm_ref, x_ref, sems, 2 * g + 2).wait()
-
-    fetch(x_hbm_ref, x_ref, sems, 2 * g + 1).wait()
+        fetch(x_hbm_ref, x_ref, sems, 2 * g + 2, base).wait()
+
+    fetch(x_hbm_ref, x_ref, sems, 2 * g + 1, base).wait()
     count = live_count(limits)
     phase(0, even_ref, 2 * g + 1, odd_ref)
     if with_stats:
@@ -307,7 +343,10 @@
             row_statistics(
                 lambda h, n: out_ref[2 * g + 1, h, :n].astype(jnp.float32), limits, count, sums_ref, squares_ref, samples - 1
             )
-            store_group_stats(sums_ref, squares_ref, count, stats_ref)
+            at = pl.ds(first // (LANES // GROUPS), samples * GROUPS // LANES)
+            if first:
+                stats_ref[...] = given_ref[...]
+            store_group_stats(sums_ref, squares_ref, count, stats_ref.at[:, at])
 
     @pl.when(g == pl.num_programs(0) - 1)
     def _():
@@ -315,25 +354,29 @@
             store(b).wait()
 
 
-def convolve(x, halos, weight, parts, points, flags, dilation, which, with_stats):
-    samples, rows, width, channels = x.shape
+def convolve(x, halos, weight, parts, points, flags, given, dilation, which, with_stats, first, base, halo):
+    _, rows, width, channels = x.shape
     d = dilation
+    total = flags.shape[0]
+    samples = total // 2
+
     def whole(shape):
         return pl.BlockSpec(shape, lambda g, *_: (0,) * len(shape))
 
-    out_shape = [jax.ShapeDtypeStruct(x.shape, jnp.bfloat16)]
+    half = jax.ShapeDtypeStruct((samples, rows, width, channels), jnp.bfloat16)
+    out_shape = [half if with_stats else jax.ShapeDtypeStruct((total, *half.shape[1:]), jnp.bfloat16)]
     out_specs = [pl.BlockSpec(memory_space=pltpu.HBM)]
     act = pltpu.VMEM((rows + 2 * d, width, 3 * channels), jnp.bfloat16)
-    scratch = [pltpu.VMEM(x.shape, x.dtype), pltpu.SemaphoreType.DMA((samples,))] * 2
-    scratch += [pltpu.VMEM((2, samples, channels), jnp.float32), act, act]
+    scratch = [pltpu.VMEM(half.shape, x.dtype), pltpu.SemaphoreType.DMA((samples,))] * 2
+    scratch += [pltpu.VMEM((2, total, channels), jnp.float32), act, act]
     if with_stats:
-        shape = (2, samples * GROUPS // LANES, LANES)
-        out_shape.append(jax.ShapeDtypeStruct(shape, jnp.float32))
-        out_specs.append(whole(shape))
+        shape = (3, total * GROUPS // LANES, LANES)
+        out_shape += [jax.ShapeDtypeStruct(shape, jnp.float32), *edge_shapes(half, SECOND_DILATION)]
+        out_specs += [whole(shape), *edge_specs(half, SECOND_DILATION, 2)]
         scratch += [pltpu.VMEM((samples, channels), jnp.float32)] * 2
         scratch += [pltpu.VMEM((rows, width, channels), jnp.bfloat16)]
     return pl.pallas_call(
-        functools.partial(conv_kernel, d, CHUNK, which, with_stats),
+        functools.partial(conv_kernel, d, CHUNK, which, with_stats, first, base, halo),
         out_shape=out_shape,
         grid_spec=pltpu.PrefetchScalarGridSpec(
             num_scalar_prefetch=2,
@@ -344,93 +387,89 @@
                 pl.BlockSpec(memory_space=pltpu.HBM),
                 *[in_vmem()] * len(halos),
                 in_vmem(),
+                *([in_vmem() if with_stats else pl.BlockSpec(memory_space=pltpu.HBM)] if first else []),
             ],
             out_specs=out_specs,
             scratch_shapes=scratch,
         ),
+        input_output_aliases={10: 0} if first and not with_stats else {},
         compiler_params=pltpu.CompilerParams(
             dimension_semantics=("arbitrary",), vmem_limit_bytes=VMEM_LIMIT
         ),
         cost_estimate=pl.CostEstimate(
-            flops=2 * x.size * 9 * channels, bytes_accessed=5 * x.size, transcendentals=2 * x.size
-        ),
-        name="conv%d" % d,
-    )(points, flags, parts, points[None], x, *halos, weight)
-
-
-def exchange_sides(x, d):
-    samples, rows, width, channels = x.shape
-    lat, lon = lax.axis_size(LAT), lax.axis_size(LON)
-    up = [(i, i + 1) for i in range(lat - 1)]
-    down = [(i + 1, i) for i in range(lat - 1)]
-    top = lax.ppermute(x[:, rows - d :], LAT, up)
-    bottom = lax.ppermute(x[:, :d], LAT, down)
-    east = [(i, (i + 1) % lon) for i in range(lon)]
-    west = [((i + 1) % lon, i) for i in range(lon)]
-    left = lax.ppermute(x[:, :, width - d :].reshape(samples, rows * d, channels), LON, east)
-    right = lax.ppermute(x[:, :, :d].reshape(samples, rows * d, channels), LON, west)
-    return top, bottom, left, right
-
-
-def exchange_corners(top, bottom):
+            flops=18 * samples * rows * width * channels * channels,
+            bytes_accessed=5 * samples * rows * width * channels,
+            transcendentals=2 * samples * rows * width * channels,
+        ),
+        name="conv%d_%d" % (d, first),
+    )(points, flags, parts, points[None], x, *halos, weight, *([given] if first else []))
+
+
+def exchange_rows(edges):
+    lat = lax.axis_size(LAT)
+    top = lax.ppermute(edges[1], LAT, [(i, i + 1) for i in range(lat - 1)])
+    bottom = lax.ppermute(edges[0], LAT, [(i + 1, i) for i in range(lat - 1)])
+    return top, bottom
+
+
+def exchange_columns(edges, top, bottom):
     samples, d, width, channels = top.shape
     lon = lax.axis_size(LON)
-    east = [(i, (i + 1) % lon) for i in range(lon)]
-    west = [((i + 1) % lon, i) for i in range(lon)]
-
-    def packed(lo, hi):
-        ends = jnp.concatenate([top[:, :, lo:hi], bottom[:, :, lo:hi]], axis=1)
-        return ends.reshape(samples, 2 * d * d, channels)
-
-    left = lax.ppermute(packed(width - d, width), LON, east)
-    right = lax.ppermute(packed(0, d), LON, west)
+
+    def packed(cols, lo, hi):
+        above = top[:, :, lo:hi].reshape(samples, d * d, channels)
+        below = bottom[:, :, lo:hi].reshape(samples, d * d, channels)
+        return jnp.concatenate([above, cols, below], axis=1)
+
+    left = lax.ppermute(packed(edges[3], width - d, width), LON, [(i, (i + 1) % lon) for i in range(lon)])
+    right = lax.ppermute(packed(edges[2], 0, d), LON, [((i + 1) % lon, i) for i in range(lon)])
     return left, right
 
 
-def share_statistics(local, own_count, other_count, core_axis="core"):
-    other = lax.ppermute(local, core_axis, [(0, 1), (1, 0)])
-    both = own_count + other_count
+def merge_cores(local):
+    other = lax.ppermute(local, "core", [(0, 1), (1, 0)])
+    own_count, other_count = local[2], other[2]
+    both = jnp.maximum(own_count + other_count, 1.0)
     gap = local[0] / jnp.maximum(own_count, 1.0) - other[0] / jnp.maximum(other_count, 1.0)
-    squares = local[1] + other[1] + gap * gap * (own_count * other_count / jnp.maximum(both, 1.0))
+    squares = local[1] + other[1] + gap * gap * (own_count * other_count / both)
     merged = jnp.stack([local[0] + other[0], squares])
-    chips = lax.axis_size(CHIPS)
-    return lax.all_to_all(jnp.broadcast_to(merged[None], (chips, *merged.shape)), CHIPS, 0, 0)
-
-
-def tile_count(band_points, rows, width, size, core):
-    _, lon = tile_position()
-    lat = lax.axis_index("zh") * lax.axis_size("core") + core
-    row = jnp.arange(band_points.shape[0], dtype=jnp.int32)
-    live = jnp.clip(band_points - lon * width, 0, width)
-    return jnp.where(row // rows == lat, live, 0).sum().astype(jnp.float32) * size
+    return jnp.broadcast_to(merged[None], (lax.axis_size(CHIPS), *merged.shape))
 
 
 def per_device(features, band_points, survival_flags, first_kernel_weight, second_kernel_weight):
-    _, rows, width, channels = features.shape
-    core = lax.axis_index("core")
-    size = channels // GROUPS
-    own_count = tile_count(band_points, rows, width, size, core)
-    other_count = tile_count(band_points, rows, width, size, 1 - core)
+    samples, _, _, channels = features.shape
+    half = samples // 2
     first_weight = first_kernel_weight.reshape(3, 3 * channels, channels)
     second_weight = second_kernel_weight.reshape(3, 3 * channels, channels)
 
-    top, bottom, left, right = exchange_sides(features, FIRST_DILATION)
-    local = local_statistics(features, band_points)
-    local, top, bottom = lax.optimization_barrier((local, top, bottom))
-    ends = exchange_corners(top, bottom)
-    parts = share_statistics(local, own_count, other_count)
-    halos = (top, bottom, left, right, *ends)
-    first, local = convolve(
-        features, halos, first_weight, parts, band_points, survival_flags, FIRST_DILATION, 0, True
-    )
-    top, bottom, left, right = exchange_sides(first, SECOND_DILATION)
-    parts = share_statistics(local, own_count, other_count)
-    ends = exchange_corners(top, bottom)
-    halos = (top, bottom, left, right, *ends)
-    (section,) = convolve(
-        first, halos, second_weight, parts, band_points, survival_flags, SECOND_DILATION, 1, False
-    )
-    return section
+    local, *edges = local_statistics(features, band_points)
+    top, bottom = exchange_rows(edges)
+    mine = merge_cores(local)
+    mine, top, bottom = lax.optimization_barrier((mine, top, bottom))
+    parts = lax.all_to_all(mine, CHIPS, 0, 0)
+    halos = (top, bottom, *exchange_columns(edges, top, bottom))
+
+    def first_half(start, given):
+        return convolve(
+            features, halos, first_weight, parts, band_points, survival_flags, given, FIRST_DILATION, 0, True, start, start, start
+        )
+
+    def second_half(start, x, halos, parts, given):
+        return convolve(
+            x, halos, second_weight, parts, band_points, survival_flags, given, SECOND_DILATION, 1, False, start, 0, 0
+        )[0]
+
+    early, local, *early_edges = first_half(0, None)
+    early_rows = exchange_rows(early_edges)
+    late, local, *late_edges = first_half(half, local)
+    local, *early_rows = lax.optimization_barrier((local, *early_rows))
+    late_rows = exchange_rows(late_edges)
+    early_columns = exchange_columns(early_edges, *early_rows)
+    mine = merge_cores(local)
+    parts = lax.all_to_all(mine, CHIPS, 0, 0)
+    late_columns = exchange_columns(late_edges, *late_rows)
+    section = second_half(0, early, (*early_rows, *early_columns), parts, None)
+    return second_half(half, late, (*late_rows, *late_columns), parts, section)
 
 
 def solution(mesh):

time: 135 us -> 147 us (1.089)
  the two profiles are of different devices: /device:TPU:0 before, /device:TPU:1 now
where the time goes in v3:
time: 147 us; the launch traced here: 146 us
  Pallas kernels  56.2 us (38%)
  starting transfers between devices  55.7 us (38%)
  waiting for transfers between devices  25.4 us (17%)
  local copies, waits for them, and re-layouts  4.94 us (3%)
  other arithmetic  2.89 us (2%)
    pallas_call x4, Pallas kernels, convolve(): pl.pallas_call(functools.partial(conv_kernel, d, CHUNK, which, with_stats...  49.3 us
    ppermute x3, starting transfers between devices, exchange_columns(): lax.ppermute(packed(edges[2], 0, d), LON, [((i + 1) % lon, i) for i in ra...  19.2 us
    ppermute x3, starting transfers between devices, exchange_rows(): top = lax.ppermute(edges[1], LAT, [(i, i + 1) for i in range(lat - 1)])  15.1 us
    all_to_all x2, starting transfers between devices, per_device(): parts = lax.all_to_all(mine, CHIPS, 0, 0)  12.6 us
    ppermute x3, waiting for transfers between devices, exchange_rows(): bottom = lax.ppermute(edges[0], LAT, [(i + 1, i) for i in range(lat - 1)])  11.5 us
    all_to_all x2, waiting for transfers between devices, per_device(): parts = lax.all_to_all(mine, CHIPS, 0, 0)  11.5 us
    pallas_call x1, Pallas kernels, local_statistics(): pl.pallas_call(stats_kernel, out_shape=[jax.ShapeDtypeStruct(shape, jnp.f...  6.87 us
    ppermute x3, starting transfers between devices, exchange_rows(): bottom = lax.ppermute(edges[0], LAT, [(i + 1, i) for i in range(lat - 1)])  5.94 us
  transfers between devices with their start and end apart: 16, of which 6 were waited for; matrix products, arithmetic and copies ran while one was open for 2% of the time, Pallas kernels for 17%

profile of v3, /device:TPU:1, one launch (start us, length us, event | category | flops | bytes accessed | tf_op | source)
XLA Modules:
  0.0 145.8 jit_solution(8521565050974201144)
XLA Ops:
  0.0 6.9 %stats.1 = (f32[3,2,128]{2,1,0:T(2,128)}, bf16[8,2,32,256]{3,2,1,0:T(8,128)(2,1)}, bf16[8,2,32,256]{3,2,1,0:T(8,128)(2,1)}, bf16[8,64,256]{2,1,0:T(8,128)(2,1)}, bf16[8,64,256]{2,1,0:T(8,128)(2,1)}) custom-call(s32[128]{0:T(128)} %points_ref.9, bf16[8,32,32,256]{3,2,1,0:T(8,128)(2,1)} %refs_1_.3), custom_call_target="tpu_custom_call" | custom-call | flops 16777216 | bytes 4194304 | tf_op jit(solution)/shard_map/stats/pallas_call | solution.py:172
  6.9 1.5 %collective-permute-start = (f32[3,2,128]{2,1,0:T(2,128)}, f32[3,2,128]{2,1,0:T(2,128)S(1)}, u32[]{:S(2)}, u32[]{:S(2)}) collective-permute-start(f32[3,2,128]{2,1,0:T(2,128)} %get-tuple-element.28), channel_id=1, source_target_pairs={{0,32},{32,0},{1,33},{33,1},{2,34},{34,2},{3,35},{35,3},{4,36},{36... | collective-permute-start | bytes 9224 | tf_op jit(solution)/shard_map/ppermute | solution.py:430
  8.4 5.5 %collective-permute-start.1 = (bf16[8,2,32,256]{3,2,1,0:T(8,128)(2,1)}, bf16[8,2,32,256]{3,2,1,0:T(8,128)(2,1)S(1)}, u32[]{:S(2)}, u32[]{:S(2)}) collective-permute-start(bf16[8,2,32,256]{3,2,1,0:T(8,128)(2,1)} %get-tuple-element.29), channel_id=1, source_target_pairs={{0,32},{32,64},{64,96},{1,33},{33,65},{65,97},{2,34},{34,66},{66,9... | collective-permute-start | bytes 786440 | tf_op jit(solution)/shard_map/ppermute | solution.py:410
  13.9 1.9 %collective-permute-start.2 = (bf16[8,2,32,256]{3,2,1,0:T(8,128)(2,1)}, bf16[8,2,32,256]{3,2,1,0:T(8,128)(2,1)S(1)}, u32[]{:S(2)}, u32[]{:S(2)}) collective-permute-start(bf16[8,2,32,256]{3,2,1,0:T(8,128)(2,1)} %get-tuple-element.30), channel_id=1, source_target_pairs={{32,0},{64,32},{96,64},{33,1},{65,33},{97,65},{34,2},{66,34},{98,6... | collective-permute-start | bytes 786440 | tf_op jit(solution)/shard_map/ppermute | solution.py:411
  15.8 0.0 collective-permute-done
  15.8 0.7 slice_add_fusion.3
  16.5 1.0 collective-permute-done.1.refs_2_
  17.5 5.8 %collective-permute-done.2.refs_3_ = bf16[8,2,32,256]{3,2,1,0:T(8,128)(2,1)S(1)} collective-permute-done((bf16[8,2,32,256]{3,2,1,0:T(8,128)(2,1)}, bf16[8,2,32,256]{3,2,1,0:T(8,128)(2,1)S(1)}, u32[]{:S(2)}, u32[]{:S(2)}) %collective-permute-start.2) | collective-permute-done | bytes 262176 | tf_op jit(solution)/shard_map/ppermute | solution.py:411
  23.3 0.7 broadcast_in_dim.6
  24.0 0.1 fusion.6
  24.2 1.0 pad_maximum_fusion.5
  25.2 8.6 %collective-permute-start.4 = (bf16[8,72,256]{2,1,0:T(8,128)(2,1)S(1)}, bf16[8,72,256]{2,1,0:T(8,128)(2,1)S(1)}, u32[]{:S(2)}, u32[]{:S(2)}) collective-permute-start(bf16[8,72,256]{2,1,0:T(8,128)(2,1)S(1)} %pad_maximum_fusion.5), channel_id=1, source_target_pairs={{1,0},{2,1},{3,2},{4,3},{5,4},{6,5},{7,6},{8,7},{9,8},{10,9},{11,1... | collective-permute-start | bytes 884744 | tf_op jit(solution)/shard_map/ppermute | solution.py:425
  33.8 1.0 pad_maximum_fusion.4
  34.9 0.1 collective-permute-start.3
  35.0 8.0 %all-to-all-start = ((f32[64,2,2,128]{3,2,1,0:T(2,128)}), f32[64,2,2,128]{3,2,1,0:T(2,128)S(1)}, u32[]{:S(2)}, u32[]{:S(2)}) async-start(f32[64,2,2,128]{3,2,1,0:T(2,128)} %broadcast_in_dim.6), calls=%async_computation | async-start | bytes 262144 | tf_op jit(solution)/shard_map/all_to_all | solution.py:449
  42.9 0.0 copy-done.13
  42.9 0.7 copy.10.flags_ref
  43.6 8.1 %all-to-all-done.parts_ref = f32[64,2,2,128]{3,2,1,0:T(2,128)S(1)} async-done(((f32[64,2,2,128]{3,2,1,0:T(2,128)}), f32[64,2,2,128]{3,2,1,0:T(2,128)S(1)}, u32[]{:S(2)}, u32[]{:S(2)}) %all-to-all-start) | async-done | bytes 131104 | tf_op jit(solution)/shard_map/all_to_all | solution.py:449
  51.7 0.0 collective-permute-done.4.refs_5_
  51.7 0.0 collective-permute-done.3.refs_4_
  51.7 0.0 copy-start.18
  51.8 0.0 copy-done.10
  51.8 0.0 copy-done.11
  51.8 0.6 copy-done.5
  52.4 0.1 copy-done.17
  52.5 0.1 copy-done.18
  52.6 13.3 %conv2_0.1 = (bf16[4,32,32,256]{3,2,1,0:T(8,128)(2,1)}, f32[3,2,128]{2,1,0:T(2,128)}, bf16[4,4,32,256]{3,2,1,0:T(8,128)(2,1)}, bf16[4,4,32,256]{3,2,1,0:T(8,128)...) custom-call(s32[128]{0:T(128)} %points_ref.9, s32[8,2]{1,0:T(8,128)} %copy.10.flags_ref, ...), custom_call_target="tpu_custom_call" | custom-call | flops 4831838208 | bytes 5242880 | tf_op jit(solution)/shard_map/conv2_0/pallas_call | solution.py:378
  65.9 4.3 %collective-permute-start.5 = (bf16[4,4,32,256]{3,2,1,0:T(8,128)(2,1)}, bf16[4,4,32,256]{3,2,1,0:T(8,128)(2,1)S(1)}, u32[]{:S(2)}, u32[]{:S(2)}) collective-permute-start(bf16[4,4,32,256]{3,2,1,0:T(8,128)(2,1)} %get-tuple-element.38), channel_id=1, source_target_pairs={{0,32},{32,64},{64,96},{1,33},{33,65},{65,97},{2,34},{34,66},{66,9... | collective-permute-start | bytes 786440 | tf_op jit(solution)/shard_map/ppermute | solution.py:410
  70.2 2.1 %collective-permute-start.6 = (bf16[4,4,32,256]{3,2,1,0:T(8,128)(2,1)}, bf16[4,4,32,256]{3,2,1,0:T(8,128)(2,1)S(1)}, u32[]{:S(2)}, u32[]{:S(2)}) collective-permute-start(bf16[4,4,32,256]{3,2,1,0:T(8,128)(2,1)} %get-tuple-element.39), channel_id=1, source_target_pairs={{32,0},{64,32},{96,64},{33,1},{65,33},{97,65},{34,2},{66,34},{98,6... | collective-permute-start | bytes 786440 | tf_op jit(solution)/shard_map/ppermute | solution.py:411
  72.3 0.0 copy-start.3
  72.3 0.0 copy-start.2
  72.3 13.5 %conv2_4.1 = (bf16[4,32,32,256]{3,2,1,0:T(8,128)(2,1)}, f32[3,2,128]{2,1,0:T(2,128)}, bf16[4,4,32,256]{3,2,1,0:T(8,128)(2,1)}, bf16[4,4,32,256]{3,2,1,0:T(8,128)...) custom-call(s32[128]{0:T(128)} %points_ref.9, s32[8,2]{1,0:T(8,128)} %copy.10.flags_ref, ...), custom_call_target="tpu_custom_call" | custom-call | flops 4831838208 | bytes 5242880 | tf_op jit(solution)/shard_map/conv2_4/pallas_call | solution.py:378
  85.9 0.0 copy-start.12
  85.9 0.0 copy-start.1
  85.9 0.0 copy-start
  85.9 5.3 %collective-permute-start.8 = (bf16[4,4,32,256]{3,2,1,0:T(8,128)(2,1)}, bf16[4,4,32,256]{3,2,1,0:T(8,128)(2,1)S(1)}, u32[]{:S(2)}, u32[]{:S(2)}) collective-permute-start(bf16[4,4,32,256]{3,2,1,0:T(8,128)(2,1)} %get-tuple-element.42), channel_id=1, source_target_pairs={{0,32},{32,64},{64,96},{1,33},{33,65},{65,97},{2,34},{34,66},{66,9... | collective-permute-start | bytes 786440 | tf_op jit(solution)/shard_map/ppermute | solution.py:410
  91.2 1.9 %collective-permute-start.9 = (bf16[4,4,32,256]{3,2,1,0:T(8,128)(2,1)}, bf16[4,4,32,256]{3,2,1,0:T(8,128)(2,1)S(1)}, u32[]{:S(2)}, u32[]{:S(2)}) collective-permute-start(bf16[4,4,32,256]{3,2,1,0:T(8,128)(2,1)} %get-tuple-element.43), channel_id=1, source_target_pairs={{32,0},{64,32},{96,64},{33,1},{65,33},{97,65},{34,2},{66,34},{98,6... | collective-permute-start | bytes 786440 | tf_op jit(solution)/shard_map/ppermute | solution.py:411
  93.1 0.0 collective-permute-done.5.refs_2_
  93.1 0.0 copy-start.6
  93.1 0.0 collective-permute-done.6.refs_3_
  93.1 0.0 copy-start.7
  93.1 0.1 collective-permute-start.7
  93.4 1.4 collective-permute-done.8.refs_2_
  94.8 5.7 %collective-permute-done.9.refs_3_ = bf16[4,4,32,256]{3,2,1,0:T(8,128)(2,1)S(1)} collective-permute-done((bf16[4,4,32,256]{3,2,1,0:T(8,128)(2,1)}, bf16[4,4,32,256]{3,2,1,0:T(8,128)(2,1)S(1)}, u32[]{:S(2)}, u32[]{:S(2)}) %collective-permute-start.9) | collective-permute-done | bytes 262176 | tf_op jit(solution)/shard_map/ppermute | solution.py:411
  100.6 0.0 copy-done.3
  100.7 0.3 collective-permute-start.12
  101.0 0.0 copy-done.2
  101.0 5.5 %collective-permute-start.13 = (bf16[4,160,256]{2,1,0:T(8,128)(2,1)S(1)}, bf16[4,160,256]{2,1,0:T(8,128)(2,1)S(1)}, u32[]{:S(2)}, u32[]{:S(2)}) collective-permute-start(bf16[4,160,256]{2,1,0:T(8,128)(2,1)S(1)} %pad_maximum_fusion.3), channel_id=1, source_target_pairs={{1,0},{2,1},{3,2},{4,3},{5,4},{6,5},{7,6},{8,7},{9,8},{10,9},{11,1... | collective-permute-start | bytes 983048 | tf_op jit(solution)/shard_map/ppermute | solution.py:425
  106.5 0.0 collective-permute-done.7
  106.6 0.7 broadcast_in_dim.8
  107.2 4.6 %all-to-all-start.1 = ((f32[64,2,2,128]{3,2,1,0:T(2,128)}), f32[64,2,2,128]{3,2,1,0:T(2,128)S(1)}, u32[]{:S(2)}, u32[]{:S(2)}) async-start(f32[64,2,2,128]{3,2,1,0:T(2,128)} %broadcast_in_dim.8), calls=%async_computation.1 | async-start | bytes 262144 | tf_op jit(solution)/shard_map/all_to_all | solution.py:469
  112.0 1.0 collective-permute-start.10
  113.0 5.1 %collective-permute-start.11 = (bf16[4,160,256]{2,1,0:T(8,128)(2,1)S(1)}, bf16[4,160,256]{2,1,0:T(8,128)(2,1)S(1)}, u32[]{:S(2)}, u32[]{:S(2)}) collective-permute-start(bf16[4,160,256]{2,1,0:T(8,128)(2,1)S(1)} %pad_maximum_fusion.1), channel_id=1, source_target_pairs={{1,0},{2,1},{3,2},{4,3},{5,4},{6,5},{7,6},{8,7},{9,8},{10,9},{11,1... | collective-permute-start | bytes 983048 | tf_op jit(solution)/shard_map/ppermute | solution.py:425
  118.0 3.3 %all-to-all-done.1.parts_ref = f32[64,2,2,128]{3,2,1,0:T(2,128)S(1)} async-done(((f32[64,2,2,128]{3,2,1,0:T(2,128)}), f32[64,2,2,128]{3,2,1,0:T(2,128)S(1)}, u32[]{:S(2)}, u32[]{:S(2)}) %all-to-all-start.1) | async-done | bytes 131104 | tf_op jit(solution)/shard_map/all_to_all | solution.py:469
  121.4 0.0 collective-permute-done.12.refs_4_
  121.4 0.0 collective-permute-done.13.refs_5_
  121.4 0.6 copy-done.4
  122.0 0.1 copy-done.14
  122.1 0.1 copy-done.15
  122.3 11.3 %conv4_0.1.refs_7_ = bf16[8,32,32,256]{3,2,1,0:T(8,128)(2,1)} custom-call(s32[128]{0:T(128)} %points_ref.9, s32[8,2]{1,0:T(8,128)} %copy.10.flags_ref, f32[64,2,2,128]{3,2,1,0:T(2,128)} %copy-done.4, s32[1,128]{1,0:T(1,128)} %bitcast.5, bf16[4,32,32,256]{3,2,1,0:T(8,128)(2,1)} %get-tuple-element.46.refs_1_, bf16[4,4,32,256]{3,2,1,0:T(8,128)(2,1)} %copy-done.6, ...), custom_call_target="tpu_custom_call" | custom-call | flops 4831838208 | bytes 5242880 | tf_op jit(solution)/shard_map/conv4_0/pallas_call | solution.py:378
  133.6 0.0 collective-permute-done.10.refs_4_
  133.6 0.0 collective-permute-done.11.refs_5_
  133.6 0.7 copy-done.16
  134.3 11.3 %conv4_4.1 = bf16[8,32,32,256]{3,2,1,0:T(8,128)(2,1)} custom-call(s32[128]{0:T(128)} %points_ref.9, s32[8,2]{1,0:T(8,128)} %copy.10.flags_ref, f32[64,2,2,128]{3,2,1,0:T(2,128)} %copy-done.4, s32[1,128]{1,0:T(1,128)} %bitcast.6, bf16[4,32,32,256]{3,2,1,0:T(8,128)(2,1)} %get-tuple-element.41.refs_1_, ...), custom_call_target="tpu_custom_call", output_to_operand_aliasing={{}: (10, {})} | custom-call | flops 4831838208 | bytes 5242880 | tf_op jit(solution)/shard_map/conv4_4/pallas_call | solution.py:378
  (41 shorter events, 0.5 us)
Async XLA Ops:
  0.0 42.9 %copy-start.13 = (s32[8,2]{0,1:T(2,128)S(1)}, s32[8,2]{0,1:T(2,128)}, u32[]{:S(2)}) copy-start(s32[8,2]{0,1:T(2,128)} %param.7) | copy-start | bytes 196
  6.9 8.9 %collective-permute-start = (f32[3,2,128]{2,1,0:T(2,128)}, f32[3,2,128]{2,1,0:T(2,128)S(1)}, u32[]{:S(2)}, u32[]{:S(2)}) collective-permute-start(f32[3,2,128]{2,1,0:T(2,128)} %get-tuple-element.28), channel_id=1, source_target_pairs={{0,32},{32,0},{1,33},{33,1},{2,34},{34,2},{3,35},{35,3},{4,36},{36... | collective-permute-start | bytes 9224 | tf_op jit(solution)/shard_map/ppermute | solution.py:430
  8.4 9.1 %collective-permute-start.1 = (bf16[8,2,32,256]{3,2,1,0:T(8,128)(2,1)}, bf16[8,2,32,256]{3,2,1,0:T(8,128)(2,1)S(1)}, u32[]{:S(2)}, u32[]{:S(2)}) collective-permute-start(bf16[8,2,32,256]{3,2,1,0:T(8,128)(2,1)} %get-tuple-element.29), channel_id=1, source_target_pairs={{0,32},{32,64},{64,96},{1,33},{33,65},{65,97},{2,34},{34,66},{66,9... | collective-permute-start | bytes 786440 | tf_op jit(solution)/shard_map/ppermute | solution.py:410
  13.9 9.4 %collective-permute-start.2 = (bf16[8,2,32,256]{3,2,1,0:T(8,128)(2,1)}, bf16[8,2,32,256]{3,2,1,0:T(8,128)(2,1)S(1)}, u32[]{:S(2)}, u32[]{:S(2)}) collective-permute-start(bf16[8,2,32,256]{3,2,1,0:T(8,128)(2,1)} %get-tuple-element.30), channel_id=1, source_target_pairs={{32,0},{64,32},{96,64},{33,1},{65,33},{97,65},{34,2},{66,34},{98,6... | collective-permute-start | bytes 786440 | tf_op jit(solution)/shard_map/ppermute | solution.py:411
  17.5 34.3 %copy-start.10 = (bf16[8,2,32,256]{3,2,1,0:T(8,128)(2,1)}, bf16[8,2,32,256]{3,2,1,0:T(8,128)(2,1)S(1)}, u32[]{:S(2)}) copy-start(bf16[8,2,32,256]{3,2,1,0:T(8,128)(2,1)S(1)} %collective-permute-done.1.refs_2_) | copy-start | bytes 786436
  23.3 28.5 %copy-start.11 = (bf16[8,2,32,256]{3,2,1,0:T(8,128)(2,1)}, bf16[8,2,32,256]{3,2,1,0:T(8,128)(2,1)S(1)}, u32[]{:S(2)}) copy-start(bf16[8,2,32,256]{3,2,1,0:T(8,128)(2,1)S(1)} %collective-permute-done.2.refs_3_) | copy-start | bytes 786436
  25.2 26.5 %collective-permute-start.4 = (bf16[8,72,256]{2,1,0:T(8,128)(2,1)S(1)}, bf16[8,72,256]{2,1,0:T(8,128)(2,1)S(1)}, u32[]{:S(2)}, u32[]{:S(2)}) collective-permute-start(bf16[8,72,256]{2,1,0:T(8,128)(2,1)S(1)} %pad_maximum_fusion.5), channel_id=1, source_target_pairs={{1,0},{2,1},{3,2},{4,3},{5,4},{6,5},{7,6},{8,7},{9,8},{10,9},{11,1... | collective-permute-start | bytes 884744 | tf_op jit(solution)/shard_map/ppermute | solution.py:425
  34.9 16.9 %collective-permute-start.3 = (bf16[8,72,256]{2,1,0:T(8,128)(2,1)S(1)}, bf16[8,72,256]{2,1,0:T(8,128)(2,1)S(1)}, u32[]{:S(2)}, u32[]{:S(2)}) collective-permute-start(bf16[8,72,256]{2,1,0:T(8,128)(2,1)S(1)} %pad_maximum_fusion.4), channel_id=1, source_target_pairs={{0,1},{1,2},{2,3},{3,4},{4,5},{5,6},{6,7},{7,8},{8,9},{9,10},{10,1... | collective-permute-start | bytes 884744 | tf_op jit(solution)/shard_map/ppermute | solution.py:424
  35.0 16.8 %all-to-all-start = ((f32[64,2,2,128]{3,2,1,0:T(2,128)}), f32[64,2,2,128]{3,2,1,0:T(2,128)S(1)}, u32[]{:S(2)}, u32[]{:S(2)}) async-start(f32[64,2,2,128]{3,2,1,0:T(2,128)} %broadcast_in_dim.6), calls=%async_computation | async-start | bytes 262144 | tf_op jit(solution)/shard_map/all_to_all | solution.py:449
  51.7 0.6 copy-start.5
  51.7 0.8 copy-start.17
  51.7 0.8 copy-start.18
  65.9 27.2 %collective-permute-start.5 = (bf16[4,4,32,256]{3,2,1,0:T(8,128)(2,1)}, bf16[4,4,32,256]{3,2,1,0:T(8,128)(2,1)S(1)}, u32[]{:S(2)}, u32[]{:S(2)}) collective-permute-start(bf16[4,4,32,256]{3,2,1,0:T(8,128)(2,1)} %get-tuple-element.38), channel_id=1, source_target_pairs={{0,32},{32,64},{64,96},{1,33},{33,65},{65,97},{2,34},{34,66},{66,9... | collective-permute-start | bytes 786440 | tf_op jit(solution)/shard_map/ppermute | solution.py:410
  70.2 22.9 %collective-permute-start.6 = (bf16[4,4,32,256]{3,2,1,0:T(8,128)(2,1)}, bf16[4,4,32,256]{3,2,1,0:T(8,128)(2,1)S(1)}, u32[]{:S(2)}, u32[]{:S(2)}) collective-permute-start(bf16[4,4,32,256]{3,2,1,0:T(8,128)(2,1)} %get-tuple-element.39), channel_id=1, source_target_pairs={{32,0},{64,32},{96,64},{33,1},{65,33},{97,65},{34,2},{66,34},{98,6... | collective-permute-start | bytes 786440 | tf_op jit(solution)/shard_map/ppermute | solution.py:411
  72.3 28.3 %copy-start.3 = (bf16[4,128,256]{2,1,0:T(8,128)(2,1)S(1)}, bf16[4,128,256]{2,1,0:T(8,128)(2,1)}, u32[]{:S(2)}) copy-start(bf16[4,128,256]{2,1,0:T(8,128)(2,1)} %get-tuple-element.49) | copy-start | bytes 786436
  72.3 28.7 %copy-start.2 = (bf16[4,128,256]{2,1,0:T(8,128)(2,1)S(1)}, bf16[4,128,256]{2,1,0:T(8,128)(2,1)}, u32[]{:S(2)}) copy-start(bf16[4,128,256]{2,1,0:T(8,128)(2,1)} %get-tuple-element.50) | copy-start | bytes 786436
  85.9 20.7 %copy-start.12 = (f32[3,2,128]{2,1,0:T(2,128)S(1)}, f32[3,2,128]{2,1,0:T(2,128)}, u32[]{:S(2)}) copy-start(f32[3,2,128]{2,1,0:T(2,128)} %get-tuple-element.40) | copy-start | bytes 9220
  85.9 26.0 %copy-start.1 = (bf16[4,128,256]{2,1,0:T(8,128)(2,1)S(1)}, bf16[4,128,256]{2,1,0:T(8,128)(2,1)}, u32[]{:S(2)}) copy-start(bf16[4,128,256]{2,1,0:T(8,128)(2,1)} %get-tuple-element.44) | copy-start | bytes 786436
  85.9 27.1 %copy-start = (bf16[4,128,256]{2,1,0:T(8,128)(2,1)S(1)}, bf16[4,128,256]{2,1,0:T(8,128)(2,1)}, u32[]{:S(2)}) copy-start(bf16[4,128,256]{2,1,0:T(8,128)(2,1)} %get-tuple-element.45) | copy-start | bytes 786436
  85.9 8.9 %collective-permute-start.8 = (bf16[4,4,32,256]{3,2,1,0:T(8,128)(2,1)}, bf16[4,4,32,256]{3,2,1,0:T(8,128)(2,1)S(1)}, u32[]{:S(2)}, u32[]{:S(2)}) collective-permute-start(bf16[4,4,32,256]{3,2,1,0:T(8,128)(2,1)} %get-tuple-element.42), channel_id=1, source_target_pairs={{0,32},{32,64},{64,96},{1,33},{33,65},{65,97},{2,34},{34,66},{66,9... | collective-permute-start | bytes 786440 | tf_op jit(solution)/shard_map/ppermute | solution.py:410
  91.2 9.4 %collective-permute-start.9 = (bf16[4,4,32,256]{3,2,1,0:T(8,128)(2,1)}, bf16[4,4,32,256]{3,2,1,0:T(8,128)(2,1)S(1)}, u32[]{:S(2)}, u32[]{:S(2)}) collective-permute-start(bf16[4,4,32,256]{3,2,1,0:T(8,128)(2,1)} %get-tuple-element.43), channel_id=1, source_target_pairs={{32,0},{64,32},{96,64},{33,1},{65,33},{97,65},{34,2},{66,34},{98,6... | collective-permute-start | bytes 786440 | tf_op jit(solution)/shard_map/ppermute | solution.py:411
  93.1 28.3 %copy-start.6 = (bf16[4,4,32,256]{3,2,1,0:T(8,128)(2,1)}, bf16[4,4,32,256]{3,2,1,0:T(8,128)(2,1)S(1)}, u32[]{:S(2)}) copy-start(bf16[4,4,32,256]{3,2,1,0:T(8,128)(2,1)S(1)} %collective-permute-done.5.refs_2_) | copy-start | bytes 786436
  93.1 28.3 %copy-start.7 = (bf16[4,4,32,256]{3,2,1,0:T(8,128)(2,1)}, bf16[4,4,32,256]{3,2,1,0:T(8,128)(2,1)S(1)}, u32[]{:S(2)}) copy-start(bf16[4,4,32,256]{3,2,1,0:T(8,128)(2,1)S(1)} %collective-permute-done.6.refs_3_) | copy-start | bytes 786436
  93.1 13.4 %collective-permute-start.7 = (f32[3,2,128]{2,1,0:T(2,128)}, f32[3,2,128]{2,1,0:T(2,128)S(1)}, u32[]{:S(2)}, u32[]{:S(2)}) collective-permute-start(f32[3,2,128]{2,1,0:T(2,128)} %get-tuple-element.40), channel_id=1, source_target_pairs={{0,32},{32,0},{1,33},{33,1},{2,34},{34,2},{3,35},{35,3},{4,36},{36... | collective-permute-start | bytes 9224 | tf_op jit(solution)/shard_map/ppermute | solution.py:430
  94.8 38.8 %copy-start.8 = (bf16[4,4,32,256]{3,2,1,0:T(8,128)(2,1)}, bf16[4,4,32,256]{3,2,1,0:T(8,128)(2,1)S(1)}, u32[]{:S(2)}) copy-start(bf16[4,4,32,256]{3,2,1,0:T(8,128)(2,1)S(1)} %collective-permute-done.8.refs_2_) | copy-start | bytes 786436
  100.6 33.0 %copy-start.9 = (bf16[4,4,32,256]{3,2,1,0:T(8,128)(2,1)}, bf16[4,4,32,256]{3,2,1,0:T(8,128)(2,1)S(1)}, u32[]{:S(2)}) copy-start(bf16[4,4,32,256]{3,2,1,0:T(8,128)(2,1)S(1)} %collective-permute-done.9.refs_3_) | copy-start | bytes 786436
  100.7 20.7 %collective-permute-start.12 = (bf16[4,160,256]{2,1,0:T(8,128)(2,1)S(1)}, bf16[4,160,256]{2,1,0:T(8,128)(2,1)S(1)}, u32[]{:S(2)}, u32[]{:S(2)}) collective-permute-start(bf16[4,160,256]{2,1,0:T(8,128)(2,1)S(1)} %pad_maximum_fusion.2), channel_id=1, source_target_pairs={{0,1},{1,2},{2,3},{3,4},{4,5},{5,6},{6,7},{7,8},{8,9},{9,10},{10,1... | collective-permute-start | bytes 983048 | tf_op jit(solution)/shard_map/ppermute | solution.py:424
  101.0 20.3 %collective-permute-start.13 = (bf16[4,160,256]{2,1,0:T(8,128)(2,1)S(1)}, bf16[4,160,256]{2,1,0:T(8,128)(2,1)S(1)}, u32[]{:S(2)}, u32[]{:S(2)}) collective-permute-start(bf16[4,160,256]{2,1,0:T(8,128)(2,1)S(1)} %pad_maximum_fusion.3), channel_id=1, source_target_pairs={{1,0},{2,1},{3,2},{4,3},{5,4},{6,5},{7,6},{8,7},{9,8},{10,9},{11,1... | collective-permute-start | bytes 983048 | tf_op jit(solution)/shard_map/ppermute | solution.py:425
  107.2 14.1 %all-to-all-start.1 = ((f32[64,2,2,128]{3,2,1,0:T(2,128)}), f32[64,2,2,128]{3,2,1,0:T(2,128)S(1)}, u32[]{:S(2)}, u32[]{:S(2)}) async-start(f32[64,2,2,128]{3,2,1,0:T(2,128)} %broadcast_in_dim.8), calls=%async_computation.1 | async-start | bytes 262144 | tf_op jit(solution)/shard_map/all_to_all | solution.py:469
  112.0 21.6 %collective-permute-start.10 = (bf16[4,160,256]{2,1,0:T(8,128)(2,1)S(1)}, bf16[4,160,256]{2,1,0:T(8,128)(2,1)}, u32[]{:S(2)}, u32[]{:S(2)}) collective-permute-start(bf16[4,160,256]{2,1,0:T(8,128)(2,1)S(1)} %pad_maximum_fusion), channel_id=1, source_target_pairs={{0,1},{1,2},{2,3},{3,4},{4,5},{5,6},{6,7},{7,8},{8,9},{9,10},{10,1... | collective-permute-start | bytes 983048 | tf_op jit(solution)/shard_map/ppermute | solution.py:424
  113.0 20.6 %collective-permute-start.11 = (bf16[4,160,256]{2,1,0:T(8,128)(2,1)S(1)}, bf16[4,160,256]{2,1,0:T(8,128)(2,1)S(1)}, u32[]{:S(2)}, u32[]{:S(2)}) collective-permute-start(bf16[4,160,256]{2,1,0:T(8,128)(2,1)S(1)} %pad_maximum_fusion.1), channel_id=1, source_target_pairs={{1,0},{2,1},{3,2},{4,3},{5,4},{6,5},{7,6},{8,7},{9,8},{10,9},{11,1... | collective-permute-start | bytes 983048 | tf_op jit(solution)/shard_map/ppermute | solution.py:425
  121.4 0.7 copy-start.4
  121.4 0.8 copy-start.14
  121.4 0.9 copy-start.15
  133.6 0.7 copy-start.16

commit v4 on v2

--- a/solution.py
+++ b/solution.py
@@ -64,6 +64,7 @@
     group_squares = exact_dot(squares_ref[...] + count * offset * offset, fold)
     out_ref[0] = packed(group_sum)
     out_ref[1] = packed(group_squares)
+    out_ref[2] = jnp.full(out_ref.shape[1:], count * size, jnp.float32)
 
 
 def row_statistics(rows, limits, count, sums_ref, squares_ref, b):
@@ -119,7 +120,31 @@
     return pltpu.make_async_copy(x_hbm_ref.at[b], x_ref.at[b], sems.at[b])
 
 
-def stats_kernel(points_ref, x_hbm_ref, out_ref, x_ref, sems, sums_ref, squares_ref):
+def pack_edges(x_ref, b, d, edges, k):
+    _, rows, cols, _ = x_ref.shape
+    first_row_ref, last_row_ref, first_col_ref, last_col_ref = edges
+    first_row_ref[k] = x_ref[b, :d]
+    last_row_ref[k] = x_ref[b, rows - d :]
+    for h in range(rows):
+        first_col_ref[k, h * d : (h + 1) * d] = x_ref[b, h, :d]
+        last_col_ref[k, h * d : (h + 1) * d] = x_ref[b, h, cols - d :]
+
+
+def edge_shapes(x, d):
+    samples, rows, width, channels = x.shape
+    shapes = [(samples, d, width, channels)] * 2 + [(samples, rows * d, channels)] * 2
+    return [jax.ShapeDtypeStruct(shape, x.dtype) for shape in shapes]
+
+
+def edge_specs(x, d, block):
+    return [
+        pl.BlockSpec((block, *e.shape[1:]), lambda g, *_, n=len(e.shape): (g,) + (0,) * (n - 1))
+        for e in edge_shapes(x, d)
+    ]
+
+
+def stats_kernel(points_ref, x_hbm_ref, out_ref, *refs):
+    *edges, x_ref, sems, sums_ref, squares_ref = refs
     g = pl.program_id(0)
 
     @pl.when(g == 0)
@@ -134,6 +159,7 @@
     row_statistics(
         lambda h, n: x_ref[g, h, :n].astype(jnp.float32), limits, count, sums_ref, squares_ref, g
     )
+    pack_edges(x_ref, g, FIRST_DILATION, edges, 0)
 
     @pl.when(g == pl.num_programs(0) - 1)
     def _():
@@ -142,15 +168,18 @@
 
 def local_statistics(x, points):
     samples, rows, width, channels = x.shape
-    shape = (2, samples * GROUPS // LANES, LANES)
+    shape = (3, samples * GROUPS // LANES, LANES)
     return pl.pallas_call(
         stats_kernel,
-        out_shape=jax.ShapeDtypeStruct(shape, jnp.float32),
+        out_shape=[jax.ShapeDtypeStruct(shape, jnp.float32), *edge_shapes(x, FIRST_DILATION)],
         grid_spec=pltpu.PrefetchScalarGridSpec(
             num_scalar_prefetch=1,
             grid=(samples,),
             in_specs=[pl.BlockSpec(memory_space=pltpu.HBM)],
-            out_specs=pl.BlockSpec(shape, lambda g, *_: (0, 0, 0)),
+            out_specs=[
+                pl.BlockSpec(shape, lambda g, *_: (0, 0, 0)),
+                *edge_specs(x, FIRST_DILATION, 1),
+            ],
             scratch_shapes=[
                 pltpu.VMEM(x.shape, x.dtype),
                 pltpu.SemaphoreType.DMA((samples,)),
@@ -206,7 +235,8 @@
     d = dilation
     x_hbm_ref, top_ref, bottom_ref, left_ref, right_ref, left_end_ref, right_end_ref, w_ref, out_hbm_ref, *rest = refs
     if with_stats:
-        stats_ref, x_ref, sems, out_ref, out_sems, norm_ref, even_ref, odd_ref, sums_ref, squares_ref, kept_ref = rest
+        stats_ref, *edges = rest[:5]
+        x_ref, sems, out_ref, out_sems, norm_ref, even_ref, odd_ref, sums_ref, squares_ref, kept_ref = rest[5:]
     else:
         x_ref, sems, out_ref, out_sems, norm_ref, even_ref, odd_ref = rest
     g = pl.program_id(0)
@@ -271,6 +301,8 @@
             activate_rows(follow, next_ref, step * each, last)
             convolve_rows(k, scale, act_ref, step * chunk)
         store(2 * g + k).start()
+        if with_stats:
+            pack_edges(out_ref, 2 * g + k, SECOND_DILATION, edges, k)
 
     def store(b):
         return pltpu.make_async_copy(out_ref.at[b], out_hbm_ref.at[b], out_sems.at[b])
@@ -327,9 +359,9 @@
     scratch = [pltpu.VMEM(x.shape, x.dtype), pltpu.SemaphoreType.DMA((samples,))] * 2
     scratch += [pltpu.VMEM((2, samples, channels), jnp.float32), act, act]
     if with_stats:
-        shape = (2, samples * GROUPS // LANES, LANES)
-        out_shape.append(jax.ShapeDtypeStruct(shape, jnp.float32))
-        out_specs.append(whole(shape))
+        shape = (3, samples * GROUPS // LANES, LANES)
+        out_shape += [jax.ShapeDtypeStruct(shape, jnp.float32), *edge_shapes(x, SECOND_DILATION)]
+        out_specs += [whole(shape), *edge_specs(x, SECOND_DILATION, 2)]
         scratch += [pltpu.VMEM((samples, channels), jnp.float32)] * 2
         scratch += [pltpu.VMEM((rows, width, channels), jnp.bfloat16)]
     return pl.pallas_call(
@@ -358,17 +390,17 @@
     )(points, flags, parts, points[None], x, *halos, weight)
 
 
-def exchange_sides(x, d):
-    samples, rows, width, channels = x.shape
+def exchange_sides(edges):
+    first_row, last_row, first_col, last_col = edges
     lat, lon = lax.axis_size(LAT), lax.axis_size(LON)
     up = [(i, i + 1) for i in range(lat - 1)]
     down = [(i + 1, i) for i in range(lat - 1)]
-    top = lax.ppermute(x[:, rows - d :], LAT, up)
-    bottom = lax.ppermute(x[:, :d], LAT, down)
     east = [(i, (i + 1) % lon) for i in range(lon)]
     west = [((i + 1) % lon, i) for i in range(lon)]
-    left = lax.ppermute(x[:, :, width - d :].reshape(samples, rows * d, channels), LON, east)
-    right = lax.ppermute(x[:, :, :d].reshape(samples, rows * d, channels), LON, west)
+    top = lax.ppermute(last_row, LAT, up)
+    bottom = lax.ppermute(first_row, LAT, down)
+    left = lax.ppermute(last_col, LON, east)
+    right = lax.ppermute(first_col, LON, west)
     return top, bottom, left, right
 
 
@@ -387,46 +419,33 @@
     return left, right
 
 
-def share_statistics(local, own_count, other_count, core_axis="core"):
-    other = lax.ppermute(local, core_axis, [(0, 1), (1, 0)])
-    both = own_count + other_count
+def merge_cores(local):
+    other = lax.ppermute(local, "core", [(0, 1), (1, 0)])
+    own_count, other_count = local[2], other[2]
+    both = jnp.maximum(own_count + other_count, 1.0)
     gap = local[0] / jnp.maximum(own_count, 1.0) - other[0] / jnp.maximum(other_count, 1.0)
-    squares = local[1] + other[1] + gap * gap * (own_count * other_count / jnp.maximum(both, 1.0))
+    squares = local[1] + other[1] + gap * gap * (own_count * other_count / both)
     merged = jnp.stack([local[0] + other[0], squares])
-    chips = lax.axis_size(CHIPS)
-    return lax.all_to_all(jnp.broadcast_to(merged[None], (chips, *merged.shape)), CHIPS, 0, 0)
-
-
-def tile_count(band_points, rows, width, size, core):
-    _, lon = tile_position()
-    lat = lax.axis_index("zh") * lax.axis_size("core") + core
-    row = jnp.arange(band_points.shape[0], dtype=jnp.int32)
-    live = jnp.clip(band_points - lon * width, 0, width)
-    return jnp.where(row // rows == lat, live, 0).sum().astype(jnp.float32) * size
+    return jnp.broadcast_to(merged[None], (lax.axis_size(CHIPS), *merged.shape))
+
+
+def exchange(local, edges):
+    top, bottom, left, right = exchange_sides(edges)
+    parts = lax.all_to_all(merge_cores(local), CHIPS, 0, 0)
+    parts, top, bottom = lax.optimization_barrier((parts, top, bottom))
+    return parts, (top, bottom, left, right, *exchange_corners(top, bottom))
 
 
 def per_device(features, band_points, survival_flags, first_kernel_weight, second_kernel_weight):
-    _, rows, width, channels = features.shape
-    core = lax.axis_index("core")
-    size = channels // GROUPS
-    own_count = tile_count(band_points, rows, width, size, core)
-    other_count = tile_count(band_points, rows, width, size, 1 - core)
+    channels = features.shape[3]
     first_weight = first_kernel_weight.reshape(3, 3 * channels, channels)
     second_weight = second_kernel_weight.reshape(3, 3 * channels, channels)
-
-    top, bottom, left, right = exchange_sides(features, FIRST_DILATION)
-    local = local_statistics(features, band_points)
-    local, top, bottom = lax.optimization_barrier((local, top, bottom))
-    ends = exchange_corners(top, bottom)
-    parts = share_statistics(local, own_count, other_count)
-    halos = (top, bottom, left, right, *ends)
-    first, local = convolve(
+    local, *edges = local_statistics(features, band_points)
+    parts, halos = exchange(local, edges)
+    first, local, *edges = convolve(
         features, halos, first_weight, parts, band_points, survival_flags, FIRST_DILATION, 0, True
     )
-    top, bottom, left, right = exchange_sides(first, SECOND_DILATION)
-    parts = share_statistics(local, own_count, other_count)
-    ends = exchange_corners(top, bottom)
-    halos = (top, bottom, left, right, *ends)
+    parts, halos = exchange(local, edges)
     (section,) = convolve(
         first, halos, second_weight, parts, band_points, survival_flags, SECOND_DILATION, 1, False
     )

time: 135 us -> 128 us (0.948)
  the two profiles are of different devices: /device:TPU:0 before, /device:TPU:1 now
where the time goes in v4:
time: 128 us; the launch traced here: 127 us
  starting transfers between devices  60.5 us (47%)
  Pallas kernels  45.9 us (36%)
  waiting for transfers between devices  15.1 us (12%)
  local copies, waits for them, and re-layouts  3.6 us (3%)
  other arithmetic  1.68 us (1%)
    pallas_call x2, Pallas kernels, convolve(): pl.pallas_call(functools.partial(conv_kernel, d, CHUNK, which, with_stats...  39.1 us
    all_to_all x2, starting transfers between devices, exchange(): parts = lax.all_to_all(merge_cores(local), CHIPS, 0, 0)  17.9 us
    ppermute x2, starting transfers between devices, exchange_sides(): top = lax.ppermute(last_row, LAT, up)  13.9 us
    ppermute x2, starting transfers between devices, exchange_corners(): right = lax.ppermute(packed(0, d), LON, west)  11.2 us
    ppermute x2, starting transfers between devices, exchange_sides(): right = lax.ppermute(first_col, LON, west)  9.35 us
    pallas_call x1, Pallas kernels, local_statistics(): pl.pallas_call(stats_kernel, out_shape=[jax.ShapeDtypeStruct(shape, jnp.f...  6.85 us
    all_to_all x2, waiting for transfers between devices, exchange(): parts = lax.all_to_all(merge_cores(local), CHIPS, 0, 0)  6.71 us
    ppermute x2, starting transfers between devices, exchange_sides(): bottom = lax.ppermute(first_row, LAT, down)  3.84 us
  transfers between devices with their start and end apart: 16, of which 6 were waited for; matrix products, arithmetic and copies ran while one was open for 3% of the time, Pallas kernels for 0%

profile of v4, /device:TPU:1, one launch (start us, length us, event | category | flops | bytes accessed | tf_op | source)
XLA Modules:
  0.0 127.2 jit_solution(3687458124262753929)
XLA Ops:
  0.0 0.0 copy-start.6
  0.0 6.9 %stats.1 = (f32[3,2,128]{2,1,0:T(2,128)}, bf16[8,2,32,256]{3,2,1,0:T(8,128)(2,1)}, bf16[8,2,32,256]{3,2,1,0:T(8,128)(2,1)}, bf16[8,64,256]{2,1,0:T(8,128)(2,1)}, bf16[8,64,256]{2,1,0:T(8,128)(2,1)}) custom-call(s32[128]{0:T(128)} %points_ref.5, bf16[8,32,32,256]{3,2,1,0:T(8,128)(2,1)} %refs_0_.1), custom_call_target="tpu_custom_call" | custom-call | flops 16777216 | bytes 4194304 | tf_op jit(solution)/shard_map/stats/pallas_call | solution.py:172
  6.9 1.5 %collective-permute-start = (f32[3,2,128]{2,1,0:T(2,128)}, f32[3,2,128]{2,1,0:T(2,128)S(1)}, u32[]{:S(2)}, u32[]{:S(2)}) collective-permute-start(f32[3,2,128]{2,1,0:T(2,128)} %get-tuple-element.22), channel_id=1, source_target_pairs={{0,32},{32,0},{1,33},{33,1},{2,34},{34,2},{3,35},{35,3},{4,36},{36... | collective-permute-start | bytes 9224 | tf_op jit(solution)/shard_map/ppermute | solution.py:423
  8.4 5.5 %collective-permute-start.1 = (bf16[8,2,32,256]{3,2,1,0:T(8,128)(2,1)}, bf16[8,2,32,256]{3,2,1,0:T(8,128)(2,1)S(1)}, u32[]{:S(2)}, u32[]{:S(2)}) collective-permute-start(bf16[8,2,32,256]{3,2,1,0:T(8,128)(2,1)} %get-tuple-element.23), channel_id=1, source_target_pairs={{0,32},{32,64},{64,96},{1,33},{33,65},{65,97},{2,34},{34,66},{66,9... | collective-permute-start | bytes 786440 | tf_op jit(solution)/shard_map/ppermute | solution.py:400
  13.9 1.9 %collective-permute-start.2 = (bf16[8,2,32,256]{3,2,1,0:T(8,128)(2,1)}, bf16[8,2,32,256]{3,2,1,0:T(8,128)(2,1)S(1)}, u32[]{:S(2)}, u32[]{:S(2)}) collective-permute-start(bf16[8,2,32,256]{3,2,1,0:T(8,128)(2,1)} %get-tuple-element.24), channel_id=1, source_target_pairs={{32,0},{64,32},{96,64},{33,1},{65,33},{97,65},{34,2},{66,34},{98,6... | collective-permute-start | bytes 786440 | tf_op jit(solution)/shard_map/ppermute | solution.py:401
  15.8 0.0 collective-permute-done
  15.8 0.7 slice_add_fusion.3
  16.5 0.7 broadcast_in_dim.6
  17.2 8.1 %all-to-all-start = ((f32[64,2,2,128]{3,2,1,0:T(2,128)}), f32[64,2,2,128]{3,2,1,0:T(2,128)S(1)}, u32[]{:S(2)}, u32[]{:S(2)}) async-start(f32[64,2,2,128]{3,2,1,0:T(2,128)} %broadcast_in_dim.6), calls=%async_computation | async-start | bytes 262144 | tf_op jit(solution)/shard_map/all_to_all | solution.py:434
  25.3 1.1 collective-permute-start.3
  26.4 4.7 %collective-permute-start.4 = (bf16[8,64,256]{2,1,0:T(8,128)(2,1)}, bf16[8,64,256]{2,1,0:T(8,128)(2,1)S(1)}, u32[]{:S(2)}, u32[]{:S(2)}) collective-permute-start(bf16[8,64,256]{2,1,0:T(8,128)(2,1)} %get-tuple-element.29), channel_id=1, source_target_pairs={{1,0},{2,1},{3,2},{4,3},{5,4},{6,5},{7,6},{8,7},{9,8},{10,9},{11,1... | collective-permute-start | bytes 786440 | tf_op jit(solution)/shard_map/ppermute | solution.py:403
  31.1 3.4 %all-to-all-done.parts_ref = f32[64,2,2,128]{3,2,1,0:T(2,128)S(1)} async-done(((f32[64,2,2,128]{3,2,1,0:T(2,128)}), f32[64,2,2,128]{3,2,1,0:T(2,128)S(1)}, u32[]{:S(2)}, u32[]{:S(2)}) %all-to-all-start) | async-done | bytes 131104 | tf_op jit(solution)/shard_map/all_to_all | solution.py:434
  34.5 0.0 collective-permute-done.1.refs_1_
  34.5 0.0 collective-permute-done.2.refs_2_
  34.5 0.0 copy-start.5
  34.5 0.1 fusion.4
  34.7 0.1 collective-permute-start.5
  34.8 5.7 %collective-permute-start.6 = (bf16[8,8,256]{2,1,0:T(8,128)(2,1)S(1)}, bf16[8,8,256]{2,1,0:T(8,128)(2,1)S(1)}, u32[]{:S(2)}, u32[]{:S(2)}) collective-permute-start(bf16[8,8,256]{2,1,0:T(8,128)(2,1)S(1)} %reshape.21), channel_id=1, source_target_pairs={{1,0},{2,1},{3,2},{4,3},{5,4},{6,5},{7,6},{8,7},{9,8},{10,9},{11,1... | collective-permute-start | bytes 98312 | tf_op jit(solution)/shard_map/ppermute | solution.py:418
  40.5 0.0 copy-done.6
  40.5 0.7 copy.7.flags_ref
  41.1 0.0 collective-permute-done.3.refs_3_
  41.2 0.0 collective-permute-done.4.refs_4_
  41.2 0.0 copy-start.10
  41.2 0.6 collective-permute-done.5.refs_5_
  41.8 0.0 collective-permute-done.6.refs_6_
  41.8 0.0 copy-done
  41.8 0.0 copy-done.4
  41.8 0.0 copy-done.5
  41.8 0.0 copy-done.9
  41.9 0.1 copy-done.10
  41.9 0.4 copy-done.13
  42.4 0.0 copy-done.14
  42.4 20.9 %conv2.1 = (bf16[8,32,32,256]{3,2,1,0:T(8,128)(2,1)}, f32[3,2,128]{2,1,0:T(2,128)}, bf16[8,4,32,256]{3,2,1,0:T(8,128)(2,1)}, bf16[8,4,32,256]{3,2,1,0:T(8,128)(2...) custom-call(s32[128]{0:T(128)} %points_ref.5, s32[8,2]{1,0:T(8,128)} %copy.7.flags_ref, ...), custom_call_target="tpu_custom_call" | custom-call | flops 9663676416 | bytes 10485760 | tf_op jit(solution)/shard_map/conv2/pallas_call | solution.py:367
  63.3 8.5 %collective-permute-start.8 = (bf16[8,4,32,256]{3,2,1,0:T(8,128)(2,1)}, bf16[8,4,32,256]{3,2,1,0:T(8,128)(2,1)S(1)}, u32[]{:S(2)}, u32[]{:S(2)}) collective-permute-start(bf16[8,4,32,256]{3,2,1,0:T(8,128)(2,1)} %get-tuple-element.31), channel_id=1, source_target_pairs={{0,32},{32,64},{64,96},{1,33},{33,65},{65,97},{2,34},{34,66},{66,9... | collective-permute-start | bytes 1572872 | tf_op jit(solution)/shard_map/ppermute | solution.py:400
  71.8 1.9 %collective-permute-start.9 = (bf16[8,4,32,256]{3,2,1,0:T(8,128)(2,1)}, bf16[8,4,32,256]{3,2,1,0:T(8,128)(2,1)S(1)}, u32[]{:S(2)}, u32[]{:S(2)}) collective-permute-start(bf16[8,4,32,256]{3,2,1,0:T(8,128)(2,1)} %get-tuple-element.32), channel_id=1, source_target_pairs={{32,0},{64,32},{96,64},{33,1},{65,33},{97,65},{34,2},{66,34},{98,6... | collective-permute-start | bytes 1572872 | tf_op jit(solution)/shard_map/ppermute | solution.py:401
  73.7 0.1 collective-permute-start.7
  73.8 1.6 %collective-permute-done.7 = f32[3,2,128]{2,1,0:T(2,128)S(1)} collective-permute-done((f32[3,2,128]{2,1,0:T(2,128)}, f32[3,2,128]{2,1,0:T(2,128)S(1)}, u32[]{:S(2)}, u32[]{:S(2)}) %collective-permute-start.7) | collective-permute-done | bytes 3104 | tf_op jit(solution)/shard_map/ppermute | solution.py:423
  75.4 0.7 slice_add_fusion.2
  76.1 0.7 broadcast_in_dim.8
  76.8 9.8 %all-to-all-start.1 = ((f32[64,2,2,128]{3,2,1,0:T(2,128)}), f32[64,2,2,128]{3,2,1,0:T(2,128)S(1)}, u32[]{:S(2)}, u32[]{:S(2)}) async-start(f32[64,2,2,128]{3,2,1,0:T(2,128)} %broadcast_in_dim.8), calls=%async_computation.1 | async-start | bytes 262144 | tf_op jit(solution)/shard_map/all_to_all | solution.py:434
  86.6 1.1 collective-permute-start.10
  87.7 4.7 %collective-permute-start.11 = (bf16[8,128,256]{2,1,0:T(8,128)(2,1)}, bf16[8,128,256]{2,1,0:T(8,128)(2,1)S(1)}, u32[]{:S(2)}, u32[]{:S(2)}) collective-permute-start(bf16[8,128,256]{2,1,0:T(8,128)(2,1)} %get-tuple-element.38), channel_id=1, source_target_pairs={{1,0},{2,1},{3,2},{4,3},{5,4},{6,5},{7,6},{8,7},{9,8},{10,9},{11,1... | collective-permute-start | bytes 1572872 | tf_op jit(solution)/shard_map/ppermute | solution.py:403
  92.4 3.3 %all-to-all-done.1.parts_ref = f32[64,2,2,128]{3,2,1,0:T(2,128)S(1)} async-done(((f32[64,2,2,128]{3,2,1,0:T(2,128)}), f32[64,2,2,128]{3,2,1,0:T(2,128)S(1)}, u32[]{:S(2)}, u32[]{:S(2)}) %all-to-all-start.1) | async-done | bytes 131104 | tf_op jit(solution)/shard_map/all_to_all | solution.py:434
  95.7 0.0 collective-permute-done.8.refs_1_
  95.7 0.0 collective-permute-done.9.refs_2_
  95.7 0.0 copy-start.3
  95.7 0.1 fusion.2
  95.8 0.1 fusion.3
  95.8 0.1 pad_maximum_fusion.1
  96.0 0.1 pad_maximum_fusion
  96.1 0.4 collective-permute-start.12
  96.5 5.6 %collective-permute-start.13 = (bf16[8,32,256]{2,1,0:T(8,128)(2,1)S(1)}, bf16[8,32,256]{2,1,0:T(8,128)(2,1)S(1)}, u32[]{:S(2)}, u32[]{:S(2)}) collective-permute-start(bf16[8,32,256]{2,1,0:T(8,128)(2,1)S(1)} %reshape.24), channel_id=1, source_target_pairs={{1,0},{2,1},{3,2},{4,3},{5,4},{6,5},{7,6},{8,7},{9,8},{10,9},{11,1... | collective-permute-start | bytes 393224 | tf_op jit(solution)/shard_map/ppermute | solution.py:418
  102.0 3.3 %collective-permute-done.10.refs_3_ = bf16[8,128,256]{2,1,0:T(8,128)(2,1)S(1)} collective-permute-done((bf16[8,128,256]{2,1,0:T(8,128)(2,1)}, bf16[8,128,256]{2,1,0:T(8,128)(2,1)S(1)}, u32[]{:S(2)}, u32[]{:S(2)}) %collective-permute-start.10) | collective-permute-done | bytes 524320 | tf_op jit(solution)/shard_map/ppermute | solution.py:402
  105.3 0.0 collective-permute-done.11.refs_4_
  105.3 2.8 %collective-permute-done.12.refs_5_ = bf16[8,32,256]{2,1,0:T(8,128)(2,1)S(1)} collective-permute-done((bf16[8,32,256]{2,1,0:T(8,128)(2,1)S(1)}, bf16[8,32,256]{2,1,0:T(8,128)(2,1)S(1)}, u32[]{:S(2)}, u32[]{:S(2)}) %collective-permute-start.12) | collective-permute-done | bytes 131104 | tf_op jit(solution)/shard_map/ppermute | solution.py:417
  108.1 0.0 collective-permute-done.13.refs_6_
  108.2 0.0 copy-done.1
  108.2 0.0 copy-done.2
  108.2 0.0 copy-done.3
  108.2 0.0 copy-done.7
  108.2 0.0 copy-done.8
  108.2 0.6 copy-done.11
  108.8 0.1 copy-done.12
  108.9 18.2 %conv4.1 = bf16[8,32,32,256]{3,2,1,0:T(8,128)(2,1)} custom-call(s32[128]{0:T(128)} %points_ref.5, s32[8,2]{1,0:T(8,128)} %copy.7.flags_ref, f32[64,2,2,128]{3,2,1,0:T(2,128)} %copy-done.1, s32[1,128]{1,0:T(1,128)} %bitcast.4, bf16[8,32,32,256]{3,2,1,0:T(8,128)(2,1)} %get-tuple-element.34.refs_0_, bf16[8,4,32,256]{3,2,1,0:T(8,128)(2,1)} %copy-done.2, ...), custom_call_target="tpu_custom_call" | custom-call | flops 9663676416 | bytes 10485760 | tf_op jit(solution)/shard_map/conv4/pallas_call | solution.py:367
  (19 shorter events, 0.2 us)
Async XLA Ops:
  0.0 40.5 %copy-start.6 = (s32[8,2]{0,1:T(2,128)S(1)}, s32[8,2]{0,1:T(2,128)}, u32[]{:S(2)}) copy-start(s32[8,2]{0,1:T(2,128)} %param.7) | copy-start | bytes 196
  6.9 8.9 %collective-permute-start = (f32[3,2,128]{2,1,0:T(2,128)}, f32[3,2,128]{2,1,0:T(2,128)S(1)}, u32[]{:S(2)}, u32[]{:S(2)}) collective-permute-start(f32[3,2,128]{2,1,0:T(2,128)} %get-tuple-element.22), channel_id=1, source_target_pairs={{0,32},{32,0},{1,33},{33,1},{2,34},{34,2},{3,35},{35,3},{4,36},{36... | collective-permute-start | bytes 9224 | tf_op jit(solution)/shard_map/ppermute | solution.py:423
  8.4 26.1 %collective-permute-start.1 = (bf16[8,2,32,256]{3,2,1,0:T(8,128)(2,1)}, bf16[8,2,32,256]{3,2,1,0:T(8,128)(2,1)S(1)}, u32[]{:S(2)}, u32[]{:S(2)}) collective-permute-start(bf16[8,2,32,256]{3,2,1,0:T(8,128)(2,1)} %get-tuple-element.23), channel_id=1, source_target_pairs={{0,32},{32,64},{64,96},{1,33},{33,65},{65,97},{2,34},{34,66},{66,9... | collective-permute-start | bytes 786440 | tf_op jit(solution)/shard_map/ppermute | solution.py:400
  13.9 20.6 %collective-permute-start.2 = (bf16[8,2,32,256]{3,2,1,0:T(8,128)(2,1)}, bf16[8,2,32,256]{3,2,1,0:T(8,128)(2,1)S(1)}, u32[]{:S(2)}, u32[]{:S(2)}) collective-permute-start(bf16[8,2,32,256]{3,2,1,0:T(8,128)(2,1)} %get-tuple-element.24), channel_id=1, source_target_pairs={{32,0},{64,32},{96,64},{33,1},{65,33},{97,65},{34,2},{66,34},{98,6... | collective-permute-start | bytes 786440 | tf_op jit(solution)/shard_map/ppermute | solution.py:401
  17.2 17.3 %all-to-all-start = ((f32[64,2,2,128]{3,2,1,0:T(2,128)}), f32[64,2,2,128]{3,2,1,0:T(2,128)S(1)}, u32[]{:S(2)}, u32[]{:S(2)}) async-start(f32[64,2,2,128]{3,2,1,0:T(2,128)} %broadcast_in_dim.6), calls=%async_computation | async-start | bytes 262144 | tf_op jit(solution)/shard_map/all_to_all | solution.py:434
  25.3 15.8 %collective-permute-start.3 = (bf16[8,64,256]{2,1,0:T(8,128)(2,1)}, bf16[8,64,256]{2,1,0:T(8,128)(2,1)S(1)}, u32[]{:S(2)}, u32[]{:S(2)}) collective-permute-start(bf16[8,64,256]{2,1,0:T(8,128)(2,1)} %get-tuple-element.28), channel_id=1, source_target_pairs={{0,1},{1,2},{2,3},{3,4},{4,5},{5,6},{6,7},{7,8},{8,9},{9,10},{10,1... | collective-permute-start | bytes 786440 | tf_op jit(solution)/shard_map/ppermute | solution.py:402
  26.4 14.7 %collective-permute-start.4 = (bf16[8,64,256]{2,1,0:T(8,128)(2,1)}, bf16[8,64,256]{2,1,0:T(8,128)(2,1)S(1)}, u32[]{:S(2)}, u32[]{:S(2)}) collective-permute-start(bf16[8,64,256]{2,1,0:T(8,128)(2,1)} %get-tuple-element.29), channel_id=1, source_target_pairs={{1,0},{2,1},{3,2},{4,3},{5,4},{6,5},{7,6},{8,7},{9,8},{10,9},{11,1... | collective-permute-start | bytes 786440 | tf_op jit(solution)/shard_map/ppermute | solution.py:403
  34.5 7.3 %copy-start = (f32[64,2,2,128]{3,2,1,0:T(2,128)}, f32[64,2,2,128]{3,2,1,0:T(2,128)S(1)}, u32[]{:S(2)}) copy-start(f32[64,2,2,128]{3,2,1,0:T(2,128)S(1)} %all-to-all-done.parts_ref) | copy-start | bytes 393220
  34.5 7.3 %copy-start.4 = (bf16[8,2,32,256]{3,2,1,0:T(8,128)(2,1)}, bf16[8,2,32,256]{3,2,1,0:T(8,128)(2,1)S(1)}, u32[]{:S(2)}) copy-start(bf16[8,2,32,256]{3,2,1,0:T(8,128)(2,1)S(1)} %collective-permute-done.1.refs_1_) | copy-start | bytes 786436
  34.5 7.3 %copy-start.5 = (bf16[8,2,32,256]{3,2,1,0:T(8,128)(2,1)}, bf16[8,2,32,256]{3,2,1,0:T(8,128)(2,1)S(1)}, u32[]{:S(2)}) copy-start(bf16[8,2,32,256]{3,2,1,0:T(8,128)(2,1)S(1)} %collective-permute-done.2.refs_2_) | copy-start | bytes 786436
  34.7 7.1 %collective-permute-start.5 = (bf16[8,8,256]{2,1,0:T(8,128)(2,1)S(1)}, bf16[8,8,256]{2,1,0:T(8,128)(2,1)S(1)}, u32[]{:S(2)}, u32[]{:S(2)}) collective-permute-start(bf16[8,8,256]{2,1,0:T(8,128)(2,1)S(1)} %reshape.20), channel_id=1, source_target_pairs={{0,1},{1,2},{2,3},{3,4},{4,5},{5,6},{6,7},{7,8},{8,9},{9,10},{10,1... | collective-permute-start | bytes 98312 | tf_op jit(solution)/shard_map/ppermute | solution.py:417
  34.8 7.0 %collective-permute-start.6 = (bf16[8,8,256]{2,1,0:T(8,128)(2,1)S(1)}, bf16[8,8,256]{2,1,0:T(8,128)(2,1)S(1)}, u32[]{:S(2)}, u32[]{:S(2)}) collective-permute-start(bf16[8,8,256]{2,1,0:T(8,128)(2,1)S(1)} %reshape.21), channel_id=1, source_target_pairs={{1,0},{2,1},{3,2},{4,3},{5,4},{6,5},{7,6},{8,7},{9,8},{10,9},{11,1... | collective-permute-start | bytes 98312 | tf_op jit(solution)/shard_map/ppermute | solution.py:418
  41.1 0.7 copy-start.9
  41.2 0.8 copy-start.10
  41.8 0.6 copy-start.13
  41.8 0.6 copy-start.14
  63.3 32.4 %collective-permute-start.8 = (bf16[8,4,32,256]{3,2,1,0:T(8,128)(2,1)}, bf16[8,4,32,256]{3,2,1,0:T(8,128)(2,1)S(1)}, u32[]{:S(2)}, u32[]{:S(2)}) collective-permute-start(bf16[8,4,32,256]{3,2,1,0:T(8,128)(2,1)} %get-tuple-element.31), channel_id=1, source_target_pairs={{0,32},{32,64},{64,96},{1,33},{33,65},{65,97},{2,34},{34,66},{66,9... | collective-permute-start | bytes 1572872 | tf_op jit(solution)/shard_map/ppermute | solution.py:400
  71.8 23.9 %collective-permute-start.9 = (bf16[8,4,32,256]{3,2,1,0:T(8,128)(2,1)}, bf16[8,4,32,256]{3,2,1,0:T(8,128)(2,1)S(1)}, u32[]{:S(2)}, u32[]{:S(2)}) collective-permute-start(bf16[8,4,32,256]{3,2,1,0:T(8,128)(2,1)} %get-tuple-element.32), channel_id=1, source_target_pairs={{32,0},{64,32},{96,64},{33,1},{65,33},{97,65},{34,2},{66,34},{98,6... | collective-permute-start | bytes 1572872 | tf_op jit(solution)/shard_map/ppermute | solution.py:401
  73.7 1.7 %collective-permute-start.7 = (f32[3,2,128]{2,1,0:T(2,128)}, f32[3,2,128]{2,1,0:T(2,128)S(1)}, u32[]{:S(2)}, u32[]{:S(2)}) collective-permute-start(f32[3,2,128]{2,1,0:T(2,128)} %get-tuple-element.30), channel_id=1, source_target_pairs={{0,32},{32,0},{1,33},{33,1},{2,34},{34,2},{3,35},{35,3},{4,36},{36... | collective-permute-start | bytes 9224 | tf_op jit(solution)/shard_map/ppermute | solution.py:423
  76.8 18.9 %all-to-all-start.1 = ((f32[64,2,2,128]{3,2,1,0:T(2,128)}), f32[64,2,2,128]{3,2,1,0:T(2,128)S(1)}, u32[]{:S(2)}, u32[]{:S(2)}) async-start(f32[64,2,2,128]{3,2,1,0:T(2,128)} %broadcast_in_dim.8), calls=%async_computation.1 | async-start | bytes 262144 | tf_op jit(solution)/shard_map/all_to_all | solution.py:434
  86.6 18.7 %collective-permute-start.10 = (bf16[8,128,256]{2,1,0:T(8,128)(2,1)}, bf16[8,128,256]{2,1,0:T(8,128)(2,1)S(1)}, u32[]{:S(2)}, u32[]{:S(2)}) collective-permute-start(bf16[8,128,256]{2,1,0:T(8,128)(2,1)} %get-tuple-element.37), channel_id=1, source_target_pairs={{0,1},{1,2},{2,3},{3,4},{4,5},{5,6},{6,7},{7,8},{8,9},{9,10},{10,1... | collective-permute-start | bytes 1572872 | tf_op jit(solution)/shard_map/ppermute | solution.py:402
  87.7 17.6 %collective-permute-start.11 = (bf16[8,128,256]{2,1,0:T(8,128)(2,1)}, bf16[8,128,256]{2,1,0:T(8,128)(2,1)S(1)}, u32[]{:S(2)}, u32[]{:S(2)}) collective-permute-start(bf16[8,128,256]{2,1,0:T(8,128)(2,1)} %get-tuple-element.38), channel_id=1, source_target_pairs={{1,0},{2,1},{3,2},{4,3},{5,4},{6,5},{7,6},{8,7},{9,8},{10,9},{11,1... | collective-permute-start | bytes 1572872 | tf_op jit(solution)/shard_map/ppermute | solution.py:403
  95.7 12.5 %copy-start.1 = (f32[64,2,2,128]{3,2,1,0:T(2,128)}, f32[64,2,2,128]{3,2,1,0:T(2,128)S(1)}, u32[]{:S(2)}) copy-start(f32[64,2,2,128]{3,2,1,0:T(2,128)S(1)} %all-to-all-done.1.parts_ref) | copy-start | bytes 393220
  95.7 12.5 %copy-start.2 = (bf16[8,4,32,256]{3,2,1,0:T(8,128)(2,1)}, bf16[8,4,32,256]{3,2,1,0:T(8,128)(2,1)S(1)}, u32[]{:S(2)}) copy-start(bf16[8,4,32,256]{3,2,1,0:T(8,128)(2,1)S(1)} %collective-permute-done.8.refs_1_) | copy-start | bytes 1572868
  95.7 12.5 %copy-start.3 = (bf16[8,4,32,256]{3,2,1,0:T(8,128)(2,1)}, bf16[8,4,32,256]{3,2,1,0:T(8,128)(2,1)S(1)}, u32[]{:S(2)}) copy-start(bf16[8,4,32,256]{3,2,1,0:T(8,128)(2,1)S(1)} %collective-permute-done.9.refs_2_) | copy-start | bytes 1572868
  96.1 12.0 %collective-permute-start.12 = (bf16[8,32,256]{2,1,0:T(8,128)(2,1)S(1)}, bf16[8,32,256]{2,1,0:T(8,128)(2,1)S(1)}, u32[]{:S(2)}, u32[]{:S(2)}) collective-permute-start(bf16[8,32,256]{2,1,0:T(8,128)(2,1)S(1)} %reshape.23), channel_id=1, source_target_pairs={{0,1},{1,2},{2,3},{3,4},{4,5},{5,6},{6,7},{7,8},{8,9},{9,10},{10,1... | collective-permute-start | bytes 393224 | tf_op jit(solution)/shard_map/ppermute | solution.py:417
  96.5 11.7 %collective-permute-start.13 = (bf16[8,32,256]{2,1,0:T(8,128)(2,1)S(1)}, bf16[8,32,256]{2,1,0:T(8,128)(2,1)S(1)}, u32[]{:S(2)}, u32[]{:S(2)}) collective-permute-start(bf16[8,32,256]{2,1,0:T(8,128)(2,1)S(1)} %reshape.24), channel_id=1, source_target_pairs={{1,0},{2,1},{3,2},{4,3},{5,4},{6,5},{7,6},{8,7},{9,8},{10,9},{11,1... | collective-permute-start | bytes 393224 | tf_op jit(solution)/shard_map/ppermute | solution.py:418
  105.3 2.8 %copy-start.7 = (bf16[8,128,256]{2,1,0:T(8,128)(2,1)}, bf16[8,128,256]{2,1,0:T(8,128)(2,1)S(1)}, u32[]{:S(2)}) copy-start(bf16[8,128,256]{2,1,0:T(8,128)(2,1)S(1)} %collective-permute-done.10.refs_3_) | copy-start | bytes 1572868
  105.3 2.8 %copy-start.8 = (bf16[8,128,256]{2,1,0:T(8,128)(2,1)}, bf16[8,128,256]{2,1,0:T(8,128)(2,1)S(1)}, u32[]{:S(2)}) copy-start(bf16[8,128,256]{2,1,0:T(8,128)(2,1)S(1)} %collective-permute-done.11.refs_4_) | copy-start | bytes 1572868
  108.1 0.6 copy-start.11
  108.2 0.7 copy-start.12

commit v5 on v4

--- a/solution.py
+++ b/solution.py
@@ -19,6 +19,7 @@
 LANES = 128
 VMEM_LIMIT = 59_300_000
 CHUNK = 8
+NORM_FLOPS = 10 * 10**9
 
 
 def exact_dot(a, selection):
@@ -207,7 +208,7 @@
     return jnp.where(mine, live, 0).astype(jnp.float32).sum(axis=1, keepdims=True) * size
 
 
-def combine_statistics(parts_ref, points_ref, norm_ref, rows, cols):
+def combine_kernel(rows, cols, parts_ref, points_ref, norm_ref):
     _, samples, channels = norm_ref.shape
     slots = LANES // GROUPS
     chips = parts_ref.shape[0]
@@ -231,14 +232,26 @@
     norm_ref[1] = both[samples:]
 
 
-def conv_kernel(dilation, chunk, which, with_stats, points_ref, flags_ref, parts_ref, points_row_ref, *refs):
+def combine_statistics(parts, points, x):
+    samples, rows, cols, channels = x.shape
+    return pl.pallas_call(
+        functools.partial(combine_kernel, rows, cols),
+        out_shape=jax.ShapeDtypeStruct((2, samples, channels), jnp.float32),
+        in_specs=[in_vmem(), in_vmem()],
+        out_specs=in_vmem(),
+        cost_estimate=pl.CostEstimate(flops=NORM_FLOPS, bytes_accessed=parts.size * 4, transcendentals=0),
+        name="norm",
+    )(parts, points[None])
+
+
+def conv_kernel(dilation, chunk, which, with_stats, points_ref, flags_ref, norm_ref, *refs):
     d = dilation
-    x_hbm_ref, top_ref, bottom_ref, left_ref, right_ref, left_end_ref, right_end_ref, w_ref, out_hbm_ref, *rest = refs
+    x_hbm_ref, top_ref, bottom_ref, left_ref, right_ref, w_ref, out_hbm_ref, *rest = refs
     if with_stats:
         stats_ref, *edges = rest[:5]
-        x_ref, sems, out_ref, out_sems, norm_ref, even_ref, odd_ref, sums_ref, squares_ref, kept_ref = rest[5:]
+        x_ref, sems, out_ref, out_sems, even_ref, odd_ref, sums_ref, squares_ref, kept_ref = rest[5:]
     else:
-        x_ref, sems, out_ref, out_sems, norm_ref, even_ref, odd_ref = rest
+        x_ref, sems, out_ref, out_sems, even_ref, odd_ref = rest
     g = pl.program_id(0)
     samples = norm_ref.shape[1]
     _, rows, cols, channels = x_ref.shape
@@ -262,14 +275,14 @@
 
         for e in range(lo, hi):
             if e < d:
-                row, side = top_ref[b, e], (left_end_ref, right_end_ref, e)
+                row = top_ref[b, e]
             elif e < rows + d:
-                row, side = x_ref[b, e - d], (left_ref, right_ref, e - d)
+                row = x_ref[b, e - d]
             else:
-                row, side = bottom_ref[b, e - rows - d], (left_end_ref, right_end_ref, e - rows)
-            at = slice(side[2] * d, (side[2] + 1) * d)
-            left = activated(side[0][b, at])
-            right = activated(side[1][b, at])
+                row = bottom_ref[b, e - rows - d]
+            at = slice(e * d, (e + 1) * d)
+            left = activated(left_ref[b, at])
+            right = activated(right_ref[b, at])
             mid = jnp.where(column < points[e] - origin, activated(row), 0.0)
             lhs = jnp.where(edge < points[e] - before_origin, left, 0.0)
             rhs = jnp.where(edge < points[e] - after_origin, right, 0.0)
@@ -311,7 +324,6 @@
     def _():
         for b in range(samples):
             fetch(x_hbm_ref, x_ref, sems, b).start()
-        combine_statistics(parts_ref, points_row_ref, norm_ref, rows, cols)
         fetch(x_hbm_ref, x_ref, sems, 0).wait()
         activate_rows(0, even_ref, 0, rows + 2 * d)
         if with_stats:
@@ -347,7 +359,7 @@
             store(b).wait()
 
 
-def convolve(x, halos, weight, parts, points, flags, dilation, which, with_stats):
+def convolve(x, halos, weight, norm, points, flags, dilation, which, with_stats):
     samples, rows, width, channels = x.shape
     d = dilation
     def whole(shape):
@@ -357,7 +369,7 @@
     out_specs = [pl.BlockSpec(memory_space=pltpu.HBM)]
     act = pltpu.VMEM((rows + 2 * d, width, 3 * channels), jnp.bfloat16)
     scratch = [pltpu.VMEM(x.shape, x.dtype), pltpu.SemaphoreType.DMA((samples,))] * 2
-    scratch += [pltpu.VMEM((2, samples, channels), jnp.float32), act, act]
+    scratch += [act, act]
     if with_stats:
         shape = (3, samples * GROUPS // LANES, LANES)
         out_shape += [jax.ShapeDtypeStruct(shape, jnp.float32), *edge_shapes(x, SECOND_DILATION)]
@@ -372,7 +384,6 @@
             grid=(samples // 2,),
             in_specs=[
                 in_vmem(),
-                in_vmem(),
                 pl.BlockSpec(memory_space=pltpu.HBM),
                 *[in_vmem()] * len(halos),
                 in_vmem(),
@@ -387,35 +398,27 @@
             flops=2 * x.size * 9 * channels, bytes_accessed=5 * x.size, transcendentals=2 * x.size
         ),
         name="conv%d" % d,
-    )(points, flags, parts, points[None], x, *halos, weight)
-
-
-def exchange_sides(edges):
-    first_row, last_row, first_col, last_col = edges
-    lat, lon = lax.axis_size(LAT), lax.axis_size(LON)
-    up = [(i, i + 1) for i in range(lat - 1)]
-    down = [(i + 1, i) for i in range(lat - 1)]
-    east = [(i, (i + 1) % lon) for i in range(lon)]
-    west = [((i + 1) % lon, i) for i in range(lon)]
-    top = lax.ppermute(last_row, LAT, up)
-    bottom = lax.ppermute(first_row, LAT, down)
-    left = lax.ppermute(last_col, LON, east)
-    right = lax.ppermute(first_col, LON, west)
-    return top, bottom, left, right
-
-
-def exchange_corners(top, bottom):
+    )(points, flags, norm, x, *halos, weight)
+
+
+def exchange_rows(edges):
+    lat = lax.axis_size(LAT)
+    top = lax.ppermute(edges[1], LAT, [(i, i + 1) for i in range(lat - 1)])
+    bottom = lax.ppermute(edges[0], LAT, [(i + 1, i) for i in range(lat - 1)])
+    return top, bottom
+
+
+def exchange_columns(edges, top, bottom):
     samples, d, width, channels = top.shape
     lon = lax.axis_size(LON)
-    east = [(i, (i + 1) % lon) for i in range(lon)]
-    west = [((i + 1) % lon, i) for i in range(lon)]
-
-    def packed(lo, hi):
-        ends = jnp.concatenate([top[:, :, lo:hi], bottom[:, :, lo:hi]], axis=1)
-        return ends.reshape(samples, 2 * d * d, channels)
-
-    left = lax.ppermute(packed(width - d, width), LON, east)
-    right = lax.ppermute(packed(0, d), LON, west)
+
+    def packed(cols, lo, hi):
+        above = top[:, :, lo:hi].reshape(samples, d * d, channels)
+        below = bottom[:, :, lo:hi].reshape(samples, d * d, channels)
+        return jnp.concatenate([above, cols, below], axis=1)
+
+    left = lax.ppermute(packed(edges[3], width - d, width), LON, [(i, (i + 1) % lon) for i in range(lon)])
+    right = lax.ppermute(packed(edges[2], 0, d), LON, [((i + 1) % lon, i) for i in range(lon)])
     return left, right
 
 
@@ -429,11 +432,11 @@
     return jnp.broadcast_to(merged[None], (lax.axis_size(CHIPS), *merged.shape))
 
 
-def exchange(local, edges):
-    top, bottom, left, right = exchange_sides(edges)
-    parts = lax.all_to_all(merge_cores(local), CHIPS, 0, 0)
-    parts, top, bottom = lax.optimization_barrier((parts, top, bottom))
-    return parts, (top, bottom, left, right, *exchange_corners(top, bottom))
+def exchange(local, edges, points, x):
+    mine = merge_cores(local)
+    top, bottom = exchange_rows(edges)
+    norm = combine_statistics(lax.all_to_all(mine, CHIPS, 0, 0), points, x)
+    return norm, (top, bottom, *exchange_columns(edges, top, bottom))
 
 
 def per_device(features, band_points, survival_flags, first_kernel_weight, second_kernel_weight):
@@ -441,13 +444,13 @@
     first_weight = first_kernel_weight.reshape(3, 3 * channels, channels)
     second_weight = second_kernel_weight.reshape(3, 3 * channels, channels)
     local, *edges = local_statistics(features, band_points)
-    parts, halos = exchange(local, edges)
+    norm, halos = exchange(local, edges, band_points, features)
     first, local, *edges = convolve(
-        features, halos, first_weight, parts, band_points, survival_flags, FIRST_DILATION, 0, True
+        features, halos, first_weight, norm, band_points, survival_flags, FIRST_DILATION, 0, True
     )
-    parts, halos = exchange(local, edges)
+    norm, halos = exchange(local, edges, band_points, first)
     (section,) = convolve(
-        first, halos, second_weight, parts, band_points, survival_flags, SECOND_DILATION, 1, False
+        first, halos, second_weight, norm, band_points, survival_flags, SECOND_DILATION, 1, False
     )
     return section
 

time: 128 us -> 121 us (0.945)
  starting transfers between devices: 60.5 us -> 46.9 us
  Pallas kernels: 45.9 us -> 49.5 us
  local copies, waits for them, and re-layouts: 3.6 us -> 5.42 us
    ppermute x12 -> x8, starting transfers between devices: 41 us -> 29.4 us  [the longest x2 13.3 us: exchange_rows(): top = lax.ppermute(edges[1], LAT, [(i, i + 1) for i in range(lat - 1)])]
    pallas_call x0 -> x2, Pallas kernels: none -> 3.78 us  [combine_statistics(): pl.pallas_call(functools.partial(combine_kernel, rows, cols), out_shape=j...]
    ppermute x12 -> x8, waiting for transfers between devices: 6.73 us -> 10.5 us  [the longest x2 9.92 us: exchange_columns(): lax.ppermute(packed(edges[3], width - d, width), LON, [(i, (i + 1) % lon)...]
    all_to_all x2, waiting for transfers between devices: 6.71 us -> 3.93 us  [exchange(): norm = combine_statistics(lax.all_to_all(mine, CHIPS, 0, 0), points, x)]
    all_to_all x2, starting transfers between devices: 17.9 us -> 15.9 us  [exchange(): norm = combine_statistics(lax.all_to_all(mine, CHIPS, 0, 0), points, x)]
    unnamed x31 -> x27, local copies, waits for them, and re-layouts: 1.94 us -> 3.7 us
    ppermute x2, waiting for transfers between devices: 1.64 us -> 0.01 us  [merge_cores(): other = lax.ppermute(local, 'core', [(0, 1), (1, 0)])]
  transfers between devices with their start and end apart: 16 -> 12, of which waited for: 6 -> 5; matrix products, arithmetic and copies ran while one was open for 3% -> 4% of each run, Pallas kernels for 0% -> 3%
where the time goes in v5:
time: 121 us; the launch traced here: 119 us
  Pallas kernels  49.5 us (41%)
  starting transfers between devices  46.9 us (39%)
  waiting for transfers between devices  14.4 us (12%)
  local copies, waits for them, and re-layouts  5.42 us (4%)
  other arithmetic  2.66 us (2%)
    pallas_call x2, Pallas kernels, convolve(): pl.pallas_call(functools.partial(conv_kernel, d, CHUNK, which, with_stats...  38.8 us
    all_to_all x2, starting transfers between devices, exchange(): norm = combine_statistics(lax.all_to_all(mine, CHIPS, 0, 0), points, x)  15.9 us
    ppermute x2, starting transfers between devices, exchange_rows(): top = lax.ppermute(edges[1], LAT, [(i, i + 1) for i in range(lat - 1)])  13.3 us
    ppermute x2, starting transfers between devices, exchange_columns(): lax.ppermute(packed(edges[2], 0, d), LON, [((i + 1) % lon, i) for i in ra...  10.2 us
    ppermute x2, waiting for transfers between devices, exchange_columns(): lax.ppermute(packed(edges[3], width - d, width), LON, [(i, (i + 1) % lon)...  9.92 us
    pallas_call x1, Pallas kernels, local_statistics(): pl.pallas_call(stats_kernel, out_shape=[jax.ShapeDtypeStruct(shape, jnp.f...  6.88 us
    ppermute x2, starting transfers between devices, exchange_rows(): bottom = lax.ppermute(edges[0], LAT, [(i + 1, i) for i in range(lat - 1)])  4.31 us
    all_to_all x2, waiting for transfers between devices, exchange(): norm = combine_statistics(lax.all_to_all(mine, CHIPS, 0, 0), points, x)  3.93 us
  transfers between devices with their start and end apart: 12, of which 5 were waited for; matrix products, arithmetic and copies ran while one was open for 4% of the time, Pallas kernels for 3%

profile of v5, /device:TPU:1, one launch (start us, length us, event | category | flops | bytes accessed | tf_op | source)
XLA Modules:
  0.0 119.3 jit_solution(18237344939285960202)
XLA Ops:
  0.0 0.0 copy-start.9
  0.0 6.9 %stats.1 = (f32[3,2,128]{2,1,0:T(2,128)}, bf16[8,2,32,256]{3,2,1,0:T(8,128)(2,1)}, bf16[8,2,32,256]{3,2,1,0:T(8,128)(2,1)}, bf16[8,64,256]{2,1,0:T(8,128)(2,1)}, bf16[8,64,256]{2,1,0:T(8,128)(2,1)}) custom-call(s32[128]{0:T(128)} %points_ref.5, bf16[8,32,32,256]{3,2,1,0:T(8,128)(2,1)} %refs_0_.1), custom_call_target="tpu_custom_call" | custom-call | flops 16777216 | bytes 4194304 | tf_op jit(solution)/shard_map/stats/pallas_call | solution.py:173
  6.9 0.0 copy-start.2
  6.9 1.5 %collective-permute-start = (f32[3,2,128]{2,1,0:T(2,128)}, f32[3,2,128]{2,1,0:T(2,128)S(1)}, u32[]{:S(2)}, u32[]{:S(2)}) collective-permute-start(f32[3,2,128]{2,1,0:T(2,128)} %get-tuple-element.16), channel_id=1, source_target_pairs={{0,32},{32,0},{1,33},{33,1},{2,34},{34,2},{3,35},{35,3},{4,36},{36... | collective-permute-start | bytes 9224 | tf_op jit(solution)/shard_map/ppermute | solution.py:426
  8.4 5.5 %collective-permute-start.1 = (bf16[8,2,32,256]{3,2,1,0:T(8,128)(2,1)}, bf16[8,2,32,256]{3,2,1,0:T(8,128)(2,1)S(1)}, u32[]{:S(2)}, u32[]{:S(2)}) collective-permute-start(bf16[8,2,32,256]{3,2,1,0:T(8,128)(2,1)} %get-tuple-element.17), channel_id=1, source_target_pairs={{0,32},{32,64},{64,96},{1,33},{33,65},{65,97},{2,34},{34,66},{66,9... | collective-permute-start | bytes 786440 | tf_op jit(solution)/shard_map/ppermute | solution.py:406
  13.9 1.9 %collective-permute-start.2 = (bf16[8,2,32,256]{3,2,1,0:T(8,128)(2,1)}, bf16[8,2,32,256]{3,2,1,0:T(8,128)(2,1)S(1)}, u32[]{:S(2)}, u32[]{:S(2)}) collective-permute-start(bf16[8,2,32,256]{3,2,1,0:T(8,128)(2,1)} %get-tuple-element.18), channel_id=1, source_target_pairs={{32,0},{64,32},{96,64},{33,1},{65,33},{97,65},{34,2},{66,34},{98,6... | collective-permute-start | bytes 786440 | tf_op jit(solution)/shard_map/ppermute | solution.py:407
  15.8 0.0 copy-done.9
  15.8 0.7 copy.7.flags_ref
  16.5 0.0 collective-permute-done
  16.5 0.7 slice_add_fusion.3
  17.2 0.7 broadcast_in_dim.6
  17.9 8.1 %all-to-all-start = ((f32[64,2,2,128]{3,2,1,0:T(2,128)}), f32[64,2,2,128]{3,2,1,0:T(2,128)S(1)}, u32[]{:S(2)}, u32[]{:S(2)}) async-start(f32[64,2,2,128]{3,2,1,0:T(2,128)} %broadcast_in_dim.6), calls=%async_computation | async-start | bytes 262144 | tf_op jit(solution)/shard_map/all_to_all | solution.py:438
  26.1 0.0 collective-permute-done.1.refs_1_
  26.1 0.0 copy-start.7
  26.1 0.0 collective-permute-done.2.refs_2_
  26.1 0.0 copy-start.8
  26.2 1.1 pad_maximum_fusion.2
  27.3 1.1 collective-permute-start.3
  28.4 0.0 copy-done.2
  28.4 0.1 pad_maximum_fusion.3
  28.5 4.7 %collective-permute-start.4 = (bf16[8,72,256]{2,1,0:T(8,128)(2,1)S(1)}, bf16[8,72,256]{2,1,0:T(8,128)(2,1)S(1)}, u32[]{:S(2)}, u32[]{:S(2)}) collective-permute-start(bf16[8,72,256]{2,1,0:T(8,128)(2,1)S(1)} %pad_maximum_fusion.3), channel_id=1, source_target_pairs={{1,0},{2,1},{3,2},{4,3},{5,4},{6,5},{7,6},{8,7},{9,8},{10,9},{11,1... | collective-permute-start | bytes 884744 | tf_op jit(solution)/shard_map/ppermute | solution.py:421
  33.3 1.8 %all-to-all-done.parts_ref = f32[64,2,2,128]{3,2,1,0:T(2,128)S(1)} async-done(((f32[64,2,2,128]{3,2,1,0:T(2,128)}), f32[64,2,2,128]{3,2,1,0:T(2,128)S(1)}, u32[]{:S(2)}, u32[]{:S(2)}) %all-to-all-start) | async-done | bytes 131104 | tf_op jit(solution)/shard_map/all_to_all | solution.py:438
  35.0 0.0 copy-start.3
  35.0 0.7 copy-done.3
  35.7 1.9 %norm.2.norm_ref = f32[2,8,256]{2,1,0:T(8,128)} custom-call(f32[64,2,2,128]{3,2,1,0:T(2,128)} %copy-done.3, s32[1,128]{1,0:T(1,128)} %bitcast.3), custom_call_target="tpu_custom_call" | custom-call | flops 10000000000 | bytes 131072 | tf_op jit(solution)/shard_map/norm/pallas_call | solution.py:237
  37.6 0.0 copy-done.7
  37.6 0.0 copy-done.8
  37.6 0.9 collective-permute-done.3.refs_3_
  38.5 0.0 copy-start.11
  38.5 0.0 collective-permute-done.4.refs_4_
  38.5 0.0 copy-start.12
  38.5 0.7 copy-done.11
  39.2 0.1 copy-done.12
  39.3 20.8 %conv2.1 = (bf16[8,32,32,256]{3,2,1,0:T(8,128)(2,1)}, f32[3,2,128]{2,1,0:T(2,128)}, bf16[8,4,32,256]{3,2,1,0:T(8,128)(2,1)}, bf16[8,4,32,256]{3,2,1,0:T(8,128)(2...) custom-call(s32[128]{0:T(128)} %points_ref.5, s32[8,2]{1,0:T(8,128)} %copy.7.flags_ref, ...), custom_call_target="tpu_custom_call" | custom-call | flops 9663676416 | bytes 10485760 | tf_op jit(solution)/shard_map/conv2/pallas_call | solution.py:379
  60.2 0.0 copy-start.1
  60.2 7.8 %collective-permute-start.6 = (bf16[8,4,32,256]{3,2,1,0:T(8,128)(2,1)}, bf16[8,4,32,256]{3,2,1,0:T(8,128)(2,1)S(1)}, u32[]{:S(2)}, u32[]{:S(2)}) collective-permute-start(bf16[8,4,32,256]{3,2,1,0:T(8,128)(2,1)} %get-tuple-element.23), channel_id=1, source_target_pairs={{0,32},{32,64},{64,96},{1,33},{33,65},{65,97},{2,34},{34,66},{66,9... | collective-permute-start | bytes 1572872 | tf_op jit(solution)/shard_map/ppermute | solution.py:406
  68.0 0.1 collective-permute-start.5
  68.1 2.4 %collective-permute-start.7 = (bf16[8,4,32,256]{3,2,1,0:T(8,128)(2,1)}, bf16[8,4,32,256]{3,2,1,0:T(8,128)(2,1)S(1)}, u32[]{:S(2)}, u32[]{:S(2)}) collective-permute-start(bf16[8,4,32,256]{3,2,1,0:T(8,128)(2,1)} %get-tuple-element.24), channel_id=1, source_target_pairs={{32,0},{64,32},{96,64},{33,1},{65,33},{97,65},{34,2},{66,34},{98,6... | collective-permute-start | bytes 1572872 | tf_op jit(solution)/shard_map/ppermute | solution.py:407
  70.5 0.0 collective-permute-done.5
  70.5 0.7 slice_add_fusion.2
  71.2 0.7 broadcast_in_dim.8
  71.9 0.0 copy-start
  71.9 7.7 %all-to-all-start.1 = ((f32[64,2,2,128]{3,2,1,0:T(2,128)}), f32[64,2,2,128]{3,2,1,0:T(2,128)S(1)}, u32[]{:S(2)}, u32[]{:S(2)}) async-start(f32[64,2,2,128]{3,2,1,0:T(2,128)} %broadcast_in_dim.8), calls=%async_computation.1 | async-start | bytes 262144 | tf_op jit(solution)/shard_map/all_to_all | solution.py:438
  79.6 0.0 collective-permute-done.6.refs_1_
  79.6 0.0 copy-start.5
  79.6 0.1 fusion.2
  79.7 0.6 collective-permute-done.7.refs_2_
  80.3 0.0 copy-start.6
  80.3 0.1 fusion.3
  80.4 0.0 copy-done.1
  80.5 0.5 collective-permute-start.8
  81.0 0.0 copy-done
  81.1 0.0 copy-done.5
  81.1 0.0 copy-done.6
  81.1 5.5 %collective-permute-start.9 = (bf16[8,160,256]{2,1,0:T(8,128)(2,1)S(1)}, bf16[8,160,256]{2,1,0:T(8,128)(2,1)S(1)}, u32[]{:S(2)}, u32[]{:S(2)}) collective-permute-start(bf16[8,160,256]{2,1,0:T(8,128)(2,1)S(1)} %pad_maximum_fusion.1), channel_id=1, source_target_pairs={{1,0},{2,1},{3,2},{4,3},{5,4},{6,5},{7,6},{8,7},{9,8},{10,9},{11,1... | collective-permute-start | bytes 1966088 | tf_op jit(solution)/shard_map/ppermute | solution.py:421
  86.6 2.2 %all-to-all-done.1.parts_ref = f32[64,2,2,128]{3,2,1,0:T(2,128)S(1)} async-done(((f32[64,2,2,128]{3,2,1,0:T(2,128)}), f32[64,2,2,128]{3,2,1,0:T(2,128)S(1)}, u32[]{:S(2)}, u32[]{:S(2)}) %all-to-all-start.1) | async-done | bytes 131104 | tf_op jit(solution)/shard_map/all_to_all | solution.py:438
  88.7 0.0 copy-start.4
  88.7 0.7 copy-done.4
  89.4 1.9 %norm.3.norm_ref = f32[2,8,256]{2,1,0:T(8,128)} custom-call(f32[64,2,2,128]{3,2,1,0:T(2,128)} %copy-done.4, s32[1,128]{1,0:T(1,128)} %bitcast.4), custom_call_target="tpu_custom_call" | custom-call | flops 10000000000 | bytes 131072 | tf_op jit(solution)/shard_map/norm/pallas_call | solution.py:237
  91.3 9.0 %collective-permute-done.8.refs_3_ = bf16[8,160,256]{2,1,0:T(8,128)(2,1)} collective-permute-done((bf16[8,160,256]{2,1,0:T(8,128)(2,1)S(1)}, bf16[8,160,256]{2,1,0:T(8,128)(2,1)}, u32[]{:S(2)}, u32[]{:S(2)}) %collective-permute-start.8) | collective-permute-done | bytes 655392 | tf_op jit(solution)/shard_map/ppermute | solution.py:420
  100.3 0.0 collective-permute-done.9.refs_4_
  100.3 0.0 copy-start.10
  100.3 0.9 copy-done.10
  101.2 18.0 %conv4.1 = bf16[8,32,32,256]{3,2,1,0:T(8,128)(2,1)} custom-call(s32[128]{0:T(128)} %points_ref.5, s32[8,2]{1,0:T(8,128)} %copy.7.flags_ref, f32[2,8,256]{2,1,0:T(8,128)} %norm.3.norm_ref, bf16[8,32,32,256]{3,2,1,0:T(8,128)(2,1)} %get-tuple-element.22.refs_0_, bf16[8,4,32,256]{3,2,1,0:T(8,128)(2,1)} %copy-done.5, bf16[8,4,32,256]{3,2,1,0:T(8,128)(2,1)} %copy-done.6, ...), custom_call_target="tpu_custom_call" | custom-call | flops 9663676416 | bytes 10485760 | tf_op jit(solution)/shard_map/conv4/pallas_call | solution.py:379
  (14 shorter events, 0.3 us)
Async XLA Ops:
  0.0 15.8 %copy-start.9 = (s32[8,2]{0,1:T(2,128)S(1)}, s32[8,2]{0,1:T(2,128)}, u32[]{:S(2)}) copy-start(s32[8,2]{0,1:T(2,128)} %param.7) | copy-start | bytes 196
  6.9 21.5 %copy-start.2 = (bf16[8,64,256]{2,1,0:T(8,128)(2,1)S(1)}, bf16[8,64,256]{2,1,0:T(8,128)(2,1)}, u32[]{:S(2)}) copy-start(bf16[8,64,256]{2,1,0:T(8,128)(2,1)} %get-tuple-element.20) | copy-start | bytes 786436
  6.9 9.6 %collective-permute-start = (f32[3,2,128]{2,1,0:T(2,128)}, f32[3,2,128]{2,1,0:T(2,128)S(1)}, u32[]{:S(2)}, u32[]{:S(2)}) collective-permute-start(f32[3,2,128]{2,1,0:T(2,128)} %get-tuple-element.16), channel_id=1, source_target_pairs={{0,32},{32,0},{1,33},{33,1},{2,34},{34,2},{3,35},{35,3},{4,36},{36... | collective-permute-start | bytes 9224 | tf_op jit(solution)/shard_map/ppermute | solution.py:426
  8.4 17.7 %collective-permute-start.1 = (bf16[8,2,32,256]{3,2,1,0:T(8,128)(2,1)}, bf16[8,2,32,256]{3,2,1,0:T(8,128)(2,1)S(1)}, u32[]{:S(2)}, u32[]{:S(2)}) collective-permute-start(bf16[8,2,32,256]{3,2,1,0:T(8,128)(2,1)} %get-tuple-element.17), channel_id=1, source_target_pairs={{0,32},{32,64},{64,96},{1,33},{33,65},{65,97},{2,34},{34,66},{66,9... | collective-permute-start | bytes 786440 | tf_op jit(solution)/shard_map/ppermute | solution.py:406
  13.9 12.2 %collective-permute-start.2 = (bf16[8,2,32,256]{3,2,1,0:T(8,128)(2,1)}, bf16[8,2,32,256]{3,2,1,0:T(8,128)(2,1)S(1)}, u32[]{:S(2)}, u32[]{:S(2)}) collective-permute-start(bf16[8,2,32,256]{3,2,1,0:T(8,128)(2,1)} %get-tuple-element.18), channel_id=1, source_target_pairs={{32,0},{64,32},{96,64},{33,1},{65,33},{97,65},{34,2},{66,34},{98,6... | collective-permute-start | bytes 786440 | tf_op jit(solution)/shard_map/ppermute | solution.py:407
  17.9 17.1 %all-to-all-start = ((f32[64,2,2,128]{3,2,1,0:T(2,128)}), f32[64,2,2,128]{3,2,1,0:T(2,128)S(1)}, u32[]{:S(2)}, u32[]{:S(2)}) async-start(f32[64,2,2,128]{3,2,1,0:T(2,128)} %broadcast_in_dim.6), calls=%async_computation | async-start | bytes 262144 | tf_op jit(solution)/shard_map/all_to_all | solution.py:438
  26.1 11.5 %copy-start.7 = (bf16[8,2,32,256]{3,2,1,0:T(8,128)(2,1)}, bf16[8,2,32,256]{3,2,1,0:T(8,128)(2,1)S(1)}, u32[]{:S(2)}) copy-start(bf16[8,2,32,256]{3,2,1,0:T(8,128)(2,1)S(1)} %collective-permute-done.1.refs_1_) | copy-start | bytes 786436
  26.1 11.4 %copy-start.8 = (bf16[8,2,32,256]{3,2,1,0:T(8,128)(2,1)}, bf16[8,2,32,256]{3,2,1,0:T(8,128)(2,1)S(1)}, u32[]{:S(2)}) copy-start(bf16[8,2,32,256]{3,2,1,0:T(8,128)(2,1)S(1)} %collective-permute-done.2.refs_2_) | copy-start | bytes 786436
  27.3 11.2 %collective-permute-start.3 = (bf16[8,72,256]{2,1,0:T(8,128)(2,1)S(1)}, bf16[8,72,256]{2,1,0:T(8,128)(2,1)S(1)}, u32[]{:S(2)}, u32[]{:S(2)}) collective-permute-start(bf16[8,72,256]{2,1,0:T(8,128)(2,1)S(1)} %pad_maximum_fusion.2), channel_id=1, source_target_pairs={{0,1},{1,2},{2,3},{3,4},{4,5},{5,6},{6,7},{7,8},{8,9},{9,10},{10,1... | collective-permute-start | bytes 884744 | tf_op jit(solution)/shard_map/ppermute | solution.py:420
  28.5 10.0 %collective-permute-start.4 = (bf16[8,72,256]{2,1,0:T(8,128)(2,1)S(1)}, bf16[8,72,256]{2,1,0:T(8,128)(2,1)S(1)}, u32[]{:S(2)}, u32[]{:S(2)}) collective-permute-start(bf16[8,72,256]{2,1,0:T(8,128)(2,1)S(1)} %pad_maximum_fusion.3), channel_id=1, source_target_pairs={{1,0},{2,1},{3,2},{4,3},{5,4},{6,5},{7,6},{8,7},{9,8},{10,9},{11,1... | collective-permute-start | bytes 884744 | tf_op jit(solution)/shard_map/ppermute | solution.py:421
  35.0 0.7 copy-start.3
  38.5 0.7 copy-start.11
  38.5 0.8 copy-start.12
  60.2 20.2 %copy-start.1 = (bf16[8,128,256]{2,1,0:T(8,128)(2,1)S(1)}, bf16[8,128,256]{2,1,0:T(8,128)(2,1)}, u32[]{:S(2)}) copy-start(bf16[8,128,256]{2,1,0:T(8,128)(2,1)} %get-tuple-element.25) | copy-start | bytes 1572868
  60.2 19.5 %collective-permute-start.6 = (bf16[8,4,32,256]{3,2,1,0:T(8,128)(2,1)}, bf16[8,4,32,256]{3,2,1,0:T(8,128)(2,1)S(1)}, u32[]{:S(2)}, u32[]{:S(2)}) collective-permute-start(bf16[8,4,32,256]{3,2,1,0:T(8,128)(2,1)} %get-tuple-element.23), channel_id=1, source_target_pairs={{0,32},{32,64},{64,96},{1,33},{33,65},{65,97},{2,34},{34,66},{66,9... | collective-permute-start | bytes 1572872 | tf_op jit(solution)/shard_map/ppermute | solution.py:406
  68.0 2.5 %collective-permute-start.5 = (f32[3,2,128]{2,1,0:T(2,128)}, f32[3,2,128]{2,1,0:T(2,128)S(1)}, u32[]{:S(2)}, u32[]{:S(2)}) collective-permute-start(f32[3,2,128]{2,1,0:T(2,128)} %get-tuple-element.21), channel_id=1, source_target_pairs={{0,32},{32,0},{1,33},{33,1},{2,34},{34,2},{3,35},{35,3},{4,36},{36... | collective-permute-start | bytes 9224 | tf_op jit(solution)/shard_map/ppermute | solution.py:426
  68.1 12.2 %collective-permute-start.7 = (bf16[8,4,32,256]{3,2,1,0:T(8,128)(2,1)}, bf16[8,4,32,256]{3,2,1,0:T(8,128)(2,1)S(1)}, u32[]{:S(2)}, u32[]{:S(2)}) collective-permute-start(bf16[8,4,32,256]{3,2,1,0:T(8,128)(2,1)} %get-tuple-element.24), channel_id=1, source_target_pairs={{32,0},{64,32},{96,64},{33,1},{65,33},{97,65},{34,2},{66,34},{98,6... | collective-permute-start | bytes 1572872 | tf_op jit(solution)/shard_map/ppermute | solution.py:407
  71.9 9.1 %copy-start = (bf16[8,128,256]{2,1,0:T(8,128)(2,1)S(1)}, bf16[8,128,256]{2,1,0:T(8,128)(2,1)}, u32[]{:S(2)}) copy-start(bf16[8,128,256]{2,1,0:T(8,128)(2,1)} %get-tuple-element.26) | copy-start | bytes 1572868
  71.9 16.8 %all-to-all-start.1 = ((f32[64,2,2,128]{3,2,1,0:T(2,128)}), f32[64,2,2,128]{3,2,1,0:T(2,128)S(1)}, u32[]{:S(2)}, u32[]{:S(2)}) async-start(f32[64,2,2,128]{3,2,1,0:T(2,128)} %broadcast_in_dim.8), calls=%async_computation.1 | async-start | bytes 262144 | tf_op jit(solution)/shard_map/all_to_all | solution.py:438
  79.6 1.5 %copy-start.5 = (bf16[8,4,32,256]{3,2,1,0:T(8,128)(2,1)}, bf16[8,4,32,256]{3,2,1,0:T(8,128)(2,1)S(1)}, u32[]{:S(2)}) copy-start(bf16[8,4,32,256]{3,2,1,0:T(8,128)(2,1)S(1)} %collective-permute-done.6.refs_1_) | copy-start | bytes 1572868
  80.3 0.8 copy-start.6
  80.5 19.8 %collective-permute-start.8 = (bf16[8,160,256]{2,1,0:T(8,128)(2,1)S(1)}, bf16[8,160,256]{2,1,0:T(8,128)(2,1)}, u32[]{:S(2)}, u32[]{:S(2)}) collective-permute-start(bf16[8,160,256]{2,1,0:T(8,128)(2,1)S(1)} %pad_maximum_fusion), channel_id=1, source_target_pairs={{0,1},{1,2},{2,3},{3,4},{4,5},{5,6},{6,7},{7,8},{8,9},{9,10},{10,1... | collective-permute-start | bytes 1966088 | tf_op jit(solution)/shard_map/ppermute | solution.py:420
  81.1 19.2 %collective-permute-start.9 = (bf16[8,160,256]{2,1,0:T(8,128)(2,1)S(1)}, bf16[8,160,256]{2,1,0:T(8,128)(2,1)S(1)}, u32[]{:S(2)}, u32[]{:S(2)}) collective-permute-start(bf16[8,160,256]{2,1,0:T(8,128)(2,1)S(1)} %pad_maximum_fusion.1), channel_id=1, source_target_pairs={{1,0},{2,1},{3,2},{4,3},{5,4},{6,5},{7,6},{8,7},{9,8},{10,9},{11,1... | collective-permute-start | bytes 1966088 | tf_op jit(solution)/shard_map/ppermute | solution.py:421
  88.7 0.7 copy-start.4
  100.3 0.9 copy-start.10

commit v6 on v5

--- a/solution.py
+++ b/solution.py
@@ -17,7 +17,7 @@
 LON = ("y", "zl", "x")
 CHIPS = ("zh", "y", "zl", "x")
 LANES = 128
-VMEM_LIMIT = 59_300_000
+VMEM_LIMIT = 52_000_000
 CHUNK = 8
 NORM_FLOPS = 10 * 10**9
 
@@ -189,7 +189,7 @@
             ],
         ),
         compiler_params=pltpu.CompilerParams(
-            dimension_semantics=("arbitrary",), vmem_limit_bytes=VMEM_LIMIT
+            dimension_semantics=("arbitrary",), vmem_limit_bytes=58_000_000
         ),
         cost_estimate=pl.CostEstimate(
             flops=8 * x.size, bytes_accessed=2 * x.size, transcendentals=0
@@ -239,6 +239,7 @@
         out_shape=jax.ShapeDtypeStruct((2, samples, channels), jnp.float32),
         in_specs=[in_vmem(), in_vmem()],
         out_specs=in_vmem(),
+        compiler_params=pltpu.CompilerParams(vmem_limit_bytes=4_000_000),
         cost_estimate=pl.CostEstimate(flops=NORM_FLOPS, bytes_accessed=parts.size * 4, transcendentals=0),
         name="norm",
     )(parts, points[None])
@@ -273,6 +274,8 @@
             t = (value.astype(jnp.float32) - mean) * half
             return t + t * jnp.tanh(t)
 
+        left = activated(left_ref[b, lo * d : hi * d])
+        right = activated(right_ref[b, lo * d : hi * d])
         for e in range(lo, hi):
             if e < d:
                 row = top_ref[b, e]
@@ -280,17 +283,15 @@
                 row = x_ref[b, e - d]
             else:
                 row = bottom_ref[b, e - rows - d]
-            at = slice(e * d, (e + 1) * d)
-            left = activated(left_ref[b, at])
-            right = activated(right_ref[b, at])
-            mid = jnp.where(column < points[e] - origin, activated(row), 0.0)
-            lhs = jnp.where(edge < points[e] - before_origin, left, 0.0)
-            rhs = jnp.where(edge < points[e] - after_origin, right, 0.0)
-            before = jnp.concatenate([lhs, mid[: cols - d]], axis=0)
-            after = jnp.concatenate([mid[d:], rhs], axis=0)
-            act_ref[e, :, 0:channels] = before.astype(jnp.bfloat16)
-            act_ref[e, :, channels : 2 * channels] = mid.astype(jnp.bfloat16)
-            act_ref[e, :, 2 * channels :] = after.astype(jnp.bfloat16)
+            at = slice((e - lo) * d, (e - lo + 1) * d)
+            mid = jnp.where(column < points[e] - origin, activated(row), 0.0).astype(jnp.bfloat16)
+            lhs = jnp.where(edge < points[e] - before_origin, left[at], 0.0).astype(jnp.bfloat16)
+            rhs = jnp.where(edge < points[e] - after_origin, right[at], 0.0).astype(jnp.bfloat16)
+            act_ref[e, d:, 0:channels] = mid[: cols - d]
+            act_ref[e, :d, 0:channels] = lhs
+            act_ref[e, :, channels : 2 * channels] = mid
+            act_ref[e, : cols - d, 2 * channels :] = mid[d:]
+            act_ref[e, cols - d :, 2 * channels :] = rhs
 
     def convolve_rows(k, scale, act_ref, start):
         acc = None
@@ -306,7 +307,7 @@
             kept_ref[start : start + chunk] = result
 
     def phase(k, act_ref, follow, next_ref):
-        scale = flags_ref[2 * g + k, which].astype(jnp.float32) * (1.0 / KEEP_RATE)
+        scale = flags_ref[which, 2 * g + k].astype(jnp.float32) * (1.0 / KEEP_RATE)
         steps = rows // chunk
         each = (rows + 2 * d) // steps
         for step in range(steps):
@@ -441,16 +442,17 @@
 
 def per_device(features, band_points, survival_flags, first_kernel_weight, second_kernel_weight):
     channels = features.shape[3]
+    flags = survival_flags.T
     first_weight = first_kernel_weight.reshape(3, 3 * channels, channels)
     second_weight = second_kernel_weight.reshape(3, 3 * channels, channels)
     local, *edges = local_statistics(features, band_points)
     norm, halos = exchange(local, edges, band_points, features)
     first, local, *edges = convolve(
-        features, halos, first_weight, norm, band_points, survival_flags, FIRST_DILATION, 0, True
+        features, halos, first_weight, norm, band_points, flags, FIRST_DILATION, 0, True
     )
     norm, halos = exchange(local, edges, band_points, first)
     (section,) = convolve(
-        first, halos, second_weight, norm, band_points, survival_flags, SECOND_DILATION, 1, False
+        first, halos, second_weight, norm, band_points, flags, SECOND_DILATION, 1, False
     )
     return section
 

time: 121 us -> 114 us (0.942)
  Pallas kernels: 49.5 us -> 41.5 us
  waiting for transfers between devices: 14.4 us -> 19.6 us
  local copies, waits for them, and re-layouts: 5.42 us -> 1.75 us
    ppermute x2, waiting for transfers between devices: 9.92 us -> 16.6 us  [exchange_columns(): lax.ppermute(packed(edges[3], width - d, width), LON, [(i, (i + 1) % lon)...]
    pallas_call x2, Pallas kernels: 38.8 us -> 34.1 us  [convolve(): pl.pallas_call(functools.partial(conv_kernel, d, CHUNK, which, with_stats...]
    unnamed x27 -> x10, local copies, waits for them, and re-layouts: 3.7 us -> 0.02 us
    pallas_call x2, Pallas kernels: 3.78 us -> 0.73 us  [combine_statistics(): pl.pallas_call(functools.partial(combine_kernel, rows, cols), out_shape=j...]
    all_to_all x2, waiting for transfers between devices: 3.93 us -> 1.92 us  [exchange(): norm = combine_statistics(lax.all_to_all(mine, CHIPS, 0, 0), points, x)]
    concatenate x4, other arithmetic: 1.26 us -> 2.93 us  [packed(): return jnp.concatenate([above, cols, below], axis=1)]
  transfers between devices with their start and end apart: 12 -> 12, of which waited for: 5 -> 5; matrix products, arithmetic and copies ran while one was open for 4% -> 5% of each run, Pallas kernels for 3% -> 1%
where the time goes in v6:
time: 114 us; the launch traced here: 113 us
  starting transfers between devices  46.5 us (41%)
  Pallas kernels  41.5 us (36%)
  waiting for transfers between devices  19.6 us (17%)
  other arithmetic  3.65 us (3%)
  local copies, waits for them, and re-layouts  1.75 us (2%)
    pallas_call x2, Pallas kernels, convolve(): pl.pallas_call(functools.partial(conv_kernel, d, CHUNK, which, with_stats...  34.1 us
    ppermute x2, waiting for transfers between devices, exchange_columns(): lax.ppermute(packed(edges[3], width - d, width), LON, [(i, (i + 1) % lon)...  16.6 us
    all_to_all x2, starting transfers between devices, exchange(): norm = combine_statistics(lax.all_to_all(mine, CHIPS, 0, 0), points, x)  15.8 us
    ppermute x2, starting transfers between devices, exchange_rows(): top = lax.ppermute(edges[1], LAT, [(i, i + 1) for i in range(lat - 1)])  13.2 us
    ppermute x2, starting transfers between devices, exchange_columns(): lax.ppermute(packed(edges[2], 0, d), LON, [((i + 1) % lon, i) for i in ra...  10.4 us
    pallas_call x1, Pallas kernels, local_statistics(): pl.pallas_call(stats_kernel, out_shape=[jax.ShapeDtypeStruct(shape, jnp.f...  6.73 us
    ppermute x2, starting transfers between devices, exchange_rows(): bottom = lax.ppermute(edges[0], LAT, [(i + 1, i) for i in range(lat - 1)])  4.31 us
    concatenate x4, other arithmetic, packed(): return jnp.concatenate([above, cols, below], axis=1)  2.93 us
  transfers between devices with their start and end apart: 12, of which 5 were waited for; matrix products, arithmetic and copies ran while one was open for 5% of the time, Pallas kernels for 1%

profile of v6, /device:TPU:1, one launch (start us, length us, event | category | flops | bytes accessed | tf_op | source)
XLA Modules:
  0.0 113.4 jit_solution(8668121086827986966)
XLA Ops:
  0.0 6.7 %stats.1 = (f32[3,2,128]{2,1,0:T(2,128)}, bf16[8,2,32,256]{3,2,1,0:T(8,128)(2,1)}, bf16[8,2,32,256]{3,2,1,0:T(8,128)(2,1)}, bf16[8,64,256]{2,1,0:T(8,128)(2,1)}, bf16[8,64,256]{2,1,0:T(8,128)(2,1)}) custom-call(s32[128]{0:T(128)} %points_ref.5, bf16[8,32,32,256]{3,2,1,0:T(8,128)(2,1)} %refs_0_.1), custom_call_target="tpu_custom_call" | custom-call | flops 16777216 | bytes 4194304 | tf_op jit(solution)/shard_map/stats/pallas_call | solution.py:173
  6.7 0.0 copy-start.4
  6.7 0.0 copy-start
  6.8 1.5 %collective-permute-start = (f32[3,2,128]{2,1,0:T(2,128)}, f32[3,2,128]{2,1,0:T(2,128)S(1)}, u32[]{:S(2)}, u32[]{:S(2)}) collective-permute-start(f32[3,2,128]{2,1,0:T(2,128)} %get-tuple-element.16), channel_id=1, source_target_pairs={{0,32},{32,0},{1,33},{33,1},{2,34},{34,2},{3,35},{35,3},{4,36},{36... | collective-permute-start | bytes 9224 | tf_op jit(solution)/shard_map/ppermute | solution.py:427
  8.3 5.5 %collective-permute-start.1 = (bf16[8,2,32,256]{3,2,1,0:T(8,128)(2,1)}, bf16[8,2,32,256]{3,2,1,0:T(8,128)(2,1)S(1)}, u32[]{:S(2)}, u32[]{:S(2)}) collective-permute-start(bf16[8,2,32,256]{3,2,1,0:T(8,128)(2,1)} %get-tuple-element.17), channel_id=1, source_target_pairs={{0,32},{32,64},{64,96},{1,33},{33,65},{65,97},{2,34},{34,66},{66,9... | collective-permute-start | bytes 786440 | tf_op jit(solution)/shard_map/ppermute | solution.py:407
  13.8 1.9 %collective-permute-start.2 = (bf16[8,2,32,256]{3,2,1,0:T(8,128)(2,1)}, bf16[8,2,32,256]{3,2,1,0:T(8,128)(2,1)S(1)}, u32[]{:S(2)}, u32[]{:S(2)}) collective-permute-start(bf16[8,2,32,256]{3,2,1,0:T(8,128)(2,1)} %get-tuple-element.18), channel_id=1, source_target_pairs={{32,0},{64,32},{96,64},{33,1},{65,33},{97,65},{34,2},{66,34},{98,6... | collective-permute-start | bytes 786440 | tf_op jit(solution)/shard_map/ppermute | solution.py:408
  15.7 0.0 collective-permute-done
  15.7 0.7 slice_add_fusion.3
  16.4 0.7 broadcast_in_dim.6
  17.1 8.1 %all-to-all-start = ((f32[64,2,2,128]{3,2,1,0:T(2,128)}), f32[64,2,2,128]{3,2,1,0:T(2,128)S(1)}, u32[]{:S(2)}, u32[]{:S(2)}) async-start(f32[64,2,2,128]{3,2,1,0:T(2,128)} %broadcast_in_dim.6), calls=%async_computation | async-start | bytes 262144 | tf_op jit(solution)/shard_map/all_to_all | solution.py:439
  25.2 0.0 collective-permute-done.1.refs_1_
  25.3 0.0 collective-permute-done.2.refs_2_
  25.4 1.0 pad_maximum_fusion.2
  26.5 1.1 collective-permute-start.3
  27.5 0.0 copy-done.4
  27.5 0.1 pad_maximum_fusion.3
  27.6 4.7 %collective-permute-start.4 = (bf16[8,72,256]{2,1,0:T(8,128)(2,1)S(1)}, bf16[8,72,256]{2,1,0:T(8,128)(2,1)S(1)}, u32[]{:S(2)}, u32[]{:S(2)}) collective-permute-start(bf16[8,72,256]{2,1,0:T(8,128)(2,1)S(1)} %pad_maximum_fusion.3), channel_id=1, source_target_pairs={{1,0},{2,1},{3,2},{4,3},{5,4},{6,5},{7,6},{8,7},{9,8},{10,9},{11,1... | collective-permute-start | bytes 884744 | tf_op jit(solution)/shard_map/ppermute | solution.py:422
  32.4 1.9 %all-to-all-done.parts_ref = f32[64,2,2,128]{3,2,1,0:T(2,128)S(1)} async-done(((f32[64,2,2,128]{3,2,1,0:T(2,128)}), f32[64,2,2,128]{3,2,1,0:T(2,128)S(1)}, u32[]{:S(2)}, u32[]{:S(2)}) %all-to-all-start) | async-done | bytes 131104 | tf_op jit(solution)/shard_map/all_to_all | solution.py:439
  34.2 0.0 copy-done
  34.2 0.0 copy-start.1
  34.3 0.0 copy-start.3
  34.3 0.4 norm.2.norm_ref
  34.6 3.0 %collective-permute-done.3.refs_3_ = bf16[8,72,256]{2,1,0:T(8,128)(2,1)S(1)} collective-permute-done((bf16[8,72,256]{2,1,0:T(8,128)(2,1)S(1)}, bf16[8,72,256]{2,1,0:T(8,128)(2,1)S(1)}, u32[]{:S(2)}, u32[]{:S(2)}) %collective-permute-start.3) | collective-permute-done | bytes 294944 | tf_op jit(solution)/shard_map/ppermute | solution.py:421
  37.6 0.0 collective-permute-done.4.refs_4_
  37.6 0.0 copy-done.1
  37.6 0.0 copy-done.3
  37.6 17.5 %conv2.1 = (bf16[8,32,32,256]{3,2,1,0:T(8,128)(2,1)}, f32[3,2,128]{2,1,0:T(2,128)S(1)}, bf16[8,4,32,256]{3,2,1,0:T(8,128)(2,1)S(1)}, bf16[8,4,32,256]{3,2,1,0:T(...) custom-call(s32[128]{0:T(128)S(1)} %copy-done, s32[2,8]{1,0:T(2,128)S(1)} %bitcast.8, ...), custom_call_target="tpu_custom_call" | custom-call | flops 9663676416 | bytes 10485760 | tf_op jit(solution)/shard_map/conv2/pallas_call | solution.py:380
  55.1 7.7 %collective-permute-start.6 = (bf16[8,4,32,256]{3,2,1,0:T(8,128)(2,1)S(1)}, bf16[8,4,32,256]{3,2,1,0:T(8,128)(2,1)S(1)}, u32[]{:S(2)}, u32[]{:S(2)}) collective-permute-start(bf16[8,4,32,256]{3,2,1,0:T(8,128)(2,1)S(1)} %get-tuple-element.23), channel_id=1, source_target_pairs={{0,32},{32,64},{64,96},{1,33},{33,65},{65,97},{2,34},{34,66},{66,9... | collective-permute-start | bytes 1572872 | tf_op jit(solution)/shard_map/ppermute | solution.py:407
  62.8 0.1 collective-permute-start.5
  62.9 2.4 %collective-permute-start.7 = (bf16[8,4,32,256]{3,2,1,0:T(8,128)(2,1)S(1)}, bf16[8,4,32,256]{3,2,1,0:T(8,128)(2,1)S(1)}, u32[]{:S(2)}, u32[]{:S(2)}) collective-permute-start(bf16[8,4,32,256]{3,2,1,0:T(8,128)(2,1)S(1)} %get-tuple-element.24), channel_id=1, source_target_pairs={{32,0},{64,32},{96,64},{33,1},{65,33},{97,65},{34,2},{66,34},{98,6... | collective-permute-start | bytes 1572872 | tf_op jit(solution)/shard_map/ppermute | solution.py:408
  65.3 0.0 collective-permute-done.5
  65.3 0.7 broadcast_in_dim.8
  66.0 7.7 %all-to-all-start.1 = ((f32[64,2,2,128]{3,2,1,0:T(2,128)}), f32[64,2,2,128]{3,2,1,0:T(2,128)S(1)}, u32[]{:S(2)}, u32[]{:S(2)}) async-start(f32[64,2,2,128]{3,2,1,0:T(2,128)} %broadcast_in_dim.8), calls=%async_computation.1 | async-start | bytes 262144 | tf_op jit(solution)/shard_map/all_to_all | solution.py:439
  73.7 0.0 collective-permute-done.6.refs_1_
  73.7 0.1 fusion.2
  73.8 1.1 collective-permute-done.7.refs_2_
  74.9 0.1 fusion.3
  75.0 0.9 pad_maximum_fusion
  75.9 0.1 collective-permute-start.8
  76.0 0.9 pad_maximum_fusion.1
  76.9 0.0 copy-start.2
  76.9 5.7 %collective-permute-start.9 = (bf16[8,160,256]{2,1,0:T(8,128)(2,1)}, bf16[8,160,256]{2,1,0:T(8,128)(2,1)S(1)}, u32[]{:S(2)}, u32[]{:S(2)}) collective-permute-start(bf16[8,160,256]{2,1,0:T(8,128)(2,1)} %pad_maximum_fusion.1), channel_id=1, source_target_pairs={{1,0},{2,1},{3,2},{4,3},{5,4},{6,5},{7,6},{8,7},{9,8},{10,9},{11,1... | collective-permute-start | bytes 1966088 | tf_op jit(solution)/shard_map/ppermute | solution.py:422
  82.6 0.1 all-to-all-done.1.parts_ref
  82.6 0.4 norm.3.norm_ref
  83.0 13.6 %collective-permute-done.8.refs_3_ = bf16[8,160,256]{2,1,0:T(8,128)(2,1)} collective-permute-done((bf16[8,160,256]{2,1,0:T(8,128)(2,1)}, bf16[8,160,256]{2,1,0:T(8,128)(2,1)}, u32[]{:S(2)}, u32[]{:S(2)}) %collective-permute-start.8) | collective-permute-done | bytes 655392 | tf_op jit(solution)/shard_map/ppermute | solution.py:421
  96.6 0.0 collective-permute-done.9.refs_4_
  96.6 0.0 copy-done.2
  96.6 16.6 %conv4.1 = bf16[8,32,32,256]{3,2,1,0:T(8,128)(2,1)} custom-call(s32[128]{0:T(128)S(1)} %copy-done, s32[2,8]{1,0:T(2,128)S(1)} %bitcast.9, f32[2,8,256]{2,1,0:T(8,128)S(1)} %norm.3.norm_ref, bf16[8,32,32,256]{3,2,1,0:T(8,128)(2,1)} %get-tuple-element.22.refs_0_, bf16[8,4,32,256]{3,2,1,0:T(8,128)(2,1)S(1)} %collective-permute-done.6.refs_1_, ...), custom_call_target="tpu_custom_call" | custom-call | flops 9663676416 | bytes 10485760 | tf_op jit(solution)/shard_map/conv4/pallas_call | solution.py:380
  (13 shorter events, 0.2 us)
Async XLA Ops:
  6.7 20.8 %copy-start.4 = (bf16[8,64,256]{2,1,0:T(8,128)(2,1)S(1)}, bf16[8,64,256]{2,1,0:T(8,128)(2,1)}, u32[]{:S(2)}) copy-start(bf16[8,64,256]{2,1,0:T(8,128)(2,1)} %get-tuple-element.20) | copy-start | bytes 786436
  6.7 27.5 %copy-start = (s32[128]{0:T(128)S(1)}, s32[128]{0:T(128)}, u32[]{:S(2)}) copy-start(s32[128]{0:T(128)} %points_ref.5) | copy-start | bytes 1540
  6.8 8.9 %collective-permute-start = (f32[3,2,128]{2,1,0:T(2,128)}, f32[3,2,128]{2,1,0:T(2,128)S(1)}, u32[]{:S(2)}, u32[]{:S(2)}) collective-permute-start(f32[3,2,128]{2,1,0:T(2,128)} %get-tuple-element.16), channel_id=1, source_target_pairs={{0,32},{32,0},{1,33},{33,1},{2,34},{34,2},{3,35},{35,3},{4,36},{36... | collective-permute-start | bytes 9224 | tf_op jit(solution)/shard_map/ppermute | solution.py:427
  8.3 17.0 %collective-permute-start.1 = (bf16[8,2,32,256]{3,2,1,0:T(8,128)(2,1)}, bf16[8,2,32,256]{3,2,1,0:T(8,128)(2,1)S(1)}, u32[]{:S(2)}, u32[]{:S(2)}) collective-permute-start(bf16[8,2,32,256]{3,2,1,0:T(8,128)(2,1)} %get-tuple-element.17), channel_id=1, source_target_pairs={{0,32},{32,64},{64,96},{1,33},{33,65},{65,97},{2,34},{34,66},{66,9... | collective-permute-start | bytes 786440 | tf_op jit(solution)/shard_map/ppermute | solution.py:407
  13.8 11.6 %collective-permute-start.2 = (bf16[8,2,32,256]{3,2,1,0:T(8,128)(2,1)}, bf16[8,2,32,256]{3,2,1,0:T(8,128)(2,1)S(1)}, u32[]{:S(2)}, u32[]{:S(2)}) collective-permute-start(bf16[8,2,32,256]{3,2,1,0:T(8,128)(2,1)} %get-tuple-element.18), channel_id=1, source_target_pairs={{32,0},{64,32},{96,64},{33,1},{65,33},{97,65},{34,2},{66,34},{98,6... | collective-permute-start | bytes 786440 | tf_op jit(solution)/shard_map/ppermute | solution.py:408
  17.1 17.2 %all-to-all-start = ((f32[64,2,2,128]{3,2,1,0:T(2,128)}), f32[64,2,2,128]{3,2,1,0:T(2,128)S(1)}, u32[]{:S(2)}, u32[]{:S(2)}) async-start(f32[64,2,2,128]{3,2,1,0:T(2,128)} %broadcast_in_dim.6), calls=%async_computation | async-start | bytes 262144 | tf_op jit(solution)/shard_map/all_to_all | solution.py:439
  26.5 11.2 %collective-permute-start.3 = (bf16[8,72,256]{2,1,0:T(8,128)(2,1)S(1)}, bf16[8,72,256]{2,1,0:T(8,128)(2,1)S(1)}, u32[]{:S(2)}, u32[]{:S(2)}) collective-permute-start(bf16[8,72,256]{2,1,0:T(8,128)(2,1)S(1)} %pad_maximum_fusion.2), channel_id=1, source_target_pairs={{0,1},{1,2},{2,3},{3,4},{4,5},{5,6},{6,7},{7,8},{8,9},{9,10},{10,1... | collective-permute-start | bytes 884744 | tf_op jit(solution)/shard_map/ppermute | solution.py:421
  27.6 10.0 %collective-permute-start.4 = (bf16[8,72,256]{2,1,0:T(8,128)(2,1)S(1)}, bf16[8,72,256]{2,1,0:T(8,128)(2,1)S(1)}, u32[]{:S(2)}, u32[]{:S(2)}) collective-permute-start(bf16[8,72,256]{2,1,0:T(8,128)(2,1)S(1)} %pad_maximum_fusion.3), channel_id=1, source_target_pairs={{1,0},{2,1},{3,2},{4,3},{5,4},{6,5},{7,6},{8,7},{9,8},{10,9},{11,1... | collective-permute-start | bytes 884744 | tf_op jit(solution)/shard_map/ppermute | solution.py:422
  34.2 3.4 %copy-start.1 = (bf16[3,3,256,256]{3,2,1,0:T(8,128)(2,1)S(1)}, bf16[3,3,256,256]{3,2,1,0:T(8,128)(2,1)}, u32[]{:S(2)}) copy-start(bf16[3,3,256,256]{3,2,1,0:T(8,128)(2,1)} %param.8) | copy-start | bytes 3538948
  34.3 3.4 %copy-start.3 = (s32[8,2]{0,1:T(2,128)S(1)}, s32[8,2]{0,1:T(2,128)}, u32[]{:S(2)}) copy-start(s32[8,2]{0,1:T(2,128)} %param.7) | copy-start | bytes 196
  55.1 18.6 %collective-permute-start.6 = (bf16[8,4,32,256]{3,2,1,0:T(8,128)(2,1)S(1)}, bf16[8,4,32,256]{3,2,1,0:T(8,128)(2,1)S(1)}, u32[]{:S(2)}, u32[]{:S(2)}) collective-permute-start(bf16[8,4,32,256]{3,2,1,0:T(8,128)(2,1)S(1)} %get-tuple-element.23), channel_id=1, source_target_pairs={{0,32},{32,64},{64,96},{1,33},{33,65},{65,97},{2,34},{34,66},{66,9... | collective-permute-start | bytes 1572872 | tf_op jit(solution)/shard_map/ppermute | solution.py:407
  62.8 2.5 %collective-permute-start.5 = (f32[3,2,128]{2,1,0:T(2,128)S(1)}, f32[3,2,128]{2,1,0:T(2,128)S(1)}, u32[]{:S(2)}, u32[]{:S(2)}) collective-permute-start(f32[3,2,128]{2,1,0:T(2,128)S(1)} %get-tuple-element.21), channel_id=1, source_target_pairs={{0,32},{32,0},{1,33},{33,1},{2,34},{34,2},{3,35},{35,3},{4,36},{36... | collective-permute-start | bytes 9224 | tf_op jit(solution)/shard_map/ppermute | solution.py:427
  62.9 12.0 %collective-permute-start.7 = (bf16[8,4,32,256]{3,2,1,0:T(8,128)(2,1)S(1)}, bf16[8,4,32,256]{3,2,1,0:T(8,128)(2,1)S(1)}, u32[]{:S(2)}, u32[]{:S(2)}) collective-permute-start(bf16[8,4,32,256]{3,2,1,0:T(8,128)(2,1)S(1)} %get-tuple-element.24), channel_id=1, source_target_pairs={{32,0},{64,32},{96,64},{33,1},{65,33},{97,65},{34,2},{66,34},{98,6... | collective-permute-start | bytes 1572872 | tf_op jit(solution)/shard_map/ppermute | solution.py:408
  66.0 16.6 %all-to-all-start.1 = ((f32[64,2,2,128]{3,2,1,0:T(2,128)}), f32[64,2,2,128]{3,2,1,0:T(2,128)S(1)}, u32[]{:S(2)}, u32[]{:S(2)}) async-start(f32[64,2,2,128]{3,2,1,0:T(2,128)} %broadcast_in_dim.8), calls=%async_computation.1 | async-start | bytes 262144 | tf_op jit(solution)/shard_map/all_to_all | solution.py:439
  75.9 20.7 %collective-permute-start.8 = (bf16[8,160,256]{2,1,0:T(8,128)(2,1)}, bf16[8,160,256]{2,1,0:T(8,128)(2,1)}, u32[]{:S(2)}, u32[]{:S(2)}) collective-permute-start(bf16[8,160,256]{2,1,0:T(8,128)(2,1)} %pad_maximum_fusion), channel_id=1, source_target_pairs={{0,1},{1,2},{2,3},{3,4},{4,5},{5,6},{6,7},{7,8},{8,9},{9,10},{10,1... | collective-permute-start | bytes 1966088 | tf_op jit(solution)/shard_map/ppermute | solution.py:421
  76.9 19.7 %copy-start.2 = (bf16[3,3,256,256]{3,2,1,0:T(8,128)(2,1)S(1)}, bf16[3,3,256,256]{3,2,1,0:T(8,128)(2,1)}, u32[]{:S(2)}) copy-start(bf16[3,3,256,256]{3,2,1,0:T(8,128)(2,1)} %param.9) | copy-start | bytes 3538948
  76.9 19.7 %collective-permute-start.9 = (bf16[8,160,256]{2,1,0:T(8,128)(2,1)}, bf16[8,160,256]{2,1,0:T(8,128)(2,1)S(1)}, u32[]{:S(2)}, u32[]{:S(2)}) collective-permute-start(bf16[8,160,256]{2,1,0:T(8,128)(2,1)} %pad_maximum_fusion.1), channel_id=1, source_target_pairs={{1,0},{2,1},{3,2},{4,3},{5,4},{6,5},{7,6},{8,7},{9,8},{10,9},{11,1... | collective-permute-start | bytes 1966088 | tf_op jit(solution)/shard_map/ppermute | solution.py:422

commit v7 on v6

--- a/solution.py
+++ b/solution.py
@@ -245,9 +245,13 @@
     )(parts, points[None])
 
 
-def conv_kernel(dilation, chunk, which, with_stats, points_ref, flags_ref, norm_ref, *refs):
+def conv_kernel(dilation, chunk, which, with_stats, ends, points_ref, flags_ref, norm_ref, *refs):
     d = dilation
-    x_hbm_ref, top_ref, bottom_ref, left_ref, right_ref, w_ref, out_hbm_ref, *rest = refs
+    x_hbm_ref, top_ref, bottom_ref, left_ref, right_ref, *refs = refs
+    left_end_ref = right_end_ref = None
+    if ends:
+        left_end_ref, right_end_ref, *refs = refs
+    w_ref, out_hbm_ref, *rest = refs
     if with_stats:
         stats_ref, *edges = rest[:5]
         x_ref, sems, out_ref, out_sems, even_ref, odd_ref, sums_ref, squares_ref, kept_ref = rest[5:]
@@ -266,6 +270,17 @@
     before_origin = (origin + lon_total - d) % lon_total
     after_origin = (origin + cols) % lon_total
 
+    def beside(side_ref, end_ref, b, lo, hi):
+        if end_ref is None:
+            return side_ref[b, lo * d : hi * d]
+        above, below = min(hi, d), max(lo, rows + d)
+        pieces = [
+            end_ref[b, lo * d : above * d] if lo < above else None,
+            side_ref[b, (max(lo, d) - d) * d : (min(hi, rows + d) - d) * d],
+            end_ref[b, (below - rows) * d : (hi - rows) * d] if below < hi else None,
+        ]
+        return jnp.concatenate([p.astype(jnp.float32) for p in pieces if p is not None], axis=0)
+
     def activate_rows(b, act_ref, lo, hi):
         mean = norm_ref[0, pl.ds(b, 1)]
         half = norm_ref[1, pl.ds(b, 1)]
@@ -274,8 +289,8 @@
             t = (value.astype(jnp.float32) - mean) * half
             return t + t * jnp.tanh(t)
 
-        left = activated(left_ref[b, lo * d : hi * d])
-        right = activated(right_ref[b, lo * d : hi * d])
+        left = activated(beside(left_ref, left_end_ref, b, lo, hi))
+        right = activated(beside(right_ref, right_end_ref, b, lo, hi))
         for e in range(lo, hi):
             if e < d:
                 row = top_ref[b, e]
@@ -378,7 +393,7 @@
         scratch += [pltpu.VMEM((samples, channels), jnp.float32)] * 2
         scratch += [pltpu.VMEM((rows, width, channels), jnp.bfloat16)]
     return pl.pallas_call(
-        functools.partial(conv_kernel, d, CHUNK, which, with_stats),
+        functools.partial(conv_kernel, d, CHUNK, which, with_stats, len(halos) > 4),
         out_shape=out_shape,
         grid_spec=pltpu.PrefetchScalarGridSpec(
             num_scalar_prefetch=2,
@@ -433,6 +448,32 @@
     return jnp.broadcast_to(merged[None], (lax.axis_size(CHIPS), *merged.shape))
 
 
+def exchange_apart(edges):
+    lon = lax.axis_size(LON)
+    east = [(i, (i + 1) % lon) for i in range(lon)]
+    west = [((i + 1) % lon, i) for i in range(lon)]
+    top, bottom = exchange_rows(edges)
+    left = lax.ppermute(edges[3], LON, east)
+    right = lax.ppermute(edges[2], LON, west)
+    top, bottom, left, right = lax.optimization_barrier((top, bottom, left, right))
+    samples, d, width, channels = top.shape
+
+    def packed(lo, hi):
+        above = top[:, :, lo:hi].reshape(samples, d * d, channels)
+        below = bottom[:, :, lo:hi].reshape(samples, d * d, channels)
+        return jnp.concatenate([above, below], axis=1)
+
+    left_end = lax.ppermute(packed(width - d, width), LON, east)
+    right_end = lax.ppermute(packed(0, d), LON, west)
+    return top, bottom, left, right, left_end, right_end
+
+
+def exchange_late(local, edges, points, x):
+    mine = merge_cores(local)
+    norm = combine_statistics(lax.all_to_all(mine, CHIPS, 0, 0), points, x)
+    return norm, exchange_apart(edges)
+
+
 def exchange(local, edges, points, x):
     mine = merge_cores(local)
     top, bottom = exchange_rows(edges)
@@ -450,7 +491,7 @@
     first, local, *edges = convolve(
         features, halos, first_weight, norm, band_points, flags, FIRST_DILATION, 0, True
     )
-    norm, halos = exchange(local, edges, band_points, first)
+    norm, halos = exchange_late(local, edges, band_points, first)
     (section,) = convolve(
         first, halos, second_weight, norm, band_points, flags, SECOND_DILATION, 1, False
     )

time: 114 us -> 120 us (1.053)
  starting transfers between devices: 46.5 us -> 52 us
    ppermute x2 -> x1, waiting for transfers between devices: 16.6 us -> 2.99 us  [exchange_columns(): lax.ppermute(packed(edges[3], width - d, width), LON, [(i, (i + 1) % lon)...]
    ppermute x0 -> x4, starting transfers between devices: none -> 12.3 us  [the longest x1 6.35 us: exchange_apart(): right_end = lax.ppermute(packed(0, d), LON, west)]
    ppermute x0 -> x4, waiting for transfers between devices: none -> 7.98 us  [the longest x1 6.76 us: exchange_apart(): left_end = lax.ppermute(packed(width - d, width), LON, east)]
    all_to_all x2 -> x1, starting transfers between devices: 15.8 us -> 8.14 us  [exchange(): norm = combine_statistics(lax.all_to_all(mine, CHIPS, 0, 0), points, x)]
    all_to_all x0 -> x1, starting transfers between devices: none -> 6.67 us  [exchange_late(): norm = combine_statistics(lax.all_to_all(mine, CHIPS, 0, 0), points, x)]
    ppermute x2 -> x1, starting transfers between devices: 10.4 us -> 4.74 us  [exchange_columns(): lax.ppermute(packed(edges[2], 0, d), LON, [((i + 1) % lon, i) for i in ra...]
    ppermute x2, waiting for transfers between devices: 1.07 us -> 4.37 us  [exchange_rows(): bottom = lax.ppermute(edges[0], LAT, [(i + 1, i) for i in range(lat - 1)])]
    concatenate x0 -> x2, other arithmetic: none -> 1.33 us  [packed(): return jnp.concatenate([above, below], axis=1)]
  transfers between devices with their start and end apart: 12 -> 14, of which waited for: 5 -> 7; matrix products, arithmetic and copies ran while one was open for 5% -> 5% of each run, Pallas kernels for 1% -> 1%
where the time goes in v7:
time: 120 us; the launch traced here: 119 us
  starting transfers between devices  52 us (43%)
  Pallas kernels  42.3 us (35%)
  waiting for transfers between devices  18.7 us (16%)
  other arithmetic  4.12 us (3%)
  local copies, waits for them, and re-layouts  1.72 us (1%)
    pallas_call x2, Pallas kernels, convolve(): pl.pallas_call(functools.partial(conv_kernel, d, CHUNK, which, with_stats...  34.7 us
    ppermute x2, starting transfers between devices, exchange_rows(): top = lax.ppermute(edges[1], LAT, [(i, i + 1) for i in range(lat - 1)])  13.7 us
    all_to_all x1, starting transfers between devices, exchange(): norm = combine_statistics(lax.all_to_all(mine, CHIPS, 0, 0), points, x)  8.14 us
    pallas_call x1, Pallas kernels, local_statistics(): pl.pallas_call(stats_kernel, out_shape=[jax.ShapeDtypeStruct(shape, jnp.f...  6.86 us
    ppermute x1, waiting for transfers between devices, exchange_apart(): left_end = lax.ppermute(packed(width - d, width), LON, east)  6.76 us
    all_to_all x1, starting transfers between devices, exchange_late(): norm = combine_statistics(lax.all_to_all(mine, CHIPS, 0, 0), points, x)  6.67 us
    ppermute x1, starting transfers between devices, exchange_apart(): right_end = lax.ppermute(packed(0, d), LON, west)  6.35 us
    ppermute x1, starting transfers between devices, exchange_apart(): right = lax.ppermute(edges[2], LON, west)  5.88 us
  transfers between devices with their start and end apart: 14, of which 7 were waited for; matrix products, arithmetic and copies ran while one was open for 5% of the time, Pallas kernels for 1%

profile of v7, /device:TPU:1, one launch (start us, length us, event | category | flops | bytes accessed | tf_op | source)
XLA Modules:
  0.0 119.1 jit_solution(1256240021522027625)
XLA Ops:
  0.0 0.0 copy-start
  0.0 6.9 %stats.1 = (f32[3,2,128]{2,1,0:T(2,128)}, bf16[8,2,32,256]{3,2,1,0:T(8,128)(2,1)}, bf16[8,2,32,256]{3,2,1,0:T(8,128)(2,1)}, bf16[8,64,256]{2,1,0:T(8,128)(2,1)}, bf16[8,64,256]{2,1,0:T(8,128)(2,1)}) custom-call(s32[128]{0:T(128)} %points_ref.5, bf16[8,32,32,256]{3,2,1,0:T(8,128)(2,1)} %refs_0_.1), custom_call_target="tpu_custom_call" | custom-call | flops 16777216 | bytes 4194304 | tf_op jit(solution)/shard_map/stats/pallas_call | solution.py:173
  6.9 1.5 %collective-permute-start = (f32[3,2,128]{2,1,0:T(2,128)}, f32[3,2,128]{2,1,0:T(2,128)S(1)}, u32[]{:S(2)}, u32[]{:S(2)}) collective-permute-start(f32[3,2,128]{2,1,0:T(2,128)} %get-tuple-element.20), channel_id=1, source_target_pairs={{0,32},{32,0},{1,33},{33,1},{2,34},{34,2},{3,35},{35,3},{4,36},{36... | collective-permute-start | bytes 9224 | tf_op jit(solution)/shard_map/ppermute | solution.py:442
  8.4 5.5 %collective-permute-start.1 = (bf16[8,2,32,256]{3,2,1,0:T(8,128)(2,1)}, bf16[8,2,32,256]{3,2,1,0:T(8,128)(2,1)S(1)}, u32[]{:S(2)}, u32[]{:S(2)}) collective-permute-start(bf16[8,2,32,256]{3,2,1,0:T(8,128)(2,1)} %get-tuple-element.21), channel_id=1, source_target_pairs={{0,32},{32,64},{64,96},{1,33},{33,65},{65,97},{2,34},{34,66},{66,9... | collective-permute-start | bytes 786440 | tf_op jit(solution)/shard_map/ppermute | solution.py:422
  13.9 1.9 %collective-permute-start.2 = (bf16[8,2,32,256]{3,2,1,0:T(8,128)(2,1)}, bf16[8,2,32,256]{3,2,1,0:T(8,128)(2,1)S(1)}, u32[]{:S(2)}, u32[]{:S(2)}) collective-permute-start(bf16[8,2,32,256]{3,2,1,0:T(8,128)(2,1)} %get-tuple-element.22), channel_id=1, source_target_pairs={{32,0},{64,32},{96,64},{33,1},{65,33},{97,65},{34,2},{66,34},{98,6... | collective-permute-start | bytes 786440 | tf_op jit(solution)/shard_map/ppermute | solution.py:423
  15.8 0.0 collective-permute-done
  15.8 0.7 slice_add_fusion.3
  16.5 0.7 broadcast_in_dim.6
  17.2 8.1 %all-to-all-start = ((f32[64,2,2,128]{3,2,1,0:T(2,128)}), f32[64,2,2,128]{3,2,1,0:T(2,128)S(1)}, u32[]{:S(2)}, u32[]{:S(2)}) async-start(f32[64,2,2,128]{3,2,1,0:T(2,128)} %broadcast_in_dim.6), calls=%async_computation | async-start | bytes 262144 | tf_op jit(solution)/shard_map/all_to_all | solution.py:480
  25.3 0.0 collective-permute-done.1.refs_1_
  25.4 0.0 collective-permute-done.2.refs_2_
  25.5 1.0 pad_maximum_fusion
  26.6 1.1 collective-permute-start.3
  27.7 1.0 pad_maximum_fusion.1
  28.7 4.7 %collective-permute-start.4 = (bf16[8,72,256]{2,1,0:T(8,128)(2,1)S(1)}, bf16[8,72,256]{2,1,0:T(8,128)(2,1)S(1)}, u32[]{:S(2)}, u32[]{:S(2)}) collective-permute-start(bf16[8,72,256]{2,1,0:T(8,128)(2,1)S(1)} %pad_maximum_fusion.1), channel_id=1, source_target_pairs={{1,0},{2,1},{3,2},{4,3},{5,4},{6,5},{7,6},{8,7},{9,8},{10,9},{11,1... | collective-permute-start | bytes 884744 | tf_op jit(solution)/shard_map/ppermute | solution.py:437
  33.4 0.9 all-to-all-done.parts_ref
  34.4 0.0 copy-done
  34.4 0.0 copy-start.1
  34.4 0.0 copy-start.3
  34.4 0.4 norm.2.norm_ref
  34.8 3.0 %collective-permute-done.3.refs_3_ = bf16[8,72,256]{2,1,0:T(8,128)(2,1)S(1)} collective-permute-done((bf16[8,72,256]{2,1,0:T(8,128)(2,1)S(1)}, bf16[8,72,256]{2,1,0:T(8,128)(2,1)S(1)}, u32[]{:S(2)}, u32[]{:S(2)}) %collective-permute-start.3) | collective-permute-done | bytes 294944 | tf_op jit(solution)/shard_map/ppermute | solution.py:436
  37.7 0.0 collective-permute-done.4.refs_4_
  37.7 0.0 copy-done.1
  37.7 0.0 copy-done.3
  37.7 18.2 %conv2.1 = (bf16[8,32,32,256]{3,2,1,0:T(8,128)(2,1)}, f32[3,2,128]{2,1,0:T(2,128)S(1)}, bf16[8,4,32,256]{3,2,1,0:T(8,128)(2,1)}, bf16[8,4,32,256]{3,2,1,0:T(8,12...) custom-call(s32[128]{0:T(128)S(1)} %copy-done, s32[2,8]{1,0:T(2,128)S(1)} %bitcast.8, ...), custom_call_target="tpu_custom_call" | custom-call | flops 9663676416 | bytes 10485760 | tf_op jit(solution)/shard_map/conv2/pallas_call | solution.py:395
  56.0 8.2 %collective-permute-start.6 = (bf16[8,4,32,256]{3,2,1,0:T(8,128)(2,1)}, bf16[8,4,32,256]{3,2,1,0:T(8,128)(2,1)S(1)}, u32[]{:S(2)}, u32[]{:S(2)}) collective-permute-start(bf16[8,4,32,256]{3,2,1,0:T(8,128)(2,1)} %get-tuple-element.27), channel_id=1, source_target_pairs={{0,32},{32,64},{64,96},{1,33},{33,65},{65,97},{2,34},{34,66},{66,9... | collective-permute-start | bytes 1572872 | tf_op jit(solution)/shard_map/ppermute | solution.py:422
  64.2 1.9 %collective-permute-start.7 = (bf16[8,4,32,256]{3,2,1,0:T(8,128)(2,1)}, bf16[8,4,32,256]{3,2,1,0:T(8,128)(2,1)S(1)}, u32[]{:S(2)}, u32[]{:S(2)}) collective-permute-start(bf16[8,4,32,256]{3,2,1,0:T(8,128)(2,1)} %get-tuple-element.28), channel_id=1, source_target_pairs={{32,0},{64,32},{96,64},{33,1},{65,33},{97,65},{34,2},{66,34},{98,6... | collective-permute-start | bytes 1572872 | tf_op jit(solution)/shard_map/ppermute | solution.py:423
  66.1 0.1 collective-permute-start.8
  66.2 5.9 %collective-permute-start.9 = (bf16[8,128,256]{2,1,0:T(8,128)(2,1)S(1)}, bf16[8,128,256]{2,1,0:T(8,128)(2,1)S(1)}, u32[]{:S(2)}, u32[]{:S(2)}) collective-permute-start(bf16[8,128,256]{2,1,0:T(8,128)(2,1)S(1)} %get-tuple-element.30), channel_id=1, source_target_pairs={{1,0},{2,1},{3,2},{4,3},{5,4},{6,5},{7,6},{8,7},{9,8},{10,9},{11,1... | collective-permute-start | bytes 1572872 | tf_op jit(solution)/shard_map/ppermute | solution.py:457
  72.1 0.0 collective-permute-start.5
  72.1 1.2 collective-permute-done.5
  73.3 0.7 broadcast_in_dim.8
  74.0 6.7 %all-to-all-start.1 = ((f32[64,2,2,128]{3,2,1,0:T(2,128)}), f32[64,2,2,128]{3,2,1,0:T(2,128)S(1)}, u32[]{:S(2)}, u32[]{:S(2)}) async-start(f32[64,2,2,128]{3,2,1,0:T(2,128)} %broadcast_in_dim.8), calls=%async_computation.1 | async-start | bytes 262144 | tf_op jit(solution)/shard_map/all_to_all | solution.py:473
  80.7 1.2 %collective-permute-done.6.refs_1_ = bf16[8,4,32,256]{3,2,1,0:T(8,128)(2,1)S(1)} collective-permute-done((bf16[8,4,32,256]{3,2,1,0:T(8,128)(2,1)}, bf16[8,4,32,256]{3,2,1,0:T(8,128)(2,1)S(1)}, u32[]{:S(2)}, u32[]{:S(2)}) %collective-permute-start.6) | collective-permute-done | bytes 524320 | tf_op jit(solution)/shard_map/ppermute | solution.py:422
  81.9 4.4 %collective-permute-done.7.refs_2_ = bf16[8,4,32,256]{3,2,1,0:T(8,128)(2,1)S(1)} collective-permute-done((bf16[8,4,32,256]{3,2,1,0:T(8,128)(2,1)}, bf16[8,4,32,256]{3,2,1,0:T(8,128)(2,1)S(1)}, u32[]{:S(2)}, u32[]{:S(2)}) %collective-permute-start.7) | collective-permute-done | bytes 524320 | tf_op jit(solution)/shard_map/ppermute | solution.py:423
  86.2 0.0 collective-permute-done.8.refs_3_
  86.2 0.0 collective-permute-done.9.refs_4_
  86.2 0.1 fusion.2
  86.4 0.7 pad_maximum_fusion.3
  87.1 6.3 %collective-permute-start.11 = (bf16[8,32,256]{2,1,0:T(8,128)(2,1)}, bf16[8,32,256]{2,1,0:T(8,128)(2,1)S(1)}, u32[]{:S(2)}, u32[]{:S(2)}) collective-permute-start(bf16[8,32,256]{2,1,0:T(8,128)(2,1)} %pad_maximum_fusion.3), channel_id=1, source_target_pairs={{1,0},{2,1},{3,2},{4,3},{5,4},{6,5},{7,6},{8,7},{9,8},{10,9},{11,1... | collective-permute-start | bytes 393224 | tf_op jit(solution)/shard_map/ppermute | solution.py:467
  93.5 0.7 pad_maximum_fusion.2
  94.1 0.0 copy-start.2
  94.1 0.0 collective-permute-start.10
  94.1 0.0 all-to-all-done.1.parts_ref
  94.1 0.4 norm.3.norm_ref
  94.5 1.2 %collective-permute-done.11.refs_6_ = bf16[8,32,256]{2,1,0:T(8,128)(2,1)S(1)} collective-permute-done((bf16[8,32,256]{2,1,0:T(8,128)(2,1)}, bf16[8,32,256]{2,1,0:T(8,128)(2,1)S(1)}, u32[]{:S(2)}, u32[]{:S(2)}) %collective-permute-start.11) | collective-permute-done | bytes 131104 | tf_op jit(solution)/shard_map/ppermute | solution.py:467
  95.7 6.8 %collective-permute-done.10.refs_5_ = bf16[8,32,256]{2,1,0:T(8,128)(2,1)} collective-permute-done((bf16[8,32,256]{2,1,0:T(8,128)(2,1)}, bf16[8,32,256]{2,1,0:T(8,128)(2,1)}, u32[]{:S(2)}, u32[]{:S(2)}) %collective-permute-start.10) | collective-permute-done | bytes 131104 | tf_op jit(solution)/shard_map/ppermute | solution.py:466
  102.5 0.0 copy-done.2
  102.5 16.5 %conv4.1 = bf16[8,32,32,256]{3,2,1,0:T(8,128)(2,1)} custom-call(s32[128]{0:T(128)S(1)} %copy-done, s32[2,8]{1,0:T(2,128)S(1)} %bitcast.9, f32[2,8,256]{2,1,0:T(8,128)S(1)} %norm.3.norm_ref, bf16[8,32,32,256]{3,2,1,0:T(8,128)(2,1)} %get-tuple-element.26.refs_0_, bf16[8,4,32,256]{3,2,1,0:T(8,128)(2,1)S(1)} %collective-permute-done.6.refs_1_, ...), custom_call_target="tpu_custom_call" | custom-call | flops 9663676416 | bytes 10485760 | tf_op jit(solution)/shard_map/conv4/pallas_call | solution.py:395
  (13 shorter events, 0.2 us)
Async XLA Ops:
  0.0 34.4 %copy-start = (s32[128]{0:T(128)S(1)}, s32[128]{0:T(128)}, u32[]{:S(2)}) copy-start(s32[128]{0:T(128)} %points_ref.5) | copy-start | bytes 1540
  6.9 8.9 %collective-permute-start = (f32[3,2,128]{2,1,0:T(2,128)}, f32[3,2,128]{2,1,0:T(2,128)S(1)}, u32[]{:S(2)}, u32[]{:S(2)}) collective-permute-start(f32[3,2,128]{2,1,0:T(2,128)} %get-tuple-element.20), channel_id=1, source_target_pairs={{0,32},{32,0},{1,33},{33,1},{2,34},{34,2},{3,35},{35,3},{4,36},{36... | collective-permute-start | bytes 9224 | tf_op jit(solution)/shard_map/ppermute | solution.py:442
  8.4 17.0 %collective-permute-start.1 = (bf16[8,2,32,256]{3,2,1,0:T(8,128)(2,1)}, bf16[8,2,32,256]{3,2,1,0:T(8,128)(2,1)S(1)}, u32[]{:S(2)}, u32[]{:S(2)}) collective-permute-start(bf16[8,2,32,256]{3,2,1,0:T(8,128)(2,1)} %get-tuple-element.21), channel_id=1, source_target_pairs={{0,32},{32,64},{64,96},{1,33},{33,65},{65,97},{2,34},{34,66},{66,9... | collective-permute-start | bytes 786440 | tf_op jit(solution)/shard_map/ppermute | solution.py:422
  13.9 11.6 %collective-permute-start.2 = (bf16[8,2,32,256]{3,2,1,0:T(8,128)(2,1)}, bf16[8,2,32,256]{3,2,1,0:T(8,128)(2,1)S(1)}, u32[]{:S(2)}, u32[]{:S(2)}) collective-permute-start(bf16[8,2,32,256]{3,2,1,0:T(8,128)(2,1)} %get-tuple-element.22), channel_id=1, source_target_pairs={{32,0},{64,32},{96,64},{33,1},{65,33},{97,65},{34,2},{66,34},{98,6... | collective-permute-start | bytes 786440 | tf_op jit(solution)/shard_map/ppermute | solution.py:423
  17.2 17.2 %all-to-all-start = ((f32[64,2,2,128]{3,2,1,0:T(2,128)}), f32[64,2,2,128]{3,2,1,0:T(2,128)S(1)}, u32[]{:S(2)}, u32[]{:S(2)}) async-start(f32[64,2,2,128]{3,2,1,0:T(2,128)} %broadcast_in_dim.6), calls=%async_computation | async-start | bytes 262144 | tf_op jit(solution)/shard_map/all_to_all | solution.py:480
  26.6 11.2 %collective-permute-start.3 = (bf16[8,72,256]{2,1,0:T(8,128)(2,1)S(1)}, bf16[8,72,256]{2,1,0:T(8,128)(2,1)S(1)}, u32[]{:S(2)}, u32[]{:S(2)}) collective-permute-start(bf16[8,72,256]{2,1,0:T(8,128)(2,1)S(1)} %pad_maximum_fusion), channel_id=1, source_target_pairs={{0,1},{1,2},{2,3},{3,4},{4,5},{5,6},{6,7},{7,8},{8,9},{9,10},{10,1... | collective-permute-start | bytes 884744 | tf_op jit(solution)/shard_map/ppermute | solution.py:436
  28.7 9.0 %collective-permute-start.4 = (bf16[8,72,256]{2,1,0:T(8,128)(2,1)S(1)}, bf16[8,72,256]{2,1,0:T(8,128)(2,1)S(1)}, u32[]{:S(2)}, u32[]{:S(2)}) collective-permute-start(bf16[8,72,256]{2,1,0:T(8,128)(2,1)S(1)} %pad_maximum_fusion.1), channel_id=1, source_target_pairs={{1,0},{2,1},{3,2},{4,3},{5,4},{6,5},{7,6},{8,7},{9,8},{10,9},{11,1... | collective-permute-start | bytes 884744 | tf_op jit(solution)/shard_map/ppermute | solution.py:437
  34.4 3.4 %copy-start.1 = (bf16[3,3,256,256]{3,2,1,0:T(8,128)(2,1)S(1)}, bf16[3,3,256,256]{3,2,1,0:T(8,128)(2,1)}, u32[]{:S(2)}) copy-start(bf16[3,3,256,256]{3,2,1,0:T(8,128)(2,1)} %param.8) | copy-start | bytes 3538948
  34.4 3.4 %copy-start.3 = (s32[8,2]{0,1:T(2,128)S(1)}, s32[8,2]{0,1:T(2,128)}, u32[]{:S(2)}) copy-start(s32[8,2]{0,1:T(2,128)} %param.7) | copy-start | bytes 196
  56.0 25.9 %collective-permute-start.6 = (bf16[8,4,32,256]{3,2,1,0:T(8,128)(2,1)}, bf16[8,4,32,256]{3,2,1,0:T(8,128)(2,1)S(1)}, u32[]{:S(2)}, u32[]{:S(2)}) collective-permute-start(bf16[8,4,32,256]{3,2,1,0:T(8,128)(2,1)} %get-tuple-element.27), channel_id=1, source_target_pairs={{0,32},{32,64},{64,96},{1,33},{33,65},{65,97},{2,34},{34,66},{66,9... | collective-permute-start | bytes 1572872 | tf_op jit(solution)/shard_map/ppermute | solution.py:422
  64.2 22.0 %collective-permute-start.7 = (bf16[8,4,32,256]{3,2,1,0:T(8,128)(2,1)}, bf16[8,4,32,256]{3,2,1,0:T(8,128)(2,1)S(1)}, u32[]{:S(2)}, u32[]{:S(2)}) collective-permute-start(bf16[8,4,32,256]{3,2,1,0:T(8,128)(2,1)} %get-tuple-element.28), channel_id=1, source_target_pairs={{32,0},{64,32},{96,64},{33,1},{65,33},{97,65},{34,2},{66,34},{98,6... | collective-permute-start | bytes 1572872 | tf_op jit(solution)/shard_map/ppermute | solution.py:423
  66.1 20.1 %collective-permute-start.8 = (bf16[8,128,256]{2,1,0:T(8,128)(2,1)S(1)}, bf16[8,128,256]{2,1,0:T(8,128)(2,1)S(1)}, u32[]{:S(2)}, u32[]{:S(2)}) collective-permute-start(bf16[8,128,256]{2,1,0:T(8,128)(2,1)S(1)} %get-tuple-element.29), channel_id=1, source_target_pairs={{0,1},{1,2},{2,3},{3,4},{4,5},{5,6},{6,7},{7,8},{8,9},{9,10},{10,1... | collective-permute-start | bytes 1572872 | tf_op jit(solution)/shard_map/ppermute | solution.py:456
  66.2 20.0 %collective-permute-start.9 = (bf16[8,128,256]{2,1,0:T(8,128)(2,1)S(1)}, bf16[8,128,256]{2,1,0:T(8,128)(2,1)S(1)}, u32[]{:S(2)}, u32[]{:S(2)}) collective-permute-start(bf16[8,128,256]{2,1,0:T(8,128)(2,1)S(1)} %get-tuple-element.30), channel_id=1, source_target_pairs={{1,0},{2,1},{3,2},{4,3},{5,4},{6,5},{7,6},{8,7},{9,8},{10,9},{11,1... | collective-permute-start | bytes 1572872 | tf_op jit(solution)/shard_map/ppermute | solution.py:457
  72.1 1.2 collective-permute-start.5
  74.0 20.2 %all-to-all-start.1 = ((f32[64,2,2,128]{3,2,1,0:T(2,128)}), f32[64,2,2,128]{3,2,1,0:T(2,128)S(1)}, u32[]{:S(2)}, u32[]{:S(2)}) async-start(f32[64,2,2,128]{3,2,1,0:T(2,128)} %broadcast_in_dim.8), calls=%async_computation.1 | async-start | bytes 262144 | tf_op jit(solution)/shard_map/all_to_all | solution.py:473
  87.1 8.6 %collective-permute-start.11 = (bf16[8,32,256]{2,1,0:T(8,128)(2,1)}, bf16[8,32,256]{2,1,0:T(8,128)(2,1)S(1)}, u32[]{:S(2)}, u32[]{:S(2)}) collective-permute-start(bf16[8,32,256]{2,1,0:T(8,128)(2,1)} %pad_maximum_fusion.3), channel_id=1, source_target_pairs={{1,0},{2,1},{3,2},{4,3},{5,4},{6,5},{7,6},{8,7},{9,8},{10,9},{11,1... | collective-permute-start | bytes 393224 | tf_op jit(solution)/shard_map/ppermute | solution.py:467
  94.1 8.4 %copy-start.2 = (bf16[3,3,256,256]{3,2,1,0:T(8,128)(2,1)S(1)}, bf16[3,3,256,256]{3,2,1,0:T(8,128)(2,1)}, u32[]{:S(2)}) copy-start(bf16[3,3,256,256]{3,2,1,0:T(8,128)(2,1)} %param.9) | copy-start | bytes 3538948
  94.1 8.4 %collective-permute-start.10 = (bf16[8,32,256]{2,1,0:T(8,128)(2,1)}, bf16[8,32,256]{2,1,0:T(8,128)(2,1)}, u32[]{:S(2)}, u32[]{:S(2)}) collective-permute-start(bf16[8,32,256]{2,1,0:T(8,128)(2,1)} %pad_maximum_fusion.2), channel_id=1, source_target_pairs={{0,1},{1,2},{2,3},{3,4},{4,5},{5,6},{6,7},{7,8},{8,9},{9,10},{10,1... | collective-permute-start | bytes 393224 | tf_op jit(solution)/shard_map/ppermute | solution.py:466

commit v8 on v6

--- a/solution.py
+++ b/solution.py
@@ -19,7 +19,6 @@
 LANES = 128
 VMEM_LIMIT = 52_000_000
 CHUNK = 8
-NORM_FLOPS = 10 * 10**9
 
 
 def exact_dot(a, selection):
@@ -232,7 +231,7 @@
     norm_ref[1] = both[samples:]
 
 
-def combine_statistics(parts, points, x):
+def combine_statistics(parts, points, x, flops):
     samples, rows, cols, channels = x.shape
     return pl.pallas_call(
         functools.partial(combine_kernel, rows, cols),
@@ -240,7 +239,7 @@
         in_specs=[in_vmem(), in_vmem()],
         out_specs=in_vmem(),
         compiler_params=pltpu.CompilerParams(vmem_limit_bytes=4_000_000),
-        cost_estimate=pl.CostEstimate(flops=NORM_FLOPS, bytes_accessed=parts.size * 4, transcendentals=0),
+        cost_estimate=pl.CostEstimate(flops=flops, bytes_accessed=parts.size * 4, transcendentals=0),
         name="norm",
     )(parts, points[None])
 
@@ -433,11 +432,19 @@
     return jnp.broadcast_to(merged[None], (lax.axis_size(CHIPS), *merged.shape))
 
 
-def exchange(local, edges, points, x):
+def exchange_first(local, edges, points, x):
     mine = merge_cores(local)
     top, bottom = exchange_rows(edges)
-    norm = combine_statistics(lax.all_to_all(mine, CHIPS, 0, 0), points, x)
+    norm = combine_statistics(lax.all_to_all(mine, CHIPS, 0, 0), points, x, 10**10)
     return norm, (top, bottom, *exchange_columns(edges, top, bottom))
+
+
+def exchange_second(local, edges, points, x):
+    mine = merge_cores(local)
+    mine, top, bottom = lax.optimization_barrier((mine, *exchange_rows(edges)))
+    columns = exchange_columns(edges, top, bottom)
+    norm = combine_statistics(lax.all_to_all(mine, CHIPS, 0, 0), points, x, 10**9)
+    return norm, (top, bottom, *columns)
 
 
 def per_device(features, band_points, survival_flags, first_kernel_weight, second_kernel_weight):
@@ -446,11 +453,11 @@
     first_weight = first_kernel_weight.reshape(3, 3 * channels, channels)
     second_weight = second_kernel_weight.reshape(3, 3 * channels, channels)
     local, *edges = local_statistics(features, band_points)
-    norm, halos = exchange(local, edges, band_points, features)
+    norm, halos = exchange_first(local, edges, band_points, features)
     first, local, *edges = convolve(
         features, halos, first_weight, norm, band_points, flags, FIRST_DILATION, 0, True
     )
-    norm, halos = exchange(local, edges, band_points, first)
+    norm, halos = exchange_second(local, edges, band_points, first)
     (section,) = convolve(
         first, halos, second_weight, norm, band_points, flags, SECOND_DILATION, 1, False
     )

time: 114 us -> 129 us (1.13)
  blocking collectives: 0 us -> 16.5 us
  starting transfers between devices: 46.5 us -> 52.1 us
  waiting for transfers between devices: 19.6 us -> 14.9 us
  other arithmetic: 3.65 us -> 1.93 us
    all_to_all x0 -> x1, blocking collectives: none -> 16.5 us  [exchange_second(): lax.all_to_all(mine, CHIPS, 0, 0)]
    ppermute x2, starting transfers between devices: 10.4 us -> 24.2 us  [exchange_columns(): lax.ppermute(packed(edges[2], 0, d), LON, [((i + 1) % lon, i) for i in ra...]
    ppermute x2, waiting for transfers between devices: 16.6 us -> 3.02 us  [exchange_columns(): lax.ppermute(packed(edges[3], width - d, width), LON, [(i, (i + 1) % lon)...]
    all_to_all x2 -> x1, starting transfers between devices: 15.8 us -> 8.14 us  [exchange_first(): lax.all_to_all(mine, CHIPS, 0, 0)]
    ppermute x2, waiting for transfers between devices: 1.07 us -> 5.9 us  [exchange_rows(): bottom = lax.ppermute(edges[0], LAT, [(i + 1, i) for i in range(lat - 1)])]
    ppermute x2, waiting for transfers between devices: 0.01 us -> 2.63 us  [exchange_rows(): top = lax.ppermute(edges[1], LAT, [(i, i + 1) for i in range(lat - 1)])]
    concatenate x4, other arithmetic: 2.93 us -> 1.22 us  [packed(): return jnp.concatenate([above, cols, below], axis=1)]
    ppermute x2, waiting for transfers between devices: 0.01 us -> 1.43 us  [merge_cores(): other = lax.ppermute(local, 'core', [(0, 1), (1, 0)])]
  transfers between devices with their start and end apart: 12 -> 11, of which waited for: 5 -> 5; matrix products, arithmetic and copies ran while one was open for 5% -> 2% of each run, Pallas kernels for 1% -> 1%
where the time goes in v8:
time: 129 us; the launch traced here: 128 us
  starting transfers between devices  52.1 us (40%)
  Pallas kernels  40.7 us (32%)
  blocking collectives  16.5 us (13%)
  waiting for transfers between devices  14.9 us (12%)
  local copies, waits for them, and re-layouts  1.94 us (2%)
  other arithmetic  1.93 us (1%)
    pallas_call x2, Pallas kernels, convolve(): pl.pallas_call(functools.partial(conv_kernel, d, CHUNK, which, with_stats...  33.2 us
    ppermute x2, starting transfers between devices, exchange_columns(): lax.ppermute(packed(edges[2], 0, d), LON, [((i + 1) % lon, i) for i in ra...  24.2 us
    all_to_all x1, blocking collectives, exchange_second(): lax.all_to_all(mine, CHIPS, 0, 0)  16.5 us
    ppermute x2, starting transfers between devices, exchange_rows(): top = lax.ppermute(edges[1], LAT, [(i, i + 1) for i in range(lat - 1)])  13.2 us
    all_to_all x1, starting transfers between devices, exchange_first(): lax.all_to_all(mine, CHIPS, 0, 0)  8.14 us
    pallas_call x1, Pallas kernels, local_statistics(): pl.pallas_call(stats_kernel, out_shape=[jax.ShapeDtypeStruct(shape, jnp.f...  6.72 us
    ppermute x2, waiting for transfers between devices, exchange_rows(): bottom = lax.ppermute(edges[0], LAT, [(i + 1, i) for i in range(lat - 1)])  5.9 us
    ppermute x2, starting transfers between devices, exchange_rows(): bottom = lax.ppermute(edges[0], LAT, [(i + 1, i) for i in range(lat - 1)])  3.84 us
  transfers between devices with their start and end apart: 11, of which 5 were waited for; matrix products, arithmetic and copies ran while one was open for 2% of the time, Pallas kernels for 1%

profile of v8, /device:TPU:1, one launch (start us, length us, event | category | flops | bytes accessed | tf_op | source)
XLA Modules:
  0.0 128.5 jit_solution(11396024702219843103)
XLA Ops:
  0.0 6.7 %stats.1 = (f32[3,2,128]{2,1,0:T(2,128)}, bf16[8,2,32,256]{3,2,1,0:T(8,128)(2,1)}, bf16[8,2,32,256]{3,2,1,0:T(8,128)(2,1)}, bf16[8,64,256]{2,1,0:T(8,128)(2,1)}, bf16[8,64,256]{2,1,0:T(8,128)(2,1)}) custom-call(s32[128]{0:T(128)} %points_ref.5, bf16[8,32,32,256]{3,2,1,0:T(8,128)(2,1)} %refs_0_.1), custom_call_target="tpu_custom_call" | custom-call | flops 16777216 | bytes 4194304 | tf_op jit(solution)/shard_map/stats/pallas_call | solution.py:172
  6.7 0.0 copy-start.4
  6.7 0.0 copy-start
  6.8 1.5 %collective-permute-start = (f32[3,2,128]{2,1,0:T(2,128)}, f32[3,2,128]{2,1,0:T(2,128)S(1)}, u32[]{:S(2)}, u32[]{:S(2)}) collective-permute-start(f32[3,2,128]{2,1,0:T(2,128)} %get-tuple-element.19), channel_id=1, source_target_pairs={{0,32},{32,0},{1,33},{33,1},{2,34},{34,2},{3,35},{35,3},{4,36},{36... | collective-permute-start | bytes 9224 | tf_op jit(solution)/shard_map/ppermute | solution.py:426
  8.3 5.5 %collective-permute-start.1 = (bf16[8,2,32,256]{3,2,1,0:T(8,128)(2,1)}, bf16[8,2,32,256]{3,2,1,0:T(8,128)(2,1)S(1)}, u32[]{:S(2)}, u32[]{:S(2)}) collective-permute-start(bf16[8,2,32,256]{3,2,1,0:T(8,128)(2,1)} %get-tuple-element.20), channel_id=1, source_target_pairs={{0,32},{32,64},{64,96},{1,33},{33,65},{65,97},{2,34},{34,66},{66,9... | collective-permute-start | bytes 786440 | tf_op jit(solution)/shard_map/ppermute | solution.py:406
  13.7 1.9 %collective-permute-start.2 = (bf16[8,2,32,256]{3,2,1,0:T(8,128)(2,1)}, bf16[8,2,32,256]{3,2,1,0:T(8,128)(2,1)S(1)}, u32[]{:S(2)}, u32[]{:S(2)}) collective-permute-start(bf16[8,2,32,256]{3,2,1,0:T(8,128)(2,1)} %get-tuple-element.21), channel_id=1, source_target_pairs={{32,0},{64,32},{96,64},{33,1},{65,33},{97,65},{34,2},{66,34},{98,6... | collective-permute-start | bytes 786440 | tf_op jit(solution)/shard_map/ppermute | solution.py:407
  15.7 0.0 collective-permute-done
  15.7 0.7 slice_add_fusion.3
  16.4 0.7 broadcast_in_dim.6
  17.1 8.1 %all-to-all-start = ((f32[64,2,2,128]{3,2,1,0:T(2,128)}), f32[64,2,2,128]{3,2,1,0:T(2,128)S(1)}, u32[]{:S(2)}, u32[]{:S(2)}) async-start(f32[64,2,2,128]{3,2,1,0:T(2,128)} %broadcast_in_dim.6), calls=%async_computation | async-start | bytes 262144 | tf_op jit(solution)/shard_map/all_to_all | solution.py:438
  25.2 0.0 collective-permute-done.1.refs_1_
  25.3 0.0 collective-permute-done.2.refs_2_
  25.4 1.0 pad_maximum_fusion.2
  26.4 1.1 collective-permute-start.3
  27.5 0.0 copy-done.4
  27.5 0.1 pad_maximum_fusion.3
  27.6 4.7 %collective-permute-start.4 = (bf16[8,72,256]{2,1,0:T(8,128)(2,1)S(1)}, bf16[8,72,256]{2,1,0:T(8,128)(2,1)S(1)}, u32[]{:S(2)}, u32[]{:S(2)}) collective-permute-start(bf16[8,72,256]{2,1,0:T(8,128)(2,1)S(1)} %pad_maximum_fusion.3), channel_id=1, source_target_pairs={{1,0},{2,1},{3,2},{4,3},{5,4},{6,5},{7,6},{8,7},{9,8},{10,9},{11,1... | collective-permute-start | bytes 884744 | tf_op jit(solution)/shard_map/ppermute | solution.py:421
  32.4 1.9 %all-to-all-done.parts_ref = f32[64,2,2,128]{3,2,1,0:T(2,128)S(1)} async-done(((f32[64,2,2,128]{3,2,1,0:T(2,128)}), f32[64,2,2,128]{3,2,1,0:T(2,128)S(1)}, u32[]{:S(2)}, u32[]{:S(2)}) %all-to-all-start) | async-done | bytes 131104 | tf_op jit(solution)/shard_map/all_to_all | solution.py:438
  34.2 0.0 copy-done
  34.2 0.0 copy-start.1
  34.2 0.0 copy-start.3
  34.2 0.4 norm.2.norm_ref
  34.6 3.0 %collective-permute-done.3.refs_3_ = bf16[8,72,256]{2,1,0:T(8,128)(2,1)S(1)} collective-permute-done((bf16[8,72,256]{2,1,0:T(8,128)(2,1)S(1)}, bf16[8,72,256]{2,1,0:T(8,128)(2,1)S(1)}, u32[]{:S(2)}, u32[]{:S(2)}) %collective-permute-start.3) | collective-permute-done | bytes 294944 | tf_op jit(solution)/shard_map/ppermute | solution.py:420
  37.6 0.0 collective-permute-done.4.refs_4_
  37.6 0.0 copy-done.1
  37.6 0.0 copy-done.3
  37.6 17.5 %conv2.1 = (bf16[8,32,32,256]{3,2,1,0:T(8,128)(2,1)}, f32[3,2,128]{2,1,0:T(2,128)S(1)}, bf16[8,4,32,256]{3,2,1,0:T(8,128)(2,1)S(1)}, bf16[8,4,32,256]{3,2,1,0:T(...) custom-call(s32[128]{0:T(128)S(1)} %copy-done, s32[2,8]{1,0:T(2,128)S(1)} %bitcast.8, ...), custom_call_target="tpu_custom_call" | custom-call | flops 9663676416 | bytes 10485760 | tf_op jit(solution)/shard_map/conv2/pallas_call | solution.py:379
  55.1 7.7 %collective-permute-start.6 = (bf16[8,4,32,256]{3,2,1,0:T(8,128)(2,1)S(1)}, bf16[8,4,32,256]{3,2,1,0:T(8,128)(2,1)S(1)}, u32[]{:S(2)}, u32[]{:S(2)}) collective-permute-start(bf16[8,4,32,256]{3,2,1,0:T(8,128)(2,1)S(1)} %get-tuple-element.25), channel_id=1, source_target_pairs={{0,32},{32,64},{64,96},{1,33},{33,65},{65,97},{2,34},{34,66},{66,9... | collective-permute-start | bytes 1572872 | tf_op jit(solution)/shard_map/ppermute | solution.py:406
  62.8 1.9 %collective-permute-start.7 = (bf16[8,4,32,256]{3,2,1,0:T(8,128)(2,1)S(1)}, bf16[8,4,32,256]{3,2,1,0:T(8,128)(2,1)S(1)}, u32[]{:S(2)}, u32[]{:S(2)}) collective-permute-start(bf16[8,4,32,256]{3,2,1,0:T(8,128)(2,1)S(1)} %get-tuple-element.26), channel_id=1, source_target_pairs={{32,0},{64,32},{96,64},{33,1},{65,33},{97,65},{34,2},{66,34},{98,6... | collective-permute-start | bytes 1572872 | tf_op jit(solution)/shard_map/ppermute | solution.py:407
  64.7 0.1 collective-permute-start.5
  64.8 1.4 %collective-permute-done.5 = f32[3,2,128]{2,1,0:T(2,128)S(1)} collective-permute-done((f32[3,2,128]{2,1,0:T(2,128)S(1)}, f32[3,2,128]{2,1,0:T(2,128)S(1)}, u32[]{:S(2)}, u32[]{:S(2)}) %collective-permute-start.5) | collective-permute-done | bytes 3104 | tf_op jit(solution)/shard_map/ppermute | solution.py:426
  66.3 2.6 %collective-permute-done.6.refs_1_ = bf16[8,4,32,256]{3,2,1,0:T(8,128)(2,1)S(1)} collective-permute-done((bf16[8,4,32,256]{3,2,1,0:T(8,128)(2,1)S(1)}, bf16[8,4,32,256]{3,2,1,0:T(8,128)(2,1)S(1)}, u32[]{:S(2)}, u32[]{:S(2)}) %collective-permute-start.6) | collective-permute-done | bytes 524320 | tf_op jit(solution)/shard_map/ppermute | solution.py:406
  68.9 5.9 %collective-permute-done.7.refs_2_ = bf16[8,4,32,256]{3,2,1,0:T(8,128)(2,1)S(1)} collective-permute-done((bf16[8,4,32,256]{3,2,1,0:T(8,128)(2,1)S(1)}, bf16[8,4,32,256]{3,2,1,0:T(8,128)(2,1)S(1)}, u32[]{:S(2)}, u32[]{:S(2)}) %collective-permute-start.7) | collective-permute-done | bytes 524320 | tf_op jit(solution)/shard_map/ppermute | solution.py:407
  74.8 0.1 fusion.2
  75.1 19.5 %collective-permute-start.9 = (bf16[8,160,256]{2,1,0:T(8,128)(2,1)S(1)}, bf16[8,160,256]{2,1,0:T(8,128)(2,1)S(1)}, u32[]{:S(2)}, u32[]{:S(2)}) collective-permute-start(bf16[8,160,256]{2,1,0:T(8,128)(2,1)S(1)} %pad_maximum_fusion.1), channel_id=1, source_target_pairs={{1,0},{2,1},{3,2},{4,3},{5,4},{6,5},{7,6},{8,7},{9,8},{10,9},{11,1... | collective-permute-start | bytes 1966088 | tf_op jit(solution)/shard_map/ppermute | solution.py:421
  94.6 0.1 collective-permute-start.8
  94.7 16.5 %all_to_all.10.parts_ref = f32[64,2,2,128]{3,2,1,0:T(2,128)S(1)} all-to-all(f32[64,2,2,128]{3,2,1,0:T(2,128)S(1)} %broadcast_in_dim.8), channel_id=1, replica_groups=mesh['zh'=2,'core'=2,'y'=4,'zl'=2,'x'=4] {'zh','y','zl','x'}, dimensions={0} | all-to-all | bytes 262144 | tf_op jit(solution)/shard_map/all_to_all | solution.py:446
  111.3 0.0 copy-start.2
  111.3 0.4 norm.3.norm_ref
  111.6 0.0 collective-permute-done.9.refs_4_
  111.6 0.0 collective-permute-done.8.refs_3_
  111.7 0.9 copy-done.2
  112.5 15.8 %conv4.1 = bf16[8,32,32,256]{3,2,1,0:T(8,128)(2,1)} custom-call(s32[128]{0:T(128)S(1)} %copy-done, s32[2,8]{1,0:T(2,128)S(1)} %bitcast.9, f32[2,8,256]{2,1,0:T(8,128)S(1)} %norm.3.norm_ref, bf16[8,32,32,256]{3,2,1,0:T(8,128)(2,1)} %get-tuple-element.28.refs_0_, bf16[8,4,32,256]{3,2,1,0:T(8,128)(2,1)S(1)} %collective-permute-done.6.refs_1_, ...), custom_call_target="tpu_custom_call" | custom-call | flops 9663676416 | bytes 10485760 | tf_op jit(solution)/shard_map/conv4/pallas_call | solution.py:379
  (16 shorter events, 0.4 us)
Async XLA Ops:
  6.7 20.8 %copy-start.4 = (bf16[8,64,256]{2,1,0:T(8,128)(2,1)S(1)}, bf16[8,64,256]{2,1,0:T(8,128)(2,1)}, u32[]{:S(2)}) copy-start(bf16[8,64,256]{2,1,0:T(8,128)(2,1)} %get-tuple-element.23) | copy-start | bytes 786436
  6.7 27.5 %copy-start = (s32[128]{0:T(128)S(1)}, s32[128]{0:T(128)}, u32[]{:S(2)}) copy-start(s32[128]{0:T(128)} %points_ref.5) | copy-start | bytes 1540
  6.8 8.9 %collective-permute-start = (f32[3,2,128]{2,1,0:T(2,128)}, f32[3,2,128]{2,1,0:T(2,128)S(1)}, u32[]{:S(2)}, u32[]{:S(2)}) collective-permute-start(f32[3,2,128]{2,1,0:T(2,128)} %get-tuple-element.19), channel_id=1, source_target_pairs={{0,32},{32,0},{1,33},{33,1},{2,34},{34,2},{3,35},{35,3},{4,36},{36... | collective-permute-start | bytes 9224 | tf_op jit(solution)/shard_map/ppermute | solution.py:426
  8.3 17.0 %collective-permute-start.1 = (bf16[8,2,32,256]{3,2,1,0:T(8,128)(2,1)}, bf16[8,2,32,256]{3,2,1,0:T(8,128)(2,1)S(1)}, u32[]{:S(2)}, u32[]{:S(2)}) collective-permute-start(bf16[8,2,32,256]{3,2,1,0:T(8,128)(2,1)} %get-tuple-element.20), channel_id=1, source_target_pairs={{0,32},{32,64},{64,96},{1,33},{33,65},{65,97},{2,34},{34,66},{66,9... | collective-permute-start | bytes 786440 | tf_op jit(solution)/shard_map/ppermute | solution.py:406
  13.7 11.5 %collective-permute-start.2 = (bf16[8,2,32,256]{3,2,1,0:T(8,128)(2,1)}, bf16[8,2,32,256]{3,2,1,0:T(8,128)(2,1)S(1)}, u32[]{:S(2)}, u32[]{:S(2)}) collective-permute-start(bf16[8,2,32,256]{3,2,1,0:T(8,128)(2,1)} %get-tuple-element.21), channel_id=1, source_target_pairs={{32,0},{64,32},{96,64},{33,1},{65,33},{97,65},{34,2},{66,34},{98,6... | collective-permute-start | bytes 786440 | tf_op jit(solution)/shard_map/ppermute | solution.py:407
  17.1 17.2 %all-to-all-start = ((f32[64,2,2,128]{3,2,1,0:T(2,128)}), f32[64,2,2,128]{3,2,1,0:T(2,128)S(1)}, u32[]{:S(2)}, u32[]{:S(2)}) async-start(f32[64,2,2,128]{3,2,1,0:T(2,128)} %broadcast_in_dim.6), calls=%async_computation | async-start | bytes 262144 | tf_op jit(solution)/shard_map/all_to_all | solution.py:438
  26.4 11.2 %collective-permute-start.3 = (bf16[8,72,256]{2,1,0:T(8,128)(2,1)S(1)}, bf16[8,72,256]{2,1,0:T(8,128)(2,1)S(1)}, u32[]{:S(2)}, u32[]{:S(2)}) collective-permute-start(bf16[8,72,256]{2,1,0:T(8,128)(2,1)S(1)} %pad_maximum_fusion.2), channel_id=1, source_target_pairs={{0,1},{1,2},{2,3},{3,4},{4,5},{5,6},{6,7},{7,8},{8,9},{9,10},{10,1... | collective-permute-start | bytes 884744 | tf_op jit(solution)/shard_map/ppermute | solution.py:420
  27.6 10.0 %collective-permute-start.4 = (bf16[8,72,256]{2,1,0:T(8,128)(2,1)S(1)}, bf16[8,72,256]{2,1,0:T(8,128)(2,1)S(1)}, u32[]{:S(2)}, u32[]{:S(2)}) collective-permute-start(bf16[8,72,256]{2,1,0:T(8,128)(2,1)S(1)} %pad_maximum_fusion.3), channel_id=1, source_target_pairs={{1,0},{2,1},{3,2},{4,3},{5,4},{6,5},{7,6},{8,7},{9,8},{10,9},{11,1... | collective-permute-start | bytes 884744 | tf_op jit(solution)/shard_map/ppermute | solution.py:421
  34.2 3.4 %copy-start.1 = (bf16[3,3,256,256]{3,2,1,0:T(8,128)(2,1)S(1)}, bf16[3,3,256,256]{3,2,1,0:T(8,128)(2,1)}, u32[]{:S(2)}) copy-start(bf16[3,3,256,256]{3,2,1,0:T(8,128)(2,1)} %param.8) | copy-start | bytes 3538948
  34.2 3.4 %copy-start.3 = (s32[8,2]{0,1:T(2,128)S(1)}, s32[8,2]{0,1:T(2,128)}, u32[]{:S(2)}) copy-start(s32[8,2]{0,1:T(2,128)} %param.7) | copy-start | bytes 196
  55.1 13.8 %collective-permute-start.6 = (bf16[8,4,32,256]{3,2,1,0:T(8,128)(2,1)S(1)}, bf16[8,4,32,256]{3,2,1,0:T(8,128)(2,1)S(1)}, u32[]{:S(2)}, u32[]{:S(2)}) collective-permute-start(bf16[8,4,32,256]{3,2,1,0:T(8,128)(2,1)S(1)} %get-tuple-element.25), channel_id=1, source_target_pairs={{0,32},{32,64},{64,96},{1,33},{33,65},{65,97},{2,34},{34,66},{66,9... | collective-permute-start | bytes 1572872 | tf_op jit(solution)/shard_map/ppermute | solution.py:406
  62.8 12.0 %collective-permute-start.7 = (bf16[8,4,32,256]{3,2,1,0:T(8,128)(2,1)S(1)}, bf16[8,4,32,256]{3,2,1,0:T(8,128)(2,1)S(1)}, u32[]{:S(2)}, u32[]{:S(2)}) collective-permute-start(bf16[8,4,32,256]{3,2,1,0:T(8,128)(2,1)S(1)} %get-tuple-element.26), channel_id=1, source_target_pairs={{32,0},{64,32},{96,64},{33,1},{65,33},{97,65},{34,2},{66,34},{98,6... | collective-permute-start | bytes 1572872 | tf_op jit(solution)/shard_map/ppermute | solution.py:407
  64.7 1.5 %collective-permute-start.5 = (f32[3,2,128]{2,1,0:T(2,128)S(1)}, f32[3,2,128]{2,1,0:T(2,128)S(1)}, u32[]{:S(2)}, u32[]{:S(2)}) collective-permute-start(f32[3,2,128]{2,1,0:T(2,128)S(1)} %get-tuple-element.24), channel_id=1, source_target_pairs={{0,32},{32,0},{1,33},{33,1},{2,34},{34,2},{3,35},{35,3},{4,36},{36... | collective-permute-start | bytes 9224 | tf_op jit(solution)/shard_map/ppermute | solution.py:426
  75.1 36.6 %collective-permute-start.9 = (bf16[8,160,256]{2,1,0:T(8,128)(2,1)S(1)}, bf16[8,160,256]{2,1,0:T(8,128)(2,1)S(1)}, u32[]{:S(2)}, u32[]{:S(2)}) collective-permute-start(bf16[8,160,256]{2,1,0:T(8,128)(2,1)S(1)} %pad_maximum_fusion.1), channel_id=1, source_target_pairs={{1,0},{2,1},{3,2},{4,3},{5,4},{6,5},{7,6},{8,7},{9,8},{10,9},{11,1... | collective-permute-start | bytes 1966088 | tf_op jit(solution)/shard_map/ppermute | solution.py:421
  94.6 17.0 %collective-permute-start.8 = (bf16[8,160,256]{2,1,0:T(8,128)(2,1)S(1)}, bf16[8,160,256]{2,1,0:T(8,128)(2,1)S(1)}, u32[]{:S(2)}, u32[]{:S(2)}) collective-permute-start(bf16[8,160,256]{2,1,0:T(8,128)(2,1)S(1)} %pad_maximum_fusion), channel_id=1, source_target_pairs={{0,1},{1,2},{2,3},{3,4},{4,5},{5,6},{6,7},{7,8},{8,9},{9,10},{10,1... | collective-permute-start | bytes 1966088 | tf_op jit(solution)/shard_map/ppermute | solution.py:420
  111.3 1.3 copy-start.2

commit v9 on v6

--- a/solution.py
+++ b/solution.py
@@ -409,28 +409,59 @@
     return top, bottom
 
 
+def pack_kernel(top_ref, bottom_ref, first_ref, last_ref, east_ref, west_ref):
+    samples, d, width, _ = top_ref.shape
+    rows = first_ref.shape[1] // d
+    for cols_ref, out_ref, lo in ((last_ref, east_ref, width - d), (first_ref, west_ref, 0)):
+        for b in range(samples):
+            for e in range(d):
+                out_ref[b, e * d : (e + 1) * d] = top_ref[b, e, lo : lo + d]
+                below = (rows + d + e) * d
+                out_ref[b, below : below + d] = bottom_ref[b, e, lo : lo + d]
+            out_ref[b, d * d : (rows + d) * d] = cols_ref[b]
+
+
 def exchange_columns(edges, top, bottom):
     samples, d, width, channels = top.shape
     lon = lax.axis_size(LON)
-
-    def packed(cols, lo, hi):
-        above = top[:, :, lo:hi].reshape(samples, d * d, channels)
-        below = bottom[:, :, lo:hi].reshape(samples, d * d, channels)
-        return jnp.concatenate([above, cols, below], axis=1)
-
-    left = lax.ppermute(packed(edges[3], width - d, width), LON, [(i, (i + 1) % lon) for i in range(lon)])
-    right = lax.ppermute(packed(edges[2], 0, d), LON, [((i + 1) % lon, i) for i in range(lon)])
+    first_col, last_col = edges[2:]
+    shape = (samples, first_col.shape[1] + 2 * d * d, channels)
+    east, west = pl.pallas_call(
+        pack_kernel,
+        out_shape=[jax.ShapeDtypeStruct(shape, top.dtype)] * 2,
+        in_specs=[in_vmem()] * 4,
+        out_specs=[in_vmem()] * 2,
+        compiler_params=pltpu.CompilerParams(vmem_limit_bytes=8_000_000),
+        cost_estimate=pl.CostEstimate(flops=0, bytes_accessed=4 * first_col.size, transcendentals=0),
+        name="pack",
+    )(top, bottom, first_col, last_col)
+    left = lax.ppermute(east, LON, [(i, (i + 1) % lon) for i in range(lon)])
+    right = lax.ppermute(west, LON, [((i + 1) % lon, i) for i in range(lon)])
     return left, right
+
+
+def merge_kernel(local_ref, other_ref, out_ref):
+    sums, other_sums = local_ref[0], other_ref[0]
+    count, other_count = local_ref[2], other_ref[2]
+    both = jnp.maximum(count + other_count, 1.0)
+    gap = sums / jnp.maximum(count, 1.0) - other_sums / jnp.maximum(other_count, 1.0)
+    squares = local_ref[1] + other_ref[1] + gap * gap * (count * other_count / both)
+    out_ref[:, 0] = jnp.broadcast_to((sums + other_sums)[None], out_ref[:, 0].shape)
+    out_ref[:, 1] = jnp.broadcast_to(squares[None], out_ref[:, 1].shape)
 
 
 def merge_cores(local):
     other = lax.ppermute(local, "core", [(0, 1), (1, 0)])
-    own_count, other_count = local[2], other[2]
-    both = jnp.maximum(own_count + other_count, 1.0)
-    gap = local[0] / jnp.maximum(own_count, 1.0) - other[0] / jnp.maximum(other_count, 1.0)
-    squares = local[1] + other[1] + gap * gap * (own_count * other_count / both)
-    merged = jnp.stack([local[0] + other[0], squares])
-    return jnp.broadcast_to(merged[None], (lax.axis_size(CHIPS), *merged.shape))
+    shape = (lax.axis_size(CHIPS), 2, *local.shape[1:])
+    return pl.pallas_call(
+        merge_kernel,
+        out_shape=jax.ShapeDtypeStruct(shape, jnp.float32),
+        in_specs=[in_vmem()] * 2,
+        out_specs=in_vmem(),
+        compiler_params=pltpu.CompilerParams(vmem_limit_bytes=4_000_000),
+        cost_estimate=pl.CostEstimate(flops=10 * local.size, bytes_accessed=4 * local.size, transcendentals=0),
+        name="merge",
+    )(local, other)
 
 
 def exchange(local, edges, points, x):

time: 114 us -> 121 us (1.061)
  other arithmetic: 3.65 us -> 0 us
  waiting for transfers between devices: 19.6 us -> 23.1 us
  Pallas kernels: 41.5 us -> 44.3 us
  local copies, waits for them, and re-layouts: 1.75 us -> 4.26 us
  starting transfers between devices: 46.5 us -> 48.3 us
    all_to_all x2, starting transfers between devices: 15.8 us -> 20.1 us  [exchange(): norm = combine_statistics(lax.all_to_all(mine, CHIPS, 0, 0), points, x)]
    unnamed x10 -> x18, local copies, waits for them, and re-layouts: 0.02 us -> 4.26 us
    concatenate x4 -> x0, other arithmetic: 2.93 us -> none  [packed(): return jnp.concatenate([above, cols, below], axis=1)]
    ppermute x2, waiting for transfers between devices: 0.01 us -> 2.79 us  [merge_cores(): other = lax.ppermute(local, 'core', [(0, 1), (1, 0)])]
    pallas_call x0 -> x4, Pallas kernels: none -> 2.68 us  [the longest x2 1.39 us: merge_cores(): pl.pallas_call(merge_kernel, out_shape=jax.ShapeDtypeStruct(shape, jnp.fl...]
    ppermute x2, starting transfers between devices: 1.59 us -> 0.17 us  [merge_cores(): other = lax.ppermute(local, 'core', [(0, 1), (1, 0)])]
    broadcast_in_dim x2 -> x0, local copies, waits for them, and re-layouts: 1.4 us -> none  [merge_cores(): return jnp.broadcast_to(merged[None], (lax.axis_size(CHIPS), *merged.shape))]
    all_to_all x2, waiting for transfers between devices: 1.92 us -> 3.2 us  [exchange(): norm = combine_statistics(lax.all_to_all(mine, CHIPS, 0, 0), points, x)]
  transfers between devices with their start and end apart: 12 -> 12, of which waited for: 5 -> 6; matrix products, arithmetic and copies ran while one was open for 5% -> 0% of each run, Pallas kernels for 1% -> 3%
where the time goes in v9:
time: 121 us; the launch traced here: 120 us
  starting transfers between devices  48.3 us (40%)
  Pallas kernels  44.3 us (37%)
  waiting for transfers between devices  23.1 us (19%)
  local copies, waits for them, and re-layouts  4.26 us (4%)
    pallas_call x2, Pallas kernels, convolve(): pl.pallas_call(functools.partial(conv_kernel, d, CHUNK, which, with_stats...  34.1 us
    all_to_all x2, starting transfers between devices, exchange(): norm = combine_statistics(lax.all_to_all(mine, CHIPS, 0, 0), points, x)  20.1 us
    ppermute x2, waiting for transfers between devices, exchange_columns(): left = lax.ppermute(east, LON, [(i, (i + 1) % lon) for i in range(lon)])  17.1 us
    ppermute x2, starting transfers between devices, exchange_rows(): top = lax.ppermute(edges[1], LAT, [(i, i + 1) for i in range(lat - 1)])  12.8 us
    ppermute x2, starting transfers between devices, exchange_columns(): right = lax.ppermute(west, LON, [((i + 1) % lon, i) for i in range(lon)])  9.35 us
    pallas_call x1, Pallas kernels, local_statistics(): pl.pallas_call(stats_kernel, out_shape=[jax.ShapeDtypeStruct(shape, jnp.f...  6.86 us
    unnamed x18, local copies, waits for them, and re-layouts  4.26 us
    ppermute x2, starting transfers between devices, exchange_rows(): bottom = lax.ppermute(edges[0], LAT, [(i + 1, i) for i in range(lat - 1)])  3.84 us
  transfers between devices with their start and end apart: 12, of which 6 were waited for; matrix products, arithmetic and copies ran while one was open for 0% of the time, Pallas kernels for 3%

profile of v9, /device:TPU:1, one launch (start us, length us, event | category | flops | bytes accessed | tf_op | source)
XLA Modules:
  0.0 120.3 jit_solution(11720987022445340918)
XLA Ops:
  0.0 0.0 copy-start.3
  0.0 6.9 %stats.1 = (f32[3,2,128]{2,1,0:T(2,128)}, bf16[8,2,32,256]{3,2,1,0:T(8,128)(2,1)}, bf16[8,2,32,256]{3,2,1,0:T(8,128)(2,1)}, bf16[8,64,256]{2,1,0:T(8,128)(2,1)}, bf16[8,64,256]{2,1,0:T(8,128)(2,1)}) custom-call(s32[128]{0:T(128)} %points_ref.5, bf16[8,32,32,256]{3,2,1,0:T(8,128)(2,1)} %refs_0_.1), custom_call_target="tpu_custom_call" | custom-call | flops 16777216 | bytes 4194304 | tf_op jit(solution)/shard_map/stats/pallas_call | solution.py:173
  6.9 6.9 %collective-permute-start.1 = (bf16[8,2,32,256]{3,2,1,0:T(8,128)(2,1)}, bf16[8,2,32,256]{3,2,1,0:T(8,128)(2,1)S(1)}, u32[]{:S(2)}, u32[]{:S(2)}) collective-permute-start(bf16[8,2,32,256]{3,2,1,0:T(8,128)(2,1)} %get-tuple-element.21), channel_id=1, source_target_pairs={{0,32},{32,64},{64,96},{1,33},{33,65},{65,97},{2,34},{34,66},{66,9... | collective-permute-start | bytes 786440 | tf_op jit(solution)/shard_map/ppermute | solution.py:407
  13.8 1.9 %collective-permute-start.2 = (bf16[8,2,32,256]{3,2,1,0:T(8,128)(2,1)}, bf16[8,2,32,256]{3,2,1,0:T(8,128)(2,1)S(1)}, u32[]{:S(2)}, u32[]{:S(2)}) collective-permute-start(bf16[8,2,32,256]{3,2,1,0:T(8,128)(2,1)} %get-tuple-element.22), channel_id=1, source_target_pairs={{32,0},{64,32},{96,64},{33,1},{65,33},{97,65},{34,2},{66,34},{98,6... | collective-permute-start | bytes 786440 | tf_op jit(solution)/shard_map/ppermute | solution.py:408
  15.7 0.1 collective-permute-start
  15.8 1.4 %collective-permute-done.other_ref = f32[3,2,128]{2,1,0:T(2,128)S(1)} collective-permute-done((f32[3,2,128]{2,1,0:T(2,128)}, f32[3,2,128]{2,1,0:T(2,128)S(1)}, u32[]{:S(2)}, u32[]{:S(2)}) %collective-permute-start) | collective-permute-done | bytes 3104 | tf_op jit(solution)/shard_map/ppermute | solution.py:454
  17.2 0.0 copy-start.2
  17.2 0.7 copy-done.2
  17.8 0.7 merge.2
  18.5 10.5 %all-to-all-start = ((f32[64,2,2,128]{3,2,1,0:T(2,128)}), f32[64,2,2,128]{3,2,1,0:T(2,128)S(1)}, u32[]{:S(2)}, u32[]{:S(2)}) async-start(f32[64,2,2,128]{3,2,1,0:T(2,128)} %merge.2), calls=%async_computation | async-start | bytes 262144 | tf_op jit(solution)/shard_map/all_to_all | solution.py:470
  29.1 0.0 collective-permute-done.1.top_ref.refs_1_
  29.1 0.0 collective-permute-done.2.bottom_ref.refs_2_
  29.1 0.0 copy-start
  29.1 0.9 copy-done
  30.1 0.0 copy-start.1
  30.1 0.9 copy-done.1
  31.0 0.1 pack.2
  31.1 1.1 collective-permute-start.3
  32.2 4.7 %collective-permute-start.4 = (bf16[8,72,256]{2,1,0:T(8,128)(2,1)S(1)}, bf16[8,72,256]{2,1,0:T(8,128)(2,1)S(1)}, u32[]{:S(2)}, u32[]{:S(2)}) collective-permute-start(bf16[8,72,256]{2,1,0:T(8,128)(2,1)S(1)} %get-tuple-element.26), channel_id=1, source_target_pairs={{1,0},{2,1},{3,2},{4,3},{5,4},{6,5},{7,6},{8,7},{9,8},{10,9},{11,1... | collective-permute-start | bytes 884744 | tf_op jit(solution)/shard_map/ppermute | solution.py:439
  36.9 1.1 all-to-all-done.parts_ref
  37.9 0.0 copy-done.3
  37.9 0.0 copy-start.4
  37.9 0.0 copy-start.8
  37.9 0.4 norm.2.norm_ref
  38.3 5.0 %collective-permute-done.3.refs_3_ = bf16[8,72,256]{2,1,0:T(8,128)(2,1)S(1)} collective-permute-done((bf16[8,72,256]{2,1,0:T(8,128)(2,1)S(1)}, bf16[8,72,256]{2,1,0:T(8,128)(2,1)S(1)}, u32[]{:S(2)}, u32[]{:S(2)}) %collective-permute-start.3) | collective-permute-done | bytes 294944 | tf_op jit(solution)/shard_map/ppermute | solution.py:438
  43.3 0.0 collective-permute-done.4.refs_4_
  43.3 0.0 copy-start.6
  43.3 0.7 copy-done.6
  44.0 0.0 copy-done.4
  44.0 0.0 copy-done.8
  44.0 0.0 copy-start.7
  44.0 1.0 copy-done.7
  45.0 17.4 %conv2.1 = (bf16[8,32,32,256]{3,2,1,0:T(8,128)(2,1)}, f32[3,2,128]{2,1,0:T(2,128)S(1)}, bf16[8,4,32,256]{3,2,1,0:T(8,128)(2,1)S(1)}, bf16[8,4,32,256]{3,2,1,0:T(...) custom-call(s32[128]{0:T(128)S(1)} %copy-done.3, s32[2,8]{1,0:T(2,128)S(1)} %bitcast.8, ...), custom_call_target="tpu_custom_call" | custom-call | flops 9663676416 | bytes 10485760 | tf_op jit(solution)/shard_map/conv2/pallas_call | solution.py:380
  62.5 5.9 %collective-permute-start.6 = (bf16[8,4,32,256]{3,2,1,0:T(8,128)(2,1)S(1)}, bf16[8,4,32,256]{3,2,1,0:T(8,128)(2,1)S(1)}, u32[]{:S(2)}, u32[]{:S(2)}) collective-permute-start(bf16[8,4,32,256]{3,2,1,0:T(8,128)(2,1)S(1)} %get-tuple-element.29), channel_id=1, source_target_pairs={{0,32},{32,64},{64,96},{1,33},{33,65},{65,97},{2,34},{34,66},{66,9... | collective-permute-start | bytes 1572872 | tf_op jit(solution)/shard_map/ppermute | solution.py:407
  68.4 1.9 %collective-permute-start.7 = (bf16[8,4,32,256]{3,2,1,0:T(8,128)(2,1)S(1)}, bf16[8,4,32,256]{3,2,1,0:T(8,128)(2,1)S(1)}, u32[]{:S(2)}, u32[]{:S(2)}) collective-permute-start(bf16[8,4,32,256]{3,2,1,0:T(8,128)(2,1)S(1)} %get-tuple-element.30), channel_id=1, source_target_pairs={{32,0},{64,32},{96,64},{33,1},{65,33},{97,65},{34,2},{66,34},{98,6... | collective-permute-start | bytes 1572872 | tf_op jit(solution)/shard_map/ppermute | solution.py:408
  70.3 0.1 collective-permute-start.5
  70.4 1.4 %collective-permute-done.5.other_ref = f32[3,2,128]{2,1,0:T(2,128)S(1)} collective-permute-done((f32[3,2,128]{2,1,0:T(2,128)S(1)}, f32[3,2,128]{2,1,0:T(2,128)S(1)}, u32[]{:S(2)}, u32[]{:S(2)}) %collective-permute-start.5) | collective-permute-done | bytes 3104 | tf_op jit(solution)/shard_map/ppermute | solution.py:454
  71.8 0.7 merge.3
  72.5 9.5 %all-to-all-start.1 = ((f32[64,2,2,128]{3,2,1,0:T(2,128)}), f32[64,2,2,128]{3,2,1,0:T(2,128)S(1)}, u32[]{:S(2)}, u32[]{:S(2)}) async-start(f32[64,2,2,128]{3,2,1,0:T(2,128)} %merge.3), calls=%async_computation.1 | async-start | bytes 262144 | tf_op jit(solution)/shard_map/all_to_all | solution.py:470
  82.0 0.0 collective-permute-done.6.top_ref.refs_1_
  82.1 0.0 collective-permute-done.7.bottom_ref.refs_2_
  82.1 1.2 pack.3
  83.3 1.0 collective-permute-start.8
  84.3 0.0 copy-start.5
  84.3 4.7 %collective-permute-start.9 = (bf16[8,160,256]{2,1,0:T(8,128)(2,1)}, bf16[8,160,256]{2,1,0:T(8,128)(2,1)}, u32[]{:S(2)}, u32[]{:S(2)}) collective-permute-start(bf16[8,160,256]{2,1,0:T(8,128)(2,1)} %get-tuple-element.34), channel_id=1, source_target_pairs={{1,0},{2,1},{3,2},{4,3},{5,4},{6,5},{7,6},{8,7},{9,8},{10,9},{11,1... | collective-permute-start | bytes 1966088 | tf_op jit(solution)/shard_map/ppermute | solution.py:439
  89.0 2.1 %all-to-all-done.1.parts_ref = f32[64,2,2,128]{3,2,1,0:T(2,128)S(1)} async-done(((f32[64,2,2,128]{3,2,1,0:T(2,128)}), f32[64,2,2,128]{3,2,1,0:T(2,128)S(1)}, u32[]{:S(2)}, u32[]{:S(2)}) %all-to-all-start.1) | async-done | bytes 131104 | tf_op jit(solution)/shard_map/all_to_all | solution.py:470
  91.1 0.4 norm.3.norm_ref
  91.5 12.0 %collective-permute-done.8.refs_3_ = bf16[8,160,256]{2,1,0:T(8,128)(2,1)S(1)} collective-permute-done((bf16[8,160,256]{2,1,0:T(8,128)(2,1)}, bf16[8,160,256]{2,1,0:T(8,128)(2,1)S(1)}, u32[]{:S(2)}, u32[]{:S(2)}) %collective-permute-start.8) | collective-permute-done | bytes 655392 | tf_op jit(solution)/shard_map/ppermute | solution.py:438
  103.5 0.0 collective-permute-done.9.refs_4_
  103.5 0.0 copy-done.5
  103.5 16.6 %conv4.1 = bf16[8,32,32,256]{3,2,1,0:T(8,128)(2,1)} custom-call(s32[128]{0:T(128)S(1)} %copy-done.3, s32[2,8]{1,0:T(2,128)S(1)} %bitcast.9, f32[2,8,256]{2,1,0:T(8,128)S(1)} %norm.3.norm_ref, bf16[8,32,32,256]{3,2,1,0:T(8,128)(2,1)} %get-tuple-element.28.refs_0_, bf16[8,4,32,256]{3,2,1,0:T(8,128)(2,1)S(1)} %collective-permute-done.6.top_ref.refs_1_, ...), custom_call_target="tpu_custom_call" | custom-call | flops 9663676416 | bytes 10485760 | tf_op jit(solution)/shard_map/conv4/pallas_call | solution.py:380
Async XLA Ops:
  0.0 37.9 %copy-start.3 = (s32[128]{0:T(128)S(1)}, s32[128]{0:T(128)}, u32[]{:S(2)}) copy-start(s32[128]{0:T(128)} %points_ref.5) | copy-start | bytes 1540
  6.9 22.2 %collective-permute-start.1 = (bf16[8,2,32,256]{3,2,1,0:T(8,128)(2,1)}, bf16[8,2,32,256]{3,2,1,0:T(8,128)(2,1)S(1)}, u32[]{:S(2)}, u32[]{:S(2)}) collective-permute-start(bf16[8,2,32,256]{3,2,1,0:T(8,128)(2,1)} %get-tuple-element.21), channel_id=1, source_target_pairs={{0,32},{32,64},{64,96},{1,33},{33,65},{65,97},{2,34},{34,66},{66,9... | collective-permute-start | bytes 786440 | tf_op jit(solution)/shard_map/ppermute | solution.py:407
  13.8 15.3 %collective-permute-start.2 = (bf16[8,2,32,256]{3,2,1,0:T(8,128)(2,1)}, bf16[8,2,32,256]{3,2,1,0:T(8,128)(2,1)S(1)}, u32[]{:S(2)}, u32[]{:S(2)}) collective-permute-start(bf16[8,2,32,256]{3,2,1,0:T(8,128)(2,1)} %get-tuple-element.22), channel_id=1, source_target_pairs={{32,0},{64,32},{96,64},{33,1},{65,33},{97,65},{34,2},{66,34},{98,6... | collective-permute-start | bytes 786440 | tf_op jit(solution)/shard_map/ppermute | solution.py:408
  15.7 1.5 %collective-permute-start = (f32[3,2,128]{2,1,0:T(2,128)}, f32[3,2,128]{2,1,0:T(2,128)S(1)}, u32[]{:S(2)}, u32[]{:S(2)}) collective-permute-start(f32[3,2,128]{2,1,0:T(2,128)} %get-tuple-element.20.local_ref), channel_id=1, source_target_pairs={{0,32},{32,0},{1,33},{33,1},{2,34},{34,2},{3,35},{35,3},{4,36},{36... | collective-permute-start | bytes 9224 | tf_op jit(solution)/shard_map/ppermute | solution.py:454
  17.2 0.7 copy-start.2
  18.5 19.4 %all-to-all-start = ((f32[64,2,2,128]{3,2,1,0:T(2,128)}), f32[64,2,2,128]{3,2,1,0:T(2,128)S(1)}, u32[]{:S(2)}, u32[]{:S(2)}) async-start(f32[64,2,2,128]{3,2,1,0:T(2,128)} %merge.2), calls=%async_computation | async-start | bytes 262144 | tf_op jit(solution)/shard_map/all_to_all | solution.py:470
  29.1 1.0 copy-start
  30.1 0.9 copy-start.1
  31.1 12.2 %collective-permute-start.3 = (bf16[8,72,256]{2,1,0:T(8,128)(2,1)S(1)}, bf16[8,72,256]{2,1,0:T(8,128)(2,1)S(1)}, u32[]{:S(2)}, u32[]{:S(2)}) collective-permute-start(bf16[8,72,256]{2,1,0:T(8,128)(2,1)S(1)} %get-tuple-element.25), channel_id=1, source_target_pairs={{0,1},{1,2},{2,3},{3,4},{4,5},{5,6},{6,7},{7,8},{8,9},{9,10},{10,1... | collective-permute-start | bytes 884744 | tf_op jit(solution)/shard_map/ppermute | solution.py:438
  32.2 11.1 %collective-permute-start.4 = (bf16[8,72,256]{2,1,0:T(8,128)(2,1)S(1)}, bf16[8,72,256]{2,1,0:T(8,128)(2,1)S(1)}, u32[]{:S(2)}, u32[]{:S(2)}) collective-permute-start(bf16[8,72,256]{2,1,0:T(8,128)(2,1)S(1)} %get-tuple-element.26), channel_id=1, source_target_pairs={{1,0},{2,1},{3,2},{4,3},{5,4},{6,5},{7,6},{8,7},{9,8},{10,9},{11,1... | collective-permute-start | bytes 884744 | tf_op jit(solution)/shard_map/ppermute | solution.py:439
  37.9 6.1 %copy-start.4 = (bf16[3,3,256,256]{3,2,1,0:T(8,128)(2,1)S(1)}, bf16[3,3,256,256]{3,2,1,0:T(8,128)(2,1)}, u32[]{:S(2)}) copy-start(bf16[3,3,256,256]{3,2,1,0:T(8,128)(2,1)} %param.8) | copy-start | bytes 3538948
  37.9 6.1 %copy-start.8 = (s32[8,2]{0,1:T(2,128)S(1)}, s32[8,2]{0,1:T(2,128)}, u32[]{:S(2)}) copy-start(s32[8,2]{0,1:T(2,128)} %param.7) | copy-start | bytes 196
  43.3 0.7 copy-start.6
  44.0 1.0 copy-start.7
  62.5 19.6 %collective-permute-start.6 = (bf16[8,4,32,256]{3,2,1,0:T(8,128)(2,1)S(1)}, bf16[8,4,32,256]{3,2,1,0:T(8,128)(2,1)S(1)}, u32[]{:S(2)}, u32[]{:S(2)}) collective-permute-start(bf16[8,4,32,256]{3,2,1,0:T(8,128)(2,1)S(1)} %get-tuple-element.29), channel_id=1, source_target_pairs={{0,32},{32,64},{64,96},{1,33},{33,65},{65,97},{2,34},{34,66},{66,9... | collective-permute-start | bytes 1572872 | tf_op jit(solution)/shard_map/ppermute | solution.py:407
  68.4 13.7 %collective-permute-start.7 = (bf16[8,4,32,256]{3,2,1,0:T(8,128)(2,1)S(1)}, bf16[8,4,32,256]{3,2,1,0:T(8,128)(2,1)S(1)}, u32[]{:S(2)}, u32[]{:S(2)}) collective-permute-start(bf16[8,4,32,256]{3,2,1,0:T(8,128)(2,1)S(1)} %get-tuple-element.30), channel_id=1, source_target_pairs={{32,0},{64,32},{96,64},{33,1},{65,33},{97,65},{34,2},{66,34},{98,6... | collective-permute-start | bytes 1572872 | tf_op jit(solution)/shard_map/ppermute | solution.py:408
  70.3 1.5 %collective-permute-start.5 = (f32[3,2,128]{2,1,0:T(2,128)S(1)}, f32[3,2,128]{2,1,0:T(2,128)S(1)}, u32[]{:S(2)}, u32[]{:S(2)}) collective-permute-start(f32[3,2,128]{2,1,0:T(2,128)S(1)} %get-tuple-element.27.local_ref), channel_id=1, source_target_pairs={{0,32},{32,0},{1,33},{33,1},{2,34},{34,2},{3,35},{35,3},{4,36},{36... | collective-permute-start | bytes 9224 | tf_op jit(solution)/shard_map/ppermute | solution.py:454
  72.5 18.6 %all-to-all-start.1 = ((f32[64,2,2,128]{3,2,1,0:T(2,128)}), f32[64,2,2,128]{3,2,1,0:T(2,128)S(1)}, u32[]{:S(2)}, u32[]{:S(2)}) async-start(f32[64,2,2,128]{3,2,1,0:T(2,128)} %merge.3), calls=%async_computation.1 | async-start | bytes 262144 | tf_op jit(solution)/shard_map/all_to_all | solution.py:470
  83.3 20.2 %collective-permute-start.8 = (bf16[8,160,256]{2,1,0:T(8,128)(2,1)}, bf16[8,160,256]{2,1,0:T(8,128)(2,1)S(1)}, u32[]{:S(2)}, u32[]{:S(2)}) collective-permute-start(bf16[8,160,256]{2,1,0:T(8,128)(2,1)} %get-tuple-element.33), channel_id=1, source_target_pairs={{0,1},{1,2},{2,3},{3,4},{4,5},{5,6},{6,7},{7,8},{8,9},{9,10},{10,1... | collective-permute-start | bytes 1966088 | tf_op jit(solution)/shard_map/ppermute | solution.py:438
  84.3 19.2 %copy-start.5 = (bf16[3,3,256,256]{3,2,1,0:T(8,128)(2,1)S(1)}, bf16[3,3,256,256]{3,2,1,0:T(8,128)(2,1)}, u32[]{:S(2)}) copy-start(bf16[3,3,256,256]{3,2,1,0:T(8,128)(2,1)} %param.9) | copy-start | bytes 3538948
  84.3 19.2 %collective-permute-start.9 = (bf16[8,160,256]{2,1,0:T(8,128)(2,1)}, bf16[8,160,256]{2,1,0:T(8,128)(2,1)}, u32[]{:S(2)}, u32[]{:S(2)}) collective-permute-start(bf16[8,160,256]{2,1,0:T(8,128)(2,1)} %get-tuple-element.34), channel_id=1, source_target_pairs={{1,0},{2,1},{3,2},{4,3},{5,4},{6,5},{7,6},{8,7},{9,8},{10,9},{11,1... | collective-permute-start | bytes 1966088 | tf_op jit(solution)/shard_map/ppermute | solution.py:439

commit v10 on v8

--- a/solution.py
+++ b/solution.py
@@ -439,12 +439,28 @@
     return norm, (top, bottom, *exchange_columns(edges, top, bottom))
 
 
+def hold_kernel(points_ref, mine_ref, out_ref):
+    out_ref[...] = points_ref[...]
+
+
+def hold(points, mine):
+    return pl.pallas_call(
+        hold_kernel,
+        out_shape=jax.ShapeDtypeStruct((1, points.shape[0]), points.dtype),
+        in_specs=[in_vmem(), pl.BlockSpec(memory_space=pltpu.HBM)],
+        out_specs=in_vmem(),
+        compiler_params=pltpu.CompilerParams(vmem_limit_bytes=4_000_000),
+        cost_estimate=pl.CostEstimate(flops=10**8, bytes_accessed=4 * points.size, transcendentals=0),
+        name="hold",
+    )(points[None], mine)[0]
+
+
 def exchange_second(local, edges, points, x):
     mine = merge_cores(local)
     mine, top, bottom = lax.optimization_barrier((mine, *exchange_rows(edges)))
     columns = exchange_columns(edges, top, bottom)
     norm = combine_statistics(lax.all_to_all(mine, CHIPS, 0, 0), points, x, 10**9)
-    return norm, (top, bottom, *columns)
+    return norm, (top, bottom, *columns), hold(points, mine)
 
 
 def per_device(features, band_points, survival_flags, first_kernel_weight, second_kernel_weight):
@@ -457,9 +473,9 @@
     first, local, *edges = convolve(
         features, halos, first_weight, norm, band_points, flags, FIRST_DILATION, 0, True
     )
-    norm, halos = exchange_second(local, edges, band_points, first)
+    norm, halos, points = exchange_second(local, edges, band_points, first)
     (section,) = convolve(
-        first, halos, second_weight, norm, band_points, flags, SECOND_DILATION, 1, False
+        first, halos, second_weight, norm, points, flags, SECOND_DILATION, 1, False
     )
     return section
 

time: 129 us -> 131 us (1.016)
  blocking collectives: 16.5 us -> 0 us
  waiting for transfers between devices: 14.9 us -> 23.4 us
  starting transfers between devices: 52.1 us -> 60.1 us
  other arithmetic: 1.93 us -> 3.64 us
    all_to_all x1 -> x0, blocking collectives: 16.5 us -> none  [exchange_second(): lax.all_to_all(mine, CHIPS, 0, 0)]
    all_to_all x0 -> x1, waiting for transfers between devices: none -> 8.59 us  [exchange_second(): lax.all_to_all(mine, CHIPS, 0, 0)]
    all_to_all x0 -> x1, starting transfers between devices: none -> 8.15 us  [exchange_second(): lax.all_to_all(mine, CHIPS, 0, 0)]
    concatenate x4, other arithmetic: 1.22 us -> 2.92 us  [packed(): return jnp.concatenate([above, cols, below], axis=1)]
  transfers between devices with their start and end apart: 11 -> 12, of which waited for: 5 -> 6; matrix products, arithmetic and copies ran while one was open for 2% -> 3% of each run, Pallas kernels for 1% -> 1%
where the time goes in v10:
time: 131 us
  starting transfers between devices  60.1 us (46%)
  Pallas kernels  41.6 us (32%)
  waiting for transfers between devices  23.4 us (18%)
  other arithmetic  3.64 us (3%)
  local copies, waits for them, and re-layouts  1.73 us (1%)
    pallas_call x2, Pallas kernels, convolve(): pl.pallas_call(functools.partial(conv_kernel, d, CHUNK, which, with_stats...  34.1 us
    ppermute x2, starting transfers between devices, exchange_columns(): lax.ppermute(packed(edges[2], 0, d), LON, [((i + 1) % lon, i) for i in ra...  24.2 us
    ppermute x2, starting transfers between devices, exchange_rows(): top = lax.ppermute(edges[1], LAT, [(i, i + 1) for i in range(lat - 1)])  13.2 us
    all_to_all x1, waiting for transfers between devices, exchange_second(): lax.all_to_all(mine, CHIPS, 0, 0)  8.59 us
    all_to_all x1, starting transfers between devices, exchange_second(): lax.all_to_all(mine, CHIPS, 0, 0)  8.15 us
    all_to_all x1, starting transfers between devices, exchange_first(): lax.all_to_all(mine, CHIPS, 0, 0)  8.14 us
    pallas_call x1, Pallas kernels, local_statistics(): pl.pallas_call(stats_kernel, out_shape=[jax.ShapeDtypeStruct(shape, jnp.f...  6.71 us
    ppermute x2, waiting for transfers between devices, exchange_rows(): bottom = lax.ppermute(edges[0], LAT, [(i + 1, i) for i in range(lat - 1)])  5.9 us
  transfers between devices with their start and end apart: 12, of which 6 were waited for; matrix products, arithmetic and copies ran while one was open for 3% of the time, Pallas kernels for 1%

profile of v10, /device:TPU:1, one launch (start us, length us, event | category | flops | bytes accessed | tf_op | source)
XLA Modules:
  0.0 130.9 jit_solution(9775340991138938636)
XLA Ops:
  0.0 6.7 %stats.1 = (f32[3,2,128]{2,1,0:T(2,128)}, bf16[8,2,32,256]{3,2,1,0:T(8,128)(2,1)}, bf16[8,2,32,256]{3,2,1,0:T(8,128)(2,1)}, bf16[8,64,256]{2,1,0:T(8,128)(2,1)}, bf16[8,64,256]{2,1,0:T(8,128)(2,1)}) custom-call(s32[128]{0:T(128)} %points_ref.3, bf16[8,32,32,256]{3,2,1,0:T(8,128)(2,1)} %refs_0_.1), custom_call_target="tpu_custom_call" | custom-call | flops 16777216 | bytes 4194304 | tf_op jit(solution)/shard_map/stats/pallas_call | solution.py:172
  6.7 0.0 copy-start.4
  6.7 0.0 copy-start
  6.7 1.5 %collective-permute-start = (f32[3,2,128]{2,1,0:T(2,128)}, f32[3,2,128]{2,1,0:T(2,128)S(1)}, u32[]{:S(2)}, u32[]{:S(2)}) collective-permute-start(f32[3,2,128]{2,1,0:T(2,128)} %get-tuple-element.19), channel_id=1, source_target_pairs={{0,32},{32,0},{1,33},{33,1},{2,34},{34,2},{3,35},{35,3},{4,36},{36... | collective-permute-start | bytes 9224 | tf_op jit(solution)/shard_map/ppermute | solution.py:426
  8.2 5.5 %collective-permute-start.1 = (bf16[8,2,32,256]{3,2,1,0:T(8,128)(2,1)}, bf16[8,2,32,256]{3,2,1,0:T(8,128)(2,1)S(1)}, u32[]{:S(2)}, u32[]{:S(2)}) collective-permute-start(bf16[8,2,32,256]{3,2,1,0:T(8,128)(2,1)} %get-tuple-element.20), channel_id=1, source_target_pairs={{0,32},{32,64},{64,96},{1,33},{33,65},{65,97},{2,34},{34,66},{66,9... | collective-permute-start | bytes 786440 | tf_op jit(solution)/shard_map/ppermute | solution.py:406
  13.7 1.9 %collective-permute-start.2 = (bf16[8,2,32,256]{3,2,1,0:T(8,128)(2,1)}, bf16[8,2,32,256]{3,2,1,0:T(8,128)(2,1)S(1)}, u32[]{:S(2)}, u32[]{:S(2)}) collective-permute-start(bf16[8,2,32,256]{3,2,1,0:T(8,128)(2,1)} %get-tuple-element.21), channel_id=1, source_target_pairs={{32,0},{64,32},{96,64},{33,1},{65,33},{97,65},{34,2},{66,34},{98,6... | collective-permute-start | bytes 786440 | tf_op jit(solution)/shard_map/ppermute | solution.py:407
  15.7 0.0 collective-permute-done
  15.7 0.7 slice_add_fusion.3
  16.4 0.7 broadcast_in_dim.7
  17.1 8.1 %all-to-all-start = ((f32[64,2,2,128]{3,2,1,0:T(2,128)}), f32[64,2,2,128]{3,2,1,0:T(2,128)S(1)}, u32[]{:S(2)}, u32[]{:S(2)}) async-start(f32[64,2,2,128]{3,2,1,0:T(2,128)} %broadcast_in_dim.7), calls=%async_computation | async-start | bytes 262144 | tf_op jit(solution)/shard_map/all_to_all | solution.py:438
  25.2 0.0 collective-permute-done.1.refs_1_
  25.3 0.0 collective-permute-done.2.refs_2_
  25.4 1.0 pad_maximum_fusion.2
  26.5 1.1 collective-permute-start.3
  27.5 0.0 copy-done.4
  27.5 0.1 pad_maximum_fusion.3
  27.6 4.7 %collective-permute-start.4 = (bf16[8,72,256]{2,1,0:T(8,128)(2,1)S(1)}, bf16[8,72,256]{2,1,0:T(8,128)(2,1)S(1)}, u32[]{:S(2)}, u32[]{:S(2)}) collective-permute-start(bf16[8,72,256]{2,1,0:T(8,128)(2,1)S(1)} %pad_maximum_fusion.3), channel_id=1, source_target_pairs={{1,0},{2,1},{3,2},{4,3},{5,4},{6,5},{7,6},{8,7},{9,8},{10,9},{11,1... | collective-permute-start | bytes 884744 | tf_op jit(solution)/shard_map/ppermute | solution.py:421
  32.4 1.9 %all-to-all-done.parts_ref = f32[64,2,2,128]{3,2,1,0:T(2,128)S(1)} async-done(((f32[64,2,2,128]{3,2,1,0:T(2,128)}), f32[64,2,2,128]{3,2,1,0:T(2,128)S(1)}, u32[]{:S(2)}, u32[]{:S(2)}) %all-to-all-start) | async-done | bytes 131104 | tf_op jit(solution)/shard_map/all_to_all | solution.py:438
  34.2 0.0 copy-done
  34.2 0.0 copy-start.1
  34.2 0.0 copy-start.3
  34.2 0.4 norm.2.norm_ref
  34.6 3.0 %collective-permute-done.3.refs_3_ = bf16[8,72,256]{2,1,0:T(8,128)(2,1)S(1)} collective-permute-done((bf16[8,72,256]{2,1,0:T(8,128)(2,1)S(1)}, bf16[8,72,256]{2,1,0:T(8,128)(2,1)S(1)}, u32[]{:S(2)}, u32[]{:S(2)}) %collective-permute-start.3) | collective-permute-done | bytes 294944 | tf_op jit(solution)/shard_map/ppermute | solution.py:420
  37.6 0.0 collective-permute-done.4.refs_4_
  37.6 0.0 copy-done.1
  37.6 0.0 copy-done.3
  37.6 17.5 %conv2.1 = (bf16[8,32,32,256]{3,2,1,0:T(8,128)(2,1)}, f32[3,2,128]{2,1,0:T(2,128)S(1)}, bf16[8,4,32,256]{3,2,1,0:T(8,128)(2,1)S(1)}, bf16[8,4,32,256]{3,2,1,0:T(...) custom-call(s32[128]{0:T(128)S(1)} %copy-done, s32[2,8]{1,0:T(2,128)S(1)} %bitcast.10, ...), custom_call_target="tpu_custom_call" | custom-call | flops 9663676416 | bytes 10485760 | tf_op jit(solution)/shard_map/conv2/pallas_call | solution.py:379
  55.1 7.7 %collective-permute-start.6 = (bf16[8,4,32,256]{3,2,1,0:T(8,128)(2,1)S(1)}, bf16[8,4,32,256]{3,2,1,0:T(8,128)(2,1)S(1)}, u32[]{:S(2)}, u32[]{:S(2)}) collective-permute-start(bf16[8,4,32,256]{3,2,1,0:T(8,128)(2,1)S(1)} %get-tuple-element.25), channel_id=1, source_target_pairs={{0,32},{32,64},{64,96},{1,33},{33,65},{65,97},{2,34},{34,66},{66,9... | collective-permute-start | bytes 1572872 | tf_op jit(solution)/shard_map/ppermute | solution.py:406
  62.8 1.9 %collective-permute-start.7 = (bf16[8,4,32,256]{3,2,1,0:T(8,128)(2,1)S(1)}, bf16[8,4,32,256]{3,2,1,0:T(8,128)(2,1)S(1)}, u32[]{:S(2)}, u32[]{:S(2)}) collective-permute-start(bf16[8,4,32,256]{3,2,1,0:T(8,128)(2,1)S(1)} %get-tuple-element.26), channel_id=1, source_target_pairs={{32,0},{64,32},{96,64},{33,1},{65,33},{97,65},{34,2},{66,34},{98,6... | collective-permute-start | bytes 1572872 | tf_op jit(solution)/shard_map/ppermute | solution.py:407
  64.7 0.1 collective-permute-start.5
  64.8 1.4 %collective-permute-done.5 = f32[3,2,128]{2,1,0:T(2,128)S(1)} collective-permute-done((f32[3,2,128]{2,1,0:T(2,128)S(1)}, f32[3,2,128]{2,1,0:T(2,128)S(1)}, u32[]{:S(2)}, u32[]{:S(2)}) %collective-permute-start.5) | collective-permute-done | bytes 3104 | tf_op jit(solution)/shard_map/ppermute | solution.py:426
  66.3 2.6 %collective-permute-done.6.refs_1_ = bf16[8,4,32,256]{3,2,1,0:T(8,128)(2,1)S(1)} collective-permute-done((bf16[8,4,32,256]{3,2,1,0:T(8,128)(2,1)S(1)}, bf16[8,4,32,256]{3,2,1,0:T(8,128)(2,1)S(1)}, u32[]{:S(2)}, u32[]{:S(2)}) %collective-permute-start.6) | collective-permute-done | bytes 524320 | tf_op jit(solution)/shard_map/ppermute | solution.py:406
  68.9 5.9 %collective-permute-done.7.refs_2_ = bf16[8,4,32,256]{3,2,1,0:T(8,128)(2,1)S(1)} collective-permute-done((bf16[8,4,32,256]{3,2,1,0:T(8,128)(2,1)S(1)}, bf16[8,4,32,256]{3,2,1,0:T(8,128)(2,1)S(1)}, u32[]{:S(2)}, u32[]{:S(2)}) %collective-permute-start.7) | collective-permute-done | bytes 524320 | tf_op jit(solution)/shard_map/ppermute | solution.py:407
  74.8 0.7 broadcast_in_dim.8.mine_ref
  75.5 0.1 fusion.2
  75.7 0.9 pad_maximum_fusion.1
  76.6 19.4 %collective-permute-start.9 = (bf16[8,160,256]{2,1,0:T(8,128)(2,1)}, bf16[8,160,256]{2,1,0:T(8,128)(2,1)}, u32[]{:S(2)}, u32[]{:S(2)}) collective-permute-start(bf16[8,160,256]{2,1,0:T(8,128)(2,1)} %pad_maximum_fusion.1), channel_id=1, source_target_pairs={{1,0},{2,1},{3,2},{4,3},{5,4},{6,5},{7,6},{8,7},{9,8},{10,9},{11,1... | collective-permute-start | bytes 1966088 | tf_op jit(solution)/shard_map/ppermute | solution.py:421
  96.0 0.9 pad_maximum_fusion
  96.9 0.0 collective-permute-start.8
  96.9 8.1 %all-to-all-start.1 = ((f32[64,2,2,128]{3,2,1,0:T(2,128)}), f32[64,2,2,128]{3,2,1,0:T(2,128)S(1)}, u32[]{:S(2)}, u32[]{:S(2)}) async-start(f32[64,2,2,128]{3,2,1,0:T(2,128)} %broadcast_in_dim.8.mine_ref), calls=%async_computation.1 | async-start | bytes 262144 | tf_op jit(solution)/shard_map/all_to_all | solution.py:462
  105.1 0.0 copy-start.2
  105.1 8.6 %all-to-all-done.1.parts_ref = f32[64,2,2,128]{3,2,1,0:T(2,128)S(1)} async-done(((f32[64,2,2,128]{3,2,1,0:T(2,128)}), f32[64,2,2,128]{3,2,1,0:T(2,128)S(1)}, u32[]{:S(2)}, u32[]{:S(2)}) %all-to-all-start.1) | async-done | bytes 131104 | tf_op jit(solution)/shard_map/all_to_all | solution.py:462
  113.7 0.4 norm.3.norm_ref
  114.0 0.0 collective-permute-done.9.refs_4_
  114.0 0.0 collective-permute-done.8.refs_3_
  114.1 0.0 copy-done.2
  114.1 16.7 %conv4.1 = bf16[8,32,32,256]{3,2,1,0:T(8,128)(2,1)} custom-call(s32[128]{0:T(128)S(1)} %bitcast.12, s32[2,8]{1,0:T(2,128)S(1)} %bitcast.11, f32[2,8,256]{2,1,0:T(8,128)S(1)} %norm.3.norm_ref, bf16[8,32,32,256]{3,2,1,0:T(8,128)(2,1)} %get-tuple-element.28.refs_0_, bf16[8,4,32,256]{3,2,1,0:T(8,128)(2,1)S(1)} %collective-permute-done.6.refs_1_, ...), custom_call_target="tpu_custom_call" | custom-call | flops 9663676416 | bytes 10485760 | tf_op jit(solution)/shard_map/conv4/pallas_call | solution.py:379
  (14 shorter events, 0.2 us)
Async XLA Ops:
  6.7 20.8 %copy-start.4 = (bf16[8,64,256]{2,1,0:T(8,128)(2,1)S(1)}, bf16[8,64,256]{2,1,0:T(8,128)(2,1)}, u32[]{:S(2)}) copy-start(bf16[8,64,256]{2,1,0:T(8,128)(2,1)} %get-tuple-element.23) | copy-start | bytes 786436
  6.7 27.5 %copy-start = (s32[128]{0:T(128)S(1)}, s32[128]{0:T(128)}, u32[]{:S(2)}) copy-start(s32[128]{0:T(128)} %points_ref.3) | copy-start | bytes 1540
  6.7 8.9 %collective-permute-start = (f32[3,2,128]{2,1,0:T(2,128)}, f32[3,2,128]{2,1,0:T(2,128)S(1)}, u32[]{:S(2)}, u32[]{:S(2)}) collective-permute-start(f32[3,2,128]{2,1,0:T(2,128)} %get-tuple-element.19), channel_id=1, source_target_pairs={{0,32},{32,0},{1,33},{33,1},{2,34},{34,2},{3,35},{35,3},{4,36},{36... | collective-permute-start | bytes 9224 | tf_op jit(solution)/shard_map/ppermute | solution.py:426
  8.2 17.0 %collective-permute-start.1 = (bf16[8,2,32,256]{3,2,1,0:T(8,128)(2,1)}, bf16[8,2,32,256]{3,2,1,0:T(8,128)(2,1)S(1)}, u32[]{:S(2)}, u32[]{:S(2)}) collective-permute-start(bf16[8,2,32,256]{3,2,1,0:T(8,128)(2,1)} %get-tuple-element.20), channel_id=1, source_target_pairs={{0,32},{32,64},{64,96},{1,33},{33,65},{65,97},{2,34},{34,66},{66,9... | collective-permute-start | bytes 786440 | tf_op jit(solution)/shard_map/ppermute | solution.py:406
  13.7 11.6 %collective-permute-start.2 = (bf16[8,2,32,256]{3,2,1,0:T(8,128)(2,1)}, bf16[8,2,32,256]{3,2,1,0:T(8,128)(2,1)S(1)}, u32[]{:S(2)}, u32[]{:S(2)}) collective-permute-start(bf16[8,2,32,256]{3,2,1,0:T(8,128)(2,1)} %get-tuple-element.21), channel_id=1, source_target_pairs={{32,0},{64,32},{96,64},{33,1},{65,33},{97,65},{34,2},{66,34},{98,6... | collective-permute-start | bytes 786440 | tf_op jit(solution)/shard_map/ppermute | solution.py:407
  17.1 17.2 %all-to-all-start = ((f32[64,2,2,128]{3,2,1,0:T(2,128)}), f32[64,2,2,128]{3,2,1,0:T(2,128)S(1)}, u32[]{:S(2)}, u32[]{:S(2)}) async-start(f32[64,2,2,128]{3,2,1,0:T(2,128)} %broadcast_in_dim.7), calls=%async_computation | async-start | bytes 262144 | tf_op jit(solution)/shard_map/all_to_all | solution.py:438
  26.5 11.2 %collective-permute-start.3 = (bf16[8,72,256]{2,1,0:T(8,128)(2,1)S(1)}, bf16[8,72,256]{2,1,0:T(8,128)(2,1)S(1)}, u32[]{:S(2)}, u32[]{:S(2)}) collective-permute-start(bf16[8,72,256]{2,1,0:T(8,128)(2,1)S(1)} %pad_maximum_fusion.2), channel_id=1, source_target_pairs={{0,1},{1,2},{2,3},{3,4},{4,5},{5,6},{6,7},{7,8},{8,9},{9,10},{10,1... | collective-permute-start | bytes 884744 | tf_op jit(solution)/shard_map/ppermute | solution.py:420
  27.6 10.0 %collective-permute-start.4 = (bf16[8,72,256]{2,1,0:T(8,128)(2,1)S(1)}, bf16[8,72,256]{2,1,0:T(8,128)(2,1)S(1)}, u32[]{:S(2)}, u32[]{:S(2)}) collective-permute-start(bf16[8,72,256]{2,1,0:T(8,128)(2,1)S(1)} %pad_maximum_fusion.3), channel_id=1, source_target_pairs={{1,0},{2,1},{3,2},{4,3},{5,4},{6,5},{7,6},{8,7},{9,8},{10,9},{11,1... | collective-permute-start | bytes 884744 | tf_op jit(solution)/shard_map/ppermute | solution.py:421
  34.2 3.4 %copy-start.1 = (bf16[3,3,256,256]{3,2,1,0:T(8,128)(2,1)S(1)}, bf16[3,3,256,256]{3,2,1,0:T(8,128)(2,1)}, u32[]{:S(2)}) copy-start(bf16[3,3,256,256]{3,2,1,0:T(8,128)(2,1)} %param.8) | copy-start | bytes 3538948
  34.2 3.4 %copy-start.3 = (s32[8,2]{0,1:T(2,128)S(1)}, s32[8,2]{0,1:T(2,128)}, u32[]{:S(2)}) copy-start(s32[8,2]{0,1:T(2,128)} %param.7) | copy-start | bytes 196
  55.1 13.8 %collective-permute-start.6 = (bf16[8,4,32,256]{3,2,1,0:T(8,128)(2,1)S(1)}, bf16[8,4,32,256]{3,2,1,0:T(8,128)(2,1)S(1)}, u32[]{:S(2)}, u32[]{:S(2)}) collective-permute-start(bf16[8,4,32,256]{3,2,1,0:T(8,128)(2,1)S(1)} %get-tuple-element.25), channel_id=1, source_target_pairs={{0,32},{32,64},{64,96},{1,33},{33,65},{65,97},{2,34},{34,66},{66,9... | collective-permute-start | bytes 1572872 | tf_op jit(solution)/shard_map/ppermute | solution.py:406
  62.8 12.0 %collective-permute-start.7 = (bf16[8,4,32,256]{3,2,1,0:T(8,128)(2,1)S(1)}, bf16[8,4,32,256]{3,2,1,0:T(8,128)(2,1)S(1)}, u32[]{:S(2)}, u32[]{:S(2)}) collective-permute-start(bf16[8,4,32,256]{3,2,1,0:T(8,128)(2,1)S(1)} %get-tuple-element.26), channel_id=1, source_target_pairs={{32,0},{64,32},{96,64},{33,1},{65,33},{97,65},{34,2},{66,34},{98,6... | collective-permute-start | bytes 1572872 | tf_op jit(solution)/shard_map/ppermute | solution.py:407
  64.7 1.5 %collective-permute-start.5 = (f32[3,2,128]{2,1,0:T(2,128)S(1)}, f32[3,2,128]{2,1,0:T(2,128)S(1)}, u32[]{:S(2)}, u32[]{:S(2)}) collective-permute-start(f32[3,2,128]{2,1,0:T(2,128)S(1)} %get-tuple-element.24), channel_id=1, source_target_pairs={{0,32},{32,0},{1,33},{33,1},{2,34},{34,2},{3,35},{35,3},{4,36},{36... | collective-permute-start | bytes 9224 | tf_op jit(solution)/shard_map/ppermute | solution.py:426
  76.6 37.5 %collective-permute-start.9 = (bf16[8,160,256]{2,1,0:T(8,128)(2,1)}, bf16[8,160,256]{2,1,0:T(8,128)(2,1)}, u32[]{:S(2)}, u32[]{:S(2)}) collective-permute-start(bf16[8,160,256]{2,1,0:T(8,128)(2,1)} %pad_maximum_fusion.1), channel_id=1, source_target_pairs={{1,0},{2,1},{3,2},{4,3},{5,4},{6,5},{7,6},{8,7},{9,8},{10,9},{11,1... | collective-permute-start | bytes 1966088 | tf_op jit(solution)/shard_map/ppermute | solution.py:421
  96.9 17.2 %collective-permute-start.8 = (bf16[8,160,256]{2,1,0:T(8,128)(2,1)}, bf16[8,160,256]{2,1,0:T(8,128)(2,1)S(1)}, u32[]{:S(2)}, u32[]{:S(2)}) collective-permute-start(bf16[8,160,256]{2,1,0:T(8,128)(2,1)} %pad_maximum_fusion), channel_id=1, source_target_pairs={{0,1},{1,2},{2,3},{3,4},{4,5},{5,6},{6,7},{7,8},{8,9},{9,10},{10,1... | collective-permute-start | bytes 1966088 | tf_op jit(solution)/shard_map/ppermute | solution.py:420
  96.9 16.8 %all-to-all-start.1 = ((f32[64,2,2,128]{3,2,1,0:T(2,128)}), f32[64,2,2,128]{3,2,1,0:T(2,128)S(1)}, u32[]{:S(2)}, u32[]{:S(2)}) async-start(f32[64,2,2,128]{3,2,1,0:T(2,128)} %broadcast_in_dim.8.mine_ref), calls=%async_computation.1 | async-start | bytes 262144 | tf_op jit(solution)/shard_map/all_to_all | solution.py:462
  105.1 9.0 %copy-start.2 = (bf16[3,3,256,256]{3,2,1,0:T(8,128)(2,1)S(1)}, bf16[3,3,256,256]{3,2,1,0:T(8,128)(2,1)}, u32[]{:S(2)}) copy-start(bf16[3,3,256,256]{3,2,1,0:T(8,128)(2,1)} %param.9) | copy-start | bytes 3538948

commit v11 on v6

--- a/solution.py
+++ b/solution.py
@@ -423,18 +423,19 @@
     return left, right
 
 
-def merge_cores(local):
+def merge_cores(local, edges):
     other = lax.ppermute(local, "core", [(0, 1), (1, 0)])
+    other, *edges = lax.optimization_barrier((other, *edges))
     own_count, other_count = local[2], other[2]
     both = jnp.maximum(own_count + other_count, 1.0)
     gap = local[0] / jnp.maximum(own_count, 1.0) - other[0] / jnp.maximum(other_count, 1.0)
     squares = local[1] + other[1] + gap * gap * (own_count * other_count / both)
     merged = jnp.stack([local[0] + other[0], squares])
-    return jnp.broadcast_to(merged[None], (lax.axis_size(CHIPS), *merged.shape))
+    return jnp.broadcast_to(merged[None], (lax.axis_size(CHIPS), *merged.shape)), edges
 
 
 def exchange(local, edges, points, x):
-    mine = merge_cores(local)
+    mine, edges = merge_cores(local, edges)
     top, bottom = exchange_rows(edges)
     norm = combine_statistics(lax.all_to_all(mine, CHIPS, 0, 0), points, x)
     return norm, (top, bottom, *exchange_columns(edges, top, bottom))

time: 114 us -> 117 us (1.026)
  waiting for transfers between devices: 19.6 us -> 21.9 us
    ppermute x2, starting transfers between devices: 1.59 us -> 4.88 us  [merge_cores(): other = lax.ppermute(local, 'core', [(0, 1), (1, 0)])]
    ppermute x2, starting transfers between devices: 13.2 us -> 10.5 us  [exchange_rows(): top = lax.ppermute(edges[1], LAT, [(i, i + 1) for i in range(lat - 1)])]
    ppermute x2, waiting for transfers between devices: 0.01 us -> 1.85 us  [merge_cores(): other = lax.ppermute(local, 'core', [(0, 1), (1, 0)])]
  transfers between devices with their start and end apart: 12 -> 12, of which waited for: 5 -> 6; matrix products, arithmetic and copies ran while one was open for 5% -> 5% of each run, Pallas kernels for 1% -> 1%
where the time goes in v11:
time: 117 us; the launch traced here: 116 us
  starting transfers between devices  46.6 us (40%)
  Pallas kernels  41.5 us (35%)
  waiting for transfers between devices  21.9 us (19%)
  other arithmetic  3.65 us (3%)
  local copies, waits for them, and re-layouts  1.75 us (1%)
    pallas_call x2, Pallas kernels, convolve(): pl.pallas_call(functools.partial(conv_kernel, d, CHUNK, which, with_stats...  34.1 us
    ppermute x2, waiting for transfers between devices, exchange_columns(): lax.ppermute(packed(edges[3], width - d, width), LON, [(i, (i + 1) % lon)...  16.6 us
    all_to_all x2, starting transfers between devices, exchange(): norm = combine_statistics(lax.all_to_all(mine, CHIPS, 0, 0), points, x)  15.8 us
    ppermute x2, starting transfers between devices, exchange_rows(): top = lax.ppermute(edges[1], LAT, [(i, i + 1) for i in range(lat - 1)])  10.5 us
    ppermute x2, starting transfers between devices, exchange_columns(): lax.ppermute(packed(edges[2], 0, d), LON, [((i + 1) % lon, i) for i in ra...  10.4 us
    pallas_call x1, Pallas kernels, local_statistics(): pl.pallas_call(stats_kernel, out_shape=[jax.ShapeDtypeStruct(shape, jnp.f...  6.73 us
    ppermute x2, starting transfers between devices, merge_cores(): other = lax.ppermute(local, 'core', [(0, 1), (1, 0)])  4.88 us
    ppermute x2, starting transfers between devices, exchange_rows(): bottom = lax.ppermute(edges[0], LAT, [(i + 1, i) for i in range(lat - 1)])  3.84 us
  transfers between devices with their start and end apart: 12, of which 6 were waited for; matrix products, arithmetic and copies ran while one was open for 5% of the time, Pallas kernels for 1%

profile of v11, /device:TPU:1, one launch (start us, length us, event | category | flops | bytes accessed | tf_op | source)
XLA Modules:
  0.0 115.8 jit_solution(5772947539291632489)
XLA Ops:
  0.0 6.7 %stats.1 = (f32[3,2,128]{2,1,0:T(2,128)}, bf16[8,2,32,256]{3,2,1,0:T(8,128)(2,1)}, bf16[8,2,32,256]{3,2,1,0:T(8,128)(2,1)}, bf16[8,64,256]{2,1,0:T(8,128)(2,1)}, bf16[8,64,256]{2,1,0:T(8,128)(2,1)}) custom-call(s32[128]{0:T(128)} %points_ref.5, bf16[8,32,32,256]{3,2,1,0:T(8,128)(2,1)} %refs_0_.1), custom_call_target="tpu_custom_call" | custom-call | flops 16777216 | bytes 4194304 | tf_op jit(solution)/shard_map/stats/pallas_call | solution.py:173
  6.7 0.0 copy-start.4
  6.7 0.0 copy-start
  6.8 1.5 %collective-permute-start = (f32[3,2,128]{2,1,0:T(2,128)}, f32[3,2,128]{2,1,0:T(2,128)S(1)}, u32[]{:S(2)}, u32[]{:S(2)}) collective-permute-start(f32[3,2,128]{2,1,0:T(2,128)} %get-tuple-element.26), channel_id=1, source_target_pairs={{0,32},{32,0},{1,33},{33,1},{2,34},{34,2},{3,35},{35,3},{4,36},{36... | collective-permute-start | bytes 9224 | tf_op jit(solution)/shard_map/ppermute | solution.py:427
  8.3 1.0 collective-permute-done
  9.3 5.8 %collective-permute-start.1 = (bf16[8,2,32,256]{3,2,1,0:T(8,128)(2,1)}, bf16[8,2,32,256]{3,2,1,0:T(8,128)(2,1)S(1)}, u32[]{:S(2)}, u32[]{:S(2)}) collective-permute-start(bf16[8,2,32,256]{3,2,1,0:T(8,128)(2,1)} %get-tuple-element.32), channel_id=1, source_target_pairs={{0,32},{32,64},{64,96},{1,33},{33,65},{65,97},{2,34},{34,66},{66,9... | collective-permute-start | bytes 786440 | tf_op jit(solution)/shard_map/ppermute | solution.py:407
  15.1 1.9 %collective-permute-start.2 = (bf16[8,2,32,256]{3,2,1,0:T(8,128)(2,1)}, bf16[8,2,32,256]{3,2,1,0:T(8,128)(2,1)S(1)}, u32[]{:S(2)}, u32[]{:S(2)}) collective-permute-start(bf16[8,2,32,256]{3,2,1,0:T(8,128)(2,1)} %get-tuple-element.33), channel_id=1, source_target_pairs={{32,0},{64,32},{96,64},{33,1},{65,33},{97,65},{34,2},{66,34},{98,6... | collective-permute-start | bytes 786440 | tf_op jit(solution)/shard_map/ppermute | solution.py:408
  17.0 0.7 slice_add_fusion.1
  17.7 0.7 broadcast_in_dim.6
  18.4 8.1 %all-to-all-start = ((f32[64,2,2,128]{3,2,1,0:T(2,128)}), f32[64,2,2,128]{3,2,1,0:T(2,128)S(1)}, u32[]{:S(2)}, u32[]{:S(2)}) async-start(f32[64,2,2,128]{3,2,1,0:T(2,128)} %broadcast_in_dim.6), calls=%async_computation | async-start | bytes 262144 | tf_op jit(solution)/shard_map/all_to_all | solution.py:440
  26.6 0.0 collective-permute-done.1.refs_1_
  26.6 0.0 collective-permute-done.2.refs_2_
  26.7 1.0 pad_maximum_fusion.2
  27.8 1.1 collective-permute-start.3
  28.9 0.0 copy-done.4
  28.9 0.1 pad_maximum_fusion.3
  29.0 4.7 %collective-permute-start.4 = (bf16[8,72,256]{2,1,0:T(8,128)(2,1)S(1)}, bf16[8,72,256]{2,1,0:T(8,128)(2,1)S(1)}, u32[]{:S(2)}, u32[]{:S(2)}) collective-permute-start(bf16[8,72,256]{2,1,0:T(8,128)(2,1)S(1)} %pad_maximum_fusion.3), channel_id=1, source_target_pairs={{1,0},{2,1},{3,2},{4,3},{5,4},{6,5},{7,6},{8,7},{9,8},{10,9},{11,1... | collective-permute-start | bytes 884744 | tf_op jit(solution)/shard_map/ppermute | solution.py:422
  33.7 1.9 %all-to-all-done.parts_ref = f32[64,2,2,128]{3,2,1,0:T(2,128)S(1)} async-done(((f32[64,2,2,128]{3,2,1,0:T(2,128)}), f32[64,2,2,128]{3,2,1,0:T(2,128)S(1)}, u32[]{:S(2)}, u32[]{:S(2)}) %all-to-all-start) | async-done | bytes 131104 | tf_op jit(solution)/shard_map/all_to_all | solution.py:440
  35.6 0.0 copy-done
  35.6 0.0 copy-start.1
  35.6 0.0 copy-start.3
  35.6 0.4 norm.2.norm_ref
  35.9 3.0 %collective-permute-done.3.refs_3_ = bf16[8,72,256]{2,1,0:T(8,128)(2,1)S(1)} collective-permute-done((bf16[8,72,256]{2,1,0:T(8,128)(2,1)S(1)}, bf16[8,72,256]{2,1,0:T(8,128)(2,1)S(1)}, u32[]{:S(2)}, u32[]{:S(2)}) %collective-permute-start.3) | collective-permute-done | bytes 294944 | tf_op jit(solution)/shard_map/ppermute | solution.py:421
  38.9 0.0 collective-permute-done.4.refs_4_
  38.9 0.0 copy-done.1
  38.9 0.0 copy-done.3
  38.9 17.5 %conv2.1 = (bf16[8,32,32,256]{3,2,1,0:T(8,128)(2,1)}, f32[3,2,128]{2,1,0:T(2,128)S(1)}, bf16[8,4,32,256]{3,2,1,0:T(8,128)(2,1)S(1)}, bf16[8,4,32,256]{3,2,1,0:T(...) custom-call(s32[128]{0:T(128)S(1)} %copy-done, s32[2,8]{1,0:T(2,128)S(1)} %bitcast.8, ...), custom_call_target="tpu_custom_call" | custom-call | flops 9663676416 | bytes 10485760 | tf_op jit(solution)/shard_map/conv2/pallas_call | solution.py:380
  56.4 3.4 %collective-permute-start.5 = (f32[3,2,128]{2,1,0:T(2,128)S(1)}, f32[3,2,128]{2,1,0:T(2,128)S(1)}, u32[]{:S(2)}, u32[]{:S(2)}) collective-permute-start(f32[3,2,128]{2,1,0:T(2,128)S(1)} %get-tuple-element.36), channel_id=1, source_target_pairs={{0,32},{32,0},{1,33},{33,1},{2,34},{34,2},{3,35},{35,3},{4,36},{36... | collective-permute-start | bytes 9224 | tf_op jit(solution)/shard_map/ppermute | solution.py:427
  59.8 0.8 collective-permute-done.5
  60.6 4.7 %collective-permute-start.6 = (bf16[8,4,32,256]{3,2,1,0:T(8,128)(2,1)S(1)}, bf16[8,4,32,256]{3,2,1,0:T(8,128)(2,1)S(1)}, u32[]{:S(2)}, u32[]{:S(2)}) collective-permute-start(bf16[8,4,32,256]{3,2,1,0:T(8,128)(2,1)S(1)} %get-tuple-element.43), channel_id=1, source_target_pairs={{0,32},{32,64},{64,96},{1,33},{33,65},{65,97},{2,34},{34,66},{66,9... | collective-permute-start | bytes 1572872 | tf_op jit(solution)/shard_map/ppermute | solution.py:407
  65.4 1.9 %collective-permute-start.7 = (bf16[8,4,32,256]{3,2,1,0:T(8,128)(2,1)S(1)}, bf16[8,4,32,256]{3,2,1,0:T(8,128)(2,1)S(1)}, u32[]{:S(2)}, u32[]{:S(2)}) collective-permute-start(bf16[8,4,32,256]{3,2,1,0:T(8,128)(2,1)S(1)} %get-tuple-element.44), channel_id=1, source_target_pairs={{32,0},{64,32},{96,64},{33,1},{65,33},{97,65},{34,2},{66,34},{98,6... | collective-permute-start | bytes 1572872 | tf_op jit(solution)/shard_map/ppermute | solution.py:408
  67.3 0.7 broadcast_in_dim.8
  68.0 7.7 %all-to-all-start.1 = ((f32[64,2,2,128]{3,2,1,0:T(2,128)}), f32[64,2,2,128]{3,2,1,0:T(2,128)S(1)}, u32[]{:S(2)}, u32[]{:S(2)}) async-start(f32[64,2,2,128]{3,2,1,0:T(2,128)} %broadcast_in_dim.8), calls=%async_computation.1 | async-start | bytes 262144 | tf_op jit(solution)/shard_map/all_to_all | solution.py:440
  75.7 0.0 collective-permute-done.6.refs_1_
  75.7 0.1 fusion
  75.8 1.5 %collective-permute-done.7.refs_2_ = bf16[8,4,32,256]{3,2,1,0:T(8,128)(2,1)S(1)} collective-permute-done((bf16[8,4,32,256]{3,2,1,0:T(8,128)(2,1)S(1)}, bf16[8,4,32,256]{3,2,1,0:T(8,128)(2,1)S(1)}, u32[]{:S(2)}, u32[]{:S(2)}) %collective-permute-start.7) | collective-permute-done | bytes 524320 | tf_op jit(solution)/shard_map/ppermute | solution.py:408
  77.4 0.1 fusion.1
  77.4 0.9 pad_maximum_fusion
  78.4 0.1 collective-permute-start.8
  78.5 0.9 pad_maximum_fusion.1
  79.4 0.0 copy-start.2
  79.4 5.7 %collective-permute-start.9 = (bf16[8,160,256]{2,1,0:T(8,128)(2,1)}, bf16[8,160,256]{2,1,0:T(8,128)(2,1)S(1)}, u32[]{:S(2)}, u32[]{:S(2)}) collective-permute-start(bf16[8,160,256]{2,1,0:T(8,128)(2,1)} %pad_maximum_fusion.1), channel_id=1, source_target_pairs={{1,0},{2,1},{3,2},{4,3},{5,4},{6,5},{7,6},{8,7},{9,8},{10,9},{11,1... | collective-permute-start | bytes 1966088 | tf_op jit(solution)/shard_map/ppermute | solution.py:422
  85.0 0.0 all-to-all-done.1.parts_ref
  85.0 0.4 norm.3.norm_ref
  85.4 13.6 %collective-permute-done.8.refs_3_ = bf16[8,160,256]{2,1,0:T(8,128)(2,1)} collective-permute-done((bf16[8,160,256]{2,1,0:T(8,128)(2,1)}, bf16[8,160,256]{2,1,0:T(8,128)(2,1)}, u32[]{:S(2)}, u32[]{:S(2)}) %collective-permute-start.8) | collective-permute-done | bytes 655392 | tf_op jit(solution)/shard_map/ppermute | solution.py:421
  99.1 0.0 collective-permute-done.9.refs_4_
  99.1 0.0 copy-done.2
  99.1 16.6 %conv4.1 = bf16[8,32,32,256]{3,2,1,0:T(8,128)(2,1)} custom-call(s32[128]{0:T(128)S(1)} %copy-done, s32[2,8]{1,0:T(2,128)S(1)} %bitcast.9, f32[2,8,256]{2,1,0:T(8,128)S(1)} %norm.3.norm_ref, bf16[8,32,32,256]{3,2,1,0:T(8,128)(2,1)} %get-tuple-element.42.refs_0_, bf16[8,4,32,256]{3,2,1,0:T(8,128)(2,1)S(1)} %collective-permute-done.6.refs_1_, ...), custom_call_target="tpu_custom_call" | custom-call | flops 9663676416 | bytes 10485760 | tf_op jit(solution)/shard_map/conv4/pallas_call | solution.py:380
  (13 shorter events, 0.2 us)
Async XLA Ops:
  6.7 22.1 %copy-start.4 = (bf16[8,64,256]{2,1,0:T(8,128)(2,1)S(1)}, bf16[8,64,256]{2,1,0:T(8,128)(2,1)}, u32[]{:S(2)}) copy-start(bf16[8,64,256]{2,1,0:T(8,128)(2,1)} %get-tuple-element.35) | copy-start | bytes 786436
  6.7 28.8 %copy-start = (s32[128]{0:T(128)S(1)}, s32[128]{0:T(128)}, u32[]{:S(2)}) copy-start(s32[128]{0:T(128)} %points_ref.5) | copy-start | bytes 1540
  6.8 2.5 %collective-permute-start = (f32[3,2,128]{2,1,0:T(2,128)}, f32[3,2,128]{2,1,0:T(2,128)S(1)}, u32[]{:S(2)}, u32[]{:S(2)}) collective-permute-start(f32[3,2,128]{2,1,0:T(2,128)} %get-tuple-element.26), channel_id=1, source_target_pairs={{0,32},{32,0},{1,33},{33,1},{2,34},{34,2},{3,35},{35,3},{4,36},{36... | collective-permute-start | bytes 9224 | tf_op jit(solution)/shard_map/ppermute | solution.py:427
  9.3 17.3 %collective-permute-start.1 = (bf16[8,2,32,256]{3,2,1,0:T(8,128)(2,1)}, bf16[8,2,32,256]{3,2,1,0:T(8,128)(2,1)S(1)}, u32[]{:S(2)}, u32[]{:S(2)}) collective-permute-start(bf16[8,2,32,256]{3,2,1,0:T(8,128)(2,1)} %get-tuple-element.32), channel_id=1, source_target_pairs={{0,32},{32,64},{64,96},{1,33},{33,65},{65,97},{2,34},{34,66},{66,9... | collective-permute-start | bytes 786440 | tf_op jit(solution)/shard_map/ppermute | solution.py:407
  15.1 11.5 %collective-permute-start.2 = (bf16[8,2,32,256]{3,2,1,0:T(8,128)(2,1)}, bf16[8,2,32,256]{3,2,1,0:T(8,128)(2,1)S(1)}, u32[]{:S(2)}, u32[]{:S(2)}) collective-permute-start(bf16[8,2,32,256]{3,2,1,0:T(8,128)(2,1)} %get-tuple-element.33), channel_id=1, source_target_pairs={{32,0},{64,32},{96,64},{33,1},{65,33},{97,65},{34,2},{66,34},{98,6... | collective-permute-start | bytes 786440 | tf_op jit(solution)/shard_map/ppermute | solution.py:408
  18.4 17.1 %all-to-all-start = ((f32[64,2,2,128]{3,2,1,0:T(2,128)}), f32[64,2,2,128]{3,2,1,0:T(2,128)S(1)}, u32[]{:S(2)}, u32[]{:S(2)}) async-start(f32[64,2,2,128]{3,2,1,0:T(2,128)} %broadcast_in_dim.6), calls=%async_computation | async-start | bytes 262144 | tf_op jit(solution)/shard_map/all_to_all | solution.py:440
  27.8 11.1 %collective-permute-start.3 = (bf16[8,72,256]{2,1,0:T(8,128)(2,1)S(1)}, bf16[8,72,256]{2,1,0:T(8,128)(2,1)S(1)}, u32[]{:S(2)}, u32[]{:S(2)}) collective-permute-start(bf16[8,72,256]{2,1,0:T(8,128)(2,1)S(1)} %pad_maximum_fusion.2), channel_id=1, source_target_pairs={{0,1},{1,2},{2,3},{3,4},{4,5},{5,6},{6,7},{7,8},{8,9},{9,10},{10,1... | collective-permute-start | bytes 884744 | tf_op jit(solution)/shard_map/ppermute | solution.py:421
  29.0 10.0 %collective-permute-start.4 = (bf16[8,72,256]{2,1,0:T(8,128)(2,1)S(1)}, bf16[8,72,256]{2,1,0:T(8,128)(2,1)S(1)}, u32[]{:S(2)}, u32[]{:S(2)}) collective-permute-start(bf16[8,72,256]{2,1,0:T(8,128)(2,1)S(1)} %pad_maximum_fusion.3), channel_id=1, source_target_pairs={{1,0},{2,1},{3,2},{4,3},{5,4},{6,5},{7,6},{8,7},{9,8},{10,9},{11,1... | collective-permute-start | bytes 884744 | tf_op jit(solution)/shard_map/ppermute | solution.py:422
  35.6 3.3 %copy-start.1 = (bf16[3,3,256,256]{3,2,1,0:T(8,128)(2,1)S(1)}, bf16[3,3,256,256]{3,2,1,0:T(8,128)(2,1)}, u32[]{:S(2)}) copy-start(bf16[3,3,256,256]{3,2,1,0:T(8,128)(2,1)} %param.8) | copy-start | bytes 3538948
  35.6 3.3 %copy-start.3 = (s32[8,2]{0,1:T(2,128)S(1)}, s32[8,2]{0,1:T(2,128)}, u32[]{:S(2)}) copy-start(s32[8,2]{0,1:T(2,128)} %param.7) | copy-start | bytes 196
  56.4 4.2 %collective-permute-start.5 = (f32[3,2,128]{2,1,0:T(2,128)S(1)}, f32[3,2,128]{2,1,0:T(2,128)S(1)}, u32[]{:S(2)}, u32[]{:S(2)}) collective-permute-start(f32[3,2,128]{2,1,0:T(2,128)S(1)} %get-tuple-element.36), channel_id=1, source_target_pairs={{0,32},{32,0},{1,33},{33,1},{2,34},{34,2},{3,35},{35,3},{4,36},{36... | collective-permute-start | bytes 9224 | tf_op jit(solution)/shard_map/ppermute | solution.py:427
  60.6 15.1 %collective-permute-start.6 = (bf16[8,4,32,256]{3,2,1,0:T(8,128)(2,1)S(1)}, bf16[8,4,32,256]{3,2,1,0:T(8,128)(2,1)S(1)}, u32[]{:S(2)}, u32[]{:S(2)}) collective-permute-start(bf16[8,4,32,256]{3,2,1,0:T(8,128)(2,1)S(1)} %get-tuple-element.43), channel_id=1, source_target_pairs={{0,32},{32,64},{64,96},{1,33},{33,65},{65,97},{2,34},{34,66},{66,9... | collective-permute-start | bytes 1572872 | tf_op jit(solution)/shard_map/ppermute | solution.py:407
  65.4 12.0 %collective-permute-start.7 = (bf16[8,4,32,256]{3,2,1,0:T(8,128)(2,1)S(1)}, bf16[8,4,32,256]{3,2,1,0:T(8,128)(2,1)S(1)}, u32[]{:S(2)}, u32[]{:S(2)}) collective-permute-start(bf16[8,4,32,256]{3,2,1,0:T(8,128)(2,1)S(1)} %get-tuple-element.44), channel_id=1, source_target_pairs={{32,0},{64,32},{96,64},{33,1},{65,33},{97,65},{34,2},{66,34},{98,6... | collective-permute-start | bytes 1572872 | tf_op jit(solution)/shard_map/ppermute | solution.py:408
  68.0 17.0 %all-to-all-start.1 = ((f32[64,2,2,128]{3,2,1,0:T(2,128)}), f32[64,2,2,128]{3,2,1,0:T(2,128)S(1)}, u32[]{:S(2)}, u32[]{:S(2)}) async-start(f32[64,2,2,128]{3,2,1,0:T(2,128)} %broadcast_in_dim.8), calls=%async_computation.1 | async-start | bytes 262144 | tf_op jit(solution)/shard_map/all_to_all | solution.py:440
  78.4 20.7 %collective-permute-start.8 = (bf16[8,160,256]{2,1,0:T(8,128)(2,1)}, bf16[8,160,256]{2,1,0:T(8,128)(2,1)}, u32[]{:S(2)}, u32[]{:S(2)}) collective-permute-start(bf16[8,160,256]{2,1,0:T(8,128)(2,1)} %pad_maximum_fusion), channel_id=1, source_target_pairs={{0,1},{1,2},{2,3},{3,4},{4,5},{5,6},{6,7},{7,8},{8,9},{9,10},{10,1... | collective-permute-start | bytes 1966088 | tf_op jit(solution)/shard_map/ppermute | solution.py:421
  79.4 19.7 %copy-start.2 = (bf16[3,3,256,256]{3,2,1,0:T(8,128)(2,1)S(1)}, bf16[3,3,256,256]{3,2,1,0:T(8,128)(2,1)}, u32[]{:S(2)}) copy-start(bf16[3,3,256,256]{3,2,1,0:T(8,128)(2,1)} %param.9) | copy-start | bytes 3538948
  79.4 19.7 %collective-permute-start.9 = (bf16[8,160,256]{2,1,0:T(8,128)(2,1)}, bf16[8,160,256]{2,1,0:T(8,128)(2,1)S(1)}, u32[]{:S(2)}, u32[]{:S(2)}) collective-permute-start(bf16[8,160,256]{2,1,0:T(8,128)(2,1)} %pad_maximum_fusion.1), channel_id=1, source_target_pairs={{1,0},{2,1},{3,2},{4,3},{5,4},{6,5},{7,6},{8,7},{9,8},{10,9},{11,1... | collective-permute-start | bytes 1966088 | tf_op jit(solution)/shard_map/ppermute | solution.py:422
